TPU v7x, 256 devices: a whole 4x4x8 slice. The times are simulated.
256 devices in a mesh: rel: 8 (over x_lo, y), tgt: 32 (over x_hi, z, core).
Axes of the slice: x: 4 (x_hi: 2, x_lo: 2; x = x_hi * 2 + x_lo), y: 4, z: 8, core: 2. Of those that a mesh axis runs over, the one named last changes fastest.
Arguments:
- features: bfloat16 [8192, 768], P('tgt'), may hold values from -6 to 6
- weights: bfloat16 [16, 768, 768], P('rel'), may hold values from -0.109375 to 0.109375
- bias: float32 [768], replicated, may hold values from -3 to 3
- cotangent: bfloat16 [8192, 768], P('tgt'), may hold values from -0.52734375 to 0.52734375
- tile_values: int32 [16, 8192, 8, 128], P('rel', 'tgt'), may hold values from 0 to 3, as said below
- tile_count: int32 [16, 64], P('rel', 'tgt'), may hold values from 1 to 8, as said below
- tile_slot: int32 [16, 64, 8], P('rel', 'tgt'), may hold values from 0 to 31, as said below
- source_blocks: int32 [32, 32], replicated, may hold values from -1 to 1, as said below
Outputs:
- output: bfloat16 [8192, 768], P('tgt', 'rel')
- grad_weights: float32 [16, 768, 768], P('rel', 'tgt')
- grad_features: float32 [64, 128, 768], P('tgt', 'rel')
Inputs may be any that keep to these rules, and one draw needn't show every extreme that they name: `tile_values`: entries in tile slots at or beyond the live count are arbitrary and take no part. `tile_count`: every relation has some tile row of targets with all 8 slots live. `tile_slot`: every tile slot, live or not, names an owner for which the target block's entry of source_blocks is not -1. `source_blocks`: entry [t, o] is a block index within owner o's 2 blocks, or -1 where target block t reads nothing from o; entry [t, t] is never -1.
All inputs are finite; a program needn't handle non-finite values.
Results may differ from a plain program's by a relative error of at most 0.01.
Values may be sent and summed in bfloat16 or wider, within the bound.
No kernel may reach another device: no remote copies, remote signals or barrier semaphores. Data moves between devices by JAX's collectives and lax.ppermute only.
A program may use at most 64 MiB of HBM per device.

v0:
```python
import jax
import jax.numpy as jnp
from jax import lax
from jax.sharding import PartitionSpec as P


def copy_for_each(value, axis):
    peers = lax.axis_size(axis)
    return lax.all_to_all(
        jnp.broadcast_to(value[None], (peers, *value.shape)), axis, 0, 0, tiled=True
    )


def of_everyone(value, axis):
    everything = copy_for_each(value, axis)
    return jnp.sum(everything, axis=0)


def split_up(value, dim, peers):
    before, after = (value.shape[:dim], value.shape[dim + 1 :])
    return jnp.moveaxis(value.reshape(*before, peers, -1, *after), dim, 0)


def sum_at_owner(value, axis, dim):
    blocks = split_up(value, dim, lax.axis_size(axis))
    arrived = lax.all_to_all(blocks, axis, split_axis=0, concat_axis=0, tiled=True)
    return arrived.sum(axis=0)


def silu_pair(values):
    sigmoid = jax.nn.sigmoid(values)
    return (values * sigmoid, sigmoid * (1.0 + values * (1.0 - sigmoid)))


def padded_messages(adjacency, fetched, tile_slot):
    sources = fetched[tile_slot]
    return jnp.einsum("rqisc,rqscd->rqid", adjacency, sources, preferred_element_type=jnp.float32)


def padded_partials(adjacency, grads_blocked, tile_slot, owners):
    owner_ids = jnp.arange(owners, dtype=jnp.int32)
    summed = None
    for relation in range(adjacency.shape[0]):
        contrib = jnp.einsum(
            "qisc,qid->qscd",
            adjacency[relation],
            grads_blocked[relation],
            preferred_element_type=jnp.float32,
        )
        selector = (tile_slot[relation][..., None] == owner_ids).astype(jnp.float32)
        addend = jnp.einsum("qso,qscd->ocd", selector, contrib, precision=lax.Precision.HIGHEST)
        summed = addend if summed is None else summed + addend
    return summed


def per_device(
    features, weights, bias, cotangent, tile_values, tile_count, tile_slot, source_blocks
):
    owners = lax.axis_size("tgt")
    groups = lax.axis_size("rel")
    target_rows = features.shape[0]
    model_width = features.shape[1]
    relations = tile_values.shape[0]
    slot_total = tile_values.shape[2]
    block_rows = tile_values.shape[3]
    sections = target_rows // block_rows
    own_blocks = features.reshape(sections, block_rows, model_width)
    requested = lax.dynamic_index_in_dim(source_blocks, lax.axis_index("tgt"), 1, keepdims=False)
    listed = requested >= 0
    chosen = jnp.maximum(requested, 0)
    piece_rows = block_rows // groups
    first_row = lax.axis_index("rel") * piece_rows
    own_piece = lax.dynamic_slice_in_dim(own_blocks, first_row, piece_rows, 1)
    outgoing = jnp.where(listed[:, None, None], own_piece[chosen], jnp.zeros((), features.dtype))
    arrived = lax.all_to_all(outgoing, "tgt", split_axis=0, concat_axis=0, tiled=True)
    fetched = lax.all_gather(arrived, "rel", axis=1, tiled=True)
    live_mask = (
        jnp.arange(slot_total, dtype=jnp.int32)[None, None, :] < tile_count[:, :, None]
    ).astype(jnp.int32)
    counted = (
        tile_values.reshape(relations, sections, block_rows, slot_total, block_rows)
        * live_mask[:, :, None, :, None]
    )
    degree = jnp.sum(counted, axis=(3, 4)).astype(jnp.float32)
    adjacency = (
        counted.astype(jnp.float32) / jnp.sqrt(jnp.maximum(degree, 1.0))[..., None, None]
    ).astype(jnp.bfloat16)
    gathered_sum = padded_messages(adjacency, fetched, tile_slot)
    messages = gathered_sum.astype(jnp.bfloat16).reshape(relations, target_rows, model_width)
    partial_pre = jnp.einsum("rnd,rde->ne", messages, weights, preferred_element_type=jnp.float32)
    column_count = model_width // groups
    first_column = lax.axis_index("rel") * column_count
    preact_full = of_everyone(partial_pre, "rel") + bias
    activated, derivative_full = silu_pair(preact_full)
    output_share = lax.dynamic_slice_in_dim(activated, first_column, column_count, 1)
    grad_pre = (cotangent.astype(jnp.float32) * derivative_full).astype(jnp.bfloat16)
    output = output_share.astype(jnp.bfloat16)
    grad_messages = jnp.einsum(
        "ne,rde->rnd", grad_pre, weights, preferred_element_type=jnp.float32
    ).astype(jnp.bfloat16)
    weight_terms = jnp.einsum("rnd,ne->rde", messages, grad_pre, preferred_element_type=jnp.float32)
    grad_weights = lax.psum_scatter(weight_terms, "tgt", scatter_dimension=1, tiled=True)
    grads_blocked = grad_messages.reshape(relations, sections, block_rows, model_width)
    partials = padded_partials(adjacency, grads_blocked, tile_slot, owners)
    section_ids = jnp.arange(sections, dtype=jnp.int32)
    returned = lax.all_to_all(
        partials.astype(jnp.bfloat16), "tgt", split_axis=0, concat_axis=0, tiled=True
    )
    placing = (requested[:, None] == section_ids[None, :]).astype(jnp.bfloat16)
    owned = jnp.einsum("tk,tcd->kcd", placing, returned, preferred_element_type=jnp.float32)
    grad_features = sum_at_owner(owned, "rel", 1)
    return (output, grad_weights, grad_features)


def solution(mesh):
    placed = (
        P("tgt", None),
        P("rel", None, None),
        P(),
        P("tgt", None),
        P("rel", "tgt", None, None),
        P("rel", "tgt"),
        P("rel", "tgt", None),
        P(),
    )
    return jax.shard_map(
        per_device,
        mesh=mesh,
        in_specs=placed,
        out_specs=(P("tgt", "rel"), P("rel", "tgt", None), P("tgt", "rel", None)),
        check_vma=False,
    )
```

profile of v0, /device:TPU:56, one launch (start us, length us, event | category | flops | bytes accessed | tf_op | source)
XLA Modules:
  0.0 429.9 jit_solution(9492132111234932785)
XLA Ops:
  7.3 1.0 dynamic-slice_reduce_fusion
  9.9 36.0 %all_to_all.20 = bf16[32,16,768]{2,1,0:T(8,128)(2,1)} all-to-all(bf16[32,16,768]{2,1,0:T(8,128)(2,1)S(1)} %broadcast_select_fusion), channel_id=1, replica_groups=mesh['rel'=8,'tgt'=32] {'tgt'}, dimensions={0} | all-to-all | bytes 1572864 | tf_op jit(solution)/shard_map/all_to_all | solution.py:75
  45.9 2.9 copy.42
  48.9 11.5 %multiply_reduce_fusion = s32[2,256]{1,0:T(2,128)S(1)} fusion(s32[2,256,8,128]{3,2,1,0:T(8,128)} %param.12, s32[2,256,8]{2,1,0:T(8,128)S(1)} %bitcast.67), kind=kLoop, calls=%fused_computation.7 | loop fusion | flops 1048064 | bytes 2115584 | tf_op jit(solution)/shard_map/reduce_sum | solution.py:84
  60.5 2.0 divide_convert_fusion
  62.5 50.7 %all-gather.2.cloned.1.call-done = bf16[32,128,768]{2,1,0:T(8,128)(2,1)} async-done(((bf16[32,16,768]{2,1,0:T(8,128)(2,1)}), bf16[32,128,768]{2,1,0:T(8,128)(2,1)}) %all-gather.2.cloned.1.call-update) | async-done | bytes 6291472 | tf_op jit(solution)/shard_map/all_gather | solution.py:76
  113.2 6.4 %gather_fusion.1 = bf16[32,128,768]{2,1,0:T(8,128)(2,1)} fusion(bf16[32,128,768]{2,1,0:T(8,128)(2,1)} %all-gather.2.cloned.1.call-done, s32[1024]{0:T(1024)S(1)} %pad_clamp_fusion), kind=kCustom, calls=%fused_computation.1 | custom fusion | bytes 12583040 | tf_op jit(solution)/shard_map/gather | solution.py:36
  119.6 3.9 bitcast_convert_fusion
  125.2 3.2 broadcast_in_dim.19
  128.4 7.4 %all-to-all-start.1 = ((f32[8,256,768]{2,1,0:T(8,128)}), f32[8,256,768]{2,1,0:T(8,128)}, u32[]{:S(2)}, u32[]{:S(2)}) async-start(f32[8,256,768]{2,1,0:T(8,128)} %broadcast_in_dim.19), calls=%async_computation.1 | async-start | bytes 12582912 | tf_op jit(solution)/shard_map/all_to_all | solution.py:9
  136.8 68.9 %all-to-all-done.1 = f32[8,256,768]{2,1,0:T(8,128)} async-done(((f32[8,256,768]{2,1,0:T(8,128)}), f32[8,256,768]{2,1,0:T(8,128)}, u32[]{:S(2)}, u32[]{:S(2)}) %all-to-all-start.1) | async-done | bytes 6291488 | tf_op jit(solution)/shard_map/all_to_all | solution.py:9
  205.8 4.1 reduce_sum.28
  209.9 2.3 add_divide_fusion
  214.2 5.2 %fusion.11 = f32[32,128,768,1]{2,0,3,1:T(8,128)S(1)} fusion(f32[2,8,128,768]{3,1,0,2:T(8,128)S(1)} %fusion.6, s32[2,8]{1,0:T(2,128)S(1)} %get-tuple-element.21), kind=kOutput, calls=%fused_computation.30 | convolution fusion | flops 603980288 | bytes 18874432 | tf_op jit(solution)/shard_map/qso,qscd->ocd/dot_general | solution.py:51
  220.4 8.2 %fusion = bf16[32,128,768]{2,0,1:T(8,128)(2,1)} fusion(f32[32,128,768,1]{2,0,3,1:T(8,128)S(1)} %fusion.11, f32[2,8,128,768]{3,1,0,2:T(8,128)S(1)} %fusion.4, s32[2,8]{1,0:T(2,128)S(1)} %get-tuple-element.20), kind=kOutput, calls=%fused_computation.3 | convolution fusion | flops 610271744 | bytes 25165888 | tf_op jit(solution)/shard_map/qso,qscd->ocd/dot_general | solution.py:51
  228.5 8.9 %copy.47 = bf16[32,128,768]{2,1,0:T(8,128)(2,1)} copy(bf16[32,128,768]{2,0,1:T(8,128)(2,1)} %fusion) | data formatting | bytes 12582912 | tf_op jit(solution)/shard_map/convert_element_type | solution.py:107
  237.5 9.9 %all-to-all-start.2 = ((bf16[32,128,768]{2,1,0:T(8,128)(2,1)}), bf16[32,128,768]{2,1,0:T(8,128)(2,1)}, u32[]{:S(2)}, u32[]{:S(2)}) async-start(bf16[32,128,768]{2,1,0:T(8,128)(2,1)} %copy.47), calls=%async_computation.3 | async-start | bytes 12582912 | tf_op jit(solution)/shard_map/all_to_all | solution.py:106
  247.5 3.0 fusion.22
  250.5 149.2 %all-to-all-done.2 = bf16[32,128,768]{2,1,0:T(8,128)(2,1)} async-done(((bf16[32,128,768]{2,1,0:T(8,128)(2,1)}), bf16[32,128,768]{2,1,0:T(8,128)(2,1)}, u32[]{:S(2)}, u32[]{:S(2)}) %all-to-all-start.2) | async-done | bytes 6291488 | tf_op jit(solution)/shard_map/all_to_all | solution.py:106
  399.7 8.4 %fusion.1 = f32[2,128,768]{2,0,1:T(2,128)} fusion(bf16[32,128,768]{2,1,0:T(8,128)(2,1)} %all-to-all-done.2, s32[32]{0:T(128)S(1)} %get-tuple-element.12), kind=kOutput, calls=%fused_computation.4 | convolution fusion | flops 12582976 | bytes 7078016 | tf_op jit(solution)/shard_map/tk,tcd->kcd/dot_general | solution.py:110
  408.0 5.3 %all-to-all-start.3 = ((f32[8,2,16,768]{3,1,2,0:T(2,128)}), f32[8,2,16,768]{3,1,2,0:T(2,128)}, u32[]{:S(2)}, u32[]{:S(2)}) async-start(f32[8,2,16,768]{3,1,2,0:T(2,128)} %bitcast.62), calls=%async_computation.4 | async-start | bytes 1572864 | tf_op jit(solution)/shard_map/all_to_all | solution.py:26
  413.3 1.1 fusion.9
  415.2 5.9 %all-to-all-done.3 = f32[8,2,16,768]{3,1,2,0:T(2,128)} async-done(((f32[8,2,16,768]{3,1,2,0:T(2,128)}), f32[8,2,16,768]{3,1,2,0:T(2,128)}, u32[]{:S(2)}, u32[]{:S(2)}) %all-to-all-start.3) | async-done | bytes 786464 | tf_op jit(solution)/shard_map/all_to_all | solution.py:26
  421.0 1.4 reduce_sum.29
  (46 shorter events, 8.9 us)
Async XLA Ops:
  7.2 117.2 %copy-start = (bf16[2,768,768]{2,1,0:T(8,128)(2,1)S(1)}, bf16[2,768,768]{2,1,0:T(8,128)(2,1)}, u32[]{:S(2)}) copy-start(bf16[2,768,768]{2,1,0:T(8,128)(2,1)} %param.9) | copy-start | bytes 7077892
  7.2 41.6 %copy-start.9 = (s32[2,2]{1,0:T(2,128)S(1)}, s32[2,2]{1,0:T(2,128)}, u32[]{:S(2)}) copy-start(s32[2,2]{1,0:T(2,128)} %param.13) | copy-start | bytes 52
  7.2 53.2 %copy-start.7 = (s32[2,2,8]{2,1,0:T(2,128)S(1)}, s32[2,2,8]{2,1,0:T(2,128)}, u32[]{:S(2)}) copy-start(s32[2,2,8]{2,1,0:T(2,128)} %param.14) | copy-start | bytes 388
  7.2 106.0 %all-gather.2.cloned.1.call-start = ((), (), s32[]{:S(2)}) async-start(), calls=%async_computation.5 | async-start | bytes 7077888 | tf_op jit(solution)/shard_map/all_gather | solution.py:76
  123.4 0.9 copy-start.2
  128.4 77.4 %all-to-all-start.1 = ((f32[8,256,768]{2,1,0:T(8,128)}), f32[8,256,768]{2,1,0:T(8,128)}, u32[]{:S(2)}, u32[]{:S(2)}) async-start(f32[8,256,768]{2,1,0:T(8,128)} %broadcast_in_dim.19), calls=%async_computation.1 | async-start | bytes 12582912 | tf_op jit(solution)/shard_map/all_to_all | solution.py:9
  135.8 74.1 %copy-start.8 = (f32[768]{0:T(1024)S(1)}, f32[768]{0:T(1024)}, u32[]{:S(2)}) copy-start(f32[768]{0:T(1024)} %param.10) | copy-start | bytes 9220
  136.8 75.4 %copy-start.6 = (bf16[256,768]{1,0:T(8,128)(2,1)S(1)}, bf16[256,768]{1,0:T(8,128)(2,1)}, u32[]{:S(2)}) copy-start(bf16[256,768]{1,0:T(8,128)(2,1)} %param.11) | copy-start | bytes 1179652
  209.9 3.3 copy-start.5
  214.1 5.3 %copy-start.4 = (bf16[2,128,8,128]{1,3,2,0:T(8,128)(2,1)S(1)}, bf16[2,128,8,128]{1,3,2,0:T(8,128)(2,1)}, u32[]{:S(2)}) copy-start(bf16[2,128,8,128]{1,3,2,0:T(8,128)(2,1)} %get-tuple-element.16) | copy-start | bytes 1572868
  237.5 10.0 %copy-start.3 = (bf16[2,2,128,768]{3,2,1,0:T(8,128)(2,1)S(1)}, bf16[2,2,128,768]{3,2,1,0:T(8,128)(2,1)}, u32[]{:S(2)}) copy-start(bf16[2,2,128,768]{3,2,1,0:T(8,128)(2,1)} %copy-done.2) | copy-start | bytes 2359300
  237.5 162.2 %all-to-all-start.2 = ((bf16[32,128,768]{2,1,0:T(8,128)(2,1)}), bf16[32,128,768]{2,1,0:T(8,128)(2,1)}, u32[]{:S(2)}, u32[]{:S(2)}) async-start(bf16[32,128,768]{2,1,0:T(8,128)(2,1)} %copy.47), calls=%async_computation.3 | async-start | bytes 12582912 | tf_op jit(solution)/shard_map/all_to_all | solution.py:106
  247.4 175.7 %reduce-scatter.2.cloned.1.call-start = ((), (), s32[]{:S(2)}) async-start(), calls=%async_computation.6 | async-start | bytes 4866048 | tf_op jit(solution)/shard_map/reduce_scatter | solution.py:102
  250.5 172.6 %copy-start.1 = (bf16[2,768,768]{2,1,0:T(8,128)(2,1)S(1)}, bf16[2,768,768]{2,1,0:T(8,128)(2,1)}, u32[]{:S(2)}) copy-start(bf16[2,768,768]{2,1,0:T(8,128)(2,1)} %param.9) | copy-start | bytes 7077892
  408.0 13.0 %all-to-all-start.3 = ((f32[8,2,16,768]{3,1,2,0:T(2,128)}), f32[8,2,16,768]{3,1,2,0:T(2,128)}, u32[]{:S(2)}, u32[]{:S(2)}) async-start(f32[8,2,16,768]{3,1,2,0:T(2,128)} %bitcast.62), calls=%async_computation.4 | async-start | bytes 1572864 | tf_op jit(solution)/shard_map/all_to_all | solution.py:26
Sparse Core Ops, SparseCore 0:
  46.0 67.1 all-gather.1
  253.1 168.2 reduce-scatter.1
where the time goes:
time: 438 us; the launch traced here: 430 us
  waiting for transfers between devices  275 us (63%)
  blocking collectives  36 us (8%)
  matrix products  32.2 us (7%)
  local copies, waits for them, and re-layouts  26.4 us (6%)
  other arithmetic  23.7 us (5%)
  starting transfers between devices  22.7 us (5%)
  between operations  14.3 us (3%)
    all_to_all x1, waiting for transfers between devices, per_device(): lax.all_to_all(partials.astype(jnp.bfloat16), 'tgt', split_axis=0, concat...  149 us
    all_to_all x1, waiting for transfers between devices, copy_for_each(): lax.all_to_all(jnp.broadcast_to(value[None], (peers, *value.shape)), axis...  68.9 us
    all_gather x1, waiting for transfers between devices, per_device(): fetched = lax.all_gather(arrived, 'rel', axis=1, tiled=True)  50.7 us
    all_to_all x1, blocking collectives, per_device(): lax.all_to_all(outgoing, 'tgt', split_axis=0, concat_axis=0, tiled=True)  36 us
    dot_general x2, matrix products, padded_partials(): jnp.einsum('qso,qscd->ocd', selector, contrib, precision=lax.Precision.HI...  13.4 us
    reduce_sum x1, other arithmetic, per_device(): degree = jnp.sum(counted, axis=(3, 4)).astype(jnp.float32)  11.5 us
    all_to_all x1, starting transfers between devices, per_device(): lax.all_to_all(partials.astype(jnp.bfloat16), 'tgt', split_axis=0, concat...  9.93 us
    convert_element_type x1, local copies, waits for them, and re-layouts, per_device(): partials.astype(jnp.bfloat16)  8.94 us
  transfers between devices with their start and end apart: 5, of which 4 were waited for; matrix products, arithmetic and copies ran while one was open for 8% of the time, Pallas kernels for 0%

commit v1 on v0

v1 whole, which is shorter than its diff:
```python
import jax
import jax.numpy as jnp
from jax import lax
from jax.experimental import pallas as pl
from jax.experimental.pallas import tpu as pltpu
from jax.sharding import Mesh, PartitionSpec as P

F32 = jnp.float32
BF16 = jnp.bfloat16
BLK = 128
REL = ("xl", "y")
TGT = ("xh", "z", "core")
VMEM_LIMIT = 60 * 1024 * 1024


def params(*semantics):
    return pltpu.CompilerParams(
        dimension_semantics=semantics or None, vmem_limit_bytes=VMEM_LIMIT
    )


def smem():
    return pl.BlockSpec(memory_space=pltpu.MemorySpace.SMEM)


def vmem():
    return pl.BlockSpec(memory_space=pltpu.MemorySpace.VMEM)


def dot(a, b, ca, cb):
    return lax.dot_general(a, b, (((ca,), (cb,)), ((), ())), preferred_element_type=F32)


def adjacency_kernel(count_ref, values_ref, out_ref):
    r, q = pl.program_id(0), pl.program_id(1)
    count = count_ref[r, q]
    slots = values_ref.shape[2]
    live, degree = [], None
    for s in range(slots):
        v = values_ref[0, :, s, :]
        v = jnp.where(s < count, v, jnp.zeros_like(v)).astype(F32)
        live.append(v)
        degree = v if degree is None else degree + v
    total = jnp.sum(degree, axis=1, keepdims=True)
    scale = 1.0 / jnp.sqrt(jnp.maximum(total, 1.0))
    for s in range(slots):
        out_ref[0, :, s * BLK : (s + 1) * BLK] = (live[s] * scale).astype(BF16)


def adjacency_of(tile_values, tile_count):
    rels, rows, slots, cols = tile_values.shape
    return pl.pallas_call(
        adjacency_kernel,
        grid=(rels, rows // BLK),
        in_specs=[smem(), pl.BlockSpec((1, BLK, slots, cols), lambda r, q: (r, q, 0, 0))],
        out_specs=pl.BlockSpec((1, BLK, slots * cols), lambda r, q: (r, q, 0)),
        out_shape=jax.ShapeDtypeStruct((rels, rows, slots * cols), BF16),
        compiler_params=params("arbitrary", "arbitrary"),
        name="adjacency",
    )(tile_count, tile_values)


def outgoing_kernel(place_ref, table_ref, features_ref, out_ref, turned_ref):
    owner, first = place_ref[0], place_ref[1]
    turned_ref[...] = features_ref[...].T
    piece = turned_ref[pl.ds(pl.multiple_of(first, 32), 96), :]
    block0, block1 = piece[:, :BLK], piece[:, BLK:]
    for t in range(out_ref.shape[0]):
        k = table_ref[t, owner]
        picked = jnp.where(k == 1, block1, block0)
        out_ref[t] = jnp.where(k >= 0, picked, jnp.zeros_like(picked))


def outgoing_of(features, source_blocks, place):
    rows, width = features.shape
    return pl.pallas_call(
        outgoing_kernel,
        in_specs=[smem(), smem(), vmem()],
        out_specs=vmem(),
        out_shape=jax.ShapeDtypeStruct((source_blocks.shape[0], 96, BLK), BF16),
        scratch_shapes=[pltpu.VMEM((width, rows), BF16)],
        compiler_params=params(),
        name="outgoing",
    )(place, source_blocks, features)


def relation_of(i, place):
    core = place[2]
    return jnp.where(i < 4, 2 * i + core, 2 * (i - 4) + 1 - core)


def forward_kernel(
    place_ref, slot_ref, adj_ref, mine_ref, theirs_ref, w_mine_ref, w_theirs_ref,
    messages_ref, pre_ref, fetched_ref, acc_ref,
):
    i = pl.program_id(0)
    r = relation_of(i, place_ref)
    xl = place_ref[3]
    slots = 8

    @pl.when(i == 0)
    def _():
        fetched_ref[:, pl.ds(pl.multiple_of(xl * 96, 32), 96), :] = mine_ref[...]
        fetched_ref[:, pl.ds(pl.multiple_of((1 - xl) * 96, 32), 96), :] = theirs_ref[...]

    for q in range(2):
        base = (r * 2 + q) * slots
        wide = jnp.concatenate([fetched_ref[slot_ref[base + s]] for s in range(slots)], axis=1)
        part = adj_ref[0, q * BLK : (q + 1) * BLK, :]
        messages_ref[0, :, q * BLK : (q + 1) * BLK] = dot(wide, part, 1, 1).astype(BF16)

    @pl.when(i == 0)
    def _():
        acc_ref[...] = dot(w_mine_ref[0], messages_ref[0], 0, 0)

    @pl.when((i > 0) & (i < 4))
    def _():
        acc_ref[...] += dot(w_mine_ref[0], messages_ref[0], 0, 0)

    @pl.when(i >= 4)
    def _():
        acc_ref[...] += dot(w_theirs_ref[0], messages_ref[0], 0, 0)

    @pl.when(i == 7)
    def _():
        pre_ref[...] = acc_ref[...].astype(BF16)


def forward_of(place, slots, adjacency, mine, theirs, w_mine, w_theirs):
    rels, rows, wide = adjacency.shape
    width = w_mine.shape[2]
    spec = pltpu.PrefetchScalarGridSpec(
        num_scalar_prefetch=2,
        grid=(rels,),
        in_specs=[
            pl.BlockSpec((1, rows, wide), lambda i, p, s: (relation_of(i, p), 0, 0)),
            pl.BlockSpec(mine.shape, lambda i, p, s: (0, 0, 0)),
            pl.BlockSpec(mine.shape, lambda i, p, s: (0, 0, 0)),
            pl.BlockSpec((1, 192, width), lambda i, p, s: (jnp.minimum(i, 3), 0, 0)),
            pl.BlockSpec((1, 192, width), lambda i, p, s: (jnp.maximum(i - 4, 0), 0, 0)),
        ],
        out_specs=[
            pl.BlockSpec((1, 192, rows), lambda i, p, s: (relation_of(i, p), 0, 0)),
            pl.BlockSpec((width, rows), lambda i, p, s: (0, 0)),
        ],
        scratch_shapes=[pltpu.VMEM((mine.shape[0], 192, BLK), BF16), pltpu.VMEM((width, rows), F32)],
    )
    return pl.pallas_call(
        forward_kernel,
        grid_spec=spec,
        out_shape=[
            jax.ShapeDtypeStruct((rels, 192, rows), BF16),
            jax.ShapeDtypeStruct((width, rows), BF16),
        ],
        compiler_params=params("arbitrary"),
        name="forward",
    )(place, slots, adjacency, mine, theirs, w_mine, w_theirs)


def activation_kernel(arrived_ref, bias_ref, cotangent_ref, act_ref, grad_ref):
    pre = bias_ref[...]
    for g in range(arrived_ref.shape[0]):
        pre = pre + arrived_ref[g].astype(F32)
    sigmoid = jax.nn.sigmoid(pre)
    act_ref[...] = (pre * sigmoid).astype(BF16)
    derivative = sigmoid * (1.0 + pre * (1.0 - sigmoid))
    grad_ref[...] = (cotangent_ref[...].astype(F32) * derivative).astype(BF16)


def activation_of(arrived, bias, cotangent):
    shape = jax.ShapeDtypeStruct(arrived.shape[1:], BF16)
    return pl.pallas_call(
        activation_kernel,
        in_specs=[vmem()] * 3,
        out_specs=[vmem()] * 2,
        out_shape=[shape, shape],
        compiler_params=params(),
        name="activation",
    )(arrived, bias, cotangent)


def backward_kernel(
    place_ref, slot_ref, adj_ref, grad_ref, w_mine_ref, w_theirs_ref, keep_ref, send_ref, acc_ref
):
    i = pl.program_id(0)
    r = relation_of(i, place_ref)
    xl = place_ref[3]
    slots = 8

    @pl.when(i == 0)
    def _():
        acc_ref[...] = jnp.zeros_like(acc_ref)

    def spread(w):
        grads = dot(w, grad_ref[...], 1, 0).astype(BF16)
        for q in range(2):
            base = (r * 2 + q) * slots
            part = adj_ref[0, q * BLK : (q + 1) * BLK, :]
            wide = dot(grads[:, q * BLK : (q + 1) * BLK], part, 1, 0)
            for s in range(slots):
                acc_ref[slot_ref[base + s]] += wide[:, s * BLK : (s + 1) * BLK]

    @pl.when(i < 4)
    def _():
        spread(w_mine_ref[0])

    @pl.when(i >= 4)
    def _():
        spread(w_theirs_ref[0])

    @pl.when(i == 7)
    def _():
        keep_ref[...] = acc_ref[:, pl.ds(pl.multiple_of(xl * 96, 32), 96), :].astype(BF16)
        send_ref[...] = acc_ref[:, pl.ds(pl.multiple_of((1 - xl) * 96, 32), 96), :].astype(BF16)


def backward_of(place, slots, adjacency, grads, w_mine, w_theirs, owners):
    rels, rows, wide = adjacency.shape
    width = w_mine.shape[2]
    half = pl.BlockSpec((owners, 96, BLK), lambda i, p, s: (0, 0, 0))
    spec = pltpu.PrefetchScalarGridSpec(
        num_scalar_prefetch=2,
        grid=(rels,),
        in_specs=[
            pl.BlockSpec((1, rows, wide), lambda i, p, s: (relation_of(i, p), 0, 0)),
            pl.BlockSpec((width, rows), lambda i, p, s: (0, 0)),
            pl.BlockSpec((1, 192, width), lambda i, p, s: (jnp.minimum(i, 3), 0, 0)),
            pl.BlockSpec((1, 192, width), lambda i, p, s: (jnp.maximum(i - 4, 0), 0, 0)),
        ],
        out_specs=[half, half],
        scratch_shapes=[pltpu.VMEM((owners, 192, BLK), F32)],
    )
    shape = jax.ShapeDtypeStruct((owners, 96, BLK), BF16)
    return pl.pallas_call(
        backward_kernel,
        grid_spec=spec,
        out_shape=[shape, shape],
        compiler_params=params("arbitrary"),
        name="backward",
    )(place, slots, adjacency, grads, w_mine, w_theirs)


def weight_kernel(messages_ref, grad_ref, out_ref):
    first = dot(messages_ref[0], grad_ref[...], 1, 1)
    second = dot(messages_ref[1], grad_ref[...], 1, 1)
    for m in range(8):
        rows = slice(m * 24, (m + 1) * 24)
        piece = jnp.concatenate([first[rows], second[rows]], axis=0)
        out_ref[m % 2, 0, m // 2] = piece.astype(BF16)


def weight_terms_of(messages, grads):
    rels, deep, rows = messages.shape
    width = grads.shape[0]
    return pl.pallas_call(
        weight_kernel,
        grid=(rels // 2,),
        in_specs=[
            pl.BlockSpec((2, deep, rows), lambda j: (j, 0, 0)),
            pl.BlockSpec((width, rows), lambda j: (0, 0)),
        ],
        out_specs=pl.BlockSpec((2, 1, 4, 48, width), lambda j: (0, j, 0, 0, 0)),
        out_shape=jax.ShapeDtypeStruct((2, rels // 2, 4, 48, width), BF16),
        compiler_params=params("arbitrary"),
        name="weight_terms",
    )(messages, grads)


def owned_kernel(place_ref, table_ref, arrived_ref, out_ref):
    owner = place_ref[0]
    zero = jnp.zeros(arrived_ref.shape[1:], F32)
    sums = [zero, zero]
    for t in range(arrived_ref.shape[0]):
        k = table_ref[t, owner]
        v = arrived_ref[t].astype(F32)
        for b in range(2):
            sums[b] = sums[b] + jnp.where(k == b, v, zero)
    for b in range(2):
        turned = sums[b].T
        for g in range(out_ref.shape[0]):
            out_ref[g, b] = turned[g * 16 : (g + 1) * 16, :]


def owned_of(place, source_blocks, arrived, groups):
    return pl.pallas_call(
        owned_kernel,
        in_specs=[smem(), smem(), vmem()],
        out_specs=vmem(),
        out_shape=jax.ShapeDtypeStruct((groups, 2, BLK // groups, 96), F32),
        compiler_params=params(),
        name="owned",
    )(place, source_blocks, arrived)


def swap(value, axis):
    return lax.ppermute(value, axis, [(0, 1), (1, 0)])


def exchange(value, axis):
    return lax.all_to_all(value, axis, 0, 0, tiled=True)


def copies(value, axis, count):
    return exchange(jnp.broadcast_to(value[None], (count, *value.shape)), axis)


def to_owner():
    def place(y, xh, z, c):
        return ((y * 2 + xh) * 8 + z) * 2 + c
    moves = []
    for y in range(4):
        for xh in range(2):
            for z in range(8):
                for c in range(2):
                    target = place(2 * xh + z // 4, y // 2, 4 * (y % 2) + z % 4, c)
                    moves.append((place(y, xh, z, c), target))
    return moves


def per_device(
    features, weights, bias, cotangent, tile_values, tile_count, tile_slot, source_blocks
):
    groups = 8
    owners = source_blocks.shape[0]
    width = features.shape[1]
    xl, y, core = lax.axis_index("xl"), lax.axis_index("y"), lax.axis_index("core")
    owner = lax.axis_index(TGT)
    group = lax.axis_index(REL)
    place = jnp.stack([owner, 192 * y + 96 * xl, core, xl]).astype(jnp.int32)

    own_adjacency = adjacency_of(tile_values, tile_count)
    adjacency = lax.all_gather(own_adjacency, "y", axis=0, tiled=True)
    mine = exchange(outgoing_of(features, source_blocks, place), TGT)
    theirs = swap(mine, "xl")
    slots = copies(tile_slot.reshape(1, -1), "y", 4).reshape(-1)
    w_own = lax.dynamic_index_in_dim(weights, core, 0, keepdims=False)
    w_mine = exchange(w_own.reshape(4, 192, width), "y")
    w_theirs = swap(w_mine, "core")

    messages, part = forward_of(place, slots, adjacency, mine, theirs, w_mine, w_theirs)
    share = width // groups
    arrived = exchange(part.reshape(groups, share, -1), REL)
    bias_share = lax.dynamic_slice_in_dim(bias, group * share, share)[:, None]
    cotangent_share = lax.dynamic_slice_in_dim(cotangent, group * share, share, 1).T
    activated, grad_share = activation_of(arrived, bias_share, cotangent_share)
    output = activated.T
    grads = copies(grad_share, REL, groups).reshape(width, -1)

    keep, send = backward_of(place, slots, adjacency, grads, w_mine, w_theirs, owners)
    received = swap(send, "xl")
    partial = (keep.astype(F32) + received.astype(F32)).astype(BF16)
    returned = exchange(partial, TGT)
    cut = owned_of(place, source_blocks, returned, groups)
    columns = exchange(cut, REL).reshape(2, 4, 2, BLK // groups, 96)
    grad_features = columns.transpose(2, 3, 1, 0, 4).reshape(2, BLK // groups, width)

    terms = weight_terms_of(messages, grads)
    pair = exchange(terms, "core").astype(F32)
    chip = (pair[0] + pair[1]).astype(BF16).reshape(16, 48, width)
    pieces = exchange(chip, ("xh", "z"))
    piece = jnp.sum(pieces.astype(F32), axis=0).reshape(2, 24, width)
    grad_weights = lax.ppermute(piece, ("y", *TGT), to_owner())
    return (output, grad_weights, grad_features)


def solution(mesh):
    fine = Mesh(mesh.devices.reshape(2, 4, 2, 8, 2), (*REL, *TGT))
    placed = (
        P(TGT, None),
        P(REL, None, None),
        P(),
        P(TGT, None),
        P(REL, TGT, None, None),
        P(REL, TGT),
        P(REL, TGT, None),
        P(),
    )
    return jax.shard_map(
        per_device,
        mesh=fine,
        in_specs=placed,
        out_specs=(P(TGT, REL), P(REL, TGT, None), P(TGT, REL, None)),
        check_vma=False,
    )
```

time: 438 us -> 249 us (0.57); the launches traced: 430 us -> 246 us
  waiting for transfers between devices: 275 us -> 94.6 us
  Pallas kernels: 0 us -> 38.2 us
  starting transfers between devices: 22.7 us -> 57.8 us
  matrix products: 32.2 us -> 0 us
  local copies, waits for them, and re-layouts: 26.4 us -> 8.79 us
  other arithmetic: 23.7 us -> 6.21 us
  blocking collectives: 36 us -> 26.4 us
    all_to_all x3 -> x6, waiting for transfers between devices: 224 us -> 59.9 us  [exchange(): return lax.all_to_all(value, axis, 0, 0, tiled=True)]
    all_gather x1, waiting for transfers between devices: 50.7 us -> 0.01 us  [per_device(): adjacency = lax.all_gather(own_adjacency, 'y', axis=0, tiled=True)]
    pallas_call x0 -> x7, Pallas kernels: none -> 38.2 us  [the longest x1 10.8 us: backward_of(): pl.pallas_call(backward_kernel, grid_spec=spec, out_shape=[shape, shape],...]
    ppermute x0 -> x4, waiting for transfers between devices: none -> 34.6 us  [the longest x3 34.6 us: swap(): return lax.ppermute(value, axis, [(0, 1), (1, 0)])]
    dot_general x9 -> x0, matrix products: 32.2 us -> none  [the longest x2 13.4 us: padded_partials(): jnp.einsum('qso,qscd->ocd', selector, contrib, precision=lax.Precision.HI...]
    all_to_all x3 -> x6, starting transfers between devices: 22.6 us -> 45.7 us  [exchange(): return lax.all_to_all(value, axis, 0, 0, tiled=True)]
    reduce_sum x3 -> x1, other arithmetic: 17 us -> 0.82 us  [per_device(): piece = jnp.sum(pieces.astype(F32), axis=0).reshape(2, 24, width)]
    ppermute x0 -> x4, starting transfers between devices: none -> 12.2 us  [the longest x1 10.4 us: per_device(): grad_weights = lax.ppermute(piece, ('y', *TGT), to_owner())]
  transfers between devices with their start and end apart: 5 -> 11, of which waited for: 4 -> 7; matrix products, arithmetic and copies ran while one was open for 8% -> 4% of each run, Pallas kernels for 0% -> 6%
where the time goes in v1:
time: 249 us; the launch traced here: 246 us
  waiting for transfers between devices  94.6 us (38%)
  starting transfers between devices  57.8 us (23%)
  Pallas kernels  38.2 us (15%)
  blocking collectives  26.4 us (11%)
  between operations  14.1 us (6%)
  local copies, waits for them, and re-layouts  8.79 us (4%)
  other arithmetic  6.21 us (2%)
    all_to_all x6, waiting for transfers between devices, exchange(): return lax.all_to_all(value, axis, 0, 0, tiled=True)  59.9 us
    all_to_all x6, starting transfers between devices, exchange(): return lax.all_to_all(value, axis, 0, 0, tiled=True)  45.7 us
    ppermute x3, waiting for transfers between devices, swap(): return lax.ppermute(value, axis, [(0, 1), (1, 0)])  34.6 us
    all_to_all x3, blocking collectives, exchange(): return lax.all_to_all(value, axis, 0, 0, tiled=True)  26.4 us
    pallas_call x1, Pallas kernels, backward_of(): pl.pallas_call(backward_kernel, grid_spec=spec, out_shape=[shape, shape],...  10.8 us
    pallas_call x1, Pallas kernels, forward_of(): pl.pallas_call(forward_kernel, grid_spec=spec, out_shape=[jax.ShapeDtypeS...  10.7 us
    ppermute x1, starting transfers between devices, per_device(): grad_weights = lax.ppermute(piece, ('y', *TGT), to_owner())  10.4 us
    pallas_call x1, Pallas kernels, adjacency_of(): pl.pallas_call(adjacency_kernel, grid=(rels, rows // BLK), in_specs=[smem...  5.89 us
  transfers between devices with their start and end apart: 11, of which 7 were waited for; matrix products, arithmetic and copies ran while one was open for 4% of the time, Pallas kernels for 6%

profile of v1, /device:TPU:56, one launch (start us, length us, event | category | flops | bytes accessed | tf_op | source)
XLA Modules:
  0.0 246.1 jit_solution(694879727876316263)
XLA Ops:
  7.2 5.9 %adjacency.1 = bf16[2,256,1024]{2,1,0:T(8,128)(2,1)} custom-call(s32[2,2]{1,0:T(2,128)} %count_ref.1, s32[2,256,8,128]{3,2,1,0:T(8,128)} %values_ref.1), custom_call_target="tpu_custom_call" | custom-call | tf_op jit(solution)/shard_map/adjacency/pallas_call | solution.py:52
  14.3 4.8 %all-to-all-start.2 = ((bf16[4,192,768]{2,1,0:T(8,128)(2,1)}), bf16[4,192,768]{2,1,0:T(8,128)(2,1)S(1)}, u32[]{:S(2)}, u32[]{:S(2)}) async-start(bf16[4,192,768]{2,1,0:T(8,128)(2,1)} %bitcast.16), calls=%async_computation.2 | async-start | bytes 2359296 | tf_op jit(solution)/shard_map/all_to_all | solution.py:300
  19.7 2.2 outgoing.1
  21.9 14.9 %all-to-all-done.2.w_mine_ref = bf16[4,192,768]{2,1,0:T(8,128)(2,1)S(1)} async-done(((bf16[4,192,768]{2,1,0:T(8,128)(2,1)}), bf16[4,192,768]{2,1,0:T(8,128)(2,1)S(1)}, u32[]{:S(2)}, u32[]{:S(2)}) %all-to-all-start.2) | async-done | bytes 1179680 | tf_op jit(solution)/shard_map/all_to_all | solution.py:300
  36.8 12.4 %all-to-all-start.1 = ((bf16[32,96,128]{2,1,0:T(8,128)(2,1)}), bf16[32,96,128]{2,1,0:T(8,128)(2,1)}, u32[]{:S(2)}, u32[]{:S(2)}) async-start(bf16[32,96,128]{2,1,0:T(8,128)(2,1)} %outgoing.1), calls=%async_computation.1 | async-start | bytes 1572864 | tf_op jit(solution)/shard_map/all_to_all | solution.py:300
  49.4 24.7 %all-to-all-done.1.mine_ref = bf16[32,96,128]{2,1,0:T(8,128)(2,1)} async-done(((bf16[32,96,128]{2,1,0:T(8,128)(2,1)}), bf16[32,96,128]{2,1,0:T(8,128)(2,1)}, u32[]{:S(2)}, u32[]{:S(2)}) %all-to-all-start.1) | async-done | bytes 786464 | tf_op jit(solution)/shard_map/all_to_all | solution.py:300
  74.8 8.2 %all_to_all.45 = s32[4,1,32]{2,1,0:T(1,128)S(1)} all-to-all(s32[4,1,32]{2,1,0:T(1,128)S(1)} %broadcast_in_dim.17), channel_id=1, replica_groups=mesh['xl'=2,'y'=4,'xh'=2,'z'=8,'core'=2] {'y'}, dimensions={0} | all-to-all | bytes 1024 | tf_op jit(solution)/shard_map/all_to_all | solution.py:300
  84.8 8.5 %collective-permute-done.theirs_ref = bf16[32,96,128]{2,1,0:T(8,128)(2,1)} collective-permute-done((bf16[32,96,128]{2,1,0:T(8,128)(2,1)}, bf16[32,96,128]{2,1,0:T(8,128)(2,1)}, u32[]{:S(2)}, u32[]{:S(2)}) %collective-permute-start) | collective-permute-done | bytes 786464 | tf_op jit(solution)/shard_map/ppermute | solution.py:296
  93.3 10.7 %forward.1 = (bf16[8,192,256]{2,1,0:T(8,128)(2,1)}, bf16[768,256]{1,0:T(8,128)(2,1)}) custom-call(s32[4]{0:T(128)} %pad_add_fusion.place_ref, s32[128]{0:T(128)} %reshape.37.slot_ref, bf16[8,256,1024]{2,1,0:T(8,128)(2,1)} %all-gather.2.cloned.1.call-done.adj_ref, bf16[32,96,128]{2,1,0:T(8,128)(2,1)} %all-to-all-done.1.mine_ref, ...), custom_call_target="tpu_custom_call" | custom-call | tf_op jit(solution)/shard_map/forward/pallas_call | solution.py:148
  104.0 6.0 %all-to-all-start.3 = ((bf16[8,96,256]{2,1,0:T(8,128)(2,1)}), bf16[8,96,256]{2,1,0:T(8,128)(2,1)S(1)}, u32[]{:S(2)}, u32[]{:S(2)}) async-start(bf16[8,96,256]{2,1,0:T(8,128)(2,1)} %bitcast.21), calls=%async_computation.3 | async-start | bytes 786432 | tf_op jit(solution)/shard_map/all_to_all | solution.py:300
  113.2 2.2 all-to-all-done.3.arrived_ref
  118.8 11.3 %all_to_all.46 = bf16[8,96,256]{2,1,0:T(8,128)(2,1)} all-to-all(bf16[8,96,256]{2,1,0:T(8,128)(2,1)S(1)} %broadcast_in_dim.19), channel_id=1, replica_groups=mesh['xl'=2,'y'=4,'xh'=2,'z'=8,'core'=2] {'xl','y'}, dimensions={0} | all-to-all | bytes 786432 | tf_op jit(solution)/shard_map/all_to_all | solution.py:300
  130.1 4.6 %weight_terms.1 = bf16[2,4,4,48,768]{4,3,2,1,0:T(8,128)(2,1)} custom-call(bf16[8,192,256]{2,1,0:T(8,128)(2,1)} %get-tuple-element.11.messages_ref, bf16[768,256]{1,0:T(8,128)(2,1)} %bitcast.18), custom_call_target="tpu_custom_call" | custom-call | tf_op jit(solution)/shard_map/weight_terms/pallas_call | solution.py:255
  134.7 6.8 %all_to_all.47 = bf16[2,4,4,48,768]{4,3,2,1,0:T(8,128)(2,1)S(1)} all-to-all(bf16[2,4,4,48,768]{4,3,2,1,0:T(8,128)(2,1)} %weight_terms.1), channel_id=1, replica_groups=mesh['xl'=2,'y'=4,'xh'=2,'z'=8,'core'=2] {'core'}, dimensions={0} | all-to-all | bytes 4718592 | tf_op jit(solution)/shard_map/all_to_all | solution.py:300
  143.4 5.2 %all-to-all-start.6 = ((bf16[16,48,768]{2,1,0:T(8,128)(2,1)}), bf16[16,48,768]{2,1,0:T(8,128)(2,1)S(1)}, u32[]{:S(2)}, u32[]{:S(2)}) async-start(bf16[16,48,768]{2,1,0:T(8,128)(2,1)} %bitcast.17), calls=%async_computation.6 | async-start | bytes 2359296 | tf_op jit(solution)/shard_map/all_to_all | solution.py:300
  148.6 10.8 %backward.1 = (bf16[32,96,128]{2,1,0:T(8,128)(2,1)}, bf16[32,96,128]{2,1,0:T(8,128)(2,1)}) custom-call(s32[4]{0:T(128)} %pad_add_fusion.place_ref, s32[128]{0:T(128)} %reshape.37.slot_ref, bf16[8,256,1024]{2,1,0:T(8,128)(2,1)} %all-gather.2.cloned.1.call-done.adj_ref, bf16[768,256]{1,0:T(8,128)(2,1)} %bitcast.19, bf16[4,192,768]{2,1,0:T(8,128)(2,1)} %copy-done.1, ...), custom_call_target="tpu_custom_call" | custom-call | tf_op jit(solution)/shard_map/backward/pallas_call | solution.py:234
  160.4 26.1 %collective-permute-done.3 = bf16[32,96,128]{2,1,0:T(8,128)(2,1)S(1)} collective-permute-done((bf16[32,96,128]{2,1,0:T(8,128)(2,1)}, bf16[32,96,128]{2,1,0:T(8,128)(2,1)S(1)}, u32[]{:S(2)}, u32[]{:S(2)}) %collective-permute-start.3) | collective-permute-done | bytes 786464 | tf_op jit(solution)/shard_map/ppermute | solution.py:296
  186.4 2.3 add_convert_fusion
  188.7 8.4 %all-to-all-start.7 = ((bf16[32,96,128]{2,1,0:T(8,128)(2,1)}), bf16[32,96,128]{2,1,0:T(8,128)(2,1)}, u32[]{:S(2)}, u32[]{:S(2)}) async-start(bf16[32,96,128]{2,1,0:T(8,128)(2,1)} %add_convert_fusion), calls=%async_computation.7 | async-start | bytes 1572864 | tf_op jit(solution)/shard_map/all_to_all | solution.py:300
  197.9 10.4 %collective-permute-start.2 = (f32[2,24,768]{2,1,0:T(8,128)}, f32[2,24,768]{2,1,0:T(8,128)S(1)}, u32[]{:S(2)}, u32[]{:S(2)}) collective-permute-start(f32[2,24,768]{2,1,0:T(8,128)} %bitcast.11), channel_id=1, source_target_pairs={{0,0},{1,1},{2,2},{3,3},{4,4},{5,5},{6,6},{7,7},{8,32},{9,33},{10,... | collective-permute-start | bytes 442376 | tf_op jit(solution)/shard_map/ppermute | solution.py:362
  208.3 13.7 %all-to-all-done.7.arrived_ref = bf16[32,96,128]{2,1,0:T(8,128)(2,1)} async-done(((bf16[32,96,128]{2,1,0:T(8,128)(2,1)}), bf16[32,96,128]{2,1,0:T(8,128)(2,1)}, u32[]{:S(2)}, u32[]{:S(2)}) %all-to-all-start.7) | async-done | bytes 786464 | tf_op jit(solution)/shard_map/all_to_all | solution.py:300
  222.0 2.3 owned.1
  224.3 8.9 %all-to-all-start.8 = ((f32[8,2,16,96]{3,2,1,0:T(8,128)}), f32[8,2,16,96]{3,2,1,0:T(8,128)S(1)}, u32[]{:S(2)}, u32[]{:S(2)}) async-start(f32[8,2,16,96]{3,2,1,0:T(8,128)} %owned.1), calls=%async_computation.8 | async-start | bytes 262144 | tf_op jit(solution)/shard_map/all_to_all | solution.py:300
  233.2 4.5 %all-to-all-done.8 = f32[8,2,16,96]{3,2,1,0:T(8,128)S(1)} async-done(((f32[8,2,16,96]{3,2,1,0:T(8,128)}), f32[8,2,16,96]{3,2,1,0:T(8,128)S(1)}, u32[]{:S(2)}, u32[]{:S(2)}) %all-to-all-start.8) | async-done | bytes 98336 | tf_op jit(solution)/shard_map/all_to_all | solution.py:300
  (36 shorter events, 16.4 us)
Async XLA Ops:
  7.2 6.0 %copy-start = (bf16[2,768,768]{2,1,0:T(8,128)(2,1)S(1)}, bf16[2,768,768]{2,1,0:T(8,128)(2,1)}, u32[]{:S(2)}) copy-start(bf16[2,768,768]{2,1,0:T(8,128)(2,1)} %param.9) | copy-start | bytes 7077892
  7.2 86.2 %all-gather.2.cloned.1.call-start = ((), (), s32[]{:S(2)}) async-start(), calls=%async_computation.9 | async-start | bytes 5242880 | tf_op jit(solution)/shard_map/all_gather | solution.py:332
  14.3 60.4 %copy-start.3 = (s32[2,2,8]{2,1,0:T(2,128)S(1)}, s32[2,2,8]{2,1,0:T(2,128)}, u32[]{:S(2)}) copy-start(s32[2,2,8]{2,1,0:T(2,128)} %param.14) | copy-start | bytes 388
  14.3 22.5 %all-to-all-start.2 = ((bf16[4,192,768]{2,1,0:T(8,128)(2,1)}), bf16[4,192,768]{2,1,0:T(8,128)(2,1)S(1)}, u32[]{:S(2)}, u32[]{:S(2)}) async-start(bf16[4,192,768]{2,1,0:T(8,128)(2,1)} %bitcast.16), calls=%async_computation.2 | async-start | bytes 2359296 | tf_op jit(solution)/shard_map/all_to_all | solution.py:300
  36.8 56.6 %copy-start.1 = (bf16[4,192,768]{2,1,0:T(8,128)(2,1)}, bf16[4,192,768]{2,1,0:T(8,128)(2,1)S(1)}, u32[]{:S(2)}) copy-start(bf16[4,192,768]{2,1,0:T(8,128)(2,1)S(1)} %all-to-all-done.2.w_mine_ref) | copy-start | bytes 3538948
  36.8 37.3 %all-to-all-start.1 = ((bf16[32,96,128]{2,1,0:T(8,128)(2,1)}), bf16[32,96,128]{2,1,0:T(8,128)(2,1)}, u32[]{:S(2)}, u32[]{:S(2)}) async-start(bf16[32,96,128]{2,1,0:T(8,128)(2,1)} %outgoing.1), calls=%async_computation.1 | async-start | bytes 1572864 | tf_op jit(solution)/shard_map/all_to_all | solution.py:300
  49.1 35.7 %collective-permute-start.1 = (bf16[4,192,768]{2,1,0:T(8,128)(2,1)S(1)}, bf16[4,192,768]{2,1,0:T(8,128)(2,1)}, u32[]{:S(2)}, u32[]{:S(2)}) collective-permute-start(bf16[4,192,768]{2,1,0:T(8,128)(2,1)S(1)} %all-to-all-done.2.w_mine_ref), channel_id=1, source_target_pairs={{0,1},{1,0},{2,3},{3,2},{4,5},{5,4},{6,7},{7,6},{8,9},{9,8},{10,11... | collective-permute-start | bytes 3538952 | tf_op jit(solution)/shard_map/ppermute | solution.py:296
  74.1 19.3 %collective-permute-start = (bf16[32,96,128]{2,1,0:T(8,128)(2,1)}, bf16[32,96,128]{2,1,0:T(8,128)(2,1)}, u32[]{:S(2)}, u32[]{:S(2)}) collective-permute-start(bf16[32,96,128]{2,1,0:T(8,128)(2,1)} %all-to-all-done.1.mine_ref), channel_id=1, source_target_pairs={{0,128},{128,0},{1,129},{129,1},{2,130},{130,2},{3,131},{131,3},{4... | collective-permute-start | bytes 2359304 | tf_op jit(solution)/shard_map/ppermute | solution.py:296
  104.0 11.4 %all-to-all-start.3 = ((bf16[8,96,256]{2,1,0:T(8,128)(2,1)}), bf16[8,96,256]{2,1,0:T(8,128)(2,1)S(1)}, u32[]{:S(2)}, u32[]{:S(2)}) async-start(bf16[8,96,256]{2,1,0:T(8,128)(2,1)} %bitcast.21), calls=%async_computation.3 | async-start | bytes 786432 | tf_op jit(solution)/shard_map/all_to_all | solution.py:300
  115.4 0.7 copy-start.2
  143.4 45.3 %all-to-all-start.6 = ((bf16[16,48,768]{2,1,0:T(8,128)(2,1)}), bf16[16,48,768]{2,1,0:T(8,128)(2,1)S(1)}, u32[]{:S(2)}, u32[]{:S(2)}) async-start(bf16[16,48,768]{2,1,0:T(8,128)(2,1)} %bitcast.17), calls=%async_computation.6 | async-start | bytes 2359296 | tf_op jit(solution)/shard_map/all_to_all | solution.py:300
  159.4 27.0 %collective-permute-start.3 = (bf16[32,96,128]{2,1,0:T(8,128)(2,1)}, bf16[32,96,128]{2,1,0:T(8,128)(2,1)S(1)}, u32[]{:S(2)}, u32[]{:S(2)}) collective-permute-start(bf16[32,96,128]{2,1,0:T(8,128)(2,1)} %get-tuple-element.14), channel_id=1, source_target_pairs={{0,128},{128,0},{1,129},{129,1},{2,130},{130,2},{3,131},{131,3},{4... | collective-permute-start | bytes 2359304 | tf_op jit(solution)/shard_map/ppermute | solution.py:296
  188.7 33.3 %all-to-all-start.7 = ((bf16[32,96,128]{2,1,0:T(8,128)(2,1)}), bf16[32,96,128]{2,1,0:T(8,128)(2,1)}, u32[]{:S(2)}, u32[]{:S(2)}) async-start(bf16[32,96,128]{2,1,0:T(8,128)(2,1)} %add_convert_fusion), calls=%async_computation.7 | async-start | bytes 1572864 | tf_op jit(solution)/shard_map/all_to_all | solution.py:300
  197.9 35.3 %collective-permute-start.2 = (f32[2,24,768]{2,1,0:T(8,128)}, f32[2,24,768]{2,1,0:T(8,128)S(1)}, u32[]{:S(2)}, u32[]{:S(2)}) collective-permute-start(f32[2,24,768]{2,1,0:T(8,128)} %bitcast.11), channel_id=1, source_target_pairs={{0,0},{1,1},{2,2},{3,3},{4,4},{5,5},{6,6},{7,7},{8,32},{9,33},{10,... | collective-permute-start | bytes 442376 | tf_op jit(solution)/shard_map/ppermute | solution.py:362
  224.3 13.3 %all-to-all-start.8 = ((f32[8,2,16,96]{3,2,1,0:T(8,128)}), f32[8,2,16,96]{3,2,1,0:T(8,128)S(1)}, u32[]{:S(2)}, u32[]{:S(2)}) async-start(f32[8,2,16,96]{3,2,1,0:T(8,128)} %owned.1), calls=%async_computation.8 | async-start | bytes 262144 | tf_op jit(solution)/shard_map/all_to_all | solution.py:300
Sparse Core Ops, SparseCore 0:
  13.3 54.3 all-gather.1

commit v2 on v1

--- a/solution.py
+++ b/solution.py
@@ -63,7 +63,7 @@
 def outgoing_kernel(place_ref, table_ref, features_ref, out_ref, turned_ref):
     owner, first = place_ref[0], place_ref[1]
     turned_ref[...] = features_ref[...].T
-    piece = turned_ref[pl.ds(pl.multiple_of(first, 32), 96), :]
+    piece = turned_ref[pl.ds(pl.multiple_of(first, 64), 192), :]
     block0, block1 = piece[:, :BLK], piece[:, BLK:]
     for t in range(out_ref.shape[0]):
         k = table_ref[t, owner]
@@ -77,7 +77,7 @@
         outgoing_kernel,
         in_specs=[smem(), smem(), vmem()],
         out_specs=vmem(),
-        out_shape=jax.ShapeDtypeStruct((source_blocks.shape[0], 96, BLK), BF16),
+        out_shape=jax.ShapeDtypeStruct((source_blocks.shape[0], 192, BLK), BF16),
         scratch_shapes=[pltpu.VMEM((width, rows), BF16)],
         compiler_params=params(),
         name="outgoing",
@@ -85,26 +85,24 @@
 
 
 def relation_of(i, place):
+    core, y = place[2], place[3]
+    parity = jnp.where(i < 4, core, 1 - core)
+    return 2 * ((y - i) & 3) + parity
+
+
+def slots_at(i, place, q):
     core = place[2]
-    return jnp.where(i < 4, 2 * i + core, 2 * (i - 4) + 1 - core)
+    parity = jnp.where(i < 4, core, 1 - core)
+    return (((i & 3) * 2 + parity) * 2 + q) * 8
 
 
 def forward_kernel(
-    place_ref, slot_ref, adj_ref, mine_ref, theirs_ref, w_mine_ref, w_theirs_ref,
-    messages_ref, pre_ref, fetched_ref, acc_ref,
+    place_ref, slot_ref, adj_ref, fetched_ref, w_mine_ref, w_theirs_ref, messages_ref, pre_ref, acc_ref
 ):
     i = pl.program_id(0)
-    r = relation_of(i, place_ref)
-    xl = place_ref[3]
     slots = 8
-
-    @pl.when(i == 0)
-    def _():
-        fetched_ref[:, pl.ds(pl.multiple_of(xl * 96, 32), 96), :] = mine_ref[...]
-        fetched_ref[:, pl.ds(pl.multiple_of((1 - xl) * 96, 32), 96), :] = theirs_ref[...]
-
     for q in range(2):
-        base = (r * 2 + q) * slots
+        base = slots_at(i, place_ref, q)
         wide = jnp.concatenate([fetched_ref[slot_ref[base + s]] for s in range(slots)], axis=1)
         part = adj_ref[0, q * BLK : (q + 1) * BLK, :]
         messages_ref[0, :, q * BLK : (q + 1) * BLK] = dot(wide, part, 1, 1).astype(BF16)
@@ -126,7 +124,7 @@
         pre_ref[...] = acc_ref[...].astype(BF16)
 
 
-def forward_of(place, slots, adjacency, mine, theirs, w_mine, w_theirs):
+def forward_of(place, slots, adjacency, fetched, w_mine, w_theirs):
     rels, rows, wide = adjacency.shape
     width = w_mine.shape[2]
     spec = pltpu.PrefetchScalarGridSpec(
@@ -134,8 +132,7 @@
         grid=(rels,),
         in_specs=[
             pl.BlockSpec((1, rows, wide), lambda i, p, s: (relation_of(i, p), 0, 0)),
-            pl.BlockSpec(mine.shape, lambda i, p, s: (0, 0, 0)),
-            pl.BlockSpec(mine.shape, lambda i, p, s: (0, 0, 0)),
+            pl.BlockSpec(fetched.shape, lambda i, p, s: (0, 0, 0)),
             pl.BlockSpec((1, 192, width), lambda i, p, s: (jnp.minimum(i, 3), 0, 0)),
             pl.BlockSpec((1, 192, width), lambda i, p, s: (jnp.maximum(i - 4, 0), 0, 0)),
         ],
@@ -143,7 +140,7 @@
             pl.BlockSpec((1, 192, rows), lambda i, p, s: (relation_of(i, p), 0, 0)),
             pl.BlockSpec((width, rows), lambda i, p, s: (0, 0)),
         ],
-        scratch_shapes=[pltpu.VMEM((mine.shape[0], 192, BLK), BF16), pltpu.VMEM((width, rows), F32)],
+        scratch_shapes=[pltpu.VMEM((width, rows), F32)],
     )
     return pl.pallas_call(
         forward_kernel,
@@ -154,7 +151,7 @@
         ],
         compiler_params=params("arbitrary"),
         name="forward",
-    )(place, slots, adjacency, mine, theirs, w_mine, w_theirs)
+    )(place, slots, adjacency, fetched, w_mine, w_theirs)
 
 
 def activation_kernel(arrived_ref, bias_ref, cotangent_ref, act_ref, grad_ref):
@@ -164,27 +161,29 @@
     sigmoid = jax.nn.sigmoid(pre)
     act_ref[...] = (pre * sigmoid).astype(BF16)
     derivative = sigmoid * (1.0 + pre * (1.0 - sigmoid))
-    grad_ref[...] = (cotangent_ref[...].astype(F32) * derivative).astype(BF16)
+    grad = (cotangent_ref[...].astype(F32) * derivative).astype(BF16)
+    for g in range(grad_ref.shape[0]):
+        grad_ref[g] = grad
 
 
 def activation_of(arrived, bias, cotangent):
-    shape = jax.ShapeDtypeStruct(arrived.shape[1:], BF16)
     return pl.pallas_call(
         activation_kernel,
         in_specs=[vmem()] * 3,
         out_specs=[vmem()] * 2,
-        out_shape=[shape, shape],
+        out_shape=[
+            jax.ShapeDtypeStruct(arrived.shape[1:], BF16),
+            jax.ShapeDtypeStruct(arrived.shape, BF16),
+        ],
         compiler_params=params(),
         name="activation",
     )(arrived, bias, cotangent)
 
 
 def backward_kernel(
-    place_ref, slot_ref, adj_ref, grad_ref, w_mine_ref, w_theirs_ref, keep_ref, send_ref, acc_ref
+    place_ref, slot_ref, adj_ref, grad_ref, w_mine_ref, w_theirs_ref, out_ref, acc_ref
 ):
     i = pl.program_id(0)
-    r = relation_of(i, place_ref)
-    xl = place_ref[3]
     slots = 8
 
     @pl.when(i == 0)
@@ -194,7 +193,7 @@
     def spread(w):
         grads = dot(w, grad_ref[...], 1, 0).astype(BF16)
         for q in range(2):
-            base = (r * 2 + q) * slots
+            base = slots_at(i, place_ref, q)
             part = adj_ref[0, q * BLK : (q + 1) * BLK, :]
             wide = dot(grads[:, q * BLK : (q + 1) * BLK], part, 1, 0)
             for s in range(slots):
@@ -210,14 +209,12 @@
 
     @pl.when(i == 7)
     def _():
-        keep_ref[...] = acc_ref[:, pl.ds(pl.multiple_of(xl * 96, 32), 96), :].astype(BF16)
-        send_ref[...] = acc_ref[:, pl.ds(pl.multiple_of((1 - xl) * 96, 32), 96), :].astype(BF16)
+        out_ref[...] = acc_ref[...].astype(BF16)
 
 
 def backward_of(place, slots, adjacency, grads, w_mine, w_theirs, owners):
     rels, rows, wide = adjacency.shape
     width = w_mine.shape[2]
-    half = pl.BlockSpec((owners, 96, BLK), lambda i, p, s: (0, 0, 0))
     spec = pltpu.PrefetchScalarGridSpec(
         num_scalar_prefetch=2,
         grid=(rels,),
@@ -227,43 +224,59 @@
             pl.BlockSpec((1, 192, width), lambda i, p, s: (jnp.minimum(i, 3), 0, 0)),
             pl.BlockSpec((1, 192, width), lambda i, p, s: (jnp.maximum(i - 4, 0), 0, 0)),
         ],
-        out_specs=[half, half],
+        out_specs=pl.BlockSpec((owners, 192, BLK), lambda i, p, s: (0, 0, 0)),
         scratch_shapes=[pltpu.VMEM((owners, 192, BLK), F32)],
     )
-    shape = jax.ShapeDtypeStruct((owners, 96, BLK), BF16)
     return pl.pallas_call(
         backward_kernel,
         grid_spec=spec,
-        out_shape=[shape, shape],
+        out_shape=jax.ShapeDtypeStruct((owners, 192, BLK), BF16),
         compiler_params=params("arbitrary"),
         name="backward",
     )(place, slots, adjacency, grads, w_mine, w_theirs)
 
 
-def weight_kernel(messages_ref, grad_ref, out_ref):
+def weight_kernel(place_ref, messages_ref, grad_ref, keep_ref, send_ref):
+    core = place_ref[2]
     first = dot(messages_ref[0], grad_ref[...], 1, 1)
     second = dot(messages_ref[1], grad_ref[...], 1, 1)
-    for m in range(8):
-        rows = slice(m * 24, (m + 1) * 24)
-        piece = jnp.concatenate([first[rows], second[rows]], axis=0)
-        out_ref[m % 2, 0, m // 2] = piece.astype(BF16)
-
-
-def weight_terms_of(messages, grads):
+
+    def cut(even_ref, odd_ref):
+        for m in range(8):
+            rows = slice(m * 24, (m + 1) * 24)
+            piece = jnp.concatenate([first[rows], second[rows]], axis=0)
+            target = odd_ref if m % 2 else even_ref
+            target[0, m // 2] = piece.astype(target.dtype)
+
+    @pl.when(core == 0)
+    def _():
+        cut(keep_ref, send_ref)
+
+    @pl.when(core == 1)
+    def _():
+        cut(send_ref, keep_ref)
+
+
+def weight_terms_of(place, messages, grads):
     rels, deep, rows = messages.shape
     width = grads.shape[0]
+    out = pl.BlockSpec((1, 4, 48, width), lambda j: (j, 0, 0, 0))
     return pl.pallas_call(
         weight_kernel,
         grid=(rels // 2,),
         in_specs=[
+            smem(),
             pl.BlockSpec((2, deep, rows), lambda j: (j, 0, 0)),
             pl.BlockSpec((width, rows), lambda j: (0, 0)),
         ],
-        out_specs=pl.BlockSpec((2, 1, 4, 48, width), lambda j: (0, j, 0, 0, 0)),
-        out_shape=jax.ShapeDtypeStruct((2, rels // 2, 4, 48, width), BF16),
+        out_specs=[out, out],
+        out_shape=[
+            jax.ShapeDtypeStruct((rels // 2, 4, 48, width), F32),
+            jax.ShapeDtypeStruct((rels // 2, 4, 48, width), BF16),
+        ],
         compiler_params=params("arbitrary"),
         name="weight_terms",
-    )(messages, grads)
+    )(place, messages, grads)
 
 
 def owned_kernel(place_ref, table_ref, arrived_ref, out_ref):
@@ -286,7 +299,7 @@
         owned_kernel,
         in_specs=[smem(), smem(), vmem()],
         out_specs=vmem(),
-        out_shape=jax.ShapeDtypeStruct((groups, 2, BLK // groups, 96), F32),
+        out_shape=jax.ShapeDtypeStruct((groups, 2, BLK // groups, arrived.shape[1]), F32),
         compiler_params=params(),
         name="owned",
     )(place, source_blocks, arrived)
@@ -300,8 +313,11 @@
     return lax.all_to_all(value, axis, 0, 0, tiled=True)
 
 
-def copies(value, axis, count):
-    return exchange(jnp.broadcast_to(value[None], (count, *value.shape)), axis)
+def around(values, axis, size):
+    return [
+        lax.ppermute(v, axis, [(i, (i + k) % size) for i in range(size)])
+        for k, v in enumerate(values, 1)
+    ]
 
 
 def to_owner():
@@ -326,40 +342,40 @@
     xl, y, core = lax.axis_index("xl"), lax.axis_index("y"), lax.axis_index("core")
     owner = lax.axis_index(TGT)
     group = lax.axis_index(REL)
-    place = jnp.stack([owner, 192 * y + 96 * xl, core, xl]).astype(jnp.int32)
+    place = jnp.stack([owner, 192 * y, core, y]).astype(jnp.int32)
 
     own_adjacency = adjacency_of(tile_values, tile_count)
     adjacency = lax.all_gather(own_adjacency, "y", axis=0, tiled=True)
-    mine = exchange(outgoing_of(features, source_blocks, place), TGT)
-    theirs = swap(mine, "xl")
-    slots = copies(tile_slot.reshape(1, -1), "y", 4).reshape(-1)
-    w_own = lax.dynamic_index_in_dim(weights, core, 0, keepdims=False)
-    w_mine = exchange(w_own.reshape(4, 192, width), "y")
+    fetched = exchange(outgoing_of(features, source_blocks, place), TGT)
+    w_cut = [
+        lax.dynamic_slice(weights, (core, ((y + k) & 3) * 192, 0), (1, 192, width))
+        for k in range(4)
+    ]
+    w_mine = jnp.concatenate([w_cut[0], *around(w_cut[1:], "y", 4)], axis=0)
     w_theirs = swap(w_mine, "core")
-
-    messages, part = forward_of(place, slots, adjacency, mine, theirs, w_mine, w_theirs)
+    own_slots = tile_slot.reshape(-1)
+    slots = jnp.concatenate([own_slots, *around([own_slots] * 3, "y", 4)])
+
+    messages, part = forward_of(place, slots, adjacency, fetched, w_mine, w_theirs)
     share = width // groups
     arrived = exchange(part.reshape(groups, share, -1), REL)
     bias_share = lax.dynamic_slice_in_dim(bias, group * share, share)[:, None]
     cotangent_share = lax.dynamic_slice_in_dim(cotangent, group * share, share, 1).T
-    activated, grad_share = activation_of(arrived, bias_share, cotangent_share)
+    activated, grad_copies = activation_of(arrived, bias_share, cotangent_share)
     output = activated.T
-    grads = copies(grad_share, REL, groups).reshape(width, -1)
-
-    keep, send = backward_of(place, slots, adjacency, grads, w_mine, w_theirs, owners)
-    received = swap(send, "xl")
-    partial = (keep.astype(F32) + received.astype(F32)).astype(BF16)
+    grads = exchange(grad_copies, REL).reshape(width, -1)
+
+    partial = backward_of(place, slots, adjacency, grads, w_mine, w_theirs, owners)
     returned = exchange(partial, TGT)
     cut = owned_of(place, source_blocks, returned, groups)
-    columns = exchange(cut, REL).reshape(2, 4, 2, BLK // groups, 96)
-    grad_features = columns.transpose(2, 3, 1, 0, 4).reshape(2, BLK // groups, width)
-
-    terms = weight_terms_of(messages, grads)
-    pair = exchange(terms, "core").astype(F32)
-    chip = (pair[0] + pair[1]).astype(BF16).reshape(16, 48, width)
-    pieces = exchange(chip, ("xh", "z"))
-    piece = jnp.sum(pieces.astype(F32), axis=0).reshape(2, 24, width)
-    grad_weights = lax.ppermute(piece, ("y", *TGT), to_owner())
+    columns = exchange(cut, REL).reshape(2, 4, 2, BLK // groups, 192).sum(axis=0)
+    grad_features = columns.transpose(1, 2, 0, 3).reshape(2, BLK // groups, width)
+
+    late_grads, _ = lax.optimization_barrier((grads, partial))
+    keep, send = weight_terms_of(place, messages, late_grads)
+    chip = (keep + swap(send, "core").astype(F32)).reshape(16, 48, width)
+    piece = lax.psum_scatter(chip, ("xh", "z"), scatter_dimension=0, tiled=True)
+    grad_weights = lax.ppermute(piece.reshape(2, 24, width), ("y", *TGT), to_owner())
     return (output, grad_weights, grad_features)
 
 

time: 249 us -> 384 us (1.54)
  waiting for transfers between devices: 94.6 us -> 206 us
  blocking collectives: 26.4 us -> 70.4 us
  starting transfers between devices: 57.8 us -> 38.5 us
    reduce_scatter x0 -> x1, waiting for transfers between devices: none -> 151 us  [per_device(): piece = lax.psum_scatter(chip, ('xh', 'z'), scatter_dimension=0, tiled=True)]
    all_to_all x6 -> x3, waiting for transfers between devices: 59.9 us -> 6.96 us  [exchange(): return lax.all_to_all(value, axis, 0, 0, tiled=True)]
    all_to_all x3 -> x2, blocking collectives: 26.4 us -> 70.4 us  [exchange(): return lax.all_to_all(value, axis, 0, 0, tiled=True)]
    ppermute x1 -> x7, waiting for transfers between devices: 0.01 us -> 36.3 us  [the longest x6 28.4 us: around(): lax.ppermute(v, axis, [(i, (i + k) % size) for i in range(size)])]
    ppermute x3 -> x2, waiting for transfers between devices: 34.6 us -> 3.06 us  [swap(): return lax.ppermute(value, axis, [(0, 1), (1, 0)])]
    all_to_all x6 -> x3, starting transfers between devices: 45.7 us -> 23.7 us  [exchange(): return lax.all_to_all(value, axis, 0, 0, tiled=True)]
    all_gather x1, waiting for transfers between devices: 0.01 us -> 8.05 us  [per_device(): adjacency = lax.all_gather(own_adjacency, 'y', axis=0, tiled=True)]
    ppermute x1 -> x7, starting transfers between devices: 10.4 us -> 14.6 us  [the longest x6 7.77 us: around(): lax.ppermute(v, axis, [(i, (i + k) % size) for i in range(size)])]
  transfers between devices with their start and end apart: 11 -> 14, of which waited for: 7 -> 12; matrix products, arithmetic and copies ran while one was open for 4% -> 2% of each run, Pallas kernels for 6% -> 1%
where the time goes in v2:
time: 384 us; the launch traced here: 381 us
  waiting for transfers between devices  206 us (54%)
  blocking collectives  70.4 us (18%)
  Pallas kernels  39.6 us (10%)
  starting transfers between devices  38.5 us (10%)
  between operations  14.2 us (4%)
  local copies, waits for them, and re-layouts  7.58 us (2%)
  other arithmetic  4.88 us (1%)
    reduce_scatter x1, waiting for transfers between devices, per_device(): piece = lax.psum_scatter(chip, ('xh', 'z'), scatter_dimension=0, tiled=True)  151 us
    all_to_all x2, blocking collectives, exchange(): return lax.all_to_all(value, axis, 0, 0, tiled=True)  70.4 us
    ppermute x6, waiting for transfers between devices, around(): lax.ppermute(v, axis, [(i, (i + k) % size) for i in range(size)])  28.4 us
    all_to_all x3, starting transfers between devices, exchange(): return lax.all_to_all(value, axis, 0, 0, tiled=True)  23.7 us
    pallas_call x1, Pallas kernels, backward_of(): pl.pallas_call(backward_kernel, grid_spec=spec, out_shape=jax.ShapeDtypeS...  10.9 us
    pallas_call x1, Pallas kernels, forward_of(): pl.pallas_call(forward_kernel, grid_spec=spec, out_shape=[jax.ShapeDtypeS...  10.6 us
    all_gather x1, waiting for transfers between devices, per_device(): adjacency = lax.all_gather(own_adjacency, 'y', axis=0, tiled=True)  8.05 us
    ppermute x1, waiting for transfers between devices, per_device(): lax.ppermute(piece.reshape(2, 24, width), ('y', *TGT), to_owner())  7.89 us
  transfers between devices with their start and end apart: 14, of which 12 were waited for; matrix products, arithmetic and copies ran while one was open for 2% of the time, Pallas kernels for 1%

profile of v2, /device:TPU:56, one launch (start us, length us, event | category | flops | bytes accessed | tf_op | source)
XLA Modules:
  0.0 380.8 jit_solution(7034603081086355056)
XLA Ops:
  7.2 5.8 %adjacency.1 = bf16[2,256,1024]{2,1,0:T(8,128)(2,1)} custom-call(s32[2,2]{1,0:T(2,128)} %count_ref.1, s32[2,256,8,128]{3,2,1,0:T(8,128)} %values_ref.1), custom_call_target="tpu_custom_call" | custom-call | tf_op jit(solution)/shard_map/adjacency/pallas_call | solution.py:52
  13.7 2.7 outgoing.1
  16.4 11.2 %all-to-all-start = ((bf16[32,192,128]{2,1,0:T(8,128)(2,1)}), bf16[32,192,128]{2,1,0:T(8,128)(2,1)S(1)}, u32[]{:S(2)}, u32[]{:S(2)}) async-start(bf16[32,192,128]{2,1,0:T(8,128)(2,1)} %outgoing.1), calls=%async_computation | async-start | bytes 3145728 | tf_op jit(solution)/shard_map/all_to_all | solution.py:313
  30.8 2.2 collective-permute-start.3
  33.0 15.3 %collective-permute-done.5 = bf16[1,192,768]{2,1,0:T(8,128)(2,1)S(1)} collective-permute-done((bf16[1,192,768]{2,1,0:T(8,128)(2,1)S(1)}, bf16[1,192,768]{2,1,0:T(8,128)(2,1)S(1)}, u32[]{:S(2)}, u32[]{:S(2)}) %collective-permute-start.5) | collective-permute-done | bytes 294944 | tf_op jit(solution)/shard_map/ppermute | solution.py:318
  48.3 8.7 %collective-permute-done.4 = bf16[1,192,768]{2,1,0:T(8,128)(2,1)S(1)} collective-permute-done((bf16[1,192,768]{2,1,0:T(8,128)(2,1)S(1)}, bf16[1,192,768]{2,1,0:T(8,128)(2,1)S(1)}, u32[]{:S(2)}, u32[]{:S(2)}) %collective-permute-start.4) | collective-permute-done | bytes 294944 | tf_op jit(solution)/shard_map/ppermute | solution.py:318
  57.0 2.7 collective-permute-done.3
  61.4 2.5 collective-permute-start
  66.3 3.0 all-to-all-done.fetched_ref
  69.3 8.1 %all-gather.2.cloned.1.call-done.adj_ref = bf16[8,256,1024]{2,1,0:T(8,128)(2,1)} async-done(((bf16[2,256,1024]{2,1,0:T(8,128)(2,1)}), bf16[8,256,1024]{2,1,0:T(8,128)(2,1)}) %all-gather.2.cloned.1.call-update) | async-done | bytes 4194320 | tf_op jit(solution)/shard_map/all_gather | solution.py:348
  77.4 10.6 %forward.1 = (bf16[8,192,256]{2,1,0:T(8,128)(2,1)}, bf16[768,256]{1,0:T(8,128)(2,1)}) custom-call(s32[4]{0:T(128)} %pad_add_fusion.place_ref, s32[128]{0:T(128)} %pad_add_fusion.1.slot_ref, bf16[8,256,1024]{2,1,0:T(8,128)(2,1)} %all-gather.2.cloned.1.call-done.adj_ref, bf16[32,192,128]{2,1,0:T(8,128)(2,1)} %copy-done.2, bf16[4,192,768]{2,1,0:T(8,128)(2,1)} %copy-done.1, ...), custom_call_target="tpu_custom_call" | custom-call | tf_op jit(solution)/shard_map/forward/pallas_call | solution.py:145
  88.0 5.9 %all-to-all-start.1 = ((bf16[8,96,256]{2,1,0:T(8,128)(2,1)}), bf16[8,96,256]{2,1,0:T(8,128)(2,1)S(1)}, u32[]{:S(2)}, u32[]{:S(2)}) async-start(bf16[8,96,256]{2,1,0:T(8,128)(2,1)} %bitcast.19), calls=%async_computation.1 | async-start | bytes 786432 | tf_op jit(solution)/shard_map/all_to_all | solution.py:313
  96.2 3.9 %all-to-all-done.1.arrived_ref = bf16[8,96,256]{2,1,0:T(8,128)(2,1)S(1)} async-done(((bf16[8,96,256]{2,1,0:T(8,128)(2,1)}), bf16[8,96,256]{2,1,0:T(8,128)(2,1)S(1)}, u32[]{:S(2)}, u32[]{:S(2)}) %all-to-all-start.1) | async-done | bytes 393248 | tf_op jit(solution)/shard_map/all_to_all | solution.py:313
  102.9 12.3 %all_to_all.25 = bf16[8,96,256]{2,1,0:T(8,128)(2,1)} all-to-all(bf16[8,96,256]{2,1,0:T(8,128)(2,1)} %get-tuple-element.13), channel_id=1, replica_groups=mesh['xl'=2,'y'=4,'xh'=2,'z'=8,'core'=2] {'xl','y'}, dimensions={0} | all-to-all | bytes 786432 | tf_op jit(solution)/shard_map/all_to_all | solution.py:313
  115.2 10.9 %backward.1 = bf16[32,192,128]{2,1,0:T(8,128)(2,1)} custom-call(s32[4]{0:T(128)} %pad_add_fusion.place_ref, s32[128]{0:T(128)} %pad_add_fusion.1.slot_ref, bf16[8,256,1024]{2,1,0:T(8,128)(2,1)} %all-gather.2.cloned.1.call-done.adj_ref, bf16[768,256]{1,0:T(8,128)(2,1)} %bitcast.15, bf16[4,192,768]{2,1,0:T(8,128)(2,1)} %copy-done.1, ...), custom_call_target="tpu_custom_call" | custom-call | tf_op jit(solution)/shard_map/backward/pallas_call | solution.py:230
  126.1 4.8 %weight_terms.1 = (f32[4,4,48,768]{3,2,1,0:T(8,128)}, bf16[4,4,48,768]{3,2,1,0:T(8,128)(2,1)}) custom-call(s32[4]{0:T(128)} %pad_add_fusion.place_ref, bf16[8,192,256]{2,1,0:T(8,128)(2,1)} %get-tuple-element.12.messages_ref, bf16[768,256]{1,0:T(8,128)(2,1)} %bitcast.16), custom_call_target="tpu_custom_call" | custom-call | tf_op jit(solution)/shard_map/weight_terms/pallas_call | solution.py:264
  130.9 3.1 collective-permute-done.7
  133.9 3.4 convert_add_fusion
  138.7 58.1 %all_to_all.26.arrived_ref = bf16[32,192,128]{2,1,0:T(8,128)(2,1)} all-to-all(bf16[32,192,128]{2,1,0:T(8,128)(2,1)S(1)} %copy-done.3), channel_id=1, replica_groups=mesh['xl'=2,'y'=4,'xh'=2,'z'=8,'core'=2] {'xh','z','core'}, dimensions={0} | all-to-all | bytes 3145728 | tf_op jit(solution)/shard_map/all_to_all | solution.py:313
  196.8 3.0 owned.1
  199.8 6.6 %all-to-all-start.4 = ((f32[8,2,16,192]{3,2,1,0:T(8,128)}), f32[8,2,16,192]{3,2,1,0:T(8,128)S(1)}, u32[]{:S(2)}, u32[]{:S(2)}) async-start(f32[8,2,16,192]{3,2,1,0:T(8,128)} %owned.1), calls=%async_computation.5 | async-start | bytes 524288 | tf_op jit(solution)/shard_map/all_to_all | solution.py:313
  206.4 151.3 %reduce-scatter.2.cloned.1.call-done = f32[1,48,768]{2,1,0:T(8,128)} async-done(((f32[16,48,768]{2,1,0:T(8,128)}), f32[1,48,768]{2,1,0:T(8,128)}) %reduce-scatter.2.cloned.1.call-update) | async-done | bytes 147472 | tf_op jit(solution)/shard_map/reduce_scatter | solution.py:377
  357.7 6.9 %collective-permute-start.8 = (f32[2,24,768]{2,1,0:T(8,128)}, f32[2,24,768]{2,1,0:T(8,128)S(1)}, u32[]{:S(2)}, u32[]{:S(2)}) collective-permute-start(f32[2,24,768]{2,1,0:T(8,128)} %bitcast.21), channel_id=1, source_target_pairs={{0,0},{1,1},{2,2},{3,3},{4,4},{5,5},{6,6},{7,7},{8,32},{9,33},{10,... | collective-permute-start | bytes 442376 | tf_op jit(solution)/shard_map/ppermute | solution.py:378
  365.5 7.9 %collective-permute-done.8 = f32[2,24,768]{2,1,0:T(8,128)S(1)} collective-permute-done((f32[2,24,768]{2,1,0:T(8,128)}, f32[2,24,768]{2,1,0:T(8,128)S(1)}, u32[]{:S(2)}, u32[]{:S(2)}) %collective-permute-start.8) | collective-permute-done | bytes 147488 | tf_op jit(solution)/shard_map/ppermute | solution.py:378
  (41 shorter events, 16.0 us)
Async XLA Ops:
  7.2 88.2 %copy-start = (bf16[256,768]{1,0:T(8,128)(2,1)S(1)}, bf16[256,768]{1,0:T(8,128)(2,1)}, u32[]{:S(2)}) copy-start(bf16[256,768]{1,0:T(8,128)(2,1)} %param.11) | copy-start | bytes 1179652
  7.2 70.2 %all-gather.2.cloned.1.call-start = ((), (), s32[]{:S(2)}) async-start(), calls=%async_computation.6 | async-start | bytes 5242880 | tf_op jit(solution)/shard_map/all_gather | solution.py:348
  16.4 52.9 %all-to-all-start = ((bf16[32,192,128]{2,1,0:T(8,128)(2,1)}), bf16[32,192,128]{2,1,0:T(8,128)(2,1)S(1)}, u32[]{:S(2)}, u32[]{:S(2)}) async-start(bf16[32,192,128]{2,1,0:T(8,128)(2,1)} %outgoing.1), calls=%async_computation | async-start | bytes 3145728 | tf_op jit(solution)/shard_map/all_to_all | solution.py:313
  29.1 30.9 %copy-start.5 = (s32[2,2,8]{2,1,0:T(2,128)S(1)}, s32[2,2,8]{2,1,0:T(2,128)}, u32[]{:S(2)}) copy-start(s32[2,2,8]{2,1,0:T(2,128)} %param.14) | copy-start | bytes 388
  29.1 19.2 %collective-permute-start.5 = (bf16[1,192,768]{2,1,0:T(8,128)(2,1)S(1)}, bf16[1,192,768]{2,1,0:T(8,128)(2,1)S(1)}, u32[]{:S(2)}, u32[]{:S(2)}) collective-permute-start(bf16[1,192,768]{2,1,0:T(8,128)(2,1)S(1)} %get-tuple-element.19), channel_id=1, source_target_pairs={{0,96},{32,0},{64,32},{96,64},{1,97},{33,1},{65,33},{97,65},{2,98}... | collective-permute-start | bytes 884744 | tf_op jit(solution)/shard_map/ppermute | solution.py:318
  29.9 27.1 %collective-permute-start.4 = (bf16[1,192,768]{2,1,0:T(8,128)(2,1)S(1)}, bf16[1,192,768]{2,1,0:T(8,128)(2,1)S(1)}, u32[]{:S(2)}, u32[]{:S(2)}) collective-permute-start(bf16[1,192,768]{2,1,0:T(8,128)(2,1)S(1)} %get-tuple-element.20), channel_id=1, source_target_pairs={{0,64},{32,96},{64,0},{96,32},{1,65},{33,97},{65,1},{97,33},{2,66}... | collective-permute-start | bytes 884744 | tf_op jit(solution)/shard_map/ppermute | solution.py:318
  30.8 28.8 %collective-permute-start.3 = (bf16[1,192,768]{2,1,0:T(8,128)(2,1)S(1)}, bf16[1,192,768]{2,1,0:T(8,128)(2,1)S(1)}, u32[]{:S(2)}, u32[]{:S(2)}) collective-permute-start(bf16[1,192,768]{2,1,0:T(8,128)(2,1)S(1)} %get-tuple-element.18), channel_id=1, source_target_pairs={{0,32},{32,64},{64,96},{96,0},{1,33},{33,65},{65,97},{97,1},{2,34}... | collective-permute-start | bytes 884744 | tf_op jit(solution)/shard_map/ppermute | solution.py:318
  59.8 17.6 %copy-start.1 = (bf16[4,192,768]{2,1,0:T(8,128)(2,1)}, bf16[4,192,768]{2,1,0:T(8,128)(2,1)S(1)}, u32[]{:S(2)}) copy-start(bf16[4,192,768]{2,1,0:T(8,128)(2,1)S(1)} %pad_maximum_fusion.w_mine_ref) | copy-start | bytes 3538948
  59.8 6.5 %collective-permute-start.6 = (bf16[4,192,768]{2,1,0:T(8,128)(2,1)S(1)}, bf16[4,192,768]{2,1,0:T(8,128)(2,1)}, u32[]{:S(2)}, u32[]{:S(2)}) collective-permute-start(bf16[4,192,768]{2,1,0:T(8,128)(2,1)S(1)} %pad_maximum_fusion.w_mine_ref), channel_id=1, source_target_pairs={{0,1},{1,0},{2,3},{3,2},{4,5},{5,4},{6,7},{7,6},{8,9},{9,8},{10,11... | collective-permute-start | bytes 3538952 | tf_op jit(solution)/shard_map/ppermute | solution.py:309
  60.0 4.8 %collective-permute-start.2 = (s32[32]{0:T(128)S(1)}, s32[32]{0:T(128)S(1)}, u32[]{:S(2)}, u32[]{:S(2)}) collective-permute-start(s32[32]{0:T(128)S(1)} %reshape.27), channel_id=1, source_target_pairs={{0,96},{32,0},{64,32},{96,64},{1,97},{33,1},{65,33},{97,65},{2,98}... | collective-permute-start | bytes 392 | tf_op jit(solution)/shard_map/ppermute | solution.py:318
  60.0 5.1 %collective-permute-start.1 = (s32[32]{0:T(128)S(1)}, s32[32]{0:T(128)S(1)}, u32[]{:S(2)}, u32[]{:S(2)}) collective-permute-start(s32[32]{0:T(128)S(1)} %reshape.27), channel_id=1, source_target_pairs={{0,64},{32,96},{64,0},{96,32},{1,65},{33,97},{65,1},{97,33},{2,66}... | collective-permute-start | bytes 392 | tf_op jit(solution)/shard_map/ppermute | solution.py:318
  61.4 4.3 %collective-permute-start = (s32[32]{0:T(128)S(1)}, s32[32]{0:T(128)S(1)}, u32[]{:S(2)}, u32[]{:S(2)}) collective-permute-start(s32[32]{0:T(128)S(1)} %reshape.27), channel_id=1, source_target_pairs={{0,32},{32,64},{64,96},{96,0},{1,33},{33,65},{65,97},{97,1},{2,34}... | collective-permute-start | bytes 392 | tf_op jit(solution)/shard_map/ppermute | solution.py:318
  69.3 8.1 %copy-start.2 = (bf16[32,192,128]{2,1,0:T(8,128)(2,1)}, bf16[32,192,128]{2,1,0:T(8,128)(2,1)S(1)}, u32[]{:S(2)}) copy-start(bf16[32,192,128]{2,1,0:T(8,128)(2,1)S(1)} %all-to-all-done.fetched_ref) | copy-start | bytes 4718596
  88.0 12.2 %all-to-all-start.1 = ((bf16[8,96,256]{2,1,0:T(8,128)(2,1)}), bf16[8,96,256]{2,1,0:T(8,128)(2,1)S(1)}, u32[]{:S(2)}, u32[]{:S(2)}) async-start(bf16[8,96,256]{2,1,0:T(8,128)(2,1)} %bitcast.19), calls=%async_computation.1 | async-start | bytes 786432 | tf_op jit(solution)/shard_map/all_to_all | solution.py:313
  93.9 263.8 %reduce-scatter.2.cloned.1.call-start = ((), (), s32[]{:S(2)}) async-start(), calls=%async_computation.7 | async-start | bytes 2506752 | tf_op jit(solution)/shard_map/reduce_scatter | solution.py:377
  100.1 0.8 copy-start.4
  130.9 3.1 collective-permute-start.7
  137.3 1.4 copy-start.3
  199.8 164.8 %all-to-all-start.4 = ((f32[8,2,16,192]{3,2,1,0:T(8,128)}), f32[8,2,16,192]{3,2,1,0:T(8,128)S(1)}, u32[]{:S(2)}, u32[]{:S(2)}) async-start(f32[8,2,16,192]{3,2,1,0:T(8,128)} %owned.1), calls=%async_computation.5 | async-start | bytes 524288 | tf_op jit(solution)/shard_map/all_to_all | solution.py:313
  357.7 15.7 %collective-permute-start.8 = (f32[2,24,768]{2,1,0:T(8,128)}, f32[2,24,768]{2,1,0:T(8,128)S(1)}, u32[]{:S(2)}, u32[]{:S(2)}) collective-permute-start(f32[2,24,768]{2,1,0:T(8,128)} %bitcast.21), channel_id=1, source_target_pairs={{0,0},{1,1},{2,2},{3,3},{4,4},{5,5},{6,6},{7,7},{8,32},{9,33},{10,... | collective-permute-start | bytes 442376 | tf_op jit(solution)/shard_map/ppermute | solution.py:378
Sparse Core Ops, SparseCore 0:
  13.1 64.1 all-gather.1
  137.5 220.1 reduce-scatter.1

commit v3 on v2

v3 whole, which is shorter than its diff:
```python
import functools

import jax
import jax.numpy as jnp
from jax import lax
from jax.experimental import pallas as pl
from jax.experimental.pallas import tpu as pltpu
from jax.sharding import Mesh, PartitionSpec as P

F32 = jnp.float32
BF16 = jnp.bfloat16
BLK = 128
REL = ("xl", "y")
TGT = ("xh", "z", "core")
VMEM_LIMIT = 60 * 1024 * 1024


def params(*semantics):
    return pltpu.CompilerParams(
        dimension_semantics=semantics or None, vmem_limit_bytes=VMEM_LIMIT
    )


def smem():
    return pl.BlockSpec(memory_space=pltpu.MemorySpace.SMEM)


def vmem():
    return pl.BlockSpec(memory_space=pltpu.MemorySpace.VMEM)


def dot(a, b, ca, cb):
    return lax.dot_general(a, b, (((ca,), (cb,)), ((), ())), preferred_element_type=F32)


def adjacency_kernel(count_ref, values_ref, out_ref, *, relation):
    count = count_ref[relation, pl.program_id(0)]
    slots = values_ref.shape[2]
    live, degree = [], None
    for s in range(slots):
        v = values_ref[0, :, s, :]
        v = jnp.where(s < count, v, jnp.zeros_like(v)).astype(F32)
        live.append(v)
        degree = v if degree is None else degree + v
    total = jnp.sum(degree, axis=1, keepdims=True)
    scale = 1.0 / jnp.sqrt(jnp.maximum(total, 1.0))
    for s in range(slots):
        out_ref[:, s * BLK : (s + 1) * BLK] = (live[s] * scale).astype(BF16)


def adjacency_of(tile_values, tile_count, relation):
    _, rows, slots, cols = tile_values.shape
    return pl.pallas_call(
        functools.partial(adjacency_kernel, relation=relation),
        grid=(rows // BLK,),
        in_specs=[smem(), pl.BlockSpec((1, BLK, slots, cols), lambda q: (relation, q, 0, 0))],
        out_specs=pl.BlockSpec((BLK, slots * cols), lambda q: (q, 0)),
        out_shape=jax.ShapeDtypeStruct((rows, slots * cols), BF16),
        compiler_params=params("arbitrary"),
        name="adjacency",
    )(tile_count, tile_values)


def outgoing_kernel(place_ref, table_ref, features_ref, out_ref, turned_ref):
    owner, first = place_ref[0], place_ref[1]
    turned_ref[...] = features_ref[...].T
    piece = turned_ref[pl.ds(pl.multiple_of(first, 64), 192), :]
    block0, block1 = piece[:, :BLK], piece[:, BLK:]
    for t in range(out_ref.shape[0]):
        k = table_ref[t, owner]
        picked = jnp.where(k == 1, block1, block0)
        out_ref[t] = jnp.where(k >= 0, picked, jnp.zeros_like(picked))


def outgoing_of(features, source_blocks, place):
    rows, width = features.shape
    return pl.pallas_call(
        outgoing_kernel,
        in_specs=[smem(), smem(), vmem()],
        out_specs=vmem(),
        out_shape=jax.ShapeDtypeStruct((source_blocks.shape[0], 192, BLK), BF16),
        scratch_shapes=[pltpu.VMEM((width, rows), BF16)],
        compiler_params=params(),
        name="outgoing",
    )(place, source_blocks, features)


def start_loads(place_ref, steps, adj_refs, adj_buf, w_mine_ref, w_theirs_ref, w_buf, sems):
    core = place_ref[2]
    loads = []
    ks = sorted({k for k, _ in steps}, key=[k for k, _ in steps].index)
    for n, k in enumerate(ks):
        for half, ref in ((core, w_mine_ref), (1 - core, w_theirs_ref)):
            loads.append(pltpu.make_async_copy(ref.at[k], w_buf.at[2 * n + half], sems.at[len(loads)]))
        for p in range(2):
            at = steps.index((k, p))
            loads.append(pltpu.make_async_copy(adj_refs[at], adj_buf.at[at], sems.at[len(loads)]))
    for load in loads:
        load.start()
    return [loads[4 * n : 4 * n + 4] for n in range(len(ks))]


def forward_kernel(place_ref, slot_ref, *refs, steps, first, last):
    count = len(steps)
    adj_refs, refs = refs[:count], refs[count:]
    fetched_ref, w_mine_ref, w_theirs_ref, *refs = refs
    if not first:
        before_ref, *refs = refs
    messages_ref, pre_ref, adj_buf, w_buf, acc_ref, sems = refs
    groups = start_loads(
        place_ref, steps, adj_refs, adj_buf, w_mine_ref, w_theirs_ref, w_buf, sems
    )
    for n, (k, p) in enumerate(steps):
        if p == 0:
            for load in groups[n // 2]:
                load.wait()
        for q in range(2):
            base = ((k * 2 + p) * 2 + q) * 8
            wide = jnp.concatenate([fetched_ref[slot_ref[base + s]] for s in range(8)], axis=1)
            part = adj_buf[n, q * BLK : (q + 1) * BLK, :]
            messages_ref[n, :, q * BLK : (q + 1) * BLK] = dot(wide, part, 1, 1).astype(BF16)
        if p == 1:
            deep = 2 * w_buf.shape[1]
            w = w_buf[n - 1 : n + 1].reshape(deep, w_buf.shape[2])
            term = dot(w, messages_ref[n - 1 : n + 1].reshape(deep, -1), 0, 0)
            if n == 1 and not first:
                term = term + before_ref[...]
            if n + 1 == count:
                total = term if n == 1 else acc_ref[...] + term
                pre_ref[...] = total.astype(pre_ref.dtype)
            elif n == 1:
                acc_ref[...] = term
            else:
                acc_ref[...] += term


def anywhere():
    return pl.BlockSpec(memory_space=pl.ANY)


def forward_of(place, slots, steps, adjacencies, fetched, w_mine, w_theirs, before, last):
    rows, wide = adjacencies[0].shape
    width = w_mine.shape[2]
    count = len(steps)
    extra = [] if before is None else [before]
    return pl.pallas_call(
        functools.partial(forward_kernel, steps=steps, first=before is None, last=last),
        in_specs=[smem(), smem()] + [anywhere()] * count + [vmem(), anywhere(), anywhere()] + [vmem()] * len(extra),
        out_specs=[vmem(), vmem()],
        out_shape=[
            jax.ShapeDtypeStruct((count, 192, rows), BF16),
            jax.ShapeDtypeStruct((width, rows), BF16 if last else F32),
        ],
        scratch_shapes=[
            pltpu.VMEM((count, rows, wide), BF16),
            pltpu.VMEM((count, 192, width), BF16),
            pltpu.VMEM((width, rows), F32),
            pltpu.SemaphoreType.DMA((2 * count,)),
        ],
        compiler_params=params(),
        name="forward",
    )(place, slots, *adjacencies, fetched, w_mine, w_theirs, *extra)


def activation_kernel(arrived_ref, bias_ref, cotangent_ref, act_ref, grad_ref):
    pre = bias_ref[...]
    for g in range(arrived_ref.shape[0]):
        pre = pre + arrived_ref[g].astype(F32)
    sigmoid = jax.nn.sigmoid(pre)
    act_ref[...] = (pre * sigmoid).astype(BF16)
    derivative = sigmoid * (1.0 + pre * (1.0 - sigmoid))
    grad = (cotangent_ref[...].astype(F32) * derivative).astype(BF16)
    for g in range(grad_ref.shape[0]):
        grad_ref[g] = grad


def activation_of(arrived, bias, cotangent):
    return pl.pallas_call(
        activation_kernel,
        in_specs=[vmem()] * 3,
        out_specs=[vmem()] * 2,
        out_shape=[
            jax.ShapeDtypeStruct(arrived.shape[1:], BF16),
            jax.ShapeDtypeStruct(arrived.shape, BF16),
        ],
        compiler_params=params(),
        name="activation",
    )(arrived, bias, cotangent)


def backward_kernel(place_ref, slot_ref, *refs, steps):
    count = len(steps)
    adj_refs, refs = refs[:count], refs[count:]
    grad_ref, w_mine_ref, w_theirs_ref, out_ref, adj_buf, w_buf, acc_ref, sems = refs
    groups = start_loads(
        place_ref, steps, adj_refs, adj_buf, w_mine_ref, w_theirs_ref, w_buf, sems
    )
    acc_ref[...] = jnp.zeros_like(acc_ref)
    for n, (k, p) in enumerate(steps):
        if p == 0:
            for load in groups[n // 2]:
                load.wait()
        grads = dot(w_buf[n], grad_ref[...], 1, 0).astype(BF16)
        for q in range(2):
            base = ((k * 2 + p) * 2 + q) * 8
            part = adj_buf[n, q * BLK : (q + 1) * BLK, :]
            wide = dot(grads[:, q * BLK : (q + 1) * BLK], part, 1, 0)
            for s in range(8):
                acc_ref[slot_ref[base + s]] += wide[:, s * BLK : (s + 1) * BLK]
    out_ref[...] = acc_ref[...].astype(BF16)


def backward_of(place, slots, steps, adjacencies, grads, w_mine, w_theirs, owners):
    rows, wide = adjacencies[0].shape
    width = w_mine.shape[2]
    count = len(steps)
    return pl.pallas_call(
        functools.partial(backward_kernel, steps=steps),
        in_specs=[smem(), smem()] + [anywhere()] * count + [vmem(), anywhere(), anywhere()],
        out_specs=vmem(),
        out_shape=jax.ShapeDtypeStruct((owners, 192, BLK), BF16),
        scratch_shapes=[
            pltpu.VMEM((count, rows, wide), BF16),
            pltpu.VMEM((count, 192, width), BF16),
            pltpu.VMEM((owners, 192, BLK), F32),
            pltpu.SemaphoreType.DMA((2 * count,)),
        ],
        compiler_params=params(),
        name="backward",
    )(place, slots, *adjacencies, grads, w_mine, w_theirs)


def weight_kernel(place_ref, early_ref, late_ref, grad_ref, keep_ref, send_ref):
    core = place_ref[2]

    def cut(first, second, even_ref, odd_ref):
        for m in range(8):
            rows = slice(m * 24, (m + 1) * 24)
            piece = jnp.concatenate([first[rows], second[rows]], axis=0)
            target = odd_ref if m % 2 else even_ref
            target[0, m // 2] = piece.astype(target.dtype)

    def terms(messages_ref):
        first = dot(messages_ref[0], grad_ref[...], 1, 1)
        second = dot(messages_ref[1], grad_ref[...], 1, 1)

        @pl.when(core == 0)
        def _():
            cut(first, second, keep_ref, send_ref)

        @pl.when(core == 1)
        def _():
            cut(first, second, send_ref, keep_ref)

    @pl.when(pl.program_id(0) < 3)
    def _():
        terms(early_ref)

    @pl.when(pl.program_id(0) == 3)
    def _():
        terms(late_ref)


def weight_terms_of(place, early, late, grads):
    _, deep, rows = early.shape
    width = grads.shape[0]
    out = pl.BlockSpec((1, 4, 48, width), lambda i, p: ((p[3] - (i ^ (i >> 1))) & 3, 0, 0, 0))
    spec = pltpu.PrefetchScalarGridSpec(
        num_scalar_prefetch=1,
        grid=(4,),
        in_specs=[
            pl.BlockSpec((2, deep, rows), lambda i, p: (jnp.minimum(i, 2), 0, 0)),
            pl.BlockSpec((2, deep, rows), lambda i, p: (0, 0, 0)),
            pl.BlockSpec((width, rows), lambda i, p: (0, 0)),
        ],
        out_specs=[out, out],
    )
    return pl.pallas_call(
        weight_kernel,
        grid_spec=spec,
        out_shape=[
            jax.ShapeDtypeStruct((4, 4, 48, width), F32),
            jax.ShapeDtypeStruct((4, 4, 48, width), BF16),
        ],
        compiler_params=params("arbitrary"),
        name="weight_terms",
    )(place, early, late, grads)


def halve_kernel(bit_ref, keep_ref, came_ref, next_ref, send_ref, *, stride):
    bit = bit_ref[0]
    for i in range(next_ref.shape[0]):
        low = (i // stride) * 2 * stride + i % stride
        mine = low + bit * stride
        other = low + (1 - bit) * stride
        send_ref[i] = (keep_ref[other] + came_ref[other].astype(F32)).astype(BF16)
        next_ref[i] = keep_ref[mine] + came_ref[mine].astype(F32)


def halve(bit, keep, came, stride):
    shape = (keep.shape[0] // 2, *keep.shape[1:])
    return pl.pallas_call(
        functools.partial(halve_kernel, stride=stride),
        in_specs=[smem(), vmem(), vmem()],
        out_specs=[vmem(), vmem()],
        out_shape=[jax.ShapeDtypeStruct(shape, F32), jax.ShapeDtypeStruct(shape, BF16)],
        compiler_params=params(),
        name="halve",
    )(bit.astype(jnp.int32).reshape(1), keep, came)


def owned_kernel(place_ref, table_ref, arrived_ref, out_ref):
    owner = place_ref[0]
    zero = jnp.zeros(arrived_ref.shape[1:], F32)
    sums = [zero, zero]
    for t in range(arrived_ref.shape[0]):
        k = table_ref[t, owner]
        v = arrived_ref[t].astype(F32)
        for b in range(2):
            sums[b] = sums[b] + jnp.where(k == b, v, zero)
    for b in range(2):
        turned = sums[b].T
        for g in range(out_ref.shape[0]):
            out_ref[g, b] = turned[g * 16 : (g + 1) * 16, :]


def owned_of(place, source_blocks, arrived, groups):
    return pl.pallas_call(
        owned_kernel,
        in_specs=[smem(), smem(), vmem()],
        out_specs=vmem(),
        out_shape=jax.ShapeDtypeStruct((groups, 2, BLK // groups, arrived.shape[1]), F32),
        compiler_params=params(),
        name="owned",
    )(place, source_blocks, arrived)


def swap(value, axis, size=2, flip=1):
    return lax.ppermute(value, axis, [(i, i ^ flip) for i in range(size)])


def pass_on(value, axis, size, by):
    return lax.ppermute(value, axis, [(i, (i + by) % size) for i in range(size)])


def exchange(value, axis):
    return lax.all_to_all(value, axis, 0, 0, tiled=True)


def around(values, axis, size):
    return [
        lax.ppermute(v, axis, [(i, (i + k) % size) for i in range(size)])
        for k, v in enumerate(values, 1)
    ]


def to_owner():
    def place(y, xh, z, c):
        return ((y * 2 + xh) * 8 + z) * 2 + c
    moves = []
    for y in range(4):
        for xh in range(2):
            for z in range(8):
                for c in range(2):
                    target = place(2 * xh + z // 4, y // 2, 4 * (y % 2) + z % 4, c)
                    moves.append((place(y, xh, z, c), target))
    return moves


def per_device(
    features, weights, bias, cotangent, tile_values, tile_count, tile_slot, source_blocks
):
    groups = 8
    owners = source_blocks.shape[0]
    width = features.shape[1]
    xl, y, core = lax.axis_index("xl"), lax.axis_index("y"), lax.axis_index("core")
    owner = lax.axis_index(TGT)
    group = lax.axis_index(REL)
    place = jnp.stack([owner, 192 * y, core, y]).astype(jnp.int32)

    xh, z = lax.axis_index("xh"), lax.axis_index("z")
    own0 = adjacency_of(tile_values, tile_count, 0)
    own1 = adjacency_of(tile_values, tile_count, 1)
    features, own0, own1 = lax.optimization_barrier((features, own0, own1))
    back0, fore1 = pass_on(own0, "y", 4, 1), pass_on(own1, "y", 4, 3)
    back1, fore0 = pass_on(own1, "y", 4, 1), pass_on(own0, "y", 4, 3)
    fetched = exchange(outgoing_of(features, source_blocks, place), TGT)
    w_cut = [
        lax.dynamic_slice(weights, (core, ((y + k) & 3) * 192 + 96 * xh, 0), (1, 96, width))
        for k in range(4)
    ]
    w_part = jnp.concatenate([w_cut[0], *around(w_cut[1:], "y", 4)], axis=0)
    w_part, back0, fore1 = lax.optimization_barrier((w_part, back0, fore1))
    far0, far1 = pass_on(back0, "y", 4, 1), pass_on(fore1, "y", 4, 3)
    w_other = swap(w_part, "xh")
    w_mine = jnp.concatenate(
        [jnp.where(xh == 0, w_part, w_other), jnp.where(xh == 0, w_other, w_part)], axis=1
    )
    w_mine, back1, fore0 = lax.optimization_barrier((w_mine, back1, fore0))
    w_theirs = swap(w_mine, "core")
    own_slots = tile_slot.reshape(-1)
    slots = jnp.concatenate([own_slots, *around([own_slots] * 3, "y", 4)])

    near = ((0, 0), (0, 1), (1, 0), (1, 1), (3, 0), (3, 1))
    far = ((2, 0), (2, 1))
    adjacencies = (own0, own1, back0, back1, fore0, fore1, far0, far1)
    early, partway = forward_of(
        place, slots, near, adjacencies[:6], fetched, w_mine, w_theirs, None, False
    )
    late, part = forward_of(
        place, slots, far, adjacencies[6:], fetched, w_mine, w_theirs, partway, True
    )
    share = width // groups
    arrived = exchange(part.reshape(groups, share, -1), REL)
    bias_share = lax.dynamic_slice_in_dim(bias, group * share, share)[:, None]
    cotangent_share = lax.dynamic_slice_in_dim(cotangent, group * share, share, 1).T
    activated, grad_copies = activation_of(arrived, bias_share, cotangent_share)
    output = activated.T
    grads = exchange(grad_copies, REL).reshape(width, -1)

    partial = backward_of(
        place, slots, near + far, adjacencies, grads, w_mine, w_theirs, owners
    )
    returned = exchange(partial, TGT)
    cut = owned_of(place, source_blocks, returned, groups)
    columns = exchange(cut, REL).reshape(2, 4, 2, BLK // groups, 192).sum(axis=0)
    grad_features = columns.transpose(1, 2, 0, 3).reshape(2, BLK // groups, width)

    late_grads, _ = lax.optimization_barrier((grads, partial))
    keep, send = weight_terms_of(place, early, late, late_grads)
    keep, came = keep.reshape(16, 48, width), swap(send, "core").reshape(16, 48, width)
    keep, send = halve(xh, keep, came, 8)
    keep, send = halve(z & 1, keep, swap(send, "xh"), 1)
    keep, send = halve((z >> 1) & 1, keep, swap(send, "z", 8, 1), 1)
    keep, send = halve(z >> 2, keep, swap(send, "z", 8, 2), 1)
    piece = keep + swap(send, "z", 8, 4).astype(F32)
    grad_weights = lax.ppermute(piece.reshape(2, 24, width), ("y", *TGT), to_owner())
    return (output, grad_weights, grad_features)


def solution(mesh):
    fine = Mesh(mesh.devices.reshape(2, 4, 2, 8, 2), (*REL, *TGT))
    placed = (
        P(TGT, None),
        P(REL, None, None),
        P(),
        P(TGT, None),
        P(REL, TGT, None, None),
        P(REL, TGT),
        P(REL, TGT, None),
        P(),
    )
    return jax.shard_map(
        per_device,
        mesh=fine,
        in_specs=placed,
        out_specs=(P(TGT, REL), P(REL, TGT, None), P(TGT, REL, None)),
        check_vma=False,
    )
```

time: 384 us -> 240 us (0.62)
  waiting for transfers between devices: 206 us -> 103 us
  blocking collectives: 70.4 us -> 12.3 us
  starting transfers between devices: 38.5 us -> 60.2 us
  between operations: 14.2 us -> 0.86 us
  Pallas kernels: 39.6 us -> 50.1 us
    reduce_scatter x1 -> x0, waiting for transfers between devices: 151 us -> none  [per_device(): piece = lax.psum_scatter(chip, ('xh', 'z'), scatter_dimension=0, tiled=True)]
    all_to_all x2 -> x1, blocking collectives: 70.4 us -> 12.3 us  [exchange(): return lax.all_to_all(value, axis, 0, 0, tiled=True)]
    ppermute x2 -> x13, waiting for transfers between devices: 3.06 us -> 58 us  [the longest x7 57.9 us: swap(): return lax.ppermute(value, axis, [(i, i ^ flip) for i in range(size)])]
    ppermute x2 -> x13, starting transfers between devices: 0.1 us -> 17.8 us  [the longest x7 11.6 us: swap(): return lax.ppermute(value, axis, [(i, i ^ flip) for i in range(size)])]
    pallas_call x4 -> x10, Pallas kernels: 32 us -> 42.6 us  [the longest x2 11.9 us: forward_of(): pl.pallas_call(functools.partial(forward_kernel, steps=steps, first=befor...]
    all_gather x1 -> x0, waiting for transfers between devices: 8.05 us -> none  [per_device(): adjacency = lax.all_gather(own_adjacency, 'y', axis=0, tiled=True)]
    all_to_all x3 -> x4, starting transfers between devices: 23.7 us -> 29.6 us  [exchange(): return lax.all_to_all(value, axis, 0, 0, tiled=True)]
    unnamed x14 -> x24, local copies, waits for them, and re-layouts: 3.59 us -> 7.7 us
  transfers between devices with their start and end apart: 14 -> 24, of which waited for: 12 -> 13; matrix products, arithmetic and copies ran while one was open for 2% -> 2% of each run, Pallas kernels for 1% -> 10%
where the time goes in v3:
time: 240 us; the launch traced here: 239 us
  waiting for transfers between devices  103 us (43%)
  starting transfers between devices  60.2 us (25%)
  Pallas kernels  50.1 us (21%)
  blocking collectives  12.3 us (5%)
  local copies, waits for them, and re-layouts  11.4 us (5%)
    ppermute x7, waiting for transfers between devices, swap(): return lax.ppermute(value, axis, [(i, i ^ flip) for i in range(size)])  57.9 us
    ppermute x6, waiting for transfers between devices, around(): lax.ppermute(v, axis, [(i, (i + k) % size) for i in range(size)])  29.9 us
    all_to_all x4, starting transfers between devices, exchange(): return lax.all_to_all(value, axis, 0, 0, tiled=True)  29.6 us
    all_to_all x1, blocking collectives, exchange(): return lax.all_to_all(value, axis, 0, 0, tiled=True)  12.3 us
    pallas_call x2, Pallas kernels, forward_of(): pl.pallas_call(functools.partial(forward_kernel, steps=steps, first=befor...  11.9 us
    ppermute x1, waiting for transfers between devices, per_device(): lax.ppermute(piece.reshape(2, 24, width), ('y', *TGT), to_owner())  11.8 us
    ppermute x7, starting transfers between devices, swap(): return lax.ppermute(value, axis, [(i, i ^ flip) for i in range(size)])  11.6 us
    pallas_call x4, Pallas kernels, halve(): pl.pallas_call(functools.partial(halve_kernel, stride=stride), in_specs=[...  9.48 us
  transfers between devices with their start and end apart: 24, of which 13 were waited for; matrix products, arithmetic and copies ran while one was open for 2% of the time, Pallas kernels for 10%

profile of v3, /device:TPU:56, one launch (start us, length us, event | category | flops | bytes accessed | tf_op | source)
XLA Modules:
  0.0 239.1 jit_solution(15101727316479100672)
XLA Ops:
  0.6 3.7 %adjacency.2.refs_0_ = bf16[256,1024]{1,0:T(8,128)(2,1)} custom-call(s32[2,2]{1,0:T(2,128)} %count_ref.3, s32[2,256,8,128]{3,2,1,0:T(8,128)} %values_ref.3), custom_call_target="tpu_custom_call" | custom-call | tf_op jit(solution)/shard_map/adjacency/pallas_call | solution.py:53
  4.3 3.6 %adjacency.3.refs_1_ = bf16[256,1024]{1,0:T(8,128)(2,1)} custom-call(s32[2,2]{1,0:T(2,128)} %count_ref.3, s32[2,256,8,128]{3,2,1,0:T(8,128)} %values_ref.3), custom_call_target="tpu_custom_call" | custom-call | tf_op jit(solution)/shard_map/adjacency/pallas_call | solution.py:53
  11.1 11.2 %all-to-all-start = ((bf16[32,192,128]{2,1,0:T(8,128)(2,1)}), bf16[32,192,128]{2,1,0:T(8,128)(2,1)S(1)}, u32[]{:S(2)}, u32[]{:S(2)}) async-start(bf16[32,192,128]{2,1,0:T(8,128)(2,1)} %outgoing.1), calls=%async_computation | async-start | bytes 3145728 | tf_op jit(solution)/shard_map/all_to_all | solution.py:347
  28.5 12.1 %collective-permute-done.3 = bf16[1,96,768]{2,1,0:T(8,128)(2,1)S(1)} collective-permute-done((bf16[1,96,768]{2,1,0:T(8,128)(2,1)S(1)}, bf16[1,96,768]{2,1,0:T(8,128)(2,1)S(1)}, u32[]{:S(2)}, u32[]{:S(2)}) %collective-permute-start.3) | collective-permute-done | bytes 147488 | tf_op jit(solution)/shard_map/ppermute | solution.py:352
  44.3 3.1 %collective-permute-start.10 = (bf16[4,96,768]{2,1,0:T(8,128)(2,1)S(1)}, bf16[4,96,768]{2,1,0:T(8,128)(2,1)S(1)}, u32[]{:S(2)}, u32[]{:S(2)}) collective-permute-start(bf16[4,96,768]{2,1,0:T(8,128)(2,1)S(1)} %pad_maximum_fusion.1), channel_id=1, source_target_pairs={{0,16},{16,0},{1,17},{17,1},{2,18},{18,2},{3,19},{19,3},{4,20},{20... | collective-permute-start | bytes 1769480 | tf_op jit(solution)/shard_map/ppermute | solution.py:339
  49.4 17.2 %collective-permute-done.10 = bf16[4,96,768]{2,1,0:T(8,128)(2,1)S(1)} collective-permute-done((bf16[4,96,768]{2,1,0:T(8,128)(2,1)S(1)}, bf16[4,96,768]{2,1,0:T(8,128)(2,1)S(1)}, u32[]{:S(2)}, u32[]{:S(2)}) %collective-permute-start.10) | collective-permute-done | bytes 589856 | tf_op jit(solution)/shard_map/ppermute | solution.py:339
  71.7 9.9 %collective-permute-done = s32[32]{0:T(128)S(1)} collective-permute-done((s32[32]{0:T(128)S(1)}, s32[32]{0:T(128)S(1)}, u32[]{:S(2)}, u32[]{:S(2)}) %collective-permute-start) | collective-permute-done | bytes 160 | tf_op jit(solution)/shard_map/ppermute | solution.py:352
  82.3 4.0 %collective-permute-done.2 = s32[32]{0:T(128)S(1)} collective-permute-done((s32[32]{0:T(128)S(1)}, s32[32]{0:T(128)S(1)}, u32[]{:S(2)}, u32[]{:S(2)}) %collective-permute-start.2) | collective-permute-done | bytes 160 | tf_op jit(solution)/shard_map/ppermute | solution.py:352
  88.2 7.2 %forward.2 = (bf16[6,192,256]{2,1,0:T(8,128)(2,1)}, f32[768,256]{1,0:T(8,128)}) custom-call(s32[4]{0:T(128)} %pad_add_fusion.place_ref, s32[128]{0:T(128)} %pad_add_fusion.1.slot_ref, bf16[256,1024]{1,0:T(8,128)(2,1)} %adjacency.2.refs_0_, bf16[256,1024]{1,0:T(8,128)(2,1)} %adjacency.3.refs_1_, bf16[256,1024]{1,0:T(8,128)(2,1)} %collective-permute-done.6.refs_2_, ...), custom_call_target="tpu_custom_call" | custom-call | tf_op jit(solution)/shard_map/forward/pallas_call | solution.py:146
  95.4 4.7 %forward.3 = (bf16[2,192,256]{2,1,0:T(8,128)(2,1)}, bf16[768,256]{1,0:T(8,128)(2,1)}) custom-call(s32[4]{0:T(128)} %pad_add_fusion.place_ref, s32[128]{0:T(128)} %pad_add_fusion.1.slot_ref, bf16[256,1024]{1,0:T(8,128)(2,1)} %collective-permute-done.8.refs_0_.refs_6_, bf16[256,1024]{1,0:T(8,128)(2,1)} %collective-permute-done.9.refs_1_.refs_7_, ...), custom_call_target="tpu_custom_call" | custom-call | tf_op jit(solution)/shard_map/forward/pallas_call | solution.py:146
  100.1 4.5 %all-to-all-start.1 = ((bf16[8,96,256]{2,1,0:T(8,128)(2,1)}), bf16[8,96,256]{2,1,0:T(8,128)(2,1)S(1)}, u32[]{:S(2)}, u32[]{:S(2)}) async-start(bf16[8,96,256]{2,1,0:T(8,128)(2,1)} %bitcast.25), calls=%async_computation.1 | async-start | bytes 786432 | tf_op jit(solution)/shard_map/all_to_all | solution.py:347
  107.0 3.0 %all-to-all-done.1.arrived_ref = bf16[8,96,256]{2,1,0:T(8,128)(2,1)S(1)} async-done(((bf16[8,96,256]{2,1,0:T(8,128)(2,1)}), bf16[8,96,256]{2,1,0:T(8,128)(2,1)S(1)}, u32[]{:S(2)}, u32[]{:S(2)}) %all-to-all-start.1) | async-done | bytes 393248 | tf_op jit(solution)/shard_map/all_to_all | solution.py:347
  112.7 12.3 %all_to_all.25 = bf16[8,96,256]{2,1,0:T(8,128)(2,1)} all-to-all(bf16[8,96,256]{2,1,0:T(8,128)(2,1)} %get-tuple-element.43), channel_id=1, replica_groups=mesh['xl'=2,'y'=4,'xh'=2,'z'=8,'core'=2] {'xl','y'}, dimensions={0} | all-to-all | bytes 786432 | tf_op jit(solution)/shard_map/all_to_all | solution.py:347
  125.1 8.5 %backward.1 = bf16[32,192,128]{2,1,0:T(8,128)(2,1)} custom-call(s32[4]{0:T(128)} %pad_add_fusion.place_ref, s32[128]{0:T(128)} %pad_add_fusion.1.slot_ref, bf16[256,1024]{1,0:T(8,128)(2,1)} %adjacency.2.refs_0_, bf16[256,1024]{1,0:T(8,128)(2,1)} %adjacency.3.refs_1_, bf16[256,1024]{1,0:T(8,128)(2,1)} %collective-permute-done.6.refs_2_, ...), custom_call_target="tpu_custom_call" | custom-call | tf_op jit(solution)/shard_map/backward/pallas_call | solution.py:217
  133.6 8.5 %all-to-all-start.3 = ((bf16[32,192,128]{2,1,0:T(8,128)(2,1)}), bf16[32,192,128]{2,1,0:T(8,128)(2,1)S(1)}, u32[]{:S(2)}, u32[]{:S(2)}) async-start(bf16[32,192,128]{2,1,0:T(8,128)(2,1)} %backward.1), calls=%async_computation.3 | async-start | bytes 3145728 | tf_op jit(solution)/shard_map/all_to_all | solution.py:347
  142.0 5.4 %weight_terms.1 = (f32[4,4,48,768]{3,2,1,0:T(8,128)}, bf16[4,4,48,768]{3,2,1,0:T(8,128)(2,1)}) custom-call(s32[4]{0:T(128)} %pad_add_fusion.place_ref, bf16[6,192,256]{2,1,0:T(8,128)(2,1)} %get-tuple-element.41.early_ref, bf16[2,192,256]{2,1,0:T(8,128)(2,1)} %get-tuple-element.42.late_ref, bf16[768,256]{1,0:T(8,128)(2,1)} %bitcast.20), custom_call_target="tpu_custom_call" | custom-call | tf_op jit(solution)/shard_map/weight_terms/pallas_call | solution.py:278
  151.6 3.4 %halve.4 = (f32[8,48,768]{2,1,0:T(8,128)}, bf16[8,48,768]{2,1,0:T(8,128)(2,1)}) custom-call(s32[1]{0:T(128)} %bitcast.11.bit_ref, f32[16,48,768]{2,1,0:T(8,128)} %bitcast.21, bf16[16,48,768]{2,1,0:T(8,128)(2,1)} %bitcast.22), custom_call_target="tpu_custom_call" | custom-call | tf_op jit(solution)/shard_map/halve/pallas_call | solution.py:302
  155.0 3.0 %collective-permute-start.15 = (bf16[8,48,768]{2,1,0:T(8,128)(2,1)}, bf16[8,48,768]{2,1,0:T(8,128)(2,1)S(1)}, u32[]{:S(2)}, u32[]{:S(2)}) collective-permute-start(bf16[8,48,768]{2,1,0:T(8,128)(2,1)} %get-tuple-element.48), channel_id=1, source_target_pairs={{0,16},{16,0},{1,17},{17,1},{2,18},{18,2},{3,19},{19,3},{4,20},{20... | collective-permute-start | bytes 1769480 | tf_op jit(solution)/shard_map/ppermute | solution.py:339
  157.9 23.9 %collective-permute-done.15.came_ref = bf16[8,48,768]{2,1,0:T(8,128)(2,1)S(1)} collective-permute-done((bf16[8,48,768]{2,1,0:T(8,128)(2,1)}, bf16[8,48,768]{2,1,0:T(8,128)(2,1)S(1)}, u32[]{:S(2)}, u32[]{:S(2)}) %collective-permute-start.15) | collective-permute-done | bytes 589856 | tf_op jit(solution)/shard_map/ppermute | solution.py:339
  185.7 8.3 %collective-permute-done.16.came_ref = bf16[4,48,768]{2,1,0:T(8,128)(2,1)S(1)} collective-permute-done((bf16[4,48,768]{2,1,0:T(8,128)(2,1)}, bf16[4,48,768]{2,1,0:T(8,128)(2,1)S(1)}, u32[]{:S(2)}, u32[]{:S(2)}) %collective-permute-start.16) | collective-permute-done | bytes 294944 | tf_op jit(solution)/shard_map/ppermute | solution.py:339
  199.5 5.7 %collective-permute-done.17.came_ref = bf16[2,48,768]{2,1,0:T(8,128)(2,1)S(1)} collective-permute-done((bf16[2,48,768]{2,1,0:T(8,128)(2,1)}, bf16[2,48,768]{2,1,0:T(8,128)(2,1)S(1)}, u32[]{:S(2)}, u32[]{:S(2)}) %collective-permute-start.17) | collective-permute-done | bytes 147488 | tf_op jit(solution)/shard_map/ppermute | solution.py:339
  213.5 5.4 %all-to-all-start.4 = ((f32[8,2,16,192]{3,2,1,0:T(8,128)}), f32[8,2,16,192]{3,2,1,0:T(8,128)S(1)}, u32[]{:S(2)}, u32[]{:S(2)}) async-start(f32[8,2,16,192]{3,2,1,0:T(8,128)} %owned.1), calls=%async_computation.4 | async-start | bytes 524288 | tf_op jit(solution)/shard_map/all_to_all | solution.py:347
  218.9 6.8 %collective-permute-start.19 = (f32[2,24,768]{2,1,0:T(8,128)S(1)}, f32[2,24,768]{2,1,0:T(8,128)S(1)}, u32[]{:S(2)}, u32[]{:S(2)}) collective-permute-start(f32[2,24,768]{2,1,0:T(8,128)S(1)} %bitcast.27), channel_id=1, source_target_pairs={{0,0},{1,1},{2,2},{3,3},{4,4},{5,5},{6,6},{7,7},{8,32},{9,33},{10,... | collective-permute-start | bytes 442376 | tf_op jit(solution)/shard_map/ppermute | solution.py:437
  225.7 11.8 %collective-permute-done.19 = f32[2,24,768]{2,1,0:T(8,128)S(1)} collective-permute-done((f32[2,24,768]{2,1,0:T(8,128)S(1)}, f32[2,24,768]{2,1,0:T(8,128)S(1)}, u32[]{:S(2)}, u32[]{:S(2)}) %collective-permute-start.19) | collective-permute-done | bytes 147488 | tf_op jit(solution)/shard_map/ppermute | solution.py:437
  (76 shorter events, 51.0 us)
Async XLA Ops:
  11.1 75.9 %all-to-all-start = ((bf16[32,192,128]{2,1,0:T(8,128)(2,1)}), bf16[32,192,128]{2,1,0:T(8,128)(2,1)S(1)}, u32[]{:S(2)}, u32[]{:S(2)}) async-start(bf16[32,192,128]{2,1,0:T(8,128)(2,1)} %outgoing.1), calls=%async_computation | async-start | bytes 3145728 | tf_op jit(solution)/shard_map/all_to_all | solution.py:347
  22.3 22.0 %collective-permute-start.6 = (bf16[256,1024]{1,0:T(8,128)(2,1)}, bf16[256,1024]{1,0:T(8,128)(2,1)}, u32[]{:S(2)}, u32[]{:S(2)}) collective-permute-start(bf16[256,1024]{1,0:T(8,128)(2,1)} %adjacency.2.refs_0_), channel_id=1, source_target_pairs={{0,32},{32,64},{64,96},{96,0},{1,33},{33,65},{65,97},{97,1},{2,34}... | collective-permute-start | bytes 1572872 | tf_op jit(solution)/shard_map/ppermute | solution.py:343
  22.6 21.7 %collective-permute-start.7 = (bf16[256,1024]{1,0:T(8,128)(2,1)}, bf16[256,1024]{1,0:T(8,128)(2,1)}, u32[]{:S(2)}, u32[]{:S(2)}) collective-permute-start(bf16[256,1024]{1,0:T(8,128)(2,1)} %adjacency.3.refs_1_), channel_id=1, source_target_pairs={{0,96},{32,0},{64,32},{96,64},{1,97},{33,1},{65,33},{97,65},{2,98}... | collective-permute-start | bytes 1572872 | tf_op jit(solution)/shard_map/ppermute | solution.py:343
  25.6 14.9 %collective-permute-start.3 = (bf16[1,96,768]{2,1,0:T(8,128)(2,1)S(1)}, bf16[1,96,768]{2,1,0:T(8,128)(2,1)S(1)}, u32[]{:S(2)}, u32[]{:S(2)}) collective-permute-start(bf16[1,96,768]{2,1,0:T(8,128)(2,1)S(1)} %get-tuple-element.56), channel_id=1, source_target_pairs={{0,32},{32,64},{64,96},{96,0},{1,33},{33,65},{65,97},{97,1},{2,34}... | collective-permute-start | bytes 442376 | tf_op jit(solution)/shard_map/ppermute | solution.py:352
  27.1 14.7 %collective-permute-start.4 = (bf16[1,96,768]{2,1,0:T(8,128)(2,1)S(1)}, bf16[1,96,768]{2,1,0:T(8,128)(2,1)S(1)}, u32[]{:S(2)}, u32[]{:S(2)}) collective-permute-start(bf16[1,96,768]{2,1,0:T(8,128)(2,1)S(1)} %get-tuple-element.58), channel_id=1, source_target_pairs={{0,64},{32,96},{64,0},{96,32},{1,65},{33,97},{65,1},{97,33},{2,66}... | collective-permute-start | bytes 442376 | tf_op jit(solution)/shard_map/ppermute | solution.py:352
  28.5 15.7 %collective-permute-start.5 = (bf16[1,96,768]{2,1,0:T(8,128)(2,1)S(1)}, bf16[1,96,768]{2,1,0:T(8,128)(2,1)S(1)}, u32[]{:S(2)}, u32[]{:S(2)}) collective-permute-start(bf16[1,96,768]{2,1,0:T(8,128)(2,1)S(1)} %get-tuple-element.57), channel_id=1, source_target_pairs={{0,96},{32,0},{64,32},{96,64},{1,97},{33,1},{65,33},{97,65},{2,98}... | collective-permute-start | bytes 442376 | tf_op jit(solution)/shard_map/ppermute | solution.py:352
  44.3 22.3 %collective-permute-start.10 = (bf16[4,96,768]{2,1,0:T(8,128)(2,1)S(1)}, bf16[4,96,768]{2,1,0:T(8,128)(2,1)S(1)}, u32[]{:S(2)}, u32[]{:S(2)}) collective-permute-start(bf16[4,96,768]{2,1,0:T(8,128)(2,1)S(1)} %pad_maximum_fusion.1), channel_id=1, source_target_pairs={{0,16},{16,0},{1,17},{17,1},{2,18},{18,2},{3,19},{19,3},{4,20},{20... | collective-permute-start | bytes 1769480 | tf_op jit(solution)/shard_map/ppermute | solution.py:339
  47.4 19.5 %collective-permute-start.11 = (bf16[256,1024]{1,0:T(8,128)(2,1)}, bf16[256,1024]{1,0:T(8,128)(2,1)}, u32[]{:S(2)}, u32[]{:S(2)}) collective-permute-start(bf16[256,1024]{1,0:T(8,128)(2,1)} %adjacency.3.refs_1_), channel_id=1, source_target_pairs={{0,32},{32,64},{64,96},{96,0},{1,33},{33,65},{65,97},{97,1},{2,34}... | collective-permute-start | bytes 1572872 | tf_op jit(solution)/shard_map/ppermute | solution.py:343
  48.7 18.1 %collective-permute-start.12 = (bf16[256,1024]{1,0:T(8,128)(2,1)}, bf16[256,1024]{1,0:T(8,128)(2,1)}, u32[]{:S(2)}, u32[]{:S(2)}) collective-permute-start(bf16[256,1024]{1,0:T(8,128)(2,1)} %adjacency.2.refs_0_), channel_id=1, source_target_pairs={{0,96},{32,0},{64,32},{96,64},{1,97},{33,1},{65,33},{97,65},{2,98}... | collective-permute-start | bytes 1572872 | tf_op jit(solution)/shard_map/ppermute | solution.py:343
  66.8 20.2 %collective-permute-start.13 = (bf16[4,192,768]{2,1,0:T(8,128)(2,1)S(1)}, bf16[4,192,768]{2,1,0:T(8,128)(2,1)}, u32[]{:S(2)}, u32[]{:S(2)}) collective-permute-start(bf16[4,192,768]{2,1,0:T(8,128)(2,1)S(1)} %pad_maximum_fusion.refs_7_.refs_3_.refs_9_), channel_id=1, source_target_pairs={{0,1},{1,0},{2,3},{3,2},{4,5},{5,4},{6,7},{7,6},{8,9},{9,8},{10,11... | collective-permute-start | bytes 3538952 | tf_op jit(solution)/shard_map/ppermute | solution.py:339
  66.9 28.4 %collective-permute-start.8 = (bf16[256,1024]{1,0:T(8,128)(2,1)}, bf16[256,1024]{1,0:T(8,128)(2,1)}, u32[]{:S(2)}, u32[]{:S(2)}) collective-permute-start(bf16[256,1024]{1,0:T(8,128)(2,1)} %collective-permute-done.6.refs_2_), channel_id=1, source_target_pairs={{0,32},{32,64},{64,96},{96,0},{1,33},{33,65},{65,97},{97,1},{2,34}... | collective-permute-start | bytes 1572872 | tf_op jit(solution)/shard_map/ppermute | solution.py:343
  68.1 27.2 %collective-permute-start.9 = (bf16[256,1024]{1,0:T(8,128)(2,1)}, bf16[256,1024]{1,0:T(8,128)(2,1)}, u32[]{:S(2)}, u32[]{:S(2)}) collective-permute-start(bf16[256,1024]{1,0:T(8,128)(2,1)} %collective-permute-done.7.refs_5_), channel_id=1, source_target_pairs={{0,96},{32,0},{64,32},{96,64},{1,97},{33,1},{65,33},{97,65},{2,98}... | collective-permute-start | bytes 1572872 | tf_op jit(solution)/shard_map/ppermute | solution.py:343
  69.1 12.5 %collective-permute-start = (s32[32]{0:T(128)S(1)}, s32[32]{0:T(128)S(1)}, u32[]{:S(2)}, u32[]{:S(2)}) collective-permute-start(s32[32]{0:T(128)S(1)} %reshape.42), channel_id=1, source_target_pairs={{0,32},{32,64},{64,96},{96,0},{1,33},{33,65},{65,97},{97,1},{2,34}... | collective-permute-start | bytes 392 | tf_op jit(solution)/shard_map/ppermute | solution.py:352
  71.5 10.9 %collective-permute-start.1 = (s32[32]{0:T(128)S(1)}, s32[32]{0:T(128)S(1)}, u32[]{:S(2)}, u32[]{:S(2)}) collective-permute-start(s32[32]{0:T(128)S(1)} %reshape.42), channel_id=1, source_target_pairs={{0,64},{32,96},{64,0},{96,32},{1,65},{33,97},{65,1},{97,33},{2,66}... | collective-permute-start | bytes 392 | tf_op jit(solution)/shard_map/ppermute | solution.py:352
  81.6 4.8 %collective-permute-start.2 = (s32[32]{0:T(128)S(1)}, s32[32]{0:T(128)S(1)}, u32[]{:S(2)}, u32[]{:S(2)}) collective-permute-start(s32[32]{0:T(128)S(1)} %reshape.42), channel_id=1, source_target_pairs={{0,96},{32,0},{64,32},{96,64},{1,97},{33,1},{65,33},{97,65},{2,98}... | collective-permute-start | bytes 392 | tf_op jit(solution)/shard_map/ppermute | solution.py:352
  100.1 9.9 %all-to-all-start.1 = ((bf16[8,96,256]{2,1,0:T(8,128)(2,1)}), bf16[8,96,256]{2,1,0:T(8,128)(2,1)S(1)}, u32[]{:S(2)}, u32[]{:S(2)}) async-start(bf16[8,96,256]{2,1,0:T(8,128)(2,1)} %bitcast.25), calls=%async_computation.1 | async-start | bytes 786432 | tf_op jit(solution)/shard_map/all_to_all | solution.py:347
  133.6 75.8 %all-to-all-start.3 = ((bf16[32,192,128]{2,1,0:T(8,128)(2,1)}), bf16[32,192,128]{2,1,0:T(8,128)(2,1)S(1)}, u32[]{:S(2)}, u32[]{:S(2)}) async-start(bf16[32,192,128]{2,1,0:T(8,128)(2,1)} %backward.1), calls=%async_computation.3 | async-start | bytes 3145728 | tf_op jit(solution)/shard_map/all_to_all | solution.py:347
  147.5 3.1 %collective-permute-start.14 = (bf16[4,4,48,768]{3,2,1,0:T(8,128)(2,1)}, bf16[4,4,48,768]{3,2,1,0:T(8,128)(2,1)S(1)}, u32[]{:S(2)}, u32[]{:S(2)}) collective-permute-start(bf16[4,4,48,768]{3,2,1,0:T(8,128)(2,1)} %get-tuple-element.46), channel_id=1, source_target_pairs={{0,1},{1,0},{2,3},{3,2},{4,5},{5,4},{6,7},{7,6},{8,9},{9,8},{10,11... | collective-permute-start | bytes 3538952 | tf_op jit(solution)/shard_map/ppermute | solution.py:339
  155.0 26.9 %collective-permute-start.15 = (bf16[8,48,768]{2,1,0:T(8,128)(2,1)}, bf16[8,48,768]{2,1,0:T(8,128)(2,1)S(1)}, u32[]{:S(2)}, u32[]{:S(2)}) collective-permute-start(bf16[8,48,768]{2,1,0:T(8,128)(2,1)} %get-tuple-element.48), channel_id=1, source_target_pairs={{0,16},{16,0},{1,17},{17,1},{2,18},{18,2},{3,19},{19,3},{4,20},{20... | collective-permute-start | bytes 1769480 | tf_op jit(solution)/shard_map/ppermute | solution.py:339
  185.1 8.9 %collective-permute-start.16 = (bf16[4,48,768]{2,1,0:T(8,128)(2,1)}, bf16[4,48,768]{2,1,0:T(8,128)(2,1)S(1)}, u32[]{:S(2)}, u32[]{:S(2)}) collective-permute-start(bf16[4,48,768]{2,1,0:T(8,128)(2,1)} %get-tuple-element.50), channel_id=1, source_target_pairs={{0,2},{2,0},{4,6},{6,4},{8,10},{10,8},{12,14},{14,12},{1,3},{3,1},... | collective-permute-start | bytes 884744 | tf_op jit(solution)/shard_map/ppermute | solution.py:339
  196.7 8.4 %collective-permute-start.17 = (bf16[2,48,768]{2,1,0:T(8,128)(2,1)}, bf16[2,48,768]{2,1,0:T(8,128)(2,1)S(1)}, u32[]{:S(2)}, u32[]{:S(2)}) collective-permute-start(bf16[2,48,768]{2,1,0:T(8,128)(2,1)} %get-tuple-element.52), channel_id=1, source_target_pairs={{0,4},{2,6},{4,0},{6,2},{8,12},{10,14},{12,8},{14,10},{1,5},{3,7},... | collective-permute-start | bytes 442376 | tf_op jit(solution)/shard_map/ppermute | solution.py:339
  207.5 11.4 %collective-permute-start.18 = (bf16[1,48,768]{2,1,0:T(8,128)(2,1)}, bf16[1,48,768]{2,1,0:T(8,128)(2,1)S(1)}, u32[]{:S(2)}, u32[]{:S(2)}) collective-permute-start(bf16[1,48,768]{2,1,0:T(8,128)(2,1)} %get-tuple-element.54), channel_id=1, source_target_pairs={{0,8},{2,10},{4,12},{6,14},{8,0},{10,2},{12,4},{14,6},{1,9},{3,11}... | collective-permute-start | bytes 221192 | tf_op jit(solution)/shard_map/ppermute | solution.py:339
  213.5 24.1 %all-to-all-start.4 = ((f32[8,2,16,192]{3,2,1,0:T(8,128)}), f32[8,2,16,192]{3,2,1,0:T(8,128)S(1)}, u32[]{:S(2)}, u32[]{:S(2)}) async-start(f32[8,2,16,192]{3,2,1,0:T(8,128)} %owned.1), calls=%async_computation.4 | async-start | bytes 524288 | tf_op jit(solution)/shard_map/all_to_all | solution.py:347
  218.9 18.6 %collective-permute-start.19 = (f32[2,24,768]{2,1,0:T(8,128)S(1)}, f32[2,24,768]{2,1,0:T(8,128)S(1)}, u32[]{:S(2)}, u32[]{:S(2)}) collective-permute-start(f32[2,24,768]{2,1,0:T(8,128)S(1)} %bitcast.27), channel_id=1, source_target_pairs={{0,0},{1,1},{2,2},{3,3},{4,4},{5,5},{6,6},{7,7},{8,32},{9,33},{10,... | collective-permute-start | bytes 442376 | tf_op jit(solution)/shard_map/ppermute | solution.py:437
  (11 other events, 144.3 us)

commit v4 on v2

--- a/solution.py
+++ b/solution.py
@@ -1,3 +1,5 @@
+import functools
+
 import jax
 import jax.numpy as jnp
 from jax import lax
@@ -10,7 +12,11 @@
 BLK = 128
 REL = ("xl", "y")
 TGT = ("xh", "z", "core")
-VMEM_LIMIT = 60 * 1024 * 1024
+VMEM_LIMIT = 36 * 1024 * 1024
+
+
+def resident(value):
+    return pltpu.with_memory_space_constraint(value, pltpu.MemorySpace.VMEM)
 
 
 def params(*semantics):
@@ -32,8 +38,7 @@
 
 
 def adjacency_kernel(count_ref, values_ref, out_ref):
-    r, q = pl.program_id(0), pl.program_id(1)
-    count = count_ref[r, q]
+    count = count_ref[pl.program_id(0), pl.program_id(1)]
     slots = values_ref.shape[2]
     live, degree = [], None
     for s in range(slots):
@@ -84,72 +89,82 @@
     )(place, source_blocks, features)
 
 
-def relation_of(i, place):
-    core, y = place[2], place[3]
-    parity = jnp.where(i < 4, core, 1 - core)
-    return 2 * ((y - i) & 3) + parity
-
-
-def slots_at(i, place, q):
-    core = place[2]
-    parity = jnp.where(i < 4, core, 1 - core)
-    return (((i & 3) * 2 + parity) * 2 + q) * 8
+STEPS = tuple((k, p) for k in range(4) for p in range(2))
+
+
+def start_loads(place_ref, adj_ref, adj_buf, w_mine_ref, w_theirs_ref, w_buf, sems):
+    core, y = place_ref[2], place_ref[3]
+    loads = []
+    for k in range(4):
+        group = [
+            pltpu.make_async_copy(
+                adj_ref.at[pl.ds(2 * ((y - k) & 3), 2)], adj_buf.at[pl.ds(2 * k, 2)], sems.at[3 * k]
+            )
+        ]
+        for n, (half, ref) in enumerate(((core, w_mine_ref), (1 - core, w_theirs_ref)), 1):
+            group.append(pltpu.make_async_copy(ref.at[k], w_buf.at[2 * k + half], sems.at[3 * k + n]))
+        for load in group:
+            load.start()
+        loads.append(group)
+    return loads
+
+
+def load_scratch(rows, wide, width):
+    return [
+        pltpu.VMEM((8, rows, wide), BF16),
+        pltpu.VMEM((8, 192, width), BF16),
+        pltpu.SemaphoreType.DMA((12,)),
+    ]
+
+
+def anywhere():
+    return pl.BlockSpec(memory_space=pl.ANY)
 
 
 def forward_kernel(
-    place_ref, slot_ref, adj_ref, fetched_ref, w_mine_ref, w_theirs_ref, messages_ref, pre_ref, acc_ref
+    place_ref, slot_ref, adj_ref, fetched_ref, w_mine_ref, w_theirs_ref,
+    messages_ref, pre_ref, adj_buf, w_buf, sems, acc_ref,
 ):
-    i = pl.program_id(0)
-    slots = 8
-    for q in range(2):
-        base = slots_at(i, place_ref, q)
-        wide = jnp.concatenate([fetched_ref[slot_ref[base + s]] for s in range(slots)], axis=1)
-        part = adj_ref[0, q * BLK : (q + 1) * BLK, :]
-        messages_ref[0, :, q * BLK : (q + 1) * BLK] = dot(wide, part, 1, 1).astype(BF16)
-
-    @pl.when(i == 0)
-    def _():
-        acc_ref[...] = dot(w_mine_ref[0], messages_ref[0], 0, 0)
-
-    @pl.when((i > 0) & (i < 4))
-    def _():
-        acc_ref[...] += dot(w_mine_ref[0], messages_ref[0], 0, 0)
-
-    @pl.when(i >= 4)
-    def _():
-        acc_ref[...] += dot(w_theirs_ref[0], messages_ref[0], 0, 0)
-
-    @pl.when(i == 7)
-    def _():
-        pre_ref[...] = acc_ref[...].astype(BF16)
+    y = place_ref[3]
+    loads = start_loads(place_ref, adj_ref, adj_buf, w_mine_ref, w_theirs_ref, w_buf, sems)
+    for k in range(4):
+        for load in loads[k]:
+            load.wait()
+        pair = pl.ds(2 * ((y - k) & 3), 2)
+        both = []
+        for p in range(2):
+            halves = []
+            for q in range(2):
+                base = ((k * 2 + p) * 2 + q) * 8
+                wide = jnp.concatenate([fetched_ref[slot_ref[base + s]] for s in range(8)], axis=1)
+                part = adj_buf[2 * k + p, q * BLK : (q + 1) * BLK, :]
+                halves.append(dot(wide, part, 1, 1).astype(BF16))
+            both.append(jnp.concatenate(halves, axis=1))
+        both = jnp.stack(both)
+        messages_ref[pair] = both
+        deep = 2 * w_buf.shape[1]
+        term = dot(w_buf[2 * k : 2 * k + 2].reshape(deep, -1), both.reshape(deep, -1), 0, 0)
+        if k == 0:
+            acc_ref[...] = term
+        elif k < 3:
+            acc_ref[...] += term
+        else:
+            pre_ref[...] = (acc_ref[...] + term).astype(BF16)
 
 
 def forward_of(place, slots, adjacency, fetched, w_mine, w_theirs):
     rels, rows, wide = adjacency.shape
     width = w_mine.shape[2]
-    spec = pltpu.PrefetchScalarGridSpec(
-        num_scalar_prefetch=2,
-        grid=(rels,),
-        in_specs=[
-            pl.BlockSpec((1, rows, wide), lambda i, p, s: (relation_of(i, p), 0, 0)),
-            pl.BlockSpec(fetched.shape, lambda i, p, s: (0, 0, 0)),
-            pl.BlockSpec((1, 192, width), lambda i, p, s: (jnp.minimum(i, 3), 0, 0)),
-            pl.BlockSpec((1, 192, width), lambda i, p, s: (jnp.maximum(i - 4, 0), 0, 0)),
-        ],
-        out_specs=[
-            pl.BlockSpec((1, 192, rows), lambda i, p, s: (relation_of(i, p), 0, 0)),
-            pl.BlockSpec((width, rows), lambda i, p, s: (0, 0)),
-        ],
-        scratch_shapes=[pltpu.VMEM((width, rows), F32)],
-    )
     return pl.pallas_call(
         forward_kernel,
-        grid_spec=spec,
+        in_specs=[smem(), smem(), anywhere(), vmem(), anywhere(), anywhere()],
+        out_specs=[vmem(), vmem()],
         out_shape=[
             jax.ShapeDtypeStruct((rels, 192, rows), BF16),
             jax.ShapeDtypeStruct((width, rows), BF16),
         ],
-        compiler_params=params("arbitrary"),
+        scratch_shapes=load_scratch(rows, wide, width) + [pltpu.VMEM((width, rows), F32)],
+        compiler_params=params(),
         name="forward",
     )(place, slots, adjacency, fetched, w_mine, w_theirs)
 
@@ -181,57 +196,35 @@
 
 
 def backward_kernel(
-    place_ref, slot_ref, adj_ref, grad_ref, w_mine_ref, w_theirs_ref, out_ref, acc_ref
+    place_ref, slot_ref, adj_ref, grad_ref, w_mine_ref, w_theirs_ref, out_ref,
+    adj_buf, w_buf, sems, acc_ref,
 ):
-    i = pl.program_id(0)
-    slots = 8
-
-    @pl.when(i == 0)
-    def _():
-        acc_ref[...] = jnp.zeros_like(acc_ref)
-
-    def spread(w):
-        grads = dot(w, grad_ref[...], 1, 0).astype(BF16)
+    loads = start_loads(place_ref, adj_ref, adj_buf, w_mine_ref, w_theirs_ref, w_buf, sems)
+    acc_ref[...] = jnp.zeros_like(acc_ref)
+    for n, (k, p) in enumerate(STEPS):
+        if p == 0:
+            for load in loads[k]:
+                load.wait()
+        grads = dot(w_buf[n], grad_ref[...], 1, 0).astype(BF16)
         for q in range(2):
-            base = slots_at(i, place_ref, q)
-            part = adj_ref[0, q * BLK : (q + 1) * BLK, :]
+            base = (n * 2 + q) * 8
+            part = adj_buf[n, q * BLK : (q + 1) * BLK, :]
             wide = dot(grads[:, q * BLK : (q + 1) * BLK], part, 1, 0)
-            for s in range(slots):
+            for s in range(8):
                 acc_ref[slot_ref[base + s]] += wide[:, s * BLK : (s + 1) * BLK]
-
-    @pl.when(i < 4)
-    def _():
-        spread(w_mine_ref[0])
-
-    @pl.when(i >= 4)
-    def _():
-        spread(w_theirs_ref[0])
-
-    @pl.when(i == 7)
-    def _():
-        out_ref[...] = acc_ref[...].astype(BF16)
+    out_ref[...] = acc_ref[...].astype(BF16)
 
 
 def backward_of(place, slots, adjacency, grads, w_mine, w_theirs, owners):
     rels, rows, wide = adjacency.shape
     width = w_mine.shape[2]
-    spec = pltpu.PrefetchScalarGridSpec(
-        num_scalar_prefetch=2,
-        grid=(rels,),
-        in_specs=[
-            pl.BlockSpec((1, rows, wide), lambda i, p, s: (relation_of(i, p), 0, 0)),
-            pl.BlockSpec((width, rows), lambda i, p, s: (0, 0)),
-            pl.BlockSpec((1, 192, width), lambda i, p, s: (jnp.minimum(i, 3), 0, 0)),
-            pl.BlockSpec((1, 192, width), lambda i, p, s: (jnp.maximum(i - 4, 0), 0, 0)),
-        ],
-        out_specs=pl.BlockSpec((owners, 192, BLK), lambda i, p, s: (0, 0, 0)),
-        scratch_shapes=[pltpu.VMEM((owners, 192, BLK), F32)],
-    )
     return pl.pallas_call(
         backward_kernel,
-        grid_spec=spec,
+        in_specs=[smem(), smem(), anywhere(), vmem(), anywhere(), anywhere()],
+        out_specs=vmem(),
         out_shape=jax.ShapeDtypeStruct((owners, 192, BLK), BF16),
-        compiler_params=params("arbitrary"),
+        scratch_shapes=load_scratch(rows, wide, width) + [pltpu.VMEM((owners, 192, BLK), F32)],
+        compiler_params=params(),
         name="backward",
     )(place, slots, adjacency, grads, w_mine, w_theirs)
 
@@ -246,7 +239,7 @@
             rows = slice(m * 24, (m + 1) * 24)
             piece = jnp.concatenate([first[rows], second[rows]], axis=0)
             target = odd_ref if m % 2 else even_ref
-            target[0, m // 2] = piece.astype(target.dtype)
+            target[m // 2] = piece.astype(target.dtype)
 
     @pl.when(core == 0)
     def _():
@@ -260,7 +253,7 @@
 def weight_terms_of(place, messages, grads):
     rels, deep, rows = messages.shape
     width = grads.shape[0]
-    out = pl.BlockSpec((1, 4, 48, width), lambda j: (j, 0, 0, 0))
+    out = pl.BlockSpec((4, 48, width), lambda j: (j, 0, 0))
     return pl.pallas_call(
         weight_kernel,
         grid=(rels // 2,),
@@ -271,8 +264,8 @@
         ],
         out_specs=[out, out],
         out_shape=[
-            jax.ShapeDtypeStruct((rels // 2, 4, 48, width), F32),
-            jax.ShapeDtypeStruct((rels // 2, 4, 48, width), BF16),
+            jax.ShapeDtypeStruct((2 * rels, 48, width), F32),
+            jax.ShapeDtypeStruct((2 * rels, 48, width), BF16),
         ],
         compiler_params=params("arbitrary"),
         name="weight_terms",
@@ -305,8 +298,21 @@
     )(place, source_blocks, arrived)
 
 
-def swap(value, axis):
-    return lax.ppermute(value, axis, [(0, 1), (1, 0)])
+def halve(bit, keep, came, stride):
+    shape = (-1, 2, stride, *keep.shape[1:])
+
+    def take(which):
+        total = [
+            lax.dynamic_index_in_dim(v.reshape(shape), which, 1, keepdims=False).astype(F32)
+            for v in (keep, came)
+        ]
+        return (total[0] + total[1]).reshape(-1, *keep.shape[1:])
+
+    return take(bit), take(1 - bit).astype(BF16)
+
+
+def swap(value, axis, size=2, flip=1):
+    return lax.ppermute(value, axis, [(i, i ^ flip) for i in range(size)])
 
 
 def exchange(value, axis):
@@ -344,21 +350,27 @@
     group = lax.axis_index(REL)
     place = jnp.stack([owner, 192 * y, core, y]).astype(jnp.int32)
 
+    xh, z = lax.axis_index("xh"), lax.axis_index("z")
     own_adjacency = adjacency_of(tile_values, tile_count)
     adjacency = lax.all_gather(own_adjacency, "y", axis=0, tiled=True)
-    fetched = exchange(outgoing_of(features, source_blocks, place), TGT)
+    features, weights, _ = lax.optimization_barrier((features, weights, own_adjacency))
+    fetched = resident(exchange(outgoing_of(features, source_blocks, place), TGT))
     w_cut = [
-        lax.dynamic_slice(weights, (core, ((y + k) & 3) * 192, 0), (1, 192, width))
+        lax.dynamic_slice(weights, (core, ((y + k) & 3) * 192 + 96 * xh, 0), (1, 96, width))
         for k in range(4)
     ]
-    w_mine = jnp.concatenate([w_cut[0], *around(w_cut[1:], "y", 4)], axis=0)
+    w_part = jnp.concatenate([w_cut[0], *around(w_cut[1:], "y", 4)], axis=0)
+    w_other = swap(w_part, "xh")
+    w_mine = jnp.concatenate(
+        [jnp.where(xh == 0, w_part, w_other), jnp.where(xh == 0, w_other, w_part)], axis=1
+    )
     w_theirs = swap(w_mine, "core")
     own_slots = tile_slot.reshape(-1)
     slots = jnp.concatenate([own_slots, *around([own_slots] * 3, "y", 4)])
 
     messages, part = forward_of(place, slots, adjacency, fetched, w_mine, w_theirs)
     share = width // groups
-    arrived = exchange(part.reshape(groups, share, -1), REL)
+    arrived = resident(exchange(part.reshape(groups, share, -1), REL))
     bias_share = lax.dynamic_slice_in_dim(bias, group * share, share)[:, None]
     cotangent_share = lax.dynamic_slice_in_dim(cotangent, group * share, share, 1).T
     activated, grad_copies = activation_of(arrived, bias_share, cotangent_share)
@@ -366,15 +378,18 @@
     grads = exchange(grad_copies, REL).reshape(width, -1)
 
     partial = backward_of(place, slots, adjacency, grads, w_mine, w_theirs, owners)
-    returned = exchange(partial, TGT)
+    returned = resident(exchange(partial, TGT))
     cut = owned_of(place, source_blocks, returned, groups)
     columns = exchange(cut, REL).reshape(2, 4, 2, BLK // groups, 192).sum(axis=0)
     grad_features = columns.transpose(1, 2, 0, 3).reshape(2, BLK // groups, width)
 
     late_grads, _ = lax.optimization_barrier((grads, partial))
     keep, send = weight_terms_of(place, messages, late_grads)
-    chip = (keep + swap(send, "core").astype(F32)).reshape(16, 48, width)
-    piece = lax.psum_scatter(chip, ("xh", "z"), scatter_dimension=0, tiled=True)
+    keep, send = halve(z & 1, keep, swap(send, "core"), 1)
+    keep, send = halve(xh, keep, swap(send, "z", 8, 1), 4)
+    keep, send = halve((z >> 1) & 1, keep, swap(send, "xh"), 1)
+    keep, send = halve(z >> 2, keep, swap(send, "z", 8, 2), 1)
+    piece = keep + swap(send, "z", 8, 4).astype(F32)
     grad_weights = lax.ppermute(piece.reshape(2, 24, width), ("y", *TGT), to_owner())
     return (output, grad_weights, grad_features)
 

time: 384 us -> 238 us (0.62)
  waiting for transfers between devices: 206 us -> 104 us
  blocking collectives: 70.4 us -> 11 us
  starting transfers between devices: 38.5 us -> 58.1 us
  Pallas kernels: 39.6 us -> 27.3 us
  local copies, waits for them, and re-layouts: 7.58 us -> 15.5 us
    reduce_scatter x1 -> x0, waiting for transfers between devices: 151 us -> none  [per_device(): piece = lax.psum_scatter(chip, ('xh', 'z'), scatter_dimension=0, tiled=True)]
    ppermute x2 -> x7, waiting for transfers between devices: 3.06 us -> 72.2 us  [swap(): return lax.ppermute(value, axis, [(i, i ^ flip) for i in range(size)])]
    all_to_all x2 -> x1, blocking collectives: 70.4 us -> 11 us  [exchange(): return lax.all_to_all(value, axis, 0, 0, tiled=True)]
    ppermute x2 -> x7, starting transfers between devices: 0.1 us -> 12.8 us  [swap(): return lax.ppermute(value, axis, [(i, i ^ flip) for i in range(size)])]
    ppermute x6, waiting for transfers between devices: 28.4 us -> 15.8 us  [around(): lax.ppermute(v, axis, [(i, (i + k) % size) for i in range(size)])]
    unnamed x14 -> x36, local copies, waits for them, and re-layouts: 3.59 us -> 12.3 us
    pallas_call x2, Pallas kernels: 21.4 us -> 13.4 us  [the longest x1 6.88 us: forward_of(): pl.pallas_call(forward_kernel, in_specs=[smem(), smem(), anywhere(), vmem...]
    all_gather x1, waiting for transfers between devices: 8.05 us -> 0.02 us  [per_device(): adjacency = lax.all_gather(own_adjacency, 'y', axis=0, tiled=True)]
  transfers between devices with their start and end apart: 14 -> 19, of which waited for: 12 -> 13; matrix products, arithmetic and copies ran while one was open for 2% -> 4% of each run, Pallas kernels for 1% -> 3%
where the time goes in v4:
time: 238 us; the launch traced here: 237 us
  waiting for transfers between devices  104 us (44%)
  starting transfers between devices  58.1 us (24%)
  Pallas kernels  27.3 us (11%)
  local copies, waits for them, and re-layouts  15.5 us (7%)
  between operations  14.3 us (6%)
  blocking collectives  11 us (5%)
  other arithmetic  6.64 us (3%)
    ppermute x7, waiting for transfers between devices, swap(): return lax.ppermute(value, axis, [(i, i ^ flip) for i in range(size)])  72.2 us
    all_to_all x4, starting transfers between devices, exchange(): return lax.all_to_all(value, axis, 0, 0, tiled=True)  30.9 us
    ppermute x6, waiting for transfers between devices, around(): lax.ppermute(v, axis, [(i, (i + k) % size) for i in range(size)])  15.8 us
    ppermute x7, starting transfers between devices, swap(): return lax.ppermute(value, axis, [(i, i ^ flip) for i in range(size)])  12.8 us
    unnamed x36, local copies, waits for them, and re-layouts  12.3 us
    ppermute x1, waiting for transfers between devices, per_device(): lax.ppermute(piece.reshape(2, 24, width), ('y', *TGT), to_owner())  12 us
    all_to_all x1, blocking collectives, exchange(): return lax.all_to_all(value, axis, 0, 0, tiled=True)  11 us
    ppermute x6, starting transfers between devices, around(): lax.ppermute(v, axis, [(i, (i + k) % size) for i in range(size)])  7.76 us
  transfers between devices with their start and end apart: 19, of which 13 were waited for; matrix products, arithmetic and copies ran while one was open for 4% of the time, Pallas kernels for 3%

profile of v4, /device:TPU:56, one launch (start us, length us, event | category | flops | bytes accessed | tf_op | source)
XLA Modules:
  0.0 237.2 jit_solution(9013649582220866694)
XLA Ops:
  9.5 5.0 %adjacency.1 = bf16[2,256,1024]{2,1,0:T(8,128)(2,1)} custom-call(s32[2,2]{1,0:T(2,128)S(1)} %copy-done.15, s32[2,256,8,128]{3,2,1,0:T(8,128)S(1)} %copy-done.5), custom_call_target="tpu_custom_call" | custom-call | tf_op jit(solution)/shard_map/adjacency/pallas_call | solution.py:57
  18.0 11.2 %all-to-all-start = ((bf16[32,192,128]{2,1,0:T(8,128)(2,1)}), bf16[32,192,128]{2,1,0:T(8,128)(2,1)S(1)}, u32[]{:S(2)}, u32[]{:S(2)}) async-start(bf16[32,192,128]{2,1,0:T(8,128)(2,1)} %outgoing.1), calls=%async_computation | async-start | bytes 3145728 | tf_op jit(solution)/shard_map/all_to_all | solution.py:319
  34.4 9.2 %collective-permute-done.5 = bf16[1,96,768]{2,1,0:T(8,128)(2,1)S(1)} collective-permute-done((bf16[1,96,768]{2,1,0:T(8,128)(2,1)S(1)}, bf16[1,96,768]{2,1,0:T(8,128)(2,1)S(1)}, u32[]{:S(2)}, u32[]{:S(2)}) %collective-permute-start.5) | collective-permute-done | bytes 147488 | tf_op jit(solution)/shard_map/ppermute | solution.py:324
  45.6 2.8 %collective-permute-done.3 = bf16[1,96,768]{2,1,0:T(8,128)(2,1)S(1)} collective-permute-done((bf16[1,96,768]{2,1,0:T(8,128)(2,1)S(1)}, bf16[1,96,768]{2,1,0:T(8,128)(2,1)S(1)}, u32[]{:S(2)}, u32[]{:S(2)}) %collective-permute-start.3) | collective-permute-done | bytes 147488 | tf_op jit(solution)/shard_map/ppermute | solution.py:324
  49.3 3.0 %collective-permute-start.6 = (bf16[4,96,768]{2,1,0:T(8,128)(2,1)}, bf16[4,96,768]{2,1,0:T(8,128)(2,1)S(1)}, u32[]{:S(2)}, u32[]{:S(2)}) collective-permute-start(bf16[4,96,768]{2,1,0:T(8,128)(2,1)} %pad_maximum_fusion.1), channel_id=1, source_target_pairs={{0,16},{16,0},{1,17},{17,1},{2,18},{18,2},{3,19},{19,3},{4,20},{20... | collective-permute-start | bytes 1769480 | tf_op jit(solution)/shard_map/ppermute | solution.py:315
  52.3 19.9 %collective-permute-done.6 = bf16[4,96,768]{2,1,0:T(8,128)(2,1)S(1)} collective-permute-done((bf16[4,96,768]{2,1,0:T(8,128)(2,1)}, bf16[4,96,768]{2,1,0:T(8,128)(2,1)S(1)}, u32[]{:S(2)}, u32[]{:S(2)}) %collective-permute-start.6) | collective-permute-done | bytes 589856 | tf_op jit(solution)/shard_map/ppermute | solution.py:315
  81.0 6.9 %forward.1 = (bf16[8,192,256]{2,1,0:T(8,128)(2,1)S(1)}, bf16[768,256]{1,0:T(8,128)(2,1)}) custom-call(s32[4]{0:T(128)S(1)} %pad_add_fusion.place_ref, s32[128]{0:T(128)S(1)} %pad_add_fusion.1.slot_ref, bf16[8,256,1024]{2,1,0:T(8,128)(2,1)S(1)} %copy-done.1, bf16[32,192,128]{2,1,0:T(8,128)(2,1)S(1)} %all-to-all-done.fetched_ref, ...), custom_call_target="tpu_custom_call" | custom-call | tf_op jit(solution)/shard_map/forward/pallas_call | solution.py:158
  88.8 6.5 %all-to-all-start.1 = ((bf16[8,96,256]{2,1,0:T(8,128)(2,1)}), bf16[8,96,256]{2,1,0:T(8,128)(2,1)S(1)}, u32[]{:S(2)}, u32[]{:S(2)}) async-start(bf16[8,96,256]{2,1,0:T(8,128)(2,1)} %bitcast.4), calls=%async_computation.1 | async-start | bytes 786432 | tf_op jit(solution)/shard_map/all_to_all | solution.py:319
  96.4 4.3 %all-to-all-done.1.arrived_ref = bf16[8,96,256]{2,1,0:T(8,128)(2,1)S(1)} async-done(((bf16[8,96,256]{2,1,0:T(8,128)(2,1)}), bf16[8,96,256]{2,1,0:T(8,128)(2,1)S(1)}, u32[]{:S(2)}, u32[]{:S(2)}) %all-to-all-start.1) | async-done | bytes 393248 | tf_op jit(solution)/shard_map/all_to_all | solution.py:319
  101.5 11.0 %all_to_all.25 = bf16[8,96,256]{2,1,0:T(8,128)(2,1)S(1)} all-to-all(bf16[8,96,256]{2,1,0:T(8,128)(2,1)S(1)} %get-tuple-element.17), channel_id=1, replica_groups=mesh['xl'=2,'y'=4,'xh'=2,'z'=8,'core'=2] {'xl','y'}, dimensions={0} | all-to-all | bytes 786432 | tf_op jit(solution)/shard_map/all_to_all | solution.py:319
  114.7 6.5 %backward.1 = bf16[32,192,128]{2,1,0:T(8,128)(2,1)S(1)} custom-call(s32[4]{0:T(128)S(1)} %copy-done.11, s32[128]{0:T(128)S(1)} %copy-done.14, bf16[8,256,1024]{2,1,0:T(8,128)(2,1)S(1)} %copy-done.2, bf16[768,256]{1,0:T(8,128)(2,1)S(1)} %bitcast.43, bf16[4,192,768]{2,1,0:T(8,128)(2,1)S(1)} %pad_maximum_fusion.w_mine_ref, ...), custom_call_target="tpu_custom_call" | custom-call | tf_op jit(solution)/shard_map/backward/pallas_call | solution.py:221
  122.3 7.8 %all-to-all-start.3 = ((bf16[32,192,128]{2,1,0:T(8,128)(2,1)}), bf16[32,192,128]{2,1,0:T(8,128)(2,1)S(1)}, u32[]{:S(2)}, u32[]{:S(2)}) async-start(bf16[32,192,128]{2,1,0:T(8,128)(2,1)} %copy-done.3), calls=%async_computation.3 | async-start | bytes 3145728 | tf_op jit(solution)/shard_map/all_to_all | solution.py:319
  130.2 3.4 %weight_terms.1 = (f32[16,48,768]{2,1,0:T(8,128)S(1)}, bf16[16,48,768]{2,1,0:T(8,128)(2,1)}) custom-call(s32[4]{0:T(128)S(1)} %copy-done.12, bf16[8,192,256]{2,1,0:T(8,128)(2,1)S(1)} %copy-done.7, bf16[768,256]{1,0:T(8,128)(2,1)S(1)} %bitcast.44), custom_call_target="tpu_custom_call" | custom-call | tf_op jit(solution)/shard_map/weight_terms/pallas_call | solution.py:257
  135.2 3.0 %collective-permute-done.8 = bf16[16,48,768]{2,1,0:T(8,128)(2,1)} collective-permute-done((bf16[16,48,768]{2,1,0:T(8,128)(2,1)}, bf16[16,48,768]{2,1,0:T(8,128)(2,1)}, u32[]{:S(2)}, u32[]{:S(2)}) %collective-permute-start.8) | collective-permute-done | bytes 1179680 | tf_op jit(solution)/shard_map/ppermute | solution.py:315
  138.2 3.2 %fusion = (bf16[8,48,768]{2,1,0:T(8,128)(2,1)S(1)}, f32[8,1,1,48,768]{4,3,1,0,2:T(8,128)}) fusion(f32[8,2,1,48,768]{4,3,1,0,2:T(8,128)} %bitcast.45, s32[]{:T(128)S(6)} %select_n.85, bf16[8,2,1,48,768]{4,3,1,0,2:T(8,128)(2,1)} %bitcast.10, s32[]{:T(128)S(6)} %select_n.83), kind=kLoop, calls=%fused_computation.3 | loop fusion | flops 1474560 | bytes 5308424 | tf_op jit(solution)/shard_map/convert_element_type | solution.py:311
  141.6 36.4 %collective-permute-done.9 = bf16[8,48,768]{2,1,0:T(8,128)(2,1)S(1)} collective-permute-done((bf16[8,48,768]{2,1,0:T(8,128)(2,1)S(1)}, bf16[8,48,768]{2,1,0:T(8,128)(2,1)S(1)}, u32[]{:S(2)}, u32[]{:S(2)}) %collective-permute-start.9) | collective-permute-done | bytes 589856 | tf_op jit(solution)/shard_map/ppermute | solution.py:315
  180.1 3.2 %collective-permute-start.10 = (bf16[4,48,768]{2,1,0:T(8,128)(2,1)}, bf16[4,48,768]{2,1,0:T(8,128)(2,1)S(1)}, u32[]{:S(2)}, u32[]{:S(2)}) collective-permute-start(bf16[4,48,768]{2,1,0:T(8,128)(2,1)} %get-tuple-element.27), channel_id=1, source_target_pairs={{0,16},{16,0},{1,17},{17,1},{2,18},{18,2},{3,19},{19,3},{4,20},{20... | collective-permute-start | bytes 884744 | tf_op jit(solution)/shard_map/ppermute | solution.py:315
  183.3 7.3 %collective-permute-done.10 = bf16[4,48,768]{2,1,0:T(8,128)(2,1)S(1)} collective-permute-done((bf16[4,48,768]{2,1,0:T(8,128)(2,1)}, bf16[4,48,768]{2,1,0:T(8,128)(2,1)S(1)}, u32[]{:S(2)}, u32[]{:S(2)}) %collective-permute-start.10) | collective-permute-done | bytes 294944 | tf_op jit(solution)/shard_map/ppermute | solution.py:315
  190.6 2.6 %collective-permute-start.11 = (bf16[2,48,768]{2,1,0:T(8,128)(2,1)S(1)}, bf16[2,48,768]{2,1,0:T(8,128)(2,1)S(1)}, u32[]{:S(2)}, u32[]{:S(2)}) collective-permute-start(bf16[2,48,768]{2,1,0:T(8,128)(2,1)S(1)} %get-tuple-element.31), channel_id=1, source_target_pairs={{0,4},{2,6},{4,0},{6,2},{8,12},{10,14},{12,8},{14,10},{1,5},{3,7},... | collective-permute-start | bytes 442376 | tf_op jit(solution)/shard_map/ppermute | solution.py:315
  193.2 5.7 %collective-permute-done.11 = bf16[2,48,768]{2,1,0:T(8,128)(2,1)S(1)} collective-permute-done((bf16[2,48,768]{2,1,0:T(8,128)(2,1)S(1)}, bf16[2,48,768]{2,1,0:T(8,128)(2,1)S(1)}, u32[]{:S(2)}, u32[]{:S(2)}) %collective-permute-start.11) | collective-permute-done | bytes 147488 | tf_op jit(solution)/shard_map/ppermute | solution.py:315
  198.9 3.5 %collective-permute-start.12 = (bf16[1,48,768]{2,1,0:T(8,128)(2,1)S(1)}, bf16[1,48,768]{2,1,0:T(8,128)(2,1)S(1)}, u32[]{:S(2)}, u32[]{:S(2)}) collective-permute-start(bf16[1,48,768]{2,1,0:T(8,128)(2,1)S(1)} %fusion.6), channel_id=1, source_target_pairs={{0,8},{2,10},{4,12},{6,14},{8,0},{10,2},{12,4},{14,6},{1,9},{3,11}... | collective-permute-start | bytes 221192 | tf_op jit(solution)/shard_map/ppermute | solution.py:315
  204.7 5.5 %all-to-all-start.4 = ((f32[8,2,16,192]{3,2,1,0:T(8,128)}), f32[8,2,16,192]{3,2,1,0:T(8,128)S(1)}, u32[]{:S(2)}, u32[]{:S(2)}) async-start(f32[8,2,16,192]{3,2,1,0:T(8,128)} %owned.1), calls=%async_computation.4 | async-start | bytes 524288 | tf_op jit(solution)/shard_map/all_to_all | solution.py:319
  210.2 6.6 %collective-permute-start.13 = (f32[2,24,768]{2,1,0:T(8,128)S(1)}, f32[2,24,768]{2,1,0:T(8,128)S(1)}, u32[]{:S(2)}, u32[]{:S(2)}) collective-permute-start(f32[2,24,768]{2,1,0:T(8,128)S(1)} %bitcast.53), channel_id=1, source_target_pairs={{0,0},{1,1},{2,2},{3,3},{4,4},{5,5},{6,6},{7,7},{8,32},{9,33},{10,... | collective-permute-start | bytes 442376 | tf_op jit(solution)/shard_map/ppermute | solution.py:393
  216.8 12.0 %collective-permute-done.13 = f32[2,24,768]{2,1,0:T(8,128)S(1)} collective-permute-done((f32[2,24,768]{2,1,0:T(8,128)S(1)}, f32[2,24,768]{2,1,0:T(8,128)S(1)}, u32[]{:S(2)}, u32[]{:S(2)}) %collective-permute-start.13) | collective-permute-done | bytes 147488 | tf_op jit(solution)/shard_map/ppermute | solution.py:393
  (77 shorter events, 36.7 us)
Async XLA Ops:
  7.2 89.0 %copy-start = (bf16[256,768]{1,0:T(8,128)(2,1)S(1)}, bf16[256,768]{1,0:T(8,128)(2,1)}, u32[]{:S(2)}) copy-start(bf16[256,768]{1,0:T(8,128)(2,1)} %param.11) | copy-start | bytes 1179652
  7.2 71.6 %all-gather.2.cloned.1.call-start = ((), (), s32[]{:S(2)}) async-start(), calls=%async_computation.5 | async-start | bytes 5242880 | tf_op jit(solution)/shard_map/all_gather | solution.py:355
  15.5 63.3 %copy-start.10 = (s32[4]{0:T(128)}, s32[4]{0:T(128)S(1)}, u32[]{:S(2)}) copy-start(s32[4]{0:T(128)S(1)} %pad_add_fusion.place_ref) | copy-start | bytes 52
  18.0 60.8 %all-to-all-start = ((bf16[32,192,128]{2,1,0:T(8,128)(2,1)}), bf16[32,192,128]{2,1,0:T(8,128)(2,1)S(1)}, u32[]{:S(2)}, u32[]{:S(2)}) async-start(bf16[32,192,128]{2,1,0:T(8,128)(2,1)} %outgoing.1), calls=%async_computation | async-start | bytes 3145728 | tf_op jit(solution)/shard_map/all_to_all | solution.py:319
  30.5 13.1 %collective-permute-start.5 = (bf16[1,96,768]{2,1,0:T(8,128)(2,1)S(1)}, bf16[1,96,768]{2,1,0:T(8,128)(2,1)S(1)}, u32[]{:S(2)}, u32[]{:S(2)}) collective-permute-start(bf16[1,96,768]{2,1,0:T(8,128)(2,1)S(1)} %get-tuple-element.24), channel_id=1, source_target_pairs={{0,96},{32,0},{64,32},{96,64},{1,97},{33,1},{65,33},{97,65},{2,98}... | collective-permute-start | bytes 442376 | tf_op jit(solution)/shard_map/ppermute | solution.py:324
  31.3 14.3 %collective-permute-start.4 = (bf16[1,96,768]{2,1,0:T(8,128)(2,1)S(1)}, bf16[1,96,768]{2,1,0:T(8,128)(2,1)S(1)}, u32[]{:S(2)}, u32[]{:S(2)}) collective-permute-start(bf16[1,96,768]{2,1,0:T(8,128)(2,1)S(1)} %get-tuple-element.25), channel_id=1, source_target_pairs={{0,64},{32,96},{64,0},{96,32},{1,65},{33,97},{65,1},{97,33},{2,66}... | collective-permute-start | bytes 442376 | tf_op jit(solution)/shard_map/ppermute | solution.py:324
  32.2 16.2 %collective-permute-start.3 = (bf16[1,96,768]{2,1,0:T(8,128)(2,1)S(1)}, bf16[1,96,768]{2,1,0:T(8,128)(2,1)S(1)}, u32[]{:S(2)}, u32[]{:S(2)}) collective-permute-start(bf16[1,96,768]{2,1,0:T(8,128)(2,1)S(1)} %get-tuple-element.26), channel_id=1, source_target_pairs={{0,32},{32,64},{64,96},{96,0},{1,33},{33,65},{65,97},{97,1},{2,34}... | collective-permute-start | bytes 442376 | tf_op jit(solution)/shard_map/ppermute | solution.py:324
  49.3 22.9 %collective-permute-start.6 = (bf16[4,96,768]{2,1,0:T(8,128)(2,1)}, bf16[4,96,768]{2,1,0:T(8,128)(2,1)S(1)}, u32[]{:S(2)}, u32[]{:S(2)}) collective-permute-start(bf16[4,96,768]{2,1,0:T(8,128)(2,1)} %pad_maximum_fusion.1), channel_id=1, source_target_pairs={{0,16},{16,0},{1,17},{17,1},{2,18},{18,2},{3,19},{19,3},{4,20},{20... | collective-permute-start | bytes 1769480 | tf_op jit(solution)/shard_map/ppermute | solution.py:315
  72.4 6.4 %collective-permute-start.7 = (bf16[4,192,768]{2,1,0:T(8,128)(2,1)S(1)}, bf16[4,192,768]{2,1,0:T(8,128)(2,1)}, u32[]{:S(2)}, u32[]{:S(2)}) collective-permute-start(bf16[4,192,768]{2,1,0:T(8,128)(2,1)S(1)} %pad_maximum_fusion.w_mine_ref), channel_id=1, source_target_pairs={{0,1},{1,0},{2,3},{3,2},{4,5},{5,4},{6,7},{7,6},{8,9},{9,8},{10,11... | collective-permute-start | bytes 3538952 | tf_op jit(solution)/shard_map/ppermute | solution.py:315
  73.1 4.8 %collective-permute-start.2 = (s32[32]{0:T(128)S(1)}, s32[32]{0:T(128)S(1)}, u32[]{:S(2)}, u32[]{:S(2)}) collective-permute-start(s32[32]{0:T(128)S(1)} %reshape.223), channel_id=1, source_target_pairs={{0,96},{32,0},{64,32},{96,64},{1,97},{33,1},{65,33},{97,65},{2,98}... | collective-permute-start | bytes 392 | tf_op jit(solution)/shard_map/ppermute | solution.py:324
  73.1 5.1 %collective-permute-start.1 = (s32[32]{0:T(128)S(1)}, s32[32]{0:T(128)S(1)}, u32[]{:S(2)}, u32[]{:S(2)}) collective-permute-start(s32[32]{0:T(128)S(1)} %reshape.223), channel_id=1, source_target_pairs={{0,64},{32,96},{64,0},{96,32},{1,65},{33,97},{65,1},{97,33},{2,66}... | collective-permute-start | bytes 392 | tf_op jit(solution)/shard_map/ppermute | solution.py:324
  74.4 4.3 %collective-permute-start = (s32[32]{0:T(128)S(1)}, s32[32]{0:T(128)S(1)}, u32[]{:S(2)}, u32[]{:S(2)}) collective-permute-start(s32[32]{0:T(128)S(1)} %reshape.223), channel_id=1, source_target_pairs={{0,32},{32,64},{64,96},{96,0},{1,33},{33,65},{65,97},{97,1},{2,34}... | collective-permute-start | bytes 392 | tf_op jit(solution)/shard_map/ppermute | solution.py:324
  78.8 9.1 %copy-start.13 = (s32[128]{0:T(128)}, s32[128]{0:T(128)S(1)}, u32[]{:S(2)}) copy-start(s32[128]{0:T(128)S(1)} %pad_add_fusion.1.slot_ref) | copy-start | bytes 1540
  88.8 23.6 %copy-start.11 = (s32[4]{0:T(128)S(1)}, s32[4]{0:T(128)}, u32[]{:S(2)}) copy-start(s32[4]{0:T(128)} %copy-done.10) | copy-start | bytes 52
  88.8 23.6 %copy-start.14 = (s32[128]{0:T(128)S(1)}, s32[128]{0:T(128)}, u32[]{:S(2)}) copy-start(s32[128]{0:T(128)} %copy-done.13) | copy-start | bytes 1540
  88.8 11.9 %all-to-all-start.1 = ((bf16[8,96,256]{2,1,0:T(8,128)(2,1)}), bf16[8,96,256]{2,1,0:T(8,128)(2,1)S(1)}, u32[]{:S(2)}, u32[]{:S(2)}) async-start(bf16[8,96,256]{2,1,0:T(8,128)(2,1)} %bitcast.4), calls=%async_computation.1 | async-start | bytes 786432 | tf_op jit(solution)/shard_map/all_to_all | solution.py:319
  122.3 80.0 %all-to-all-start.3 = ((bf16[32,192,128]{2,1,0:T(8,128)(2,1)}), bf16[32,192,128]{2,1,0:T(8,128)(2,1)S(1)}, u32[]{:S(2)}, u32[]{:S(2)}) async-start(bf16[32,192,128]{2,1,0:T(8,128)(2,1)} %copy-done.3), calls=%async_computation.3 | async-start | bytes 3145728 | tf_op jit(solution)/shard_map/all_to_all | solution.py:319
  135.0 3.2 %collective-permute-start.8 = (bf16[16,48,768]{2,1,0:T(8,128)(2,1)}, bf16[16,48,768]{2,1,0:T(8,128)(2,1)}, u32[]{:S(2)}, u32[]{:S(2)}) collective-permute-start(bf16[16,48,768]{2,1,0:T(8,128)(2,1)} %get-tuple-element.20), channel_id=1, source_target_pairs={{0,1},{1,0},{2,3},{3,2},{4,5},{5,4},{6,7},{7,6},{8,9},{9,8},{10,11... | collective-permute-start | bytes 3538952 | tf_op jit(solution)/shard_map/ppermute | solution.py:315
  141.4 36.7 %collective-permute-start.9 = (bf16[8,48,768]{2,1,0:T(8,128)(2,1)S(1)}, bf16[8,48,768]{2,1,0:T(8,128)(2,1)S(1)}, u32[]{:S(2)}, u32[]{:S(2)}) collective-permute-start(bf16[8,48,768]{2,1,0:T(8,128)(2,1)S(1)} %get-tuple-element.21), channel_id=1, source_target_pairs={{0,2},{2,0},{4,6},{6,4},{8,10},{10,8},{12,14},{14,12},{1,3},{3,1},... | collective-permute-start | bytes 1769480 | tf_op jit(solution)/shard_map/ppermute | solution.py:315
  180.1 10.4 %collective-permute-start.10 = (bf16[4,48,768]{2,1,0:T(8,128)(2,1)}, bf16[4,48,768]{2,1,0:T(8,128)(2,1)S(1)}, u32[]{:S(2)}, u32[]{:S(2)}) collective-permute-start(bf16[4,48,768]{2,1,0:T(8,128)(2,1)} %get-tuple-element.27), channel_id=1, source_target_pairs={{0,16},{16,0},{1,17},{17,1},{2,18},{18,2},{3,19},{19,3},{4,20},{20... | collective-permute-start | bytes 884744 | tf_op jit(solution)/shard_map/ppermute | solution.py:315
  190.6 8.3 %collective-permute-start.11 = (bf16[2,48,768]{2,1,0:T(8,128)(2,1)S(1)}, bf16[2,48,768]{2,1,0:T(8,128)(2,1)S(1)}, u32[]{:S(2)}, u32[]{:S(2)}) collective-permute-start(bf16[2,48,768]{2,1,0:T(8,128)(2,1)S(1)} %get-tuple-element.31), channel_id=1, source_target_pairs={{0,4},{2,6},{4,0},{6,2},{8,12},{10,14},{12,8},{14,10},{1,5},{3,7},... | collective-permute-start | bytes 442376 | tf_op jit(solution)/shard_map/ppermute | solution.py:315
  198.9 11.3 %collective-permute-start.12 = (bf16[1,48,768]{2,1,0:T(8,128)(2,1)S(1)}, bf16[1,48,768]{2,1,0:T(8,128)(2,1)S(1)}, u32[]{:S(2)}, u32[]{:S(2)}) collective-permute-start(bf16[1,48,768]{2,1,0:T(8,128)(2,1)S(1)} %fusion.6), channel_id=1, source_target_pairs={{0,8},{2,10},{4,12},{6,14},{8,0},{10,2},{12,4},{14,6},{1,9},{3,11}... | collective-permute-start | bytes 221192 | tf_op jit(solution)/shard_map/ppermute | solution.py:315
  204.7 24.1 %all-to-all-start.4 = ((f32[8,2,16,192]{3,2,1,0:T(8,128)}), f32[8,2,16,192]{3,2,1,0:T(8,128)S(1)}, u32[]{:S(2)}, u32[]{:S(2)}) async-start(f32[8,2,16,192]{3,2,1,0:T(8,128)} %owned.1), calls=%async_computation.4 | async-start | bytes 524288 | tf_op jit(solution)/shard_map/all_to_all | solution.py:319
  210.2 18.6 %collective-permute-start.13 = (f32[2,24,768]{2,1,0:T(8,128)S(1)}, f32[2,24,768]{2,1,0:T(8,128)S(1)}, u32[]{:S(2)}, u32[]{:S(2)}) collective-permute-start(f32[2,24,768]{2,1,0:T(8,128)S(1)} %bitcast.53), channel_id=1, source_target_pairs={{0,0},{1,1},{2,2},{3,3},{4,4},{5,5},{6,6},{7,7},{8,32},{9,33},{10,... | collective-permute-start | bytes 442376 | tf_op jit(solution)/shard_map/ppermute | solution.py:393
  (12 other events, 32.6 us)
Sparse Core Ops, SparseCore 0:
  14.7 57.8 all-gather.1

commit v5 on v4

--- a/solution.py
+++ b/solution.py
@@ -12,7 +12,11 @@
 BLK = 128
 REL = ("xl", "y")
 TGT = ("xh", "z", "core")
-VMEM_LIMIT = 36 * 1024 * 1024
+VMEM_LIMIT = 58 * 1024 * 1024
+
+
+def in_hbm(value):
+    return pltpu.with_memory_space_constraint(value, pltpu.MemorySpace.HBM)
 
 
 def resident(value):
@@ -117,15 +121,19 @@
     ]
 
 
+def hbm():
+    return pl.BlockSpec(memory_space=pltpu.MemorySpace.HBM)
+
+
 def anywhere():
     return pl.BlockSpec(memory_space=pl.ANY)
 
 
 def forward_kernel(
     place_ref, slot_ref, adj_ref, fetched_ref, w_mine_ref, w_theirs_ref,
-    messages_ref, pre_ref, adj_buf, w_buf, sems, acc_ref,
+    keep_ref, send_ref, pre_ref, adj_buf, w_buf, sems, acc_ref,
 ):
-    y = place_ref[3]
+    core, y = place_ref[2], place_ref[3]
     loads = start_loads(place_ref, adj_ref, adj_buf, w_mine_ref, w_theirs_ref, w_buf, sems)
     for k in range(4):
         for load in loads[k]:
@@ -141,7 +149,17 @@
                 halves.append(dot(wide, part, 1, 1).astype(BF16))
             both.append(jnp.concatenate(halves, axis=1))
         both = jnp.stack(both)
-        messages_ref[pair] = both
+
+        @pl.when(core == 0)
+        def _():
+            keep_ref[pair] = both[:, :96]
+            send_ref[pair] = both[:, 96:]
+
+        @pl.when(core == 1)
+        def _():
+            keep_ref[pair] = both[:, 96:]
+            send_ref[pair] = both[:, :96]
+
         deep = 2 * w_buf.shape[1]
         term = dot(w_buf[2 * k : 2 * k + 2].reshape(deep, -1), both.reshape(deep, -1), 0, 0)
         if k == 0:
@@ -157,10 +175,11 @@
     width = w_mine.shape[2]
     return pl.pallas_call(
         forward_kernel,
-        in_specs=[smem(), smem(), anywhere(), vmem(), anywhere(), anywhere()],
-        out_specs=[vmem(), vmem()],
+        in_specs=[smem(), smem(), hbm(), vmem(), anywhere(), anywhere()],
+        out_specs=[vmem()] * 3,
         out_shape=[
-            jax.ShapeDtypeStruct((rels, 192, rows), BF16),
+            jax.ShapeDtypeStruct((rels, 96, rows), BF16),
+            jax.ShapeDtypeStruct((rels, 96, rows), BF16),
             jax.ShapeDtypeStruct((width, rows), BF16),
         ],
         scratch_shapes=load_scratch(rows, wide, width) + [pltpu.VMEM((width, rows), F32)],
@@ -220,7 +239,7 @@
     width = w_mine.shape[2]
     return pl.pallas_call(
         backward_kernel,
-        in_specs=[smem(), smem(), anywhere(), vmem(), anywhere(), anywhere()],
+        in_specs=[smem(), smem(), hbm(), vmem(), anywhere(), anywhere()],
         out_specs=vmem(),
         out_shape=jax.ShapeDtypeStruct((owners, 192, BLK), BF16),
         scratch_shapes=load_scratch(rows, wide, width) + [pltpu.VMEM((owners, 192, BLK), F32)],
@@ -229,47 +248,36 @@
     )(place, slots, adjacency, grads, w_mine, w_theirs)
 
 
-def weight_kernel(place_ref, messages_ref, grad_ref, keep_ref, send_ref):
-    core = place_ref[2]
-    first = dot(messages_ref[0], grad_ref[...], 1, 1)
-    second = dot(messages_ref[1], grad_ref[...], 1, 1)
-
-    def cut(even_ref, odd_ref):
-        for m in range(8):
-            rows = slice(m * 24, (m + 1) * 24)
-            piece = jnp.concatenate([first[rows], second[rows]], axis=0)
-            target = odd_ref if m % 2 else even_ref
-            target[m // 2] = piece.astype(target.dtype)
-
-    @pl.when(core == 0)
-    def _():
-        cut(keep_ref, send_ref)
-
-    @pl.when(core == 1)
-    def _():
-        cut(send_ref, keep_ref)
-
-
-def weight_terms_of(place, messages, grads):
-    rels, deep, rows = messages.shape
+def weight_kernel(place_ref, mine_ref, theirs_ref, grad_ref, their_grad_ref, keep_ref, send_ref):
+    xh = place_ref[4]
+    grads = jnp.concatenate([grad_ref[...], their_grad_ref[...]], axis=1)
+    for target, x in ((send_ref, 1 - xh), (keep_ref, xh)):
+        for half in range(2):
+            terms = []
+            for p in range(2):
+                r = 4 * x + 2 * half + p
+                wide = jnp.concatenate([mine_ref[r], theirs_ref[r]], axis=1)
+                terms.append(dot(wide, grads, 1, 1))
+            for m in range(4):
+                rows = slice(m * 24, (m + 1) * 24)
+                piece = jnp.concatenate([terms[0][rows], terms[1][rows]], axis=0)
+                target[4 * half + m] = piece.astype(target.dtype)
+
+
+def weight_terms_of(place, mine, theirs, grads, their_grads):
+    rels = mine.shape[0]
     width = grads.shape[0]
-    out = pl.BlockSpec((4, 48, width), lambda j: (j, 0, 0))
     return pl.pallas_call(
         weight_kernel,
-        grid=(rels // 2,),
-        in_specs=[
-            smem(),
-            pl.BlockSpec((2, deep, rows), lambda j: (j, 0, 0)),
-            pl.BlockSpec((width, rows), lambda j: (0, 0)),
+        in_specs=[smem()] + [vmem()] * 4,
+        out_specs=[vmem(), vmem()],
+        out_shape=[
+            jax.ShapeDtypeStruct((rels, 48, width), F32),
+            jax.ShapeDtypeStruct((rels, 48, width), BF16),
         ],
-        out_specs=[out, out],
-        out_shape=[
-            jax.ShapeDtypeStruct((2 * rels, 48, width), F32),
-            jax.ShapeDtypeStruct((2 * rels, 48, width), BF16),
-        ],
-        compiler_params=params("arbitrary"),
+        compiler_params=params(),
         name="weight_terms",
-    )(place, messages, grads)
+    )(place, mine, theirs, grads, their_grads)
 
 
 def owned_kernel(place_ref, table_ref, arrived_ref, out_ref):
@@ -334,7 +342,8 @@
         for xh in range(2):
             for z in range(8):
                 for c in range(2):
-                    target = place(2 * xh + z // 4, y // 2, 4 * (y % 2) + z % 4, c)
+                    m = 4 * c + z % 4
+                    target = place(2 * xh + z // 4, y // 2, 4 * (y % 2) + m // 2, m % 2)
                     moves.append((place(y, xh, z, c), target))
     return moves
 
@@ -348,27 +357,31 @@
     xl, y, core = lax.axis_index("xl"), lax.axis_index("y"), lax.axis_index("core")
     owner = lax.axis_index(TGT)
     group = lax.axis_index(REL)
-    place = jnp.stack([owner, 192 * y, core, y]).astype(jnp.int32)
-
     xh, z = lax.axis_index("xh"), lax.axis_index("z")
-    own_adjacency = adjacency_of(tile_values, tile_count)
-    adjacency = lax.all_gather(own_adjacency, "y", axis=0, tiled=True)
-    features, weights, _ = lax.optimization_barrier((features, weights, own_adjacency))
-    fetched = resident(exchange(outgoing_of(features, source_blocks, place), TGT))
+    place = jnp.stack([owner, 192 * y, core, y, xh]).astype(jnp.int32)
+
     w_cut = [
         lax.dynamic_slice(weights, (core, ((y + k) & 3) * 192 + 96 * xh, 0), (1, 96, width))
         for k in range(4)
     ]
-    w_part = jnp.concatenate([w_cut[0], *around(w_cut[1:], "y", 4)], axis=0)
+    w_cut, tile_values = lax.optimization_barrier((w_cut, tile_values))
+    w_came = around(w_cut[1:], "y", 4)
+    own_slots = tile_slot.reshape(-1)
+    slots = jnp.concatenate([own_slots, *around([own_slots] * 3, "y", 4)])
+    own_adjacency = adjacency_of(tile_values, tile_count)
+    adjacency = in_hbm(lax.all_gather(own_adjacency, "y", axis=0, tiled=True))
+    features, _ = lax.optimization_barrier((features, own_adjacency))
+    fetched = resident(exchange(outgoing_of(features, source_blocks, place), TGT))
+    w_came, slots = lax.optimization_barrier((w_came, slots))
+    w_part = jnp.concatenate([w_cut[0], *w_came], axis=0)
     w_other = swap(w_part, "xh")
     w_mine = jnp.concatenate(
         [jnp.where(xh == 0, w_part, w_other), jnp.where(xh == 0, w_other, w_part)], axis=1
     )
     w_theirs = swap(w_mine, "core")
-    own_slots = tile_slot.reshape(-1)
-    slots = jnp.concatenate([own_slots, *around([own_slots] * 3, "y", 4)])
-
-    messages, part = forward_of(place, slots, adjacency, fetched, w_mine, w_theirs)
+
+    messages, for_partner, part = forward_of(place, slots, adjacency, fetched, w_mine, w_theirs)
+    from_partner = swap(for_partner, "core")
     share = width // groups
     arrived = resident(exchange(part.reshape(groups, share, -1), REL))
     bias_share = lax.dynamic_slice_in_dim(bias, group * share, share)[:, None]
@@ -378,16 +391,15 @@
     grads = exchange(grad_copies, REL).reshape(width, -1)
 
     partial = backward_of(place, slots, adjacency, grads, w_mine, w_theirs, owners)
-    returned = resident(exchange(partial, TGT))
+    returned = resident(exchange(in_hbm(partial), TGT))
     cut = owned_of(place, source_blocks, returned, groups)
     columns = exchange(cut, REL).reshape(2, 4, 2, BLK // groups, 192).sum(axis=0)
     grad_features = columns.transpose(1, 2, 0, 3).reshape(2, BLK // groups, width)
 
-    late_grads, _ = lax.optimization_barrier((grads, partial))
-    keep, send = weight_terms_of(place, messages, late_grads)
-    keep, send = halve(z & 1, keep, swap(send, "core"), 1)
-    keep, send = halve(xh, keep, swap(send, "z", 8, 1), 4)
-    keep, send = halve((z >> 1) & 1, keep, swap(send, "xh"), 1)
+    their_grads, _ = lax.optimization_barrier((swap(grads, "core"), partial))
+    keep, send = weight_terms_of(place, messages, from_partner, grads, their_grads)
+    keep, send = halve(z & 1, keep, swap(send, "xh"), 1)
+    keep, send = halve((z >> 1) & 1, keep, swap(send, "z", 8, 1), 1)
     keep, send = halve(z >> 2, keep, swap(send, "z", 8, 2), 1)
     piece = keep + swap(send, "z", 8, 4).astype(F32)
     grad_weights = lax.ppermute(piece.reshape(2, 24, width), ("y", *TGT), to_owner())

time: 238 us -> 217 us (0.912)
  waiting for transfers between devices: 104 us -> 87.1 us
  local copies, waits for them, and re-layouts: 15.5 us -> 6.61 us
  Pallas kernels: 27.3 us -> 33.1 us
  other arithmetic: 6.64 us -> 2.28 us
    ppermute x7 -> x8, waiting for transfers between devices: 72.2 us -> 61.1 us  [swap(): return lax.ppermute(value, axis, [(i, i ^ flip) for i in range(size)])]
    unnamed x36 -> x19, local copies, waits for them, and re-layouts: 12.3 us -> 2.2 us
    ppermute x6, waiting for transfers between devices: 15.8 us -> 11.1 us  [around(): lax.ppermute(v, axis, [(i, (i + k) % size) for i in range(size)])]
    convert_element_type x4 -> x3, other arithmetic: 5.37 us -> 1.43 us  [halve(): return (take(bit), take(1 - bit).astype(BF16))]
    pallas_call x3, Pallas kernels: 16.8 us -> 20.5 us  [the longest x1 8.44 us: backward_of(): pl.pallas_call(backward_kernel, in_specs=[smem(), smem(), hbm(), vmem(),...]
    ppermute x7 -> x8, starting transfers between devices: 12.8 us -> 14.7 us  [swap(): return lax.ppermute(value, axis, [(i, i ^ flip) for i in range(size)])]
  transfers between devices with their start and end apart: 19 -> 20, of which waited for: 13 -> 12; matrix products, arithmetic and copies ran while one was open for 4% -> 3% of each run, Pallas kernels for 3% -> 4%
where the time goes in v5:
time: 217 us; the launch traced here: 214 us
  waiting for transfers between devices  87.1 us (40%)
  starting transfers between devices  58.4 us (27%)
  Pallas kernels  33.1 us (15%)
  between operations  14.3 us (7%)
  blocking collectives  12.2 us (6%)
  local copies, waits for them, and re-layouts  6.61 us (3%)
  other arithmetic  2.28 us (1%)
    ppermute x8, waiting for transfers between devices, swap(): return lax.ppermute(value, axis, [(i, i ^ flip) for i in range(size)])  61.1 us
    all_to_all x4, starting transfers between devices, exchange(): return lax.all_to_all(value, axis, 0, 0, tiled=True)  30.5 us
    ppermute x8, starting transfers between devices, swap(): return lax.ppermute(value, axis, [(i, i ^ flip) for i in range(size)])  14.7 us
    all_to_all x1, blocking collectives, exchange(): return lax.all_to_all(value, axis, 0, 0, tiled=True)  12.2 us
    ppermute x6, waiting for transfers between devices, around(): lax.ppermute(v, axis, [(i, (i + k) % size) for i in range(size)])  11.1 us
    ppermute x1, waiting for transfers between devices, per_device(): lax.ppermute(piece.reshape(2, 24, width), ('y', *TGT), to_owner())  10.5 us
    pallas_call x1, Pallas kernels, backward_of(): pl.pallas_call(backward_kernel, in_specs=[smem(), smem(), hbm(), vmem(),...  8.44 us
    pallas_call x1, Pallas kernels, forward_of(): pl.pallas_call(forward_kernel, in_specs=[smem(), smem(), hbm(), vmem(), a...  7.69 us
  transfers between devices with their start and end apart: 20, of which 12 were waited for; matrix products, arithmetic and copies ran while one was open for 3% of the time, Pallas kernels for 4%

profile of v5, /device:TPU:56, one launch (start us, length us, event | category | flops | bytes accessed | tf_op | source)
XLA Modules:
  0.0 214.0 jit_solution(2227879823951321817)
XLA Ops:
  8.5 5.7 %adjacency.1 = bf16[2,256,1024]{2,1,0:T(8,128)(2,1)} custom-call(s32[2,2]{1,0:T(2,128)} %count_ref.1, s32[2,256,8,128]{3,2,1,0:T(8,128)} %values_ref), custom_call_target="tpu_custom_call" | custom-call | tf_op jit(solution)/shard_map/adjacency/pallas_call | solution.py:61
  17.5 11.3 %all-to-all-start = ((bf16[32,192,128]{2,1,0:T(8,128)(2,1)}), bf16[32,192,128]{2,1,0:T(8,128)(2,1)S(1)}, u32[]{:S(2)}, u32[]{:S(2)}) async-start(bf16[32,192,128]{2,1,0:T(8,128)(2,1)} %outgoing.1), calls=%async_computation | async-start | bytes 3145728 | tf_op jit(solution)/shard_map/all_to_all | solution.py:327
  31.8 3.2 %collective-permute-start = (bf16[1,96,768]{2,1,0:T(8,128)(2,1)S(1)}, bf16[1,96,768]{2,1,0:T(8,128)(2,1)S(1)}, u32[]{:S(2)}, u32[]{:S(2)}) collective-permute-start(bf16[1,96,768]{2,1,0:T(8,128)(2,1)S(1)} %get-tuple-element.21), channel_id=1, source_target_pairs={{0,32},{32,64},{64,96},{96,0},{1,33},{33,65},{65,97},{97,1},{2,34}... | collective-permute-start | bytes 442376 | tf_op jit(solution)/shard_map/ppermute | solution.py:332
  37.2 6.1 %collective-permute-done = bf16[1,96,768]{2,1,0:T(8,128)(2,1)S(1)} collective-permute-done((bf16[1,96,768]{2,1,0:T(8,128)(2,1)S(1)}, bf16[1,96,768]{2,1,0:T(8,128)(2,1)S(1)}, u32[]{:S(2)}, u32[]{:S(2)}) %collective-permute-start) | collective-permute-done | bytes 147488 | tf_op jit(solution)/shard_map/ppermute | solution.py:332
  43.4 3.0 %collective-permute-done.1 = bf16[1,96,768]{2,1,0:T(8,128)(2,1)S(1)} collective-permute-done((bf16[1,96,768]{2,1,0:T(8,128)(2,1)S(1)}, bf16[1,96,768]{2,1,0:T(8,128)(2,1)S(1)}, u32[]{:S(2)}, u32[]{:S(2)}) %collective-permute-start.1) | collective-permute-done | bytes 147488 | tf_op jit(solution)/shard_map/ppermute | solution.py:332
  48.4 3.1 %collective-permute-start.6 = (bf16[4,96,768]{2,1,0:T(8,128)(2,1)S(1)}, bf16[4,96,768]{2,1,0:T(8,128)(2,1)S(1)}, u32[]{:S(2)}, u32[]{:S(2)}) collective-permute-start(bf16[4,96,768]{2,1,0:T(8,128)(2,1)S(1)} %constant_dynamic-update-slice_fusion), channel_id=1, source_target_pairs={{0,16},{16,0},{1,17},{17,1},{2,18},{18,2},{3,19},{19,3},{4,20},{20... | collective-permute-start | bytes 1769480 | tf_op jit(solution)/shard_map/ppermute | solution.py:323
  51.4 19.9 %collective-permute-done.6 = bf16[4,96,768]{2,1,0:T(8,128)(2,1)S(1)} collective-permute-done((bf16[4,96,768]{2,1,0:T(8,128)(2,1)S(1)}, bf16[4,96,768]{2,1,0:T(8,128)(2,1)S(1)}, u32[]{:S(2)}, u32[]{:S(2)}) %collective-permute-start.6) | collective-permute-done | bytes 589856 | tf_op jit(solution)/shard_map/ppermute | solution.py:323
  71.6 3.0 %collective-permute-done.7.w_theirs_ref = bf16[4,192,768]{2,1,0:T(8,128)(2,1)} collective-permute-done((bf16[4,192,768]{2,1,0:T(8,128)(2,1)S(1)}, bf16[4,192,768]{2,1,0:T(8,128)(2,1)}, u32[]{:S(2)}, u32[]{:S(2)}) %collective-permute-start.7) | collective-permute-done | bytes 1179680 | tf_op jit(solution)/shard_map/ppermute | solution.py:323
  74.5 7.7 %forward.1 = (bf16[8,96,256]{2,1,0:T(8,128)(2,1)}, bf16[8,96,256]{2,1,0:T(8,128)(2,1)}, bf16[768,256]{1,0:T(8,128)(2,1)}) custom-call(s32[5]{0:T(128)} %stack.23.place_ref, s32[128]{0:T(128)} %pad_add_fusion.slot_ref, bf16[8,256,1024]{2,1,0:T(8,128)(2,1)} %all-gather.2.cloned.1.call-done.adj_ref, bf16[32,192,128]{2,1,0:T(8,128)(2,1)S(1)} %all-to-all-done.fetched_ref, ...), custom_call_target="tpu_custom_call" | custom-call | tf_op jit(solution)/shard_map/forward/pallas_call | solution.py:176
  82.2 5.8 %all-to-all-start.1 = ((bf16[8,96,256]{2,1,0:T(8,128)(2,1)}), bf16[8,96,256]{2,1,0:T(8,128)(2,1)S(1)}, u32[]{:S(2)}, u32[]{:S(2)}) async-start(bf16[8,96,256]{2,1,0:T(8,128)(2,1)} %bitcast.57), calls=%async_computation.1 | async-start | bytes 786432 | tf_op jit(solution)/shard_map/all_to_all | solution.py:327
  90.3 4.4 %all-to-all-done.1.arrived_ref = bf16[8,96,256]{2,1,0:T(8,128)(2,1)S(1)} async-done(((bf16[8,96,256]{2,1,0:T(8,128)(2,1)}), bf16[8,96,256]{2,1,0:T(8,128)(2,1)S(1)}, u32[]{:S(2)}, u32[]{:S(2)}) %all-to-all-start.1) | async-done | bytes 393248 | tf_op jit(solution)/shard_map/all_to_all | solution.py:327
  96.5 12.2 %all_to_all.25 = bf16[8,96,256]{2,1,0:T(8,128)(2,1)} all-to-all(bf16[8,96,256]{2,1,0:T(8,128)(2,1)} %get-tuple-element.35), channel_id=1, replica_groups=mesh['xl'=2,'y'=4,'xh'=2,'z'=8,'core'=2] {'xl','y'}, dimensions={0} | all-to-all | bytes 786432 | tf_op jit(solution)/shard_map/all_to_all | solution.py:327
  108.6 8.4 %backward.1 = bf16[32,192,128]{2,1,0:T(8,128)(2,1)} custom-call(s32[5]{0:T(128)} %stack.23.place_ref, s32[128]{0:T(128)} %pad_add_fusion.slot_ref, bf16[8,256,1024]{2,1,0:T(8,128)(2,1)} %all-gather.2.cloned.1.call-done.adj_ref, bf16[768,256]{1,0:T(8,128)(2,1)} %bitcast.48, bf16[4,192,768]{2,1,0:T(8,128)(2,1)} %copy-done.1, ...), custom_call_target="tpu_custom_call" | custom-call | tf_op jit(solution)/shard_map/backward/pallas_call | solution.py:240
  117.1 8.0 %all-to-all-start.3 = ((bf16[32,192,128]{2,1,0:T(8,128)(2,1)}), bf16[32,192,128]{2,1,0:T(8,128)(2,1)S(1)}, u32[]{:S(2)}, u32[]{:S(2)}) async-start(bf16[32,192,128]{2,1,0:T(8,128)(2,1)} %backward.1), calls=%async_computation.3 | async-start | bytes 3145728 | tf_op jit(solution)/shard_map/all_to_all | solution.py:327
  128.2 4.4 %weight_terms.1 = (f32[8,48,768]{2,1,0:T(8,128)}, bf16[8,48,768]{2,1,0:T(8,128)(2,1)}) custom-call(s32[5]{0:T(128)} %stack.23.place_ref, bf16[8,96,256]{2,1,0:T(8,128)(2,1)} %get-tuple-element.33.mine_ref, bf16[8,96,256]{2,1,0:T(8,128)(2,1)} %copy-done.4, bf16[768,256]{1,0:T(8,128)(2,1)} %bitcast.49, bf16[768,256]{1,0:T(8,128)(2,1)} %copy-done.3), custom_call_target="tpu_custom_call" | custom-call | tf_op jit(solution)/shard_map/weight_terms/pallas_call | solution.py:270
  132.6 3.0 %collective-permute-start.10 = (bf16[8,48,768]{2,1,0:T(8,128)(2,1)}, bf16[8,48,768]{2,1,0:T(8,128)(2,1)S(1)}, u32[]{:S(2)}, u32[]{:S(2)}) collective-permute-start(bf16[8,48,768]{2,1,0:T(8,128)(2,1)} %get-tuple-element.38), channel_id=1, source_target_pairs={{0,16},{16,0},{1,17},{17,1},{2,18},{18,2},{3,19},{19,3},{4,20},{20... | collective-permute-start | bytes 1769480 | tf_op jit(solution)/shard_map/ppermute | solution.py:323
  135.6 24.1 %collective-permute-done.10 = bf16[8,48,768]{2,1,0:T(8,128)(2,1)S(1)} collective-permute-done((bf16[8,48,768]{2,1,0:T(8,128)(2,1)}, bf16[8,48,768]{2,1,0:T(8,128)(2,1)S(1)}, u32[]{:S(2)}, u32[]{:S(2)}) %collective-permute-start.10) | collective-permute-done | bytes 589856 | tf_op jit(solution)/shard_map/ppermute | solution.py:323
  161.9 7.3 %collective-permute-done.11 = bf16[4,48,768]{2,1,0:T(8,128)(2,1)S(1)} collective-permute-done((bf16[4,48,768]{2,1,0:T(8,128)(2,1)S(1)}, bf16[4,48,768]{2,1,0:T(8,128)(2,1)S(1)}, u32[]{:S(2)}, u32[]{:S(2)}) %collective-permute-start.11) | collective-permute-done | bytes 294944 | tf_op jit(solution)/shard_map/ppermute | solution.py:323
  169.2 3.8 %collective-permute-start.12 = (bf16[2,48,768]{2,1,0:T(8,128)(2,1)S(1)}, bf16[2,48,768]{2,1,0:T(8,128)(2,1)S(1)}, u32[]{:S(2)}, u32[]{:S(2)}) collective-permute-start(bf16[2,48,768]{2,1,0:T(8,128)(2,1)S(1)} %fusion.2), channel_id=1, source_target_pairs={{0,4},{2,6},{4,0},{6,2},{8,12},{10,14},{12,8},{14,10},{1,5},{3,7},... | collective-permute-start | bytes 442376 | tf_op jit(solution)/shard_map/ppermute | solution.py:323
  173.0 5.2 %collective-permute-done.12 = bf16[2,48,768]{2,1,0:T(8,128)(2,1)S(1)} collective-permute-done((bf16[2,48,768]{2,1,0:T(8,128)(2,1)S(1)}, bf16[2,48,768]{2,1,0:T(8,128)(2,1)S(1)}, u32[]{:S(2)}, u32[]{:S(2)}) %collective-permute-start.12) | collective-permute-done | bytes 147488 | tf_op jit(solution)/shard_map/ppermute | solution.py:323
  178.3 3.3 %collective-permute-start.13 = (bf16[1,48,768]{2,1,0:T(8,128)(2,1)S(1)}, bf16[1,48,768]{2,1,0:T(8,128)(2,1)S(1)}, u32[]{:S(2)}, u32[]{:S(2)}) collective-permute-start(bf16[1,48,768]{2,1,0:T(8,128)(2,1)S(1)} %fusion.6), channel_id=1, source_target_pairs={{0,8},{2,10},{4,12},{6,14},{8,0},{10,2},{12,4},{14,6},{1,9},{3,11}... | collective-permute-start | bytes 221192 | tf_op jit(solution)/shard_map/ppermute | solution.py:323
  184.0 5.5 %all-to-all-start.4 = ((f32[8,2,16,192]{3,2,1,0:T(8,128)}), f32[8,2,16,192]{3,2,1,0:T(8,128)S(1)}, u32[]{:S(2)}, u32[]{:S(2)}) async-start(f32[8,2,16,192]{3,2,1,0:T(8,128)} %owned.1), calls=%async_computation.4 | async-start | bytes 524288 | tf_op jit(solution)/shard_map/all_to_all | solution.py:327
  189.5 5.6 %collective-permute-start.14 = (f32[2,24,768]{2,1,0:T(8,128)S(1)}, f32[2,24,768]{2,1,0:T(8,128)S(1)}, u32[]{:S(2)}, u32[]{:S(2)}) collective-permute-start(f32[2,24,768]{2,1,0:T(8,128)S(1)} %bitcast.61), channel_id=1, source_target_pairs={{0,0},{1,4},{2,1},{3,5},{4,2},{5,6},{6,3},{7,7},{8,32},{9,36},{10,... | collective-permute-start | bytes 442376 | tf_op jit(solution)/shard_map/ppermute | solution.py:405
  195.1 10.5 %collective-permute-done.14 = f32[2,24,768]{2,1,0:T(8,128)S(1)} collective-permute-done((f32[2,24,768]{2,1,0:T(8,128)S(1)}, f32[2,24,768]{2,1,0:T(8,128)S(1)}, u32[]{:S(2)}, u32[]{:S(2)}) %collective-permute-start.14) | collective-permute-done | bytes 147488 | tf_op jit(solution)/shard_map/ppermute | solution.py:405
  (62 shorter events, 25.4 us)
Async XLA Ops:
  7.2 80.9 %copy-start = (bf16[256,768]{1,0:T(8,128)(2,1)S(1)}, bf16[256,768]{1,0:T(8,128)(2,1)}, u32[]{:S(2)}) copy-start(bf16[256,768]{1,0:T(8,128)(2,1)} %param.11) | copy-start | bytes 1179652
  7.2 67.4 %all-gather.2.cloned.1.call-start = ((), (), s32[]{:S(2)}) async-start(), calls=%async_computation.5 | async-start | bytes 5242880 | tf_op jit(solution)/shard_map/all_gather | solution.py:372
  17.5 11.3 %copy-start.5 = (s32[2,2,8]{2,1,0:T(2,128)S(1)}, s32[2,2,8]{2,1,0:T(2,128)}, u32[]{:S(2)}) copy-start(s32[2,2,8]{2,1,0:T(2,128)} %param.14) | copy-start | bytes 388
  17.5 57.0 %all-to-all-start = ((bf16[32,192,128]{2,1,0:T(8,128)(2,1)}), bf16[32,192,128]{2,1,0:T(8,128)(2,1)S(1)}, u32[]{:S(2)}, u32[]{:S(2)}) async-start(bf16[32,192,128]{2,1,0:T(8,128)(2,1)} %outgoing.1), calls=%async_computation | async-start | bytes 3145728 | tf_op jit(solution)/shard_map/all_to_all | solution.py:327
  29.0 6.2 %collective-permute-start.3 = (s32[32]{0:T(128)S(1)}, s32[32]{0:T(128)S(1)}, u32[]{:S(2)}, u32[]{:S(2)}) collective-permute-start(s32[32]{0:T(128)S(1)} %reshape.179), channel_id=1, source_target_pairs={{0,32},{32,64},{64,96},{96,0},{1,33},{33,65},{65,97},{97,1},{2,34}... | collective-permute-start | bytes 392 | tf_op jit(solution)/shard_map/ppermute | solution.py:332
  29.2 7.4 %collective-permute-start.4 = (s32[32]{0:T(128)S(1)}, s32[32]{0:T(128)S(1)}, u32[]{:S(2)}, u32[]{:S(2)}) collective-permute-start(s32[32]{0:T(128)S(1)} %reshape.179), channel_id=1, source_target_pairs={{0,64},{32,96},{64,0},{96,32},{1,65},{33,97},{65,1},{97,33},{2,66}... | collective-permute-start | bytes 392 | tf_op jit(solution)/shard_map/ppermute | solution.py:332
  31.8 4.8 %collective-permute-start.5 = (s32[32]{0:T(128)S(1)}, s32[32]{0:T(128)S(1)}, u32[]{:S(2)}, u32[]{:S(2)}) collective-permute-start(s32[32]{0:T(128)S(1)} %reshape.179), channel_id=1, source_target_pairs={{0,96},{32,0},{64,32},{96,64},{1,97},{33,1},{65,33},{97,65},{2,98}... | collective-permute-start | bytes 392 | tf_op jit(solution)/shard_map/ppermute | solution.py:332
  31.8 11.6 %collective-permute-start = (bf16[1,96,768]{2,1,0:T(8,128)(2,1)S(1)}, bf16[1,96,768]{2,1,0:T(8,128)(2,1)S(1)}, u32[]{:S(2)}, u32[]{:S(2)}) collective-permute-start(bf16[1,96,768]{2,1,0:T(8,128)(2,1)S(1)} %get-tuple-element.21), channel_id=1, source_target_pairs={{0,32},{32,64},{64,96},{96,0},{1,33},{33,65},{65,97},{97,1},{2,34}... | collective-permute-start | bytes 442376 | tf_op jit(solution)/shard_map/ppermute | solution.py:332
  35.0 11.3 %collective-permute-start.1 = (bf16[1,96,768]{2,1,0:T(8,128)(2,1)S(1)}, bf16[1,96,768]{2,1,0:T(8,128)(2,1)S(1)}, u32[]{:S(2)}, u32[]{:S(2)}) collective-permute-start(bf16[1,96,768]{2,1,0:T(8,128)(2,1)S(1)} %get-tuple-element.22), channel_id=1, source_target_pairs={{0,64},{32,96},{64,0},{96,32},{1,65},{33,97},{65,1},{97,33},{2,66}... | collective-permute-start | bytes 442376 | tf_op jit(solution)/shard_map/ppermute | solution.py:332
  35.1 13.2 %collective-permute-start.2 = (bf16[1,96,768]{2,1,0:T(8,128)(2,1)S(1)}, bf16[1,96,768]{2,1,0:T(8,128)(2,1)S(1)}, u32[]{:S(2)}, u32[]{:S(2)}) collective-permute-start(bf16[1,96,768]{2,1,0:T(8,128)(2,1)S(1)} %get-tuple-element.23), channel_id=1, source_target_pairs={{0,96},{32,0},{64,32},{96,64},{1,97},{33,1},{65,33},{97,65},{2,98}... | collective-permute-start | bytes 442376 | tf_op jit(solution)/shard_map/ppermute | solution.py:332
  48.4 22.9 %collective-permute-start.6 = (bf16[4,96,768]{2,1,0:T(8,128)(2,1)S(1)}, bf16[4,96,768]{2,1,0:T(8,128)(2,1)S(1)}, u32[]{:S(2)}, u32[]{:S(2)}) collective-permute-start(bf16[4,96,768]{2,1,0:T(8,128)(2,1)S(1)} %constant_dynamic-update-slice_fusion), channel_id=1, source_target_pairs={{0,16},{16,0},{1,17},{17,1},{2,18},{18,2},{3,19},{19,3},{4,20},{20... | collective-permute-start | bytes 1769480 | tf_op jit(solution)/shard_map/ppermute | solution.py:323
  71.5 3.1 %collective-permute-start.7 = (bf16[4,192,768]{2,1,0:T(8,128)(2,1)S(1)}, bf16[4,192,768]{2,1,0:T(8,128)(2,1)}, u32[]{:S(2)}, u32[]{:S(2)}) collective-permute-start(bf16[4,192,768]{2,1,0:T(8,128)(2,1)S(1)} %pad_maximum_fusion.w_mine_ref), channel_id=1, source_target_pairs={{0,1},{1,0},{2,3},{3,2},{4,5},{5,4},{6,7},{7,6},{8,9},{9,8},{10,11... | collective-permute-start | bytes 3538952 | tf_op jit(solution)/shard_map/ppermute | solution.py:323
  82.2 12.4 %all-to-all-start.1 = ((bf16[8,96,256]{2,1,0:T(8,128)(2,1)}), bf16[8,96,256]{2,1,0:T(8,128)(2,1)S(1)}, u32[]{:S(2)}, u32[]{:S(2)}) async-start(bf16[8,96,256]{2,1,0:T(8,128)(2,1)} %bitcast.57), calls=%async_computation.1 | async-start | bytes 786432 | tf_op jit(solution)/shard_map/all_to_all | solution.py:327
  117.1 8.0 %copy-start.2 = (bf16[8,96,256]{2,1,0:T(8,128)(2,1)S(1)}, bf16[8,96,256]{2,1,0:T(8,128)(2,1)}, u32[]{:S(2)}) copy-start(bf16[8,96,256]{2,1,0:T(8,128)(2,1)} %all_to_all.25) | copy-start | bytes 1179652
  117.1 8.2 %copy-start.6 = (bf16[8,96,256]{2,1,0:T(8,128)(2,1)S(1)}, bf16[8,96,256]{2,1,0:T(8,128)(2,1)}, u32[]{:S(2)}) copy-start(bf16[8,96,256]{2,1,0:T(8,128)(2,1)} %get-tuple-element.34) | copy-start | bytes 1179652
  117.1 64.4 %all-to-all-start.3 = ((bf16[32,192,128]{2,1,0:T(8,128)(2,1)}), bf16[32,192,128]{2,1,0:T(8,128)(2,1)S(1)}, u32[]{:S(2)}, u32[]{:S(2)}) async-start(bf16[32,192,128]{2,1,0:T(8,128)(2,1)} %backward.1), calls=%async_computation.3 | async-start | bytes 3145728 | tf_op jit(solution)/shard_map/all_to_all | solution.py:327
  125.1 1.8 collective-permute-start.9
  125.3 2.1 collective-permute-start.8
  132.6 27.0 %collective-permute-start.10 = (bf16[8,48,768]{2,1,0:T(8,128)(2,1)}, bf16[8,48,768]{2,1,0:T(8,128)(2,1)S(1)}, u32[]{:S(2)}, u32[]{:S(2)}) collective-permute-start(bf16[8,48,768]{2,1,0:T(8,128)(2,1)} %get-tuple-element.38), channel_id=1, source_target_pairs={{0,16},{16,0},{1,17},{17,1},{2,18},{18,2},{3,19},{19,3},{4,20},{20... | collective-permute-start | bytes 1769480 | tf_op jit(solution)/shard_map/ppermute | solution.py:323
  161.0 8.1 %collective-permute-start.11 = (bf16[4,48,768]{2,1,0:T(8,128)(2,1)S(1)}, bf16[4,48,768]{2,1,0:T(8,128)(2,1)S(1)}, u32[]{:S(2)}, u32[]{:S(2)}) collective-permute-start(bf16[4,48,768]{2,1,0:T(8,128)(2,1)S(1)} %get-tuple-element.43), channel_id=1, source_target_pairs={{0,2},{2,0},{4,6},{6,4},{8,10},{10,8},{12,14},{14,12},{1,3},{3,1},... | collective-permute-start | bytes 884744 | tf_op jit(solution)/shard_map/ppermute | solution.py:323
  169.2 9.0 %collective-permute-start.12 = (bf16[2,48,768]{2,1,0:T(8,128)(2,1)S(1)}, bf16[2,48,768]{2,1,0:T(8,128)(2,1)S(1)}, u32[]{:S(2)}, u32[]{:S(2)}) collective-permute-start(bf16[2,48,768]{2,1,0:T(8,128)(2,1)S(1)} %fusion.2), channel_id=1, source_target_pairs={{0,4},{2,6},{4,0},{6,2},{8,12},{10,14},{12,8},{14,10},{1,5},{3,7},... | collective-permute-start | bytes 442376 | tf_op jit(solution)/shard_map/ppermute | solution.py:323
  178.3 11.2 %collective-permute-start.13 = (bf16[1,48,768]{2,1,0:T(8,128)(2,1)S(1)}, bf16[1,48,768]{2,1,0:T(8,128)(2,1)S(1)}, u32[]{:S(2)}, u32[]{:S(2)}) collective-permute-start(bf16[1,48,768]{2,1,0:T(8,128)(2,1)S(1)} %fusion.6), channel_id=1, source_target_pairs={{0,8},{2,10},{4,12},{6,14},{8,0},{10,2},{12,4},{14,6},{1,9},{3,11}... | collective-permute-start | bytes 221192 | tf_op jit(solution)/shard_map/ppermute | solution.py:323
  184.0 21.6 %all-to-all-start.4 = ((f32[8,2,16,192]{3,2,1,0:T(8,128)}), f32[8,2,16,192]{3,2,1,0:T(8,128)S(1)}, u32[]{:S(2)}, u32[]{:S(2)}) async-start(f32[8,2,16,192]{3,2,1,0:T(8,128)} %owned.1), calls=%async_computation.4 | async-start | bytes 524288 | tf_op jit(solution)/shard_map/all_to_all | solution.py:327
  189.5 16.1 %collective-permute-start.14 = (f32[2,24,768]{2,1,0:T(8,128)S(1)}, f32[2,24,768]{2,1,0:T(8,128)S(1)}, u32[]{:S(2)}, u32[]{:S(2)}) collective-permute-start(f32[2,24,768]{2,1,0:T(8,128)S(1)} %bitcast.61), channel_id=1, source_target_pairs={{0,0},{1,4},{2,1},{3,5},{4,2},{5,6},{6,3},{7,7},{8,32},{9,36},{10,... | collective-permute-start | bytes 442376 | tf_op jit(solution)/shard_map/ppermute | solution.py:405
  (3 other events, 4.6 us)
Sparse Core Ops, SparseCore 0:
  14.3 57.8 all-gather.1

commit v6 on v5

--- a/solution.py
+++ b/solution.py
@@ -12,7 +12,7 @@
 BLK = 128
 REL = ("xl", "y")
 TGT = ("xh", "z", "core")
-VMEM_LIMIT = 58 * 1024 * 1024
+VMEM_LIMIT = 44 * 1024 * 1024
 
 
 def in_hbm(value):
@@ -93,99 +93,81 @@
     )(place, source_blocks, features)
 
 
-STEPS = tuple((k, p) for k in range(4) for p in range(2))
-
-
-def start_loads(place_ref, adj_ref, adj_buf, w_mine_ref, w_theirs_ref, w_buf, sems):
-    core, y = place_ref[2], place_ref[3]
+ORDER = (0, 1, 3, 2)
+
+
+def start_loads(adj_refs, adj_buf, sems):
+    own, back, fore, far0, far1 = adj_refs
     loads = []
-    for k in range(4):
-        group = [
-            pltpu.make_async_copy(
-                adj_ref.at[pl.ds(2 * ((y - k) & 3), 2)], adj_buf.at[pl.ds(2 * k, 2)], sems.at[3 * k]
-            )
-        ]
-        for n, (half, ref) in enumerate(((core, w_mine_ref), (1 - core, w_theirs_ref)), 1):
-            group.append(pltpu.make_async_copy(ref.at[k], w_buf.at[2 * k + half], sems.at[3 * k + n]))
+    for n, ref in enumerate((own, back, fore)):
+        loads.append([pltpu.make_async_copy(ref, adj_buf.at[pl.ds(2 * n, 2)], sems.at[n])])
+    loads.append(
+        [pltpu.make_async_copy(ref, adj_buf.at[pl.ds(6 + n, 1)], sems.at[3 + n]) for n, ref in enumerate((far0, far1))]
+    )
+    for group in loads:
         for load in group:
             load.start()
-        loads.append(group)
     return loads
 
 
-def load_scratch(rows, wide, width):
-    return [
-        pltpu.VMEM((8, rows, wide), BF16),
-        pltpu.VMEM((8, 192, width), BF16),
-        pltpu.SemaphoreType.DMA((12,)),
-    ]
+def load_scratch(rows, wide):
+    return [pltpu.VMEM((8, rows, wide), BF16), pltpu.SemaphoreType.DMA((5,))]
 
 
 def hbm():
     return pl.BlockSpec(memory_space=pltpu.MemorySpace.HBM)
 
 
-def anywhere():
-    return pl.BlockSpec(memory_space=pl.ANY)
-
-
 def forward_kernel(
-    place_ref, slot_ref, adj_ref, fetched_ref, w_mine_ref, w_theirs_ref,
-    keep_ref, send_ref, pre_ref, adj_buf, w_buf, sems, acc_ref,
+    place_ref, slot_ref, own_ref, back_ref, fore_ref, far0_ref, far1_ref, fetched_ref, w_mine_ref, w_theirs_ref,
+    keep_ref, send_ref, pre_ref, adj_buf, sems, both_ref, acc_ref,
 ):
     core, y = place_ref[2], place_ref[3]
-    loads = start_loads(place_ref, adj_ref, adj_buf, w_mine_ref, w_theirs_ref, w_buf, sems)
-    for k in range(4):
-        for load in loads[k]:
+    loads = start_loads((own_ref, back_ref, fore_ref, far0_ref, far1_ref), adj_buf, sems)
+    for n, k in enumerate(ORDER):
+        for load in loads[n]:
             load.wait()
-        pair = pl.ds(2 * ((y - k) & 3), 2)
-        both = []
         for p in range(2):
-            halves = []
             for q in range(2):
                 base = ((k * 2 + p) * 2 + q) * 8
                 wide = jnp.concatenate([fetched_ref[slot_ref[base + s]] for s in range(8)], axis=1)
-                part = adj_buf[2 * k + p, q * BLK : (q + 1) * BLK, :]
-                halves.append(dot(wide, part, 1, 1).astype(BF16))
-            both.append(jnp.concatenate(halves, axis=1))
-        both = jnp.stack(both)
+                part = adj_buf[2 * n + p, q * BLK : (q + 1) * BLK, :]
+                both_ref[p, :, q * BLK : (q + 1) * BLK] = dot(wide, part, 1, 1).astype(BF16)
+        pair = pl.ds(2 * ((y - k) & 3), 2)
 
         @pl.when(core == 0)
         def _():
-            keep_ref[pair] = both[:, :96]
-            send_ref[pair] = both[:, 96:]
+            keep_ref[pair] = both_ref[:, :96]
+            send_ref[pair] = both_ref[:, 96:]
 
         @pl.when(core == 1)
         def _():
-            keep_ref[pair] = both[:, 96:]
-            send_ref[pair] = both[:, :96]
-
-        deep = 2 * w_buf.shape[1]
-        term = dot(w_buf[2 * k : 2 * k + 2].reshape(deep, -1), both.reshape(deep, -1), 0, 0)
-        if k == 0:
+            keep_ref[pair] = both_ref[:, 96:]
+            send_ref[pair] = both_ref[:, :96]
+
+        term = dot(w_mine_ref[k], both_ref[core], 0, 0) + dot(w_theirs_ref[k], both_ref[1 - core], 0, 0)
+        if n == 0:
             acc_ref[...] = term
-        elif k < 3:
+        elif n < 3:
             acc_ref[...] += term
         else:
             pre_ref[...] = (acc_ref[...] + term).astype(BF16)
 
 
 def forward_of(place, slots, adjacency, fetched, w_mine, w_theirs):
-    rels, rows, wide = adjacency.shape
+    _, rows, wide = adjacency[0].shape
     width = w_mine.shape[2]
+    half = jax.ShapeDtypeStruct((8, 96, rows), BF16)
     return pl.pallas_call(
         forward_kernel,
-        in_specs=[smem(), smem(), hbm(), vmem(), anywhere(), anywhere()],
+        in_specs=[smem(), smem()] + [hbm()] * 5 + [vmem()] * 3,
         out_specs=[vmem()] * 3,
-        out_shape=[
-            jax.ShapeDtypeStruct((rels, 96, rows), BF16),
-            jax.ShapeDtypeStruct((rels, 96, rows), BF16),
-            jax.ShapeDtypeStruct((width, rows), BF16),
-        ],
-        scratch_shapes=load_scratch(rows, wide, width) + [pltpu.VMEM((width, rows), F32)],
+        out_shape=[half, half, jax.ShapeDtypeStruct((width, rows), BF16)],
+        scratch_shapes=load_scratch(rows, wide)
+        + [pltpu.VMEM((2, 192, rows), BF16), pltpu.VMEM((width, rows), F32)],
         compiler_params=params(),
         name="forward",
-    )(place, slots, adjacency, fetched, w_mine, w_theirs)
+    )(place, slots, *adjacency, fetched, w_mine, w_theirs)
 
 
 def activation_kernel(arrived_ref, bias_ref, cotangent_ref, act_ref, grad_ref):
@@ -215,37 +197,39 @@
 
 
 def backward_kernel(
-    place_ref, slot_ref, adj_ref, grad_ref, w_mine_ref, w_theirs_ref, out_ref,
-    adj_buf, w_buf, sems, acc_ref,
+    place_ref, slot_ref, own_ref, back_ref, fore_ref, far0_ref, far1_ref, grad_ref, w_mine_ref, w_theirs_ref,
+    out_ref, adj_buf, sems, both_ref, acc_ref,
 ):
-    loads = start_loads(place_ref, adj_ref, adj_buf, w_mine_ref, w_theirs_ref, w_buf, sems)
+    core = place_ref[2]
+    loads = start_loads((own_ref, back_ref, fore_ref, far0_ref, far1_ref), adj_buf, sems)
     acc_ref[...] = jnp.zeros_like(acc_ref)
-    for n, (k, p) in enumerate(STEPS):
-        if p == 0:
-            for load in loads[k]:
-                load.wait()
-        grads = dot(w_buf[n], grad_ref[...], 1, 0).astype(BF16)
-        for q in range(2):
-            base = (n * 2 + q) * 8
-            part = adj_buf[n, q * BLK : (q + 1) * BLK, :]
-            wide = dot(grads[:, q * BLK : (q + 1) * BLK], part, 1, 0)
-            for s in range(8):
-                acc_ref[slot_ref[base + s]] += wide[:, s * BLK : (s + 1) * BLK]
+    for n, k in enumerate(ORDER):
+        both_ref[core] = dot(w_mine_ref[k], grad_ref[...], 1, 0).astype(BF16)
+        both_ref[1 - core] = dot(w_theirs_ref[k], grad_ref[...], 1, 0).astype(BF16)
+        for load in loads[n]:
+            load.wait()
+        for p in range(2):
+            for q in range(2):
+                base = ((k * 2 + p) * 2 + q) * 8
+                part = adj_buf[2 * n + p, q * BLK : (q + 1) * BLK, :]
+                wide = dot(both_ref[p, :, q * BLK : (q + 1) * BLK], part, 1, 0)
+                for s in range(8):
+                    acc_ref[slot_ref[base + s]] += wide[:, s * BLK : (s + 1) * BLK]
     out_ref[...] = acc_ref[...].astype(BF16)
 
 
 def backward_of(place, slots, adjacency, grads, w_mine, w_theirs, owners):
-    rels, rows, wide = adjacency.shape
-    width = w_mine.shape[2]
+    _, rows, wide = adjacency[0].shape
     return pl.pallas_call(
         backward_kernel,
-        in_specs=[smem(), smem(), hbm(), vmem(), anywhere(), anywhere()],
+        in_specs=[smem(), smem()] + [hbm()] * 5 + [vmem()] * 3,
         out_specs=vmem(),
         out_shape=jax.ShapeDtypeStruct((owners, 192, BLK), BF16),
-        scratch_shapes=load_scratch(rows, wide, width) + [pltpu.VMEM((owners, 192, BLK), F32)],
+        scratch_shapes=load_scratch(rows, wide)
+        + [pltpu.VMEM((2, 192, rows), BF16), pltpu.VMEM((owners, 192, BLK), F32)],
         compiler_params=params(),
         name="backward",
-    )(place, slots, adjacency, grads, w_mine, w_theirs)
+    )(place, slots, *adjacency, grads, w_mine, w_theirs)
 
 
 def weight_kernel(place_ref, mine_ref, theirs_ref, grad_ref, their_grad_ref, keep_ref, send_ref):
@@ -319,6 +303,10 @@
     return take(bit), take(1 - bit).astype(BF16)
 
 
+def step(value, by):
+    return lax.ppermute(value, "y", [(i, (i + by) % 4) for i in range(4)])
+
+
 def swap(value, axis, size=2, flip=1):
     return lax.ppermute(value, axis, [(i, i ^ flip) for i in range(size)])
 
@@ -358,27 +346,28 @@
     owner = lax.axis_index(TGT)
     group = lax.axis_index(REL)
     xh, z = lax.axis_index("xh"), lax.axis_index("z")
-    place = jnp.stack([owner, 192 * y, core, y, xh]).astype(jnp.int32)
-
-    w_cut = [
-        lax.dynamic_slice(weights, (core, ((y + k) & 3) * 192 + 96 * xh, 0), (1, 96, width))
-        for k in range(4)
-    ]
-    w_cut, tile_values = lax.optimization_barrier((w_cut, tile_values))
-    w_came = around(w_cut[1:], "y", 4)
-    own_slots = tile_slot.reshape(-1)
-    slots = jnp.concatenate([own_slots, *around([own_slots] * 3, "y", 4)])
-    own_adjacency = adjacency_of(tile_values, tile_count)
-    adjacency = in_hbm(lax.all_gather(own_adjacency, "y", axis=0, tiled=True))
-    features, _ = lax.optimization_barrier((features, own_adjacency))
-    fetched = resident(exchange(outgoing_of(features, source_blocks, place), TGT))
-    w_came, slots = lax.optimization_barrier((w_came, slots))
-    w_part = jnp.concatenate([w_cut[0], *w_came], axis=0)
-    w_other = swap(w_part, "xh")
-    w_mine = jnp.concatenate(
-        [jnp.where(xh == 0, w_part, w_other), jnp.where(xh == 0, w_other, w_part)], axis=1
-    )
-    w_theirs = swap(w_mine, "core")
+    xh, z = lax.axis_index("xh"), lax.axis_index("z")
+    place = in_hbm(jnp.stack([owner, 192 * y, core, y, xh]).astype(jnp.int32))
+
+    own = adjacency_of(in_hbm(tile_values), in_hbm(tile_count))
+    back, fore = step(own, 1), step(own, -1)
+    far0, far1 = step(back[:1], 1), step(fore[1:], -1)
+    adjacency = [in_hbm(a) for a in (own, back, fore, far0, far1)]
+    features, weights, _ = lax.optimization_barrier((features, weights, own))
+    source_blocks = in_hbm(source_blocks)
+    outgoing = outgoing_of(in_hbm(features), source_blocks, place)
+    fetched = resident(exchange(outgoing, TGT))
+
+    own_slots = jnp.pad(tile_slot.reshape(1, 1, -1), ((0, 0), (0, 15), (0, width - 32))).astype(BF16)
+    pieces = []
+    for k in range(4):
+        cut = lax.dynamic_slice(weights, (core, ((y + k) & 3) * 192, 0), (1, 192, width))
+        pieces.append(jnp.concatenate([cut, own_slots], axis=1) if k else cut)
+    came = around(pieces[1:], "y", 4)
+    slots = jnp.concatenate([tile_slot.reshape(-1)] + [c[0, 192, :32].astype(jnp.int32) for c in came])
+    slots = in_hbm(slots)
+    w_mine = jnp.concatenate([pieces[0]] + [c[:, :192] for c in came], axis=0)
+    w_mine, w_theirs = resident(w_mine), resident(swap(w_mine, "core"))
 
     messages, for_partner, part = forward_of(place, slots, adjacency, fetched, w_mine, w_theirs)
     from_partner = swap(for_partner, "core")
@@ -390,7 +379,7 @@
     output = activated.T
     grads = exchange(grad_copies, REL).reshape(width, -1)
 
-    partial = backward_of(place, slots, adjacency, grads, w_mine, w_theirs, owners)
+    partial = backward_of(place, slots, adjacency, resident(grads), w_mine, w_theirs, owners)
     returned = resident(exchange(in_hbm(partial), TGT))
     cut = owned_of(place, source_blocks, returned, groups)
     columns = exchange(cut, REL).reshape(2, 4, 2, BLK // groups, 192).sum(axis=0)

time: 217 us -> 214 us (0.986)
  waiting for transfers between devices: 87.1 us -> 102 us
  between operations: 14.3 us -> 0.89 us
  Pallas kernels: 33.1 us -> 27.8 us
  local copies, waits for them, and re-layouts: 6.61 us -> 10.9 us
  starting transfers between devices: 58.4 us -> 54.5 us
    ppermute x0 -> x4, waiting for transfers between devices: none -> 32.8 us  [step(): return lax.ppermute(value, 'y', [(i, (i + by) % 4) for i in range(4)])]
    ppermute x8 -> x7, waiting for transfers between devices: 61.1 us -> 41.2 us  [swap(): return lax.ppermute(value, axis, [(i, i ^ flip) for i in range(size)])]
    ppermute x0 -> x4, starting transfers between devices: none -> 5.42 us  [step(): return lax.ppermute(value, 'y', [(i, (i + by) % 4) for i in range(4)])]
    ppermute x6 -> x3, starting transfers between devices: 7.59 us -> 2.89 us  [around(): lax.ppermute(v, axis, [(i, (i + k) % size) for i in range(size)])]
    ppermute x8 -> x7, starting transfers between devices: 14.7 us -> 10.2 us  [swap(): return lax.ppermute(value, axis, [(i, i ^ flip) for i in range(size)])]
    unnamed x19 -> x20, local copies, waits for them, and re-layouts: 2.2 us -> 4.53 us
    slice x0 -> x5, local copies, waits for them, and re-layouts: none -> 2.21 us  [the longest x2 2.15 us: per_device(): far0, far1 = (step(back[:1], 1), step(fore[1:], -1))]
    ppermute x6 -> x3, waiting for transfers between devices: 11.1 us -> 12 us  [around(): lax.ppermute(v, axis, [(i, (i + k) % size) for i in range(size)])]
  transfers between devices with their start and end apart: 20 -> 19, of which waited for: 12 -> 13; matrix products, arithmetic and copies ran while one was open for 3% -> 4% of each run, Pallas kernels for 4% -> 2%
where the time goes in v6:
time: 214 us; the launch traced here: 210 us
  waiting for transfers between devices  102 us (48%)
  starting transfers between devices  54.5 us (25%)
  Pallas kernels  27.8 us (13%)
  blocking collectives  11 us (5%)
  local copies, waits for them, and re-layouts  10.9 us (5%)
  other arithmetic  3 us (1%)
    ppermute x7, waiting for transfers between devices, swap(): return lax.ppermute(value, axis, [(i, i ^ flip) for i in range(size)])  41.2 us
    ppermute x4, waiting for transfers between devices, step(): return lax.ppermute(value, 'y', [(i, (i + by) % 4) for i in range(4)])  32.8 us
    all_to_all x4, starting transfers between devices, exchange(): return lax.all_to_all(value, axis, 0, 0, tiled=True)  31.8 us
    ppermute x3, waiting for transfers between devices, around(): lax.ppermute(v, axis, [(i, (i + k) % size) for i in range(size)])  12 us
    ppermute x1, waiting for transfers between devices, per_device(): lax.ppermute(piece.reshape(2, 24, width), ('y', *TGT), to_owner())  12 us
    all_to_all x1, blocking collectives, exchange(): return lax.all_to_all(value, axis, 0, 0, tiled=True)  11 us
    ppermute x7, starting transfers between devices, swap(): return lax.ppermute(value, axis, [(i, i ^ flip) for i in range(size)])  10.2 us
    pallas_call x1, Pallas kernels, forward_of(): pl.pallas_call(forward_kernel, in_specs=[smem(), smem()] + [hbm()] * 5 +...  8.62 us
  transfers between devices with their start and end apart: 19, of which 13 were waited for; matrix products, arithmetic and copies ran while one was open for 4% of the time, Pallas kernels for 2%

profile of v6, /device:TPU:56, one launch (start us, length us, event | category | flops | bytes accessed | tf_op | source)
XLA Modules:
  0.0 210.4 jit_solution(375075790915701146)
XLA Ops:
  0.7 5.0 %adjacency.1.own_ref = bf16[2,256,1024]{2,1,0:T(8,128)(2,1)S(1)} custom-call(s32[2,2]{1,0:T(2,128)} %count_ref.1, s32[2,256,8,128]{3,2,1,0:T(8,128)} %values_ref.1), custom_call_target="tpu_custom_call" | custom-call | tf_op jit(solution)/shard_map/adjacency/pallas_call | solution.py:61
  6.5 2.6 %outgoing.1 = bf16[32,192,128]{2,1,0:T(8,128)(2,1)} custom-call(s32[5]{0:T(128)} %stack.23.place_ref, s32[32,32]{1,0:T(8,128)} %table_ref.3, bf16[256,768]{1,0:T(8,128)(2,1)} %features_ref), custom_call_target="tpu_custom_call" | custom-call | tf_op jit(solution)/shard_map/outgoing/pallas_call | solution.py:85
  9.1 11.4 %all-to-all-start = ((bf16[32,192,128]{2,1,0:T(8,128)(2,1)}), bf16[32,192,128]{2,1,0:T(8,128)(2,1)}, u32[]{:S(2)}, u32[]{:S(2)}) async-start(bf16[32,192,128]{2,1,0:T(8,128)(2,1)} %outgoing.1), calls=%async_computation | async-start | bytes 3145728 | tf_op jit(solution)/shard_map/all_to_all | solution.py:315
  24.9 3.2 %collective-permute-start.3 = (bf16[2,256,1024]{2,1,0:T(8,128)(2,1)S(1)}, bf16[2,256,1024]{2,1,0:T(8,128)(2,1)}, u32[]{:S(2)}, u32[]{:S(2)}) collective-permute-start(bf16[2,256,1024]{2,1,0:T(8,128)(2,1)S(1)} %adjacency.1.own_ref), channel_id=1, source_target_pairs={{0,32},{32,64},{64,96},{96,0},{1,33},{33,65},{65,97},{97,1},{2,34}... | collective-permute-start | bytes 3145736 | tf_op jit(solution)/shard_map/ppermute | solution.py:307
  28.1 4.3 %collective-permute-done = bf16[1,208,768]{2,1,0:T(8,128)(2,1)S(1)} collective-permute-done((bf16[1,208,768]{2,1,0:T(8,128)(2,1)S(1)}, bf16[1,208,768]{2,1,0:T(8,128)(2,1)S(1)}, u32[]{:S(2)}, u32[]{:S(2)}) %collective-permute-start) | collective-permute-done | bytes 319520 | tf_op jit(solution)/shard_map/ppermute | solution.py:320
  34.2 5.9 %collective-permute-done.2 = bf16[1,208,768]{2,1,0:T(8,128)(2,1)S(1)} collective-permute-done((bf16[1,208,768]{2,1,0:T(8,128)(2,1)S(1)}, bf16[1,208,768]{2,1,0:T(8,128)(2,1)S(1)}, u32[]{:S(2)}, u32[]{:S(2)}) %collective-permute-start.2) | collective-permute-done | bytes 319520 | tf_op jit(solution)/shard_map/ppermute | solution.py:320
  40.6 20.5 %collective-permute-done.3.back_ref = bf16[2,256,1024]{2,1,0:T(8,128)(2,1)} collective-permute-done((bf16[2,256,1024]{2,1,0:T(8,128)(2,1)S(1)}, bf16[2,256,1024]{2,1,0:T(8,128)(2,1)}, u32[]{:S(2)}, u32[]{:S(2)}) %collective-permute-start.3) | collective-permute-done | bytes 1048608 | tf_op jit(solution)/shard_map/ppermute | solution.py:307
  66.7 8.7 %collective-permute-done.5.far0_ref = bf16[1,256,1024]{2,1,0:T(8,128)(2,1)S(1)} collective-permute-done((bf16[1,256,1024]{2,1,0:T(8,128)(2,1)S(1)}, bf16[1,256,1024]{2,1,0:T(8,128)(2,1)S(1)}, u32[]{:S(2)}, u32[]{:S(2)}) %collective-permute-start.5) | collective-permute-done | bytes 524320 | tf_op jit(solution)/shard_map/ppermute | solution.py:307
  75.4 3.6 %collective-permute-done.6.far1_ref = bf16[1,256,1024]{2,1,0:T(8,128)(2,1)S(1)} collective-permute-done((bf16[1,256,1024]{2,1,0:T(8,128)(2,1)S(1)}, bf16[1,256,1024]{2,1,0:T(8,128)(2,1)S(1)}, u32[]{:S(2)}, u32[]{:S(2)}) %collective-permute-start.6) | collective-permute-done | bytes 524320 | tf_op jit(solution)/shard_map/ppermute | solution.py:307
  79.9 8.6 %forward.1 = (bf16[8,96,256]{2,1,0:T(8,128)(2,1)S(1)}, bf16[8,96,256]{2,1,0:T(8,128)(2,1)S(1)}, bf16[768,256]{1,0:T(8,128)(2,1)}) custom-call(s32[5]{0:T(128)} %stack.23.place_ref, s32[128]{0:T(128)} %pad_add_fusion.slot_ref, bf16[2,256,1024]{2,1,0:T(8,128)(2,1)} %copy-done.1, bf16[2,256,1024]{2,1,0:T(8,128)(2,1)} %collective-permute-done.3.back_ref, ...), custom_call_target="tpu_custom_call" | custom-call | tf_op jit(solution)/shard_map/forward/pallas_call | solution.py:161
  89.2 4.5 %all-to-all-start.1 = ((bf16[8,96,256]{2,1,0:T(8,128)(2,1)}), bf16[8,96,256]{2,1,0:T(8,128)(2,1)S(1)}, u32[]{:S(2)}, u32[]{:S(2)}) async-start(bf16[8,96,256]{2,1,0:T(8,128)(2,1)} %bitcast.8), calls=%async_computation.1 | async-start | bytes 786432 | tf_op jit(solution)/shard_map/all_to_all | solution.py:315
  94.9 4.3 %all-to-all-done.1.arrived_ref = bf16[8,96,256]{2,1,0:T(8,128)(2,1)S(1)} async-done(((bf16[8,96,256]{2,1,0:T(8,128)(2,1)}), bf16[8,96,256]{2,1,0:T(8,128)(2,1)S(1)}, u32[]{:S(2)}, u32[]{:S(2)}) %all-to-all-start.1) | async-done | bytes 393248 | tf_op jit(solution)/shard_map/all_to_all | solution.py:315
  99.9 11.0 %all_to_all.25 = bf16[8,96,256]{2,1,0:T(8,128)(2,1)S(1)} all-to-all(bf16[8,96,256]{2,1,0:T(8,128)(2,1)S(1)} %get-tuple-element.19), channel_id=1, replica_groups=mesh['xl'=2,'y'=4,'xh'=2,'z'=8,'core'=2] {'xl','y'}, dimensions={0} | all-to-all | bytes 786432 | tf_op jit(solution)/shard_map/all_to_all | solution.py:315
  110.9 5.7 %backward.1 = bf16[32,192,128]{2,1,0:T(8,128)(2,1)S(1)} custom-call(s32[5]{0:T(128)} %stack.23.place_ref, s32[128]{0:T(128)} %pad_add_fusion.slot_ref, bf16[2,256,1024]{2,1,0:T(8,128)(2,1)} %copy-done.1, bf16[2,256,1024]{2,1,0:T(8,128)(2,1)} %collective-permute-done.3.back_ref, bf16[2,256,1024]{2,1,0:T(8,128)(2,1)} %collective-permute-done.4.fore_ref, ...), custom_call_target="tpu_custom_call" | custom-call | tf_op jit(solution)/shard_map/backward/pallas_call | solution.py:223
  117.8 10.4 %all-to-all-start.3 = ((bf16[32,192,128]{2,1,0:T(8,128)(2,1)}), bf16[32,192,128]{2,1,0:T(8,128)(2,1)S(1)}, u32[]{:S(2)}, u32[]{:S(2)}) async-start(bf16[32,192,128]{2,1,0:T(8,128)(2,1)} %copy-done.2), calls=%async_computation.3 | async-start | bytes 3145728 | tf_op jit(solution)/shard_map/all_to_all | solution.py:315
  130.8 2.7 %weight_terms.1 = (f32[8,48,768]{2,1,0:T(8,128)S(1)}, bf16[8,48,768]{2,1,0:T(8,128)(2,1)}) custom-call(s32[5]{0:T(128)} %stack.23.place_ref, bf16[8,96,256]{2,1,0:T(8,128)(2,1)S(1)} %get-tuple-element.17.mine_ref, bf16[8,96,256]{2,1,0:T(8,128)(2,1)S(1)} %collective-permute-done.8.theirs_ref, bf16[768,256]{1,0:T(8,128)(2,1)S(1)} %bitcast.65, ...), custom_call_target="tpu_custom_call" | custom-call | tf_op jit(solution)/shard_map/weight_terms/pallas_call | solution.py:254
  134.6 3.0 %collective-permute-start.10 = (bf16[8,48,768]{2,1,0:T(8,128)(2,1)}, bf16[8,48,768]{2,1,0:T(8,128)(2,1)S(1)}, u32[]{:S(2)}, u32[]{:S(2)}) collective-permute-start(bf16[8,48,768]{2,1,0:T(8,128)(2,1)} %get-tuple-element.22), channel_id=1, source_target_pairs={{0,16},{16,0},{1,17},{17,1},{2,18},{18,2},{3,19},{19,3},{4,20},{20... | collective-permute-start | bytes 1769480 | tf_op jit(solution)/shard_map/ppermute | solution.py:311
  137.5 25.0 %collective-permute-done.10 = bf16[8,48,768]{2,1,0:T(8,128)(2,1)S(1)} collective-permute-done((bf16[8,48,768]{2,1,0:T(8,128)(2,1)}, bf16[8,48,768]{2,1,0:T(8,128)(2,1)S(1)}, u32[]{:S(2)}, u32[]{:S(2)}) %collective-permute-start.10) | collective-permute-done | bytes 589856 | tf_op jit(solution)/shard_map/ppermute | solution.py:311
  164.0 8.9 %collective-permute-done.11 = bf16[4,48,768]{2,1,0:T(8,128)(2,1)S(1)} collective-permute-done((bf16[4,48,768]{2,1,0:T(8,128)(2,1)S(1)}, bf16[4,48,768]{2,1,0:T(8,128)(2,1)S(1)}, u32[]{:S(2)}, u32[]{:S(2)}) %collective-permute-start.11) | collective-permute-done | bytes 294944 | tf_op jit(solution)/shard_map/ppermute | solution.py:311
  175.5 5.3 %collective-permute-done.12 = bf16[2,48,768]{2,1,0:T(8,128)(2,1)S(1)} collective-permute-done((bf16[2,48,768]{2,1,0:T(8,128)(2,1)S(1)}, bf16[2,48,768]{2,1,0:T(8,128)(2,1)S(1)}, u32[]{:S(2)}, u32[]{:S(2)}) %collective-permute-start.12) | collective-permute-done | bytes 147488 | tf_op jit(solution)/shard_map/ppermute | solution.py:311
  180.8 3.9 %collective-permute-start.13 = (bf16[1,48,768]{2,1,0:T(8,128)(2,1)S(1)}, bf16[1,48,768]{2,1,0:T(8,128)(2,1)S(1)}, u32[]{:S(2)}, u32[]{:S(2)}) collective-permute-start(bf16[1,48,768]{2,1,0:T(8,128)(2,1)S(1)} %fusion.10), channel_id=1, source_target_pairs={{0,8},{2,10},{4,12},{6,14},{8,0},{10,2},{12,4},{14,6},{1,9},{3,11}... | collective-permute-start | bytes 221192 | tf_op jit(solution)/shard_map/ppermute | solution.py:311
  187.2 5.4 %all-to-all-start.4 = ((f32[8,2,16,192]{3,2,1,0:T(8,128)}), f32[8,2,16,192]{3,2,1,0:T(8,128)S(1)}, u32[]{:S(2)}, u32[]{:S(2)}) async-start(f32[8,2,16,192]{3,2,1,0:T(8,128)} %owned.1), calls=%async_computation.4 | async-start | bytes 524288 | tf_op jit(solution)/shard_map/all_to_all | solution.py:315
  192.7 4.2 %collective-permute-start.14 = (f32[2,24,768]{2,1,0:T(8,128)S(1)}, f32[2,24,768]{2,1,0:T(8,128)S(1)}, u32[]{:S(2)}, u32[]{:S(2)}) collective-permute-start(f32[2,24,768]{2,1,0:T(8,128)S(1)} %bitcast.75), channel_id=1, source_target_pairs={{0,0},{1,4},{2,1},{3,5},{4,2},{5,6},{6,3},{7,7},{8,32},{9,36},{10,... | collective-permute-start | bytes 442376 | tf_op jit(solution)/shard_map/ppermute | solution.py:394
  196.9 12.0 %collective-permute-done.14 = f32[2,24,768]{2,1,0:T(8,128)S(1)} collective-permute-done((f32[2,24,768]{2,1,0:T(8,128)S(1)}, f32[2,24,768]{2,1,0:T(8,128)S(1)}, u32[]{:S(2)}, u32[]{:S(2)}) %collective-permute-start.14) | collective-permute-done | bytes 147488 | tf_op jit(solution)/shard_map/ppermute | solution.py:394
  (69 shorter events, 29.3 us)
Async XLA Ops:
  0.6 93.1 %copy-start = (bf16[256,768]{1,0:T(8,128)(2,1)S(1)}, bf16[256,768]{1,0:T(8,128)(2,1)}, u32[]{:S(2)}) copy-start(bf16[256,768]{1,0:T(8,128)(2,1)} %param.11) | copy-start | bytes 1179652
  5.6 22.5 %copy-start.1 = (bf16[2,256,1024]{2,1,0:T(8,128)(2,1)}, bf16[2,256,1024]{2,1,0:T(8,128)(2,1)S(1)}, u32[]{:S(2)}) copy-start(bf16[2,256,1024]{2,1,0:T(8,128)(2,1)S(1)} %adjacency.1.own_ref) | copy-start | bytes 3145732
  9.1 11.4 %copy-start.8 = (s32[2,2,8]{2,1,0:T(2,128)S(1)}, s32[2,2,8]{2,1,0:T(2,128)}, u32[]{:S(2)}) copy-start(s32[2,2,8]{2,1,0:T(2,128)} %param.14) | copy-start | bytes 388
  9.1 69.9 %all-to-all-start = ((bf16[32,192,128]{2,1,0:T(8,128)(2,1)}), bf16[32,192,128]{2,1,0:T(8,128)(2,1)}, u32[]{:S(2)}, u32[]{:S(2)}) async-start(bf16[32,192,128]{2,1,0:T(8,128)(2,1)} %outgoing.1), calls=%async_computation | async-start | bytes 3145728 | tf_op jit(solution)/shard_map/all_to_all | solution.py:315
  22.0 10.5 %collective-permute-start = (bf16[1,208,768]{2,1,0:T(8,128)(2,1)S(1)}, bf16[1,208,768]{2,1,0:T(8,128)(2,1)S(1)}, u32[]{:S(2)}, u32[]{:S(2)}) collective-permute-start(bf16[1,208,768]{2,1,0:T(8,128)(2,1)S(1)} %get-tuple-element.29), channel_id=1, source_target_pairs={{0,32},{32,64},{64,96},{96,0},{1,33},{33,65},{65,97},{97,1},{2,34}... | collective-permute-start | bytes 958472 | tf_op jit(solution)/shard_map/ppermute | solution.py:320
  22.3 11.9 %collective-permute-start.1 = (bf16[1,208,768]{2,1,0:T(8,128)(2,1)S(1)}, bf16[1,208,768]{2,1,0:T(8,128)(2,1)S(1)}, u32[]{:S(2)}, u32[]{:S(2)}) collective-permute-start(bf16[1,208,768]{2,1,0:T(8,128)(2,1)S(1)} %get-tuple-element.30), channel_id=1, source_target_pairs={{0,64},{32,96},{64,0},{96,32},{1,65},{33,97},{65,1},{97,33},{2,66}... | collective-permute-start | bytes 958472 | tf_op jit(solution)/shard_map/ppermute | solution.py:320
  24.9 15.3 %collective-permute-start.2 = (bf16[1,208,768]{2,1,0:T(8,128)(2,1)S(1)}, bf16[1,208,768]{2,1,0:T(8,128)(2,1)S(1)}, u32[]{:S(2)}, u32[]{:S(2)}) collective-permute-start(bf16[1,208,768]{2,1,0:T(8,128)(2,1)S(1)} %get-tuple-element.31), channel_id=1, source_target_pairs={{0,96},{32,0},{64,32},{96,64},{1,97},{33,1},{65,33},{97,65},{2,98}... | collective-permute-start | bytes 958472 | tf_op jit(solution)/shard_map/ppermute | solution.py:320
  24.9 36.2 %collective-permute-start.3 = (bf16[2,256,1024]{2,1,0:T(8,128)(2,1)S(1)}, bf16[2,256,1024]{2,1,0:T(8,128)(2,1)}, u32[]{:S(2)}, u32[]{:S(2)}) collective-permute-start(bf16[2,256,1024]{2,1,0:T(8,128)(2,1)S(1)} %adjacency.1.own_ref), channel_id=1, source_target_pairs={{0,32},{32,64},{64,96},{96,0},{1,33},{33,65},{65,97},{97,1},{2,34}... | collective-permute-start | bytes 3145736 | tf_op jit(solution)/shard_map/ppermute | solution.py:307
  28.1 35.6 %collective-permute-start.4 = (bf16[2,256,1024]{2,1,0:T(8,128)(2,1)S(1)}, bf16[2,256,1024]{2,1,0:T(8,128)(2,1)}, u32[]{:S(2)}, u32[]{:S(2)}) collective-permute-start(bf16[2,256,1024]{2,1,0:T(8,128)(2,1)S(1)} %adjacency.1.own_ref), channel_id=1, source_target_pairs={{0,96},{32,0},{64,32},{96,64},{1,97},{33,1},{65,33},{97,65},{2,98}... | collective-permute-start | bytes 3145736 | tf_op jit(solution)/shard_map/ppermute | solution.py:307
  34.2 6.0 %copy-start.7 = (bf16[1,208,768]{2,1,0:T(8,128)(2,1)}, bf16[1,208,768]{2,1,0:T(8,128)(2,1)S(1)}, u32[]{:S(2)}) copy-start(bf16[1,208,768]{2,1,0:T(8,128)(2,1)S(1)} %collective-permute-done.1) | copy-start | bytes 958468
  40.4 26.4 %collective-permute-start.7 = (bf16[4,192,768]{2,1,0:T(8,128)(2,1)S(1)}, bf16[4,192,768]{2,1,0:T(8,128)(2,1)}, u32[]{:S(2)}, u32[]{:S(2)}) collective-permute-start(bf16[4,192,768]{2,1,0:T(8,128)(2,1)S(1)} %pad_maximum_fusion.w_mine_ref), channel_id=1, source_target_pairs={{0,1},{1,0},{2,3},{3,2},{4,5},{5,4},{6,7},{7,6},{8,9},{9,8},{10,11... | collective-permute-start | bytes 3538952 | tf_op jit(solution)/shard_map/ppermute | solution.py:311
  62.2 13.2 %collective-permute-start.5 = (bf16[1,256,1024]{2,1,0:T(8,128)(2,1)S(1)}, bf16[1,256,1024]{2,1,0:T(8,128)(2,1)S(1)}, u32[]{:S(2)}, u32[]{:S(2)}) collective-permute-start(bf16[1,256,1024]{2,1,0:T(8,128)(2,1)S(1)} %slice.35), channel_id=1, source_target_pairs={{0,32},{32,64},{64,96},{96,0},{1,33},{33,65},{65,97},{97,1},{2,34}... | collective-permute-start | bytes 1572872 | tf_op jit(solution)/shard_map/ppermute | solution.py:307
  64.8 14.2 %collective-permute-start.6 = (bf16[1,256,1024]{2,1,0:T(8,128)(2,1)S(1)}, bf16[1,256,1024]{2,1,0:T(8,128)(2,1)S(1)}, u32[]{:S(2)}, u32[]{:S(2)}) collective-permute-start(bf16[1,256,1024]{2,1,0:T(8,128)(2,1)S(1)} %slice.36), channel_id=1, source_target_pairs={{0,96},{32,0},{64,32},{96,64},{1,97},{33,1},{65,33},{97,65},{2,98}... | collective-permute-start | bytes 1572872 | tf_op jit(solution)/shard_map/ppermute | solution.py:307
  75.4 3.6 %copy-start.5 = (bf16[1,256,1024]{2,1,0:T(8,128)(2,1)}, bf16[1,256,1024]{2,1,0:T(8,128)(2,1)S(1)}, u32[]{:S(2)}) copy-start(bf16[1,256,1024]{2,1,0:T(8,128)(2,1)S(1)} %collective-permute-done.5.far0_ref) | copy-start | bytes 1572868
  89.2 9.9 %all-to-all-start.1 = ((bf16[8,96,256]{2,1,0:T(8,128)(2,1)}), bf16[8,96,256]{2,1,0:T(8,128)(2,1)S(1)}, u32[]{:S(2)}, u32[]{:S(2)}) async-start(bf16[8,96,256]{2,1,0:T(8,128)(2,1)} %bitcast.8), calls=%async_computation.1 | async-start | bytes 786432 | tf_op jit(solution)/shard_map/all_to_all | solution.py:315
  117.8 66.9 %all-to-all-start.3 = ((bf16[32,192,128]{2,1,0:T(8,128)(2,1)}), bf16[32,192,128]{2,1,0:T(8,128)(2,1)S(1)}, u32[]{:S(2)}, u32[]{:S(2)}) async-start(bf16[32,192,128]{2,1,0:T(8,128)(2,1)} %copy-done.2), calls=%async_computation.3 | async-start | bytes 3145728 | tf_op jit(solution)/shard_map/all_to_all | solution.py:315
  128.3 1.8 collective-permute-start.9
  128.5 2.3 %collective-permute-start.8 = (bf16[8,96,256]{2,1,0:T(8,128)(2,1)}, bf16[8,96,256]{2,1,0:T(8,128)(2,1)S(1)}, u32[]{:S(2)}, u32[]{:S(2)}) collective-permute-start(bf16[8,96,256]{2,1,0:T(8,128)(2,1)} %copy-done.4), channel_id=1, source_target_pairs={{0,1},{1,0},{2,3},{3,2},{4,5},{5,4},{6,7},{7,6},{8,9},{9,8},{10,11... | collective-permute-start | bytes 1179656 | tf_op jit(solution)/shard_map/ppermute | solution.py:311
  134.6 28.0 %collective-permute-start.10 = (bf16[8,48,768]{2,1,0:T(8,128)(2,1)}, bf16[8,48,768]{2,1,0:T(8,128)(2,1)S(1)}, u32[]{:S(2)}, u32[]{:S(2)}) collective-permute-start(bf16[8,48,768]{2,1,0:T(8,128)(2,1)} %get-tuple-element.22), channel_id=1, source_target_pairs={{0,16},{16,0},{1,17},{17,1},{2,18},{18,2},{3,19},{19,3},{4,20},{20... | collective-permute-start | bytes 1769480 | tf_op jit(solution)/shard_map/ppermute | solution.py:311
  163.9 9.0 %collective-permute-start.11 = (bf16[4,48,768]{2,1,0:T(8,128)(2,1)S(1)}, bf16[4,48,768]{2,1,0:T(8,128)(2,1)S(1)}, u32[]{:S(2)}, u32[]{:S(2)}) collective-permute-start(bf16[4,48,768]{2,1,0:T(8,128)(2,1)S(1)} %get-tuple-element.27), channel_id=1, source_target_pairs={{0,2},{2,0},{4,6},{6,4},{8,10},{10,8},{12,14},{14,12},{1,3},{3,1},... | collective-permute-start | bytes 884744 | tf_op jit(solution)/shard_map/ppermute | solution.py:311
  172.9 7.8 %collective-permute-start.12 = (bf16[2,48,768]{2,1,0:T(8,128)(2,1)S(1)}, bf16[2,48,768]{2,1,0:T(8,128)(2,1)S(1)}, u32[]{:S(2)}, u32[]{:S(2)}) collective-permute-start(bf16[2,48,768]{2,1,0:T(8,128)(2,1)S(1)} %fusion.6), channel_id=1, source_target_pairs={{0,4},{2,6},{4,0},{6,2},{8,12},{10,14},{12,8},{14,10},{1,5},{3,7},... | collective-permute-start | bytes 442376 | tf_op jit(solution)/shard_map/ppermute | solution.py:311
  180.8 11.8 %collective-permute-start.13 = (bf16[1,48,768]{2,1,0:T(8,128)(2,1)S(1)}, bf16[1,48,768]{2,1,0:T(8,128)(2,1)S(1)}, u32[]{:S(2)}, u32[]{:S(2)}) collective-permute-start(bf16[1,48,768]{2,1,0:T(8,128)(2,1)S(1)} %fusion.10), channel_id=1, source_target_pairs={{0,8},{2,10},{4,12},{6,14},{8,0},{10,2},{12,4},{14,6},{1,9},{3,11}... | collective-permute-start | bytes 221192 | tf_op jit(solution)/shard_map/ppermute | solution.py:311
  187.2 21.7 %all-to-all-start.4 = ((f32[8,2,16,192]{3,2,1,0:T(8,128)}), f32[8,2,16,192]{3,2,1,0:T(8,128)S(1)}, u32[]{:S(2)}, u32[]{:S(2)}) async-start(f32[8,2,16,192]{3,2,1,0:T(8,128)} %owned.1), calls=%async_computation.4 | async-start | bytes 524288 | tf_op jit(solution)/shard_map/all_to_all | solution.py:315
  192.7 16.2 %collective-permute-start.14 = (f32[2,24,768]{2,1,0:T(8,128)S(1)}, f32[2,24,768]{2,1,0:T(8,128)S(1)}, u32[]{:S(2)}, u32[]{:S(2)}) collective-permute-start(f32[2,24,768]{2,1,0:T(8,128)S(1)} %bitcast.75), channel_id=1, source_target_pairs={{0,0},{1,4},{2,1},{3,5},{4,2},{5,6},{6,3},{7,7},{8,32},{9,36},{10,... | collective-permute-start | bytes 442376 | tf_op jit(solution)/shard_map/ppermute | solution.py:394
  (4 other events, 3.8 us)

commit v7 on v6

--- a/solution.py
+++ b/solution.py
@@ -133,17 +133,18 @@
                 wide = jnp.concatenate([fetched_ref[slot_ref[base + s]] for s in range(8)], axis=1)
                 part = adj_buf[2 * n + p, q * BLK : (q + 1) * BLK, :]
                 both_ref[p, :, q * BLK : (q + 1) * BLK] = dot(wide, part, 1, 1).astype(BF16)
-        pair = pl.ds(2 * ((y - k) & 3), 2)
+        j = (y - k) & 3
+        side, pair = (j >> 1) ^ place_ref[4], pl.ds(2 * (j & 1), 2)
 
         @pl.when(core == 0)
         def _():
-            keep_ref[pair] = both_ref[:, :96]
-            send_ref[pair] = both_ref[:, 96:]
+            keep_ref[side, pair] = both_ref[:, :96]
+            send_ref[side, pair] = both_ref[:, 96:]
 
         @pl.when(core == 1)
         def _():
-            keep_ref[pair] = both_ref[:, 96:]
-            send_ref[pair] = both_ref[:, :96]
+            keep_ref[side, pair] = both_ref[:, 96:]
+            send_ref[side, pair] = both_ref[:, :96]
 
         term = dot(w_mine_ref[k], both_ref[core], 0, 0) + dot(w_theirs_ref[k], both_ref[1 - core], 0, 0)
         if n == 0:
@@ -157,7 +158,7 @@
 def forward_of(place, slots, adjacency, fetched, w_mine, w_theirs):
     _, rows, wide = adjacency[0].shape
     width = w_mine.shape[2]
-    half = jax.ShapeDtypeStruct((8, 96, rows), BF16)
+    half = jax.ShapeDtypeStruct((2, 4, 96, rows), BF16)
     return pl.pallas_call(
         forward_kernel,
         in_specs=[smem(), smem()] + [hbm()] * 5 + [vmem()] * 3,
@@ -232,36 +233,51 @@
     )(place, slots, *adjacency, grads, w_mine, w_theirs)
 
 
-def weight_kernel(place_ref, mine_ref, theirs_ref, grad_ref, their_grad_ref, keep_ref, send_ref):
-    xh = place_ref[4]
-    grads = jnp.concatenate([grad_ref[...], their_grad_ref[...]], axis=1)
-    for target, x in ((send_ref, 1 - xh), (keep_ref, xh)):
-        for half in range(2):
-            terms = []
-            for p in range(2):
-                r = 4 * x + 2 * half + p
-                wide = jnp.concatenate([mine_ref[r], theirs_ref[r]], axis=1)
-                terms.append(dot(wide, grads, 1, 1))
+def weight_kernel(
+    place_ref, own_ref, core_ref, far_ref, grad_ref, core_grad_ref, far_grad_ref, far_core_grad_ref, keep_ref, send_ref
+):
+    bit = place_ref[5]
+    grads = jnp.concatenate(
+        [grad_ref[...], core_grad_ref[...], far_grad_ref[...], far_core_grad_ref[...]], axis=1
+    )
+    for half in range(2):
+        terms = []
+        for p in range(2):
+            r = 2 * half + p
+            wide = jnp.concatenate([own_ref[0, r], core_ref[0, r], far_ref[0, r], far_ref[1, r]], axis=1)
+            terms.append(dot(wide, grads, 1, 1))
+
+        def piece(m):
+            rows = slice(m * 24, (m + 1) * 24)
+            return jnp.concatenate([terms[0][rows], terms[1][rows]], axis=0)
+
+        def cut(even_ref, odd_ref):
             for m in range(4):
-                rows = slice(m * 24, (m + 1) * 24)
-                piece = jnp.concatenate([terms[0][rows], terms[1][rows]], axis=0)
-                target[4 * half + m] = piece.astype(target.dtype)
-
-
-def weight_terms_of(place, mine, theirs, grads, their_grads):
-    rels = mine.shape[0]
-    width = grads.shape[0]
+                target = odd_ref if m % 2 else even_ref
+                target[2 * half + m // 2] = piece(m).astype(target.dtype)
+
+        @pl.when(bit == 0)
+        def _():
+            cut(keep_ref, send_ref)
+
+        @pl.when(bit == 1)
+        def _():
+            cut(send_ref, keep_ref)
+
+
+def weight_terms_of(place, *operands):
+    width = operands[-1].shape[0]
     return pl.pallas_call(
         weight_kernel,
-        in_specs=[smem()] + [vmem()] * 4,
+        in_specs=[smem()] + [vmem()] * 7,
         out_specs=[vmem(), vmem()],
         out_shape=[
-            jax.ShapeDtypeStruct((rels, 48, width), F32),
-            jax.ShapeDtypeStruct((rels, 48, width), BF16),
+            jax.ShapeDtypeStruct((4, 48, width), F32),
+            jax.ShapeDtypeStruct((4, 48, width), BF16),
         ],
         compiler_params=params(),
         name="weight_terms",
-    )(place, mine, theirs, grads, their_grads)
+    )(place, *operands)
 
 
 def owned_kernel(place_ref, table_ref, arrived_ref, out_ref):
@@ -347,12 +363,11 @@
     group = lax.axis_index(REL)
     xh, z = lax.axis_index("xh"), lax.axis_index("z")
     xh, z = lax.axis_index("xh"), lax.axis_index("z")
-    place = in_hbm(jnp.stack([owner, 192 * y, core, y, xh]).astype(jnp.int32))
+    place = in_hbm(jnp.stack([owner, 192 * y, core, y, xh, z & 1]).astype(jnp.int32))
 
     own = adjacency_of(in_hbm(tile_values), in_hbm(tile_count))
     back, fore = step(own, 1), step(own, -1)
     far0, far1 = step(back[:1], 1), step(fore[1:], -1)
-    adjacency = [in_hbm(a) for a in (own, back, fore, far0, far1)]
     features, weights, _ = lax.optimization_barrier((features, weights, own))
     source_blocks = in_hbm(source_blocks)
     outgoing = outgoing_of(in_hbm(features), source_blocks, place)
@@ -361,23 +376,32 @@
     own_slots = jnp.pad(tile_slot.reshape(1, 1, -1), ((0, 0), (0, 15), (0, width - 32))).astype(BF16)
     pieces = []
     for k in range(4):
-        cut = lax.dynamic_slice(weights, (core, ((y + k) & 3) * 192, 0), (1, 192, width))
+        cut = lax.dynamic_slice(weights, (core, ((y + k) & 3) * 192 + 96 * xh, 0), (1, 96, width))
         pieces.append(jnp.concatenate([cut, own_slots], axis=1) if k else cut)
     came = around(pieces[1:], "y", 4)
-    slots = jnp.concatenate([tile_slot.reshape(-1)] + [c[0, 192, :32].astype(jnp.int32) for c in came])
-    slots = in_hbm(slots)
-    w_mine = jnp.concatenate([pieces[0]] + [c[:, :192] for c in came], axis=0)
+    slots = jnp.concatenate([tile_slot.reshape(-1)] + [c[0, 96, :32].astype(jnp.int32) for c in came])
+    w_part = jnp.concatenate([pieces[0]] + [c[:, :96] for c in came], axis=0)
+    w_other = swap(w_part, "xh")
+    w_part, w_other, far0, far1 = lax.optimization_barrier((w_part, w_other, far0, far1))
+    w_mine = jnp.concatenate(
+        [jnp.where(xh == 0, w_part, w_other), jnp.where(xh == 0, w_other, w_part)], axis=1
+    )
     w_mine, w_theirs = resident(w_mine), resident(swap(w_mine, "core"))
-
-    messages, for_partner, part = forward_of(place, slots, adjacency, fetched, w_mine, w_theirs)
-    from_partner = swap(for_partner, "core")
+    adjacency = [in_hbm(a) for a in (own, back, fore, far0, far1)]
+
     share = width // groups
-    arrived = resident(exchange(part.reshape(groups, share, -1), REL))
     bias_share = lax.dynamic_slice_in_dim(bias, group * share, share)[:, None]
     cotangent_share = lax.dynamic_slice_in_dim(cotangent, group * share, share, 1).T
+    slots, bias_share, cotangent_share = lax.optimization_barrier((slots, bias_share, cotangent_share))
+    slots, bias_share, cotangent_share = in_hbm(slots), in_hbm(bias_share), in_hbm(cotangent_share)
+    messages, for_core, part = forward_of(place, slots, adjacency, fetched, w_mine, w_theirs)
+    of_core = swap(for_core, "core")
+    arrived, of_core = lax.optimization_barrier((exchange(part.reshape(groups, share, -1), REL), of_core))
+    arrived = resident(arrived)
     activated, grad_copies = activation_of(arrived, bias_share, cotangent_share)
     output = activated.T
-    grads = exchange(grad_copies, REL).reshape(width, -1)
+    of_far = swap(jnp.stack([messages[1], of_core[1]]), "xh")
+    grads, of_far = lax.optimization_barrier((exchange(grad_copies, REL).reshape(width, -1), of_far))
 
     partial = backward_of(place, slots, adjacency, resident(grads), w_mine, w_theirs, owners)
     returned = resident(exchange(in_hbm(partial), TGT))
@@ -385,9 +409,10 @@
     columns = exchange(cut, REL).reshape(2, 4, 2, BLK // groups, 192).sum(axis=0)
     grad_features = columns.transpose(1, 2, 0, 3).reshape(2, BLK // groups, width)
 
-    their_grads, _ = lax.optimization_barrier((swap(grads, "core"), partial))
-    keep, send = weight_terms_of(place, messages, from_partner, grads, their_grads)
-    keep, send = halve(z & 1, keep, swap(send, "xh"), 1)
+    far_grads = swap(grads, "xh")
+    keep, send = weight_terms_of(
+        place, messages, of_core, of_far, grads, swap(grads, "core"), far_grads, swap(far_grads, "core")
+    )
     keep, send = halve((z >> 1) & 1, keep, swap(send, "z", 8, 1), 1)
     keep, send = halve(z >> 2, keep, swap(send, "z", 8, 2), 1)
     piece = keep + swap(send, "z", 8, 4).astype(F32)

time: 214 us -> 209 us (0.977)
  waiting for transfers between devices: 102 us -> 86.6 us
  starting transfers between devices: 54.5 us -> 58.7 us
  other arithmetic: 3 us -> 7.02 us
    ppermute x4, waiting for transfers between devices: 32.8 us -> 0.01 us  [step(): return lax.ppermute(value, 'y', [(i, (i + by) % 4) for i in range(4)])]
    ppermute x7 -> x10, waiting for transfers between devices: 41.2 us -> 58.2 us  [swap(): return lax.ppermute(value, axis, [(i, i ^ flip) for i in range(size)])]
    ppermute x7 -> x10, starting transfers between devices: 10.2 us -> 14.8 us  [swap(): return lax.ppermute(value, axis, [(i, i ^ flip) for i in range(size)])]
    ppermute x1, starting transfers between devices: 4.2 us -> 6.39 us  [per_device(): lax.ppermute(piece.reshape(2, 24, width), ('y', *TGT), to_owner())]
    unnamed x20 -> x22, local copies, waits for them, and re-layouts: 4.53 us -> 2.81 us
  transfers between devices with their start and end apart: 19 -> 22, of which waited for: 13 -> 10; matrix products, arithmetic and copies ran while one was open for 4% -> 5% of each run, Pallas kernels for 2% -> 5%
where the time goes in v7:
time: 209 us; the launch traced here: 206 us
  waiting for transfers between devices  86.6 us (41%)
  starting transfers between devices  58.7 us (28%)
  Pallas kernels  29.7 us (14%)
  blocking collectives  13 us (6%)
  local copies, waits for them, and re-layouts  9.76 us (5%)
  other arithmetic  7.02 us (3%)
    ppermute x10, waiting for transfers between devices, swap(): return lax.ppermute(value, axis, [(i, i ^ flip) for i in range(size)])  58.2 us
    all_to_all x4, starting transfers between devices, exchange(): return lax.all_to_all(value, axis, 0, 0, tiled=True)  30.5 us
    ppermute x10, starting transfers between devices, swap(): return lax.ppermute(value, axis, [(i, i ^ flip) for i in range(size)])  14.8 us
    all_to_all x1, blocking collectives, exchange(): return lax.all_to_all(value, axis, 0, 0, tiled=True)  13 us
    ppermute x3, waiting for transfers between devices, around(): lax.ppermute(v, axis, [(i, (i + k) % size) for i in range(size)])  12.7 us
    ppermute x1, waiting for transfers between devices, per_device(): lax.ppermute(piece.reshape(2, 24, width), ('y', *TGT), to_owner())  10 us
    pallas_call x1, Pallas kernels, forward_of(): pl.pallas_call(forward_kernel, in_specs=[smem(), smem()] + [hbm()] * 5 +...  7.7 us
    ppermute x1, starting transfers between devices, per_device(): lax.ppermute(piece.reshape(2, 24, width), ('y', *TGT), to_owner())  6.39 us
  transfers between devices with their start and end apart: 22, of which 10 were waited for; matrix products, arithmetic and copies ran while one was open for 5% of the time, Pallas kernels for 5%

profile of v7, /device:TPU:56, one launch (start us, length us, event | category | flops | bytes accessed | tf_op | source)
XLA Modules:
  0.0 205.7 jit_solution(1320865472179052630)
XLA Ops:
  0.6 5.0 %adjacency.1.own_ref = bf16[2,256,1024]{2,1,0:T(8,128)(2,1)S(1)} custom-call(s32[2,2]{1,0:T(2,128)} %count_ref.1, s32[2,256,8,128]{3,2,1,0:T(8,128)} %values_ref.1), custom_call_target="tpu_custom_call" | custom-call | tf_op jit(solution)/shard_map/adjacency/pallas_call | solution.py:61
  8.3 2.6 %outgoing.1 = bf16[32,192,128]{2,1,0:T(8,128)(2,1)} custom-call(s32[6]{0:T(128)} %stack.30.place_ref, s32[32,32]{1,0:T(8,128)} %table_ref.3, bf16[256,768]{1,0:T(8,128)(2,1)} %features_ref), custom_call_target="tpu_custom_call" | custom-call | tf_op jit(solution)/shard_map/outgoing/pallas_call | solution.py:85
  10.9 11.4 %all-to-all-start = ((bf16[32,192,128]{2,1,0:T(8,128)(2,1)}), bf16[32,192,128]{2,1,0:T(8,128)(2,1)}, u32[]{:S(2)}, u32[]{:S(2)}) async-start(bf16[32,192,128]{2,1,0:T(8,128)(2,1)} %outgoing.1), calls=%async_computation | async-start | bytes 3145728 | tf_op jit(solution)/shard_map/all_to_all | solution.py:331
  26.5 8.9 %collective-permute-done = bf16[1,112,768]{2,1,0:T(8,128)(2,1)S(1)} collective-permute-done((bf16[1,112,768]{2,1,0:T(8,128)(2,1)S(1)}, bf16[1,112,768]{2,1,0:T(8,128)(2,1)S(1)}, u32[]{:S(2)}, u32[]{:S(2)}) %collective-permute-start) | collective-permute-done | bytes 172064 | tf_op jit(solution)/shard_map/ppermute | solution.py:336
  36.8 2.5 %collective-permute-done.2 = bf16[1,112,768]{2,1,0:T(8,128)(2,1)S(1)} collective-permute-done((bf16[1,112,768]{2,1,0:T(8,128)(2,1)S(1)}, bf16[1,112,768]{2,1,0:T(8,128)(2,1)S(1)}, u32[]{:S(2)}, u32[]{:S(2)}) %collective-permute-start.2) | collective-permute-done | bytes 172064 | tf_op jit(solution)/shard_map/ppermute | solution.py:336
  40.9 3.0 %collective-permute-start.5 = (bf16[4,96,768]{2,1,0:T(8,128)(2,1)}, bf16[4,96,768]{2,1,0:T(8,128)(2,1)}, u32[]{:S(2)}, u32[]{:S(2)}) collective-permute-start(bf16[4,96,768]{2,1,0:T(8,128)(2,1)} %pad_maximum_fusion.1), channel_id=1, source_target_pairs={{0,16},{16,0},{1,17},{17,1},{2,18},{18,2},{3,19},{19,3},{4,20},{20... | collective-permute-start | bytes 1769480 | tf_op jit(solution)/shard_map/ppermute | solution.py:327
  47.0 17.2 %collective-permute-done.5 = bf16[4,96,768]{2,1,0:T(8,128)(2,1)} collective-permute-done((bf16[4,96,768]{2,1,0:T(8,128)(2,1)}, bf16[4,96,768]{2,1,0:T(8,128)(2,1)}, u32[]{:S(2)}, u32[]{:S(2)}) %collective-permute-start.5) | collective-permute-done | bytes 589856 | tf_op jit(solution)/shard_map/ppermute | solution.py:327
  70.3 7.7 %forward.1 = (bf16[2,4,96,256]{3,2,1,0:T(8,128)(2,1)S(1)}, bf16[2,4,96,256]{3,2,1,0:T(8,128)(2,1)}, bf16[768,256]{1,0:T(8,128)(2,1)S(1)}) custom-call(s32[6]{0:T(128)} %stack.30.place_ref, s32[128]{0:T(128)} %pad_add_fusion.slot_ref, bf16[2,256,1024]{2,1,0:T(8,128)(2,1)} %copy-done.1, bf16[2,256,1024]{2,1,0:T(8,128)(2,1)} %copy-done.3, ...), custom_call_target="tpu_custom_call" | custom-call | tf_op jit(solution)/shard_map/forward/pallas_call | solution.py:162
  79.3 5.2 %all-to-all-start.1 = ((bf16[8,96,256]{2,1,0:T(8,128)(2,1)}), bf16[8,96,256]{2,1,0:T(8,128)(2,1)S(1)}, u32[]{:S(2)}, u32[]{:S(2)}) async-start(bf16[8,96,256]{2,1,0:T(8,128)(2,1)} %bitcast.57), calls=%async_computation.1 | async-start | bytes 786432 | tf_op jit(solution)/shard_map/all_to_all | solution.py:331
  85.2 5.6 %all-to-all-done.1.arrived_ref = bf16[8,96,256]{2,1,0:T(8,128)(2,1)S(1)} async-done(((bf16[8,96,256]{2,1,0:T(8,128)(2,1)}), bf16[8,96,256]{2,1,0:T(8,128)(2,1)S(1)}, u32[]{:S(2)}, u32[]{:S(2)}) %all-to-all-start.1) | async-done | bytes 393248 | tf_op jit(solution)/shard_map/all_to_all | solution.py:331
  98.0 13.0 %all_to_all.25 = bf16[8,96,256]{2,1,0:T(8,128)(2,1)S(1)} all-to-all(bf16[8,96,256]{2,1,0:T(8,128)(2,1)S(1)} %get-tuple-element.38), channel_id=1, replica_groups=mesh['xl'=2,'y'=4,'xh'=2,'z'=8,'core'=2] {'xl','y'}, dimensions={0} | all-to-all | bytes 786432 | tf_op jit(solution)/shard_map/all_to_all | solution.py:331
  111.0 6.3 %backward.1 = bf16[32,192,128]{2,1,0:T(8,128)(2,1)} custom-call(s32[6]{0:T(128)} %stack.30.place_ref, s32[128]{0:T(128)} %pad_add_fusion.slot_ref, bf16[2,256,1024]{2,1,0:T(8,128)(2,1)} %copy-done.1, bf16[2,256,1024]{2,1,0:T(8,128)(2,1)} %copy-done.3, bf16[2,256,1024]{2,1,0:T(8,128)(2,1)} %copy-done.4, ...), custom_call_target="tpu_custom_call" | custom-call | tf_op jit(solution)/shard_map/backward/pallas_call | solution.py:224
  117.3 9.2 %all-to-all-start.3 = ((bf16[32,192,128]{2,1,0:T(8,128)(2,1)}), bf16[32,192,128]{2,1,0:T(8,128)(2,1)S(1)}, u32[]{:S(2)}, u32[]{:S(2)}) async-start(bf16[32,192,128]{2,1,0:T(8,128)(2,1)} %backward.1), calls=%async_computation.3 | async-start | bytes 3145728 | tf_op jit(solution)/shard_map/all_to_all | solution.py:331
  126.6 3.1 %collective-permute-start.12 = (bf16[768,256]{1,0:T(8,128)(2,1)S(1)}, bf16[768,256]{1,0:T(8,128)(2,1)S(1)}, u32[]{:S(2)}, u32[]{:S(2)}) collective-permute-start(bf16[768,256]{1,0:T(8,128)(2,1)S(1)} %bitcast.53), channel_id=1, source_target_pairs={{0,16},{16,0},{1,17},{17,1},{2,18},{18,2},{3,19},{19,3},{4,20},{20... | collective-permute-start | bytes 1179656 | tf_op jit(solution)/shard_map/ppermute | solution.py:327
  129.7 18.9 %collective-permute-done.12.far_grad_ref = bf16[768,256]{1,0:T(8,128)(2,1)S(1)} collective-permute-done((bf16[768,256]{1,0:T(8,128)(2,1)S(1)}, bf16[768,256]{1,0:T(8,128)(2,1)S(1)}, u32[]{:S(2)}, u32[]{:S(2)}) %collective-permute-start.12) | collective-permute-done | bytes 393248 | tf_op jit(solution)/shard_map/ppermute | solution.py:327
  150.3 4.0 %weight_terms.1 = (f32[4,48,768]{2,1,0:T(8,128)S(1)}, bf16[4,48,768]{2,1,0:T(8,128)(2,1)}) custom-call(s32[6]{0:T(128)} %stack.30.place_ref, bf16[2,4,96,256]{3,2,1,0:T(8,128)(2,1)S(1)} %get-tuple-element.36.own_ref, bf16[2,4,96,256]{3,2,1,0:T(8,128)(2,1)} %collective-permute-done.9.core_ref, bf16[2,4,96,256]{3,2,1,0:T(8,128)(2,1)} %collective-permute-done.10.far_ref, ...), custom_call_target="tpu_custom_call" | custom-call | tf_op jit(solution)/shard_map/weight_terms/pallas_call | solution.py:270
  154.3 13.8 %collective-permute-done.14 = bf16[4,48,768]{2,1,0:T(8,128)(2,1)S(1)} collective-permute-done((bf16[4,48,768]{2,1,0:T(8,128)(2,1)}, bf16[4,48,768]{2,1,0:T(8,128)(2,1)S(1)}, u32[]{:S(2)}, u32[]{:S(2)}) %collective-permute-start.14) | collective-permute-done | bytes 294944 | tf_op jit(solution)/shard_map/ppermute | solution.py:327
  168.2 2.3 %collective-permute-start.15 = (bf16[2,48,768]{2,1,0:T(8,128)(2,1)S(1)}, bf16[2,48,768]{2,1,0:T(8,128)(2,1)S(1)}, u32[]{:S(2)}, u32[]{:S(2)}) collective-permute-start(bf16[2,48,768]{2,1,0:T(8,128)(2,1)S(1)} %get-tuple-element.49), channel_id=1, source_target_pairs={{0,4},{2,6},{4,0},{6,2},{8,12},{10,14},{12,8},{14,10},{1,5},{3,7},... | collective-permute-start | bytes 442376 | tf_op jit(solution)/shard_map/ppermute | solution.py:327
  170.6 6.5 %collective-permute-done.15 = bf16[2,48,768]{2,1,0:T(8,128)(2,1)S(1)} collective-permute-done((bf16[2,48,768]{2,1,0:T(8,128)(2,1)S(1)}, bf16[2,48,768]{2,1,0:T(8,128)(2,1)S(1)}, u32[]{:S(2)}, u32[]{:S(2)}) %collective-permute-start.15) | collective-permute-done | bytes 147488 | tf_op jit(solution)/shard_map/ppermute | solution.py:327
  177.1 3.5 %collective-permute-start.16 = (bf16[1,48,768]{2,1,0:T(8,128)(2,1)S(1)}, bf16[1,48,768]{2,1,0:T(8,128)(2,1)S(1)}, u32[]{:S(2)}, u32[]{:S(2)}) collective-permute-start(bf16[1,48,768]{2,1,0:T(8,128)(2,1)S(1)} %fusion.8), channel_id=1, source_target_pairs={{0,8},{2,10},{4,12},{6,14},{8,0},{10,2},{12,4},{14,6},{1,9},{3,11}... | collective-permute-start | bytes 221192 | tf_op jit(solution)/shard_map/ppermute | solution.py:327
  180.6 2.5 %owned.1 = f32[8,2,16,192]{3,2,1,0:T(8,128)} custom-call(s32[6]{0:T(128)} %stack.30.place_ref, s32[32,32]{1,0:T(8,128)} %table_ref.3, bf16[32,192,128]{2,1,0:T(8,128)(2,1)S(1)} %all-to-all-done.3.arrived_ref), custom_call_target="tpu_custom_call" | custom-call | tf_op jit(solution)/shard_map/owned/pallas_call | solution.py:299
  183.1 4.7 %all-to-all-start.4 = ((f32[8,2,16,192]{3,2,1,0:T(8,128)}), f32[8,2,16,192]{3,2,1,0:T(8,128)S(1)}, u32[]{:S(2)}, u32[]{:S(2)}) async-start(f32[8,2,16,192]{3,2,1,0:T(8,128)} %owned.1), calls=%async_computation.4 | async-start | bytes 524288 | tf_op jit(solution)/shard_map/all_to_all | solution.py:331
  187.7 6.4 %collective-permute-start.17 = (f32[2,24,768]{2,1,0:T(8,128)S(1)}, f32[2,24,768]{2,1,0:T(8,128)S(1)}, u32[]{:S(2)}, u32[]{:S(2)}) collective-permute-start(f32[2,24,768]{2,1,0:T(8,128)S(1)} %bitcast.62), channel_id=1, source_target_pairs={{0,0},{1,4},{2,1},{3,5},{4,2},{5,6},{6,3},{7,7},{8,32},{9,36},{10,... | collective-permute-start | bytes 442376 | tf_op jit(solution)/shard_map/ppermute | solution.py:419
  194.1 10.0 %collective-permute-done.17 = f32[2,24,768]{2,1,0:T(8,128)S(1)} collective-permute-done((f32[2,24,768]{2,1,0:T(8,128)S(1)}, f32[2,24,768]{2,1,0:T(8,128)S(1)}, u32[]{:S(2)}, u32[]{:S(2)}) %collective-permute-start.17) | collective-permute-done | bytes 147488 | tf_op jit(solution)/shard_map/ppermute | solution.py:419
  (80 shorter events, 31.3 us)
Async XLA Ops:
  0.6 65.4 %copy-start = (bf16[256,768]{1,0:T(8,128)(2,1)S(1)}, bf16[256,768]{1,0:T(8,128)(2,1)}, u32[]{:S(2)}) copy-start(bf16[256,768]{1,0:T(8,128)(2,1)} %param.11) | copy-start | bytes 1179652
  5.7 38.2 %collective-permute-start.3 = (bf16[2,256,1024]{2,1,0:T(8,128)(2,1)S(1)}, bf16[2,256,1024]{2,1,0:T(8,128)(2,1)S(1)}, u32[]{:S(2)}, u32[]{:S(2)}) collective-permute-start(bf16[2,256,1024]{2,1,0:T(8,128)(2,1)S(1)} %adjacency.1.own_ref), channel_id=1, source_target_pairs={{0,32},{32,64},{64,96},{96,0},{1,33},{33,65},{65,97},{97,1},{2,34}... | collective-permute-start | bytes 3145736 | tf_op jit(solution)/shard_map/ppermute | solution.py:323
  6.0 40.3 %collective-permute-start.4 = (bf16[2,256,1024]{2,1,0:T(8,128)(2,1)S(1)}, bf16[2,256,1024]{2,1,0:T(8,128)(2,1)S(1)}, u32[]{:S(2)}, u32[]{:S(2)}) collective-permute-start(bf16[2,256,1024]{2,1,0:T(8,128)(2,1)S(1)} %adjacency.1.own_ref), channel_id=1, source_target_pairs={{0,96},{32,0},{64,32},{96,64},{1,97},{33,1},{65,33},{97,65},{2,98}... | collective-permute-start | bytes 3145736 | tf_op jit(solution)/shard_map/ppermute | solution.py:323
  10.9 59.4 %all-to-all-start = ((bf16[32,192,128]{2,1,0:T(8,128)(2,1)}), bf16[32,192,128]{2,1,0:T(8,128)(2,1)}, u32[]{:S(2)}, u32[]{:S(2)}) async-start(bf16[32,192,128]{2,1,0:T(8,128)(2,1)} %outgoing.1), calls=%async_computation | async-start | bytes 3145728 | tf_op jit(solution)/shard_map/all_to_all | solution.py:331
  23.6 11.8 %collective-permute-start = (bf16[1,112,768]{2,1,0:T(8,128)(2,1)S(1)}, bf16[1,112,768]{2,1,0:T(8,128)(2,1)S(1)}, u32[]{:S(2)}, u32[]{:S(2)}) collective-permute-start(bf16[1,112,768]{2,1,0:T(8,128)(2,1)S(1)} %get-tuple-element.51), channel_id=1, source_target_pairs={{0,32},{32,64},{64,96},{96,0},{1,33},{33,65},{65,97},{97,1},{2,34}... | collective-permute-start | bytes 516104 | tf_op jit(solution)/shard_map/ppermute | solution.py:336
  25.1 11.6 %collective-permute-start.1 = (bf16[1,112,768]{2,1,0:T(8,128)(2,1)S(1)}, bf16[1,112,768]{2,1,0:T(8,128)(2,1)S(1)}, u32[]{:S(2)}, u32[]{:S(2)}) collective-permute-start(bf16[1,112,768]{2,1,0:T(8,128)(2,1)S(1)} %get-tuple-element.52), channel_id=1, source_target_pairs={{0,64},{32,96},{64,0},{96,32},{1,65},{33,97},{65,1},{97,33},{2,66}... | collective-permute-start | bytes 516104 | tf_op jit(solution)/shard_map/ppermute | solution.py:336
  26.5 12.8 %collective-permute-start.2 = (bf16[1,112,768]{2,1,0:T(8,128)(2,1)S(1)}, bf16[1,112,768]{2,1,0:T(8,128)(2,1)S(1)}, u32[]{:S(2)}, u32[]{:S(2)}) collective-permute-start(bf16[1,112,768]{2,1,0:T(8,128)(2,1)S(1)} %get-tuple-element.53), channel_id=1, source_target_pairs={{0,96},{32,0},{64,32},{96,64},{1,97},{33,1},{65,33},{97,65},{2,98}... | collective-permute-start | bytes 516104 | tf_op jit(solution)/shard_map/ppermute | solution.py:336
  40.9 23.3 %collective-permute-start.5 = (bf16[4,96,768]{2,1,0:T(8,128)(2,1)}, bf16[4,96,768]{2,1,0:T(8,128)(2,1)}, u32[]{:S(2)}, u32[]{:S(2)}) collective-permute-start(bf16[4,96,768]{2,1,0:T(8,128)(2,1)} %pad_maximum_fusion.1), channel_id=1, source_target_pairs={{0,16},{16,0},{1,17},{17,1},{2,18},{18,2},{3,19},{19,3},{4,20},{20... | collective-permute-start | bytes 1769480 | tf_op jit(solution)/shard_map/ppermute | solution.py:327
  43.9 21.8 %copy-start.3 = (bf16[2,256,1024]{2,1,0:T(8,128)(2,1)}, bf16[2,256,1024]{2,1,0:T(8,128)(2,1)S(1)}, u32[]{:S(2)}) copy-start(bf16[2,256,1024]{2,1,0:T(8,128)(2,1)S(1)} %collective-permute-done.3.back_ref) | copy-start | bytes 3145732
  44.8 19.4 %collective-permute-start.6 = (bf16[1,256,1024]{2,1,0:T(8,128)(2,1)}, bf16[1,256,1024]{2,1,0:T(8,128)(2,1)}, u32[]{:S(2)}, u32[]{:S(2)}) collective-permute-start(bf16[1,256,1024]{2,1,0:T(8,128)(2,1)} %slice.46), channel_id=1, source_target_pairs={{0,32},{32,64},{64,96},{96,0},{1,33},{33,65},{65,97},{97,1},{2,34}... | collective-permute-start | bytes 1572872 | tf_op jit(solution)/shard_map/ppermute | solution.py:323
  46.3 17.9 %collective-permute-start.7 = (bf16[1,256,1024]{2,1,0:T(8,128)(2,1)S(1)}, bf16[1,256,1024]{2,1,0:T(8,128)(2,1)S(1)}, u32[]{:S(2)}, u32[]{:S(2)}) collective-permute-start(bf16[1,256,1024]{2,1,0:T(8,128)(2,1)S(1)} %slice.47), channel_id=1, source_target_pairs={{0,96},{32,0},{64,32},{96,64},{1,97},{33,1},{65,33},{97,65},{2,98}... | collective-permute-start | bytes 1572872 | tf_op jit(solution)/shard_map/ppermute | solution.py:323
  65.9 4.4 %collective-permute-start.8 = (bf16[4,192,768]{2,1,0:T(8,128)(2,1)S(1)}, bf16[4,192,768]{2,1,0:T(8,128)(2,1)S(1)}, u32[]{:S(2)}, u32[]{:S(2)}) collective-permute-start(bf16[4,192,768]{2,1,0:T(8,128)(2,1)S(1)} %pad_maximum_fusion.w_mine_ref), channel_id=1, source_target_pairs={{0,1},{1,0},{2,3},{3,2},{4,5},{5,4},{6,7},{7,6},{8,9},{9,8},{10,11... | collective-permute-start | bytes 3538952 | tf_op jit(solution)/shard_map/ppermute | solution.py:327
  78.8 12.0 %collective-permute-start.9 = (bf16[2,4,96,256]{3,2,1,0:T(8,128)(2,1)}, bf16[2,4,96,256]{3,2,1,0:T(8,128)(2,1)}, u32[]{:S(2)}, u32[]{:S(2)}) collective-permute-start(bf16[2,4,96,256]{3,2,1,0:T(8,128)(2,1)} %get-tuple-element.31), channel_id=1, source_target_pairs={{0,1},{1,0},{2,3},{3,2},{4,5},{5,4},{6,7},{7,6},{8,9},{9,8},{10,11... | collective-permute-start | bytes 1179656 | tf_op jit(solution)/shard_map/ppermute | solution.py:327
  79.3 11.5 %all-to-all-start.1 = ((bf16[8,96,256]{2,1,0:T(8,128)(2,1)}), bf16[8,96,256]{2,1,0:T(8,128)(2,1)S(1)}, u32[]{:S(2)}, u32[]{:S(2)}) async-start(bf16[8,96,256]{2,1,0:T(8,128)(2,1)} %bitcast.57), calls=%async_computation.1 | async-start | bytes 786432 | tf_op jit(solution)/shard_map/all_to_all | solution.py:331
  93.4 17.6 %collective-permute-start.10 = (bf16[2,4,96,256]{3,2,1,0:T(8,128)(2,1)}, bf16[2,4,96,256]{3,2,1,0:T(8,128)(2,1)}, u32[]{:S(2)}, u32[]{:S(2)}) collective-permute-start(bf16[2,4,96,256]{3,2,1,0:T(8,128)(2,1)} %pad_maximum_fusion.2), channel_id=1, source_target_pairs={{0,16},{16,0},{1,17},{17,1},{2,18},{18,2},{3,19},{19,3},{4,20},{20... | collective-permute-start | bytes 1179656 | tf_op jit(solution)/shard_map/ppermute | solution.py:327
  117.3 63.2 %all-to-all-start.3 = ((bf16[32,192,128]{2,1,0:T(8,128)(2,1)}), bf16[32,192,128]{2,1,0:T(8,128)(2,1)S(1)}, u32[]{:S(2)}, u32[]{:S(2)}) async-start(bf16[32,192,128]{2,1,0:T(8,128)(2,1)} %backward.1), calls=%async_computation.3 | async-start | bytes 3145728 | tf_op jit(solution)/shard_map/all_to_all | solution.py:331
  126.6 22.0 %collective-permute-start.12 = (bf16[768,256]{1,0:T(8,128)(2,1)S(1)}, bf16[768,256]{1,0:T(8,128)(2,1)S(1)}, u32[]{:S(2)}, u32[]{:S(2)}) collective-permute-start(bf16[768,256]{1,0:T(8,128)(2,1)S(1)} %bitcast.53), channel_id=1, source_target_pairs={{0,16},{16,0},{1,17},{17,1},{2,18},{18,2},{3,19},{19,3},{4,20},{20... | collective-permute-start | bytes 1179656 | tf_op jit(solution)/shard_map/ppermute | solution.py:327
  129.6 18.9 %collective-permute-start.11 = (bf16[768,256]{1,0:T(8,128)(2,1)S(1)}, bf16[768,256]{1,0:T(8,128)(2,1)S(1)}, u32[]{:S(2)}, u32[]{:S(2)}) collective-permute-start(bf16[768,256]{1,0:T(8,128)(2,1)S(1)} %bitcast.54), channel_id=1, source_target_pairs={{0,1},{1,0},{2,3},{3,2},{4,5},{5,4},{6,7},{7,6},{8,9},{9,8},{10,11... | collective-permute-start | bytes 1179656 | tf_op jit(solution)/shard_map/ppermute | solution.py:327
  148.6 1.7 collective-permute-start.13
  154.3 13.8 %collective-permute-start.14 = (bf16[4,48,768]{2,1,0:T(8,128)(2,1)}, bf16[4,48,768]{2,1,0:T(8,128)(2,1)S(1)}, u32[]{:S(2)}, u32[]{:S(2)}) collective-permute-start(bf16[4,48,768]{2,1,0:T(8,128)(2,1)} %get-tuple-element.42), channel_id=1, source_target_pairs={{0,2},{2,0},{4,6},{6,4},{8,10},{10,8},{12,14},{14,12},{1,3},{3,1},... | collective-permute-start | bytes 884744 | tf_op jit(solution)/shard_map/ppermute | solution.py:327
  168.2 8.8 %collective-permute-start.15 = (bf16[2,48,768]{2,1,0:T(8,128)(2,1)S(1)}, bf16[2,48,768]{2,1,0:T(8,128)(2,1)S(1)}, u32[]{:S(2)}, u32[]{:S(2)}) collective-permute-start(bf16[2,48,768]{2,1,0:T(8,128)(2,1)S(1)} %get-tuple-element.49), channel_id=1, source_target_pairs={{0,4},{2,6},{4,0},{6,2},{8,12},{10,14},{12,8},{14,10},{1,5},{3,7},... | collective-permute-start | bytes 442376 | tf_op jit(solution)/shard_map/ppermute | solution.py:327
  177.1 10.6 %collective-permute-start.16 = (bf16[1,48,768]{2,1,0:T(8,128)(2,1)S(1)}, bf16[1,48,768]{2,1,0:T(8,128)(2,1)S(1)}, u32[]{:S(2)}, u32[]{:S(2)}) collective-permute-start(bf16[1,48,768]{2,1,0:T(8,128)(2,1)S(1)} %fusion.8), channel_id=1, source_target_pairs={{0,8},{2,10},{4,12},{6,14},{8,0},{10,2},{12,4},{14,6},{1,9},{3,11}... | collective-permute-start | bytes 221192 | tf_op jit(solution)/shard_map/ppermute | solution.py:327
  183.1 21.1 %all-to-all-start.4 = ((f32[8,2,16,192]{3,2,1,0:T(8,128)}), f32[8,2,16,192]{3,2,1,0:T(8,128)S(1)}, u32[]{:S(2)}, u32[]{:S(2)}) async-start(f32[8,2,16,192]{3,2,1,0:T(8,128)} %owned.1), calls=%async_computation.4 | async-start | bytes 524288 | tf_op jit(solution)/shard_map/all_to_all | solution.py:331
  187.7 16.4 %collective-permute-start.17 = (f32[2,24,768]{2,1,0:T(8,128)S(1)}, f32[2,24,768]{2,1,0:T(8,128)S(1)}, u32[]{:S(2)}, u32[]{:S(2)}) collective-permute-start(f32[2,24,768]{2,1,0:T(8,128)S(1)} %bitcast.62), channel_id=1, source_target_pairs={{0,0},{1,4},{2,1},{3,5},{4,2},{5,6},{6,3},{7,7},{8,32},{9,36},{10,... | collective-permute-start | bytes 442376 | tf_op jit(solution)/shard_map/ppermute | solution.py:419
  (8 other events, 45.5 us)

commit v8 on v7

--- a/solution.py
+++ b/solution.py
@@ -120,7 +120,7 @@
 
 def forward_kernel(
     place_ref, slot_ref, own_ref, back_ref, fore_ref, far0_ref, far1_ref, fetched_ref, w_mine_ref, w_theirs_ref,
-    keep_ref, send_ref, pre_ref, adj_buf, sems, both_ref, acc_ref,
+    keep_ref, keep_far_ref, send_ref, send_far_ref, pre_ref, adj_buf, sems, both_ref, acc_ref,
 ):
     core, y = place_ref[2], place_ref[3]
     loads = start_loads((own_ref, back_ref, fore_ref, far0_ref, far1_ref), adj_buf, sems)
@@ -134,17 +134,19 @@
                 part = adj_buf[2 * n + p, q * BLK : (q + 1) * BLK, :]
                 both_ref[p, :, q * BLK : (q + 1) * BLK] = dot(wide, part, 1, 1).astype(BF16)
         j = (y - k) & 3
-        side, pair = (j >> 1) ^ place_ref[4], pl.ds(2 * (j & 1), 2)
-
-        @pl.when(core == 0)
+        far, pair = (j >> 1) ^ place_ref[4], pl.ds(2 * (j & 1), 2)
+        keep = both_ref[:, pl.ds(pl.multiple_of(96 * core, 32), 96)]
+        send = both_ref[:, pl.ds(pl.multiple_of(96 * (1 - core), 32), 96)]
+
+        @pl.when(far == 0)
         def _():
-            keep_ref[side, pair] = both_ref[:, :96]
-            send_ref[side, pair] = both_ref[:, 96:]
-
-        @pl.when(core == 1)
+            keep_ref[pair] = keep
+            send_ref[pair] = send
+
+        @pl.when(far == 1)
         def _():
-            keep_ref[side, pair] = both_ref[:, 96:]
-            send_ref[side, pair] = both_ref[:, :96]
+            keep_far_ref[pair] = keep
+            send_far_ref[pair] = send
 
         term = dot(w_mine_ref[k], both_ref[core], 0, 0) + dot(w_theirs_ref[k], both_ref[1 - core], 0, 0)
         if n == 0:
@@ -158,12 +160,12 @@
 def forward_of(place, slots, adjacency, fetched, w_mine, w_theirs):
     _, rows, wide = adjacency[0].shape
     width = w_mine.shape[2]
-    half = jax.ShapeDtypeStruct((2, 4, 96, rows), BF16)
+    half = jax.ShapeDtypeStruct((4, 96, rows), BF16)
     return pl.pallas_call(
         forward_kernel,
         in_specs=[smem(), smem()] + [hbm()] * 5 + [vmem()] * 3,
-        out_specs=[vmem()] * 3,
-        out_shape=[half, half, jax.ShapeDtypeStruct((width, rows), BF16)],
+        out_specs=[vmem()] * 5,
+        out_shape=[half, half, half, half, jax.ShapeDtypeStruct((width, rows), BF16)],
         scratch_shapes=load_scratch(rows, wide)
         + [pltpu.VMEM((2, 192, rows), BF16), pltpu.VMEM((width, rows), F32)],
         compiler_params=params(),
@@ -234,47 +236,31 @@
 
 
 def weight_kernel(
-    place_ref, own_ref, core_ref, far_ref, grad_ref, core_grad_ref, far_grad_ref, far_core_grad_ref, keep_ref, send_ref
+    place_ref, own_ref, core_ref, far_ref, far_core_ref, grad_ref, core_grad_ref, far_grad_ref, far_core_grad_ref, *refs
 ):
-    bit = place_ref[5]
+    *out_refs, pieces_ref = refs
+    z = place_ref[5]
     grads = jnp.concatenate(
         [grad_ref[...], core_grad_ref[...], far_grad_ref[...], far_core_grad_ref[...]], axis=1
     )
-    for half in range(2):
-        terms = []
-        for p in range(2):
-            r = 2 * half + p
-            wide = jnp.concatenate([own_ref[0, r], core_ref[0, r], far_ref[0, r], far_ref[1, r]], axis=1)
-            terms.append(dot(wide, grads, 1, 1))
-
-        def piece(m):
-            rows = slice(m * 24, (m + 1) * 24)
-            return jnp.concatenate([terms[0][rows], terms[1][rows]], axis=0)
-
-        def cut(even_ref, odd_ref):
-            for m in range(4):
-                target = odd_ref if m % 2 else even_ref
-                target[2 * half + m // 2] = piece(m).astype(target.dtype)
-
-        @pl.when(bit == 0)
-        def _():
-            cut(keep_ref, send_ref)
-
-        @pl.when(bit == 1)
-        def _():
-            cut(send_ref, keep_ref)
+    for r in range(4):
+        wide = jnp.concatenate([own_ref[r], core_ref[r], far_ref[r], far_core_ref[r]], axis=1)
+        term = dot(wide, grads, 1, 1)
+        for m in range(4):
+            part = slice(24 * (r % 2), 24 * (r % 2) + 24)
+            pieces_ref[4 * (r // 2) + m, part] = term[m * 24 : (m + 1) * 24]
+    for k, out_ref in enumerate(out_refs):
+        out_ref[...] = pieces_ref[z ^ k].astype(out_ref.dtype)
 
 
 def weight_terms_of(place, *operands):
     width = operands[-1].shape[0]
     return pl.pallas_call(
         weight_kernel,
-        in_specs=[smem()] + [vmem()] * 7,
-        out_specs=[vmem(), vmem()],
-        out_shape=[
-            jax.ShapeDtypeStruct((4, 48, width), F32),
-            jax.ShapeDtypeStruct((4, 48, width), BF16),
-        ],
+        in_specs=[smem()] + [vmem()] * 8,
+        out_specs=[vmem()] * 8,
+        out_shape=[jax.ShapeDtypeStruct((48, width), F32 if k == 0 else BF16) for k in range(8)],
+        scratch_shapes=[pltpu.VMEM((8, 48, width), F32)],
         compiler_params=params(),
         name="weight_terms",
     )(place, *operands)
@@ -306,19 +292,6 @@
     )(place, source_blocks, arrived)
 
 
-def halve(bit, keep, came, stride):
-    shape = (-1, 2, stride, *keep.shape[1:])
-
-    def take(which):
-        total = [
-            lax.dynamic_index_in_dim(v.reshape(shape), which, 1, keepdims=False).astype(F32)
-            for v in (keep, came)
-        ]
-        return (total[0] + total[1]).reshape(-1, *keep.shape[1:])
-
-    return take(bit), take(1 - bit).astype(BF16)
-
-
 def step(value, by):
     return lax.ppermute(value, "y", [(i, (i + by) % 4) for i in range(4)])
 
@@ -363,11 +336,10 @@
     group = lax.axis_index(REL)
     xh, z = lax.axis_index("xh"), lax.axis_index("z")
     xh, z = lax.axis_index("xh"), lax.axis_index("z")
-    place = in_hbm(jnp.stack([owner, 192 * y, core, y, xh, z & 1]).astype(jnp.int32))
+    place = in_hbm(jnp.stack([owner, 192 * y, core, y, xh, z]).astype(jnp.int32))
 
     own = adjacency_of(in_hbm(tile_values), in_hbm(tile_count))
     back, fore = step(own, 1), step(own, -1)
-    far0, far1 = step(back[:1], 1), step(fore[1:], -1)
     features, weights, _ = lax.optimization_barrier((features, weights, own))
     source_blocks = in_hbm(source_blocks)
     outgoing = outgoing_of(in_hbm(features), source_blocks, place)
@@ -380,6 +352,15 @@
         pieces.append(jnp.concatenate([cut, own_slots], axis=1) if k else cut)
     came = around(pieces[1:], "y", 4)
     slots = jnp.concatenate([tile_slot.reshape(-1)] + [c[0, 96, :32].astype(jnp.int32) for c in came])
+    share = width // groups
+    bias_share = lax.dynamic_slice_in_dim(bias, group * share, share)
+    bias_share = jnp.broadcast_to(bias_share[:, None], (share, features.shape[0]))
+    cotangent_share = lax.dynamic_slice_in_dim(cotangent, group * share, share, 1).T
+    back, fore, slots, bias_share, cotangent_share = lax.optimization_barrier(
+        (back, fore, slots, bias_share, cotangent_share)
+    )
+    slots, bias_share, cotangent_share = in_hbm(slots), in_hbm(bias_share), in_hbm(cotangent_share)
+    far0, far1 = step(back[:1], 1), step(fore[1:], -1)
     w_part = jnp.concatenate([pieces[0]] + [c[:, :96] for c in came], axis=0)
     w_other = swap(w_part, "xh")
     w_part, w_other, far0, far1 = lax.optimization_barrier((w_part, w_other, far0, far1))
@@ -389,20 +370,19 @@
     w_mine, w_theirs = resident(w_mine), resident(swap(w_mine, "core"))
     adjacency = [in_hbm(a) for a in (own, back, fore, far0, far1)]
 
-    share = width // groups
-    bias_share = lax.dynamic_slice_in_dim(bias, group * share, share)[:, None]
-    cotangent_share = lax.dynamic_slice_in_dim(cotangent, group * share, share, 1).T
-    slots, bias_share, cotangent_share = lax.optimization_barrier((slots, bias_share, cotangent_share))
-    slots, bias_share, cotangent_share = in_hbm(slots), in_hbm(bias_share), in_hbm(cotangent_share)
-    messages, for_core, part = forward_of(place, slots, adjacency, fetched, w_mine, w_theirs)
-    of_core = swap(for_core, "core")
-    arrived, of_core = lax.optimization_barrier((exchange(part.reshape(groups, share, -1), REL), of_core))
+    own_terms, far_terms, for_core, for_far_core, part = forward_of(
+        place, slots, adjacency, fetched, w_mine, w_theirs
+    )
+    of_core, of_far = swap(for_core, "core"), swap(far_terms, "xh")
+    of_far_core = swap(for_far_core, "core")
+    arrived, of_far_core = lax.optimization_barrier((exchange(part.reshape(groups, share, -1), REL), of_far_core))
     arrived = resident(arrived)
     activated, grad_copies = activation_of(arrived, bias_share, cotangent_share)
     output = activated.T
-    of_far = swap(jnp.stack([messages[1], of_core[1]]), "xh")
-    grads, of_far = lax.optimization_barrier((exchange(grad_copies, REL).reshape(width, -1), of_far))
-
+    of_far_core = swap(of_far_core, "xh")
+    grads, of_core, of_far, of_far_core = lax.optimization_barrier(
+        (exchange(grad_copies, REL).reshape(width, -1), of_core, of_far, of_far_core)
+    )
     partial = backward_of(place, slots, adjacency, resident(grads), w_mine, w_theirs, owners)
     returned = resident(exchange(in_hbm(partial), TGT))
     cut = owned_of(place, source_blocks, returned, groups)
@@ -410,12 +390,12 @@
     grad_features = columns.transpose(1, 2, 0, 3).reshape(2, BLK // groups, width)
 
     far_grads = swap(grads, "xh")
-    keep, send = weight_terms_of(
-        place, messages, of_core, of_far, grads, swap(grads, "core"), far_grads, swap(far_grads, "core")
-    )
-    keep, send = halve((z >> 1) & 1, keep, swap(send, "z", 8, 1), 1)
-    keep, send = halve(z >> 2, keep, swap(send, "z", 8, 2), 1)
-    piece = keep + swap(send, "z", 8, 4).astype(F32)
+    piece, *others = weight_terms_of(
+        place, own_terms, of_core, of_far, of_far_core,
+        grads, swap(grads, "core"), far_grads, swap(far_grads, "core"),
+    )
+    for k, other in enumerate(others, 1):
+        piece = piece + swap(other, "z", 8, k).astype(F32)
     grad_weights = lax.ppermute(piece.reshape(2, 24, width), ("y", *TGT), to_owner())
     return (output, grad_weights, grad_features)
 

time: 209 us -> 208 us (level)
  starting transfers between devices: 58.7 us -> 79.6 us
  waiting for transfers between devices: 86.6 us -> 70.4 us
  blocking collectives: 13 us -> 0 us
  local copies, waits for them, and re-layouts: 9.76 us -> 15.7 us
    ppermute x10 -> x16, starting transfers between devices: 14.8 us -> 29.2 us  [swap(): return lax.ppermute(value, axis, [(i, i ^ flip) for i in range(size)])]
    all_to_all x1 -> x0, blocking collectives: 13 us -> none  [exchange(): return lax.all_to_all(value, axis, 0, 0, tiled=True)]
    ppermute x3, waiting for transfers between devices: 12.7 us -> 0.01 us  [around(): lax.ppermute(v, axis, [(i, (i + k) % size) for i in range(size)])]
    all_to_all x4 -> x5, starting transfers between devices: 30.5 us -> 35.9 us  [exchange(): return lax.all_to_all(value, axis, 0, 0, tiled=True)]
    ppermute x10 -> x16, waiting for transfers between devices: 58.2 us -> 54 us  [swap(): return lax.ppermute(value, axis, [(i, i ^ flip) for i in range(size)])]
    slice x3, local copies, waits for them, and re-layouts: 0.03 us -> 2.76 us  [per_device(): w_part = jnp.concatenate([pieces[0]] + [c[:, :96] for c in came], axis=0)]
    unnamed x22 -> x28, local copies, waits for them, and re-layouts: 2.81 us -> 4.94 us
    all_to_all x4 -> x5, waiting for transfers between devices: 5.63 us -> 6.66 us  [exchange(): return lax.all_to_all(value, axis, 0, 0, tiled=True)]
  transfers between devices with their start and end apart: 22 -> 29, of which waited for: 10 -> 12; matrix products, arithmetic and copies ran while one was open for 5% -> 8% of each run, Pallas kernels for 5% -> 4%
where the time goes in v8:
time: 208 us; the launch traced here: 204 us
  starting transfers between devices  79.6 us (38%)
  waiting for transfers between devices  70.4 us (34%)
  Pallas kernels  30 us (14%)
  local copies, waits for them, and re-layouts  15.7 us (8%)
  other arithmetic  7.86 us (4%)
    ppermute x16, waiting for transfers between devices, swap(): return lax.ppermute(value, axis, [(i, i ^ flip) for i in range(size)])  54 us
    all_to_all x5, starting transfers between devices, exchange(): return lax.all_to_all(value, axis, 0, 0, tiled=True)  35.9 us
    ppermute x16, starting transfers between devices, swap(): return lax.ppermute(value, axis, [(i, i ^ flip) for i in range(size)])  29.2 us
    ppermute x1, waiting for transfers between devices, per_device(): lax.ppermute(piece.reshape(2, 24, width), ('y', *TGT), to_owner())  9.24 us
    pallas_call x1, Pallas kernels, forward_of(): pl.pallas_call(forward_kernel, in_specs=[smem(), smem()] + [hbm()] * 5 +...  8.5 us
    all_to_all x5, waiting for transfers between devices, exchange(): return lax.all_to_all(value, axis, 0, 0, tiled=True)  6.66 us
    pallas_call x1, Pallas kernels, backward_of(): pl.pallas_call(backward_kernel, in_specs=[smem(), smem()] + [hbm()] * 5 +...  6.31 us
    ppermute x1, starting transfers between devices, per_device(): lax.ppermute(piece.reshape(2, 24, width), ('y', *TGT), to_owner())  6.04 us
  transfers between devices with their start and end apart: 29, of which 12 were waited for; matrix products, arithmetic and copies ran while one was open for 8% of the time, Pallas kernels for 4%

profile of v8, /device:TPU:56, one launch (start us, length us, event | category | flops | bytes accessed | tf_op | source)
XLA Modules:
  0.0 204.5 jit_solution(17302449611649346645)
XLA Ops:
  1.5 4.9 %adjacency.1.own_ref = bf16[2,256,1024]{2,1,0:T(8,128)(2,1)S(1)} custom-call(s32[2,2]{1,0:T(2,128)} %count_ref.1, s32[2,256,8,128]{3,2,1,0:T(8,128)} %values_ref.1), custom_call_target="tpu_custom_call" | custom-call | tf_op jit(solution)/shard_map/adjacency/pallas_call | solution.py:61
  18.6 11.4 %all-to-all-start = ((bf16[32,192,128]{2,1,0:T(8,128)(2,1)}), bf16[32,192,128]{2,1,0:T(8,128)(2,1)}, u32[]{:S(2)}, u32[]{:S(2)}) async-start(bf16[32,192,128]{2,1,0:T(8,128)(2,1)} %outgoing.1), calls=%async_computation | async-start | bytes 3145728 | tf_op jit(solution)/shard_map/all_to_all | solution.py:304
  37.8 3.0 %collective-permute-start.5 = (bf16[4,96,768]{2,1,0:T(8,128)(2,1)}, bf16[4,96,768]{2,1,0:T(8,128)(2,1)}, u32[]{:S(2)}, u32[]{:S(2)}) collective-permute-start(bf16[4,96,768]{2,1,0:T(8,128)(2,1)} %pad_maximum_fusion.1), channel_id=1, source_target_pairs={{0,16},{16,0},{1,17},{17,1},{2,18},{18,2},{3,19},{19,3},{4,20},{20... | collective-permute-start | bytes 1769480 | tf_op jit(solution)/shard_map/ppermute | solution.py:300
  45.5 2.6 %collective-permute-start.6 = (bf16[1,256,1024]{2,1,0:T(8,128)(2,1)}, bf16[1,256,1024]{2,1,0:T(8,128)(2,1)S(1)}, u32[]{:S(2)}, u32[]{:S(2)}) collective-permute-start(bf16[1,256,1024]{2,1,0:T(8,128)(2,1)} %slice.30), channel_id=1, source_target_pairs={{0,32},{32,64},{64,96},{96,0},{1,33},{33,65},{65,97},{97,1},{2,34}... | collective-permute-start | bytes 1572872 | tf_op jit(solution)/shard_map/ppermute | solution.py:296
  49.1 15.9 %collective-permute-done.5 = bf16[4,96,768]{2,1,0:T(8,128)(2,1)} collective-permute-done((bf16[4,96,768]{2,1,0:T(8,128)(2,1)}, bf16[4,96,768]{2,1,0:T(8,128)(2,1)}, u32[]{:S(2)}, u32[]{:S(2)}) %collective-permute-start.5) | collective-permute-done | bytes 589856 | tf_op jit(solution)/shard_map/ppermute | solution.py:300
  66.9 2.8 %collective-permute-done.8.w_theirs_ref = bf16[4,192,768]{2,1,0:T(8,128)(2,1)S(1)} collective-permute-done((bf16[4,192,768]{2,1,0:T(8,128)(2,1)S(1)}, bf16[4,192,768]{2,1,0:T(8,128)(2,1)S(1)}, u32[]{:S(2)}, u32[]{:S(2)}) %collective-permute-start.8) | collective-permute-done | bytes 1179680 | tf_op jit(solution)/shard_map/ppermute | solution.py:300
  71.8 8.5 %forward.1 = (bf16[4,96,256]{2,1,0:T(8,128)(2,1)S(1)}, bf16[4,96,256]{2,1,0:T(8,128)(2,1)S(1)}, bf16[4,96,256]{2,1,0:T(8,128)(2,1)S(1)}, bf16[4,96,256]{2,1,0:T(8,128)(2,1)S(1)}, bf16[768,256]{1,0:T(8,128)(2,1)}) custom-call(s32[6]{0:T(128)} %stack.27.place_ref, s32[128]{0:T(128)} %pad_add_fusion.slot_ref, bf16[2,256,1024]{2,1,0:T(8,128)(2,1)} %copy-done.1, ...), custom_call_target="tpu_custom_call" | custom-call | tf_op jit(solution)/shard_map/forward/pallas_call | solution.py:164
  81.7 5.5 %all-to-all-start.1 = ((bf16[8,96,256]{2,1,0:T(8,128)(2,1)}), bf16[8,96,256]{2,1,0:T(8,128)(2,1)S(1)}, u32[]{:S(2)}, u32[]{:S(2)}) async-start(bf16[8,96,256]{2,1,0:T(8,128)(2,1)} %bitcast.10), calls=%async_computation.1 | async-start | bytes 786432 | tf_op jit(solution)/shard_map/all_to_all | solution.py:304
  88.8 4.6 %all-to-all-done.1.arrived_ref = bf16[8,96,256]{2,1,0:T(8,128)(2,1)S(1)} async-done(((bf16[8,96,256]{2,1,0:T(8,128)(2,1)}), bf16[8,96,256]{2,1,0:T(8,128)(2,1)S(1)}, u32[]{:S(2)}, u32[]{:S(2)}) %all-to-all-start.1) | async-done | bytes 393248 | tf_op jit(solution)/shard_map/all_to_all | solution.py:304
  95.1 5.8 %all-to-all-start.2 = ((bf16[8,96,256]{2,1,0:T(8,128)(2,1)}), bf16[8,96,256]{2,1,0:T(8,128)(2,1)S(1)}, u32[]{:S(2)}, u32[]{:S(2)}) async-start(bf16[8,96,256]{2,1,0:T(8,128)(2,1)} %get-tuple-element.51), calls=%async_computation.2 | async-start | bytes 786432 | tf_op jit(solution)/shard_map/all_to_all | solution.py:304
  104.4 7.1 %collective-permute-done.11.far_ref = bf16[4,96,256]{2,1,0:T(8,128)(2,1)S(1)} collective-permute-done((bf16[4,96,256]{2,1,0:T(8,128)(2,1)}, bf16[4,96,256]{2,1,0:T(8,128)(2,1)S(1)}, u32[]{:S(2)}, u32[]{:S(2)}) %collective-permute-start.11) | collective-permute-done | bytes 196640 | tf_op jit(solution)/shard_map/ppermute | solution.py:300
  112.2 2.8 %collective-permute-done.12.far_core_ref = bf16[4,96,256]{2,1,0:T(8,128)(2,1)S(1)} collective-permute-done((bf16[4,96,256]{2,1,0:T(8,128)(2,1)}, bf16[4,96,256]{2,1,0:T(8,128)(2,1)S(1)}, u32[]{:S(2)}, u32[]{:S(2)}) %collective-permute-start.12) | collective-permute-done | bytes 196640 | tf_op jit(solution)/shard_map/ppermute | solution.py:300
  115.7 6.3 %backward.1 = bf16[32,192,128]{2,1,0:T(8,128)(2,1)} custom-call(s32[6]{0:T(128)} %stack.27.place_ref, s32[128]{0:T(128)} %pad_add_fusion.slot_ref, bf16[2,256,1024]{2,1,0:T(8,128)(2,1)} %copy-done.1, bf16[2,256,1024]{2,1,0:T(8,128)(2,1)} %copy-done.8, bf16[2,256,1024]{2,1,0:T(8,128)(2,1)} %copy-done.9, bf16[1,256,1024]{2,1,0:T(8,128)(2,1)} %copy-done.10, ...), custom_call_target="tpu_custom_call" | custom-call | tf_op jit(solution)/shard_map/backward/pallas_call | solution.py:226
  122.0 7.6 %all-to-all-start.3 = ((bf16[32,192,128]{2,1,0:T(8,128)(2,1)}), bf16[32,192,128]{2,1,0:T(8,128)(2,1)S(1)}, u32[]{:S(2)}, u32[]{:S(2)}) async-start(bf16[32,192,128]{2,1,0:T(8,128)(2,1)} %backward.1), calls=%async_computation.3 | async-start | bytes 3145728 | tf_op jit(solution)/shard_map/all_to_all | solution.py:304
  129.6 3.1 %collective-permute-start.14 = (bf16[768,256]{1,0:T(8,128)(2,1)S(1)}, bf16[768,256]{1,0:T(8,128)(2,1)S(1)}, u32[]{:S(2)}, u32[]{:S(2)}) collective-permute-start(bf16[768,256]{1,0:T(8,128)(2,1)S(1)} %bitcast.29), channel_id=1, source_target_pairs={{0,16},{16,0},{1,17},{17,1},{2,18},{18,2},{3,19},{19,3},{4,20},{20... | collective-permute-start | bytes 1179656 | tf_op jit(solution)/shard_map/ppermute | solution.py:300
  132.7 18.9 %collective-permute-done.14.far_grad_ref = bf16[768,256]{1,0:T(8,128)(2,1)S(1)} collective-permute-done((bf16[768,256]{1,0:T(8,128)(2,1)S(1)}, bf16[768,256]{1,0:T(8,128)(2,1)S(1)}, u32[]{:S(2)}, u32[]{:S(2)}) %collective-permute-start.14) | collective-permute-done | bytes 393248 | tf_op jit(solution)/shard_map/ppermute | solution.py:300
  153.3 3.4 %weight_terms.1 = (f32[48,768]{1,0:T(8,128)S(1)}, bf16[48,768]{1,0:T(8,128)(2,1)S(1)}, bf16[48,768]{1,0:T(8,128)(2,1)S(1)}, bf16[48,768]{1,0:T(8,128)(2,1)S(1)},...) custom-call(s32[6]{0:T(128)} %stack.27.place_ref, ...), custom_call_target="tpu_custom_call" | custom-call | tf_op jit(solution)/shard_map/weight_terms/pallas_call | solution.py:258
  156.7 3.5 %collective-permute-start.22 = (bf16[48,768]{1,0:T(8,128)(2,1)S(1)}, bf16[48,768]{1,0:T(8,128)(2,1)S(1)}, u32[]{:S(2)}, u32[]{:S(2)}) collective-permute-start(bf16[48,768]{1,0:T(8,128)(2,1)S(1)} %get-tuple-element.66), channel_id=1, source_target_pairs={{0,14},{2,12},{4,10},{6,8},{8,6},{10,4},{12,2},{14,0},{1,15},{3,13... | collective-permute-start | bytes 221192 | tf_op jit(solution)/shard_map/ppermute | solution.py:300
  160.2 6.3 %collective-permute-start.20 = (bf16[48,768]{1,0:T(8,128)(2,1)}, bf16[48,768]{1,0:T(8,128)(2,1)S(1)}, u32[]{:S(2)}, u32[]{:S(2)}) collective-permute-start(bf16[48,768]{1,0:T(8,128)(2,1)} %get-tuple-element.64), channel_id=1, source_target_pairs={{0,10},{2,8},{4,14},{6,12},{8,2},{10,0},{12,6},{14,4},{1,11},{3,9}... | collective-permute-start | bytes 221192 | tf_op jit(solution)/shard_map/ppermute | solution.py:300
  168.6 3.2 %collective-permute-done.22 = bf16[48,768]{1,0:T(8,128)(2,1)S(1)} collective-permute-done((bf16[48,768]{1,0:T(8,128)(2,1)S(1)}, bf16[48,768]{1,0:T(8,128)(2,1)S(1)}, u32[]{:S(2)}, u32[]{:S(2)}) %collective-permute-start.22) | collective-permute-done | bytes 73760 | tf_op jit(solution)/shard_map/ppermute | solution.py:300
  171.7 7.7 %collective-permute-start.17 = (bf16[48,768]{1,0:T(8,128)(2,1)S(1)}, bf16[48,768]{1,0:T(8,128)(2,1)S(1)}, u32[]{:S(2)}, u32[]{:S(2)}) collective-permute-start(bf16[48,768]{1,0:T(8,128)(2,1)S(1)} %get-tuple-element.61), channel_id=1, source_target_pairs={{0,4},{2,6},{4,0},{6,2},{8,12},{10,14},{12,8},{14,10},{1,5},{3,7},... | collective-permute-start | bytes 221192 | tf_op jit(solution)/shard_map/ppermute | solution.py:300
  181.9 5.6 %all-to-all-start.4 = ((f32[8,2,16,192]{3,2,1,0:T(8,128)}), f32[8,2,16,192]{3,2,1,0:T(8,128)S(1)}, u32[]{:S(2)}, u32[]{:S(2)}) async-start(f32[8,2,16,192]{3,2,1,0:T(8,128)} %owned.1), calls=%async_computation.4 | async-start | bytes 524288 | tf_op jit(solution)/shard_map/all_to_all | solution.py:304
  187.6 6.0 %collective-permute-start.23 = (f32[2,24,768]{2,1,0:T(8,128)S(1)}, f32[2,24,768]{2,1,0:T(8,128)S(1)}, u32[]{:S(2)}, u32[]{:S(2)}) collective-permute-start(f32[2,24,768]{2,1,0:T(8,128)S(1)} %bitcast.35), channel_id=1, source_target_pairs={{0,0},{1,4},{2,1},{3,5},{4,2},{5,6},{6,3},{7,7},{8,32},{9,36},{10,... | collective-permute-start | bytes 442376 | tf_op jit(solution)/shard_map/ppermute | solution.py:399
  193.7 9.2 %collective-permute-done.23 = f32[2,24,768]{2,1,0:T(8,128)S(1)} collective-permute-done((f32[2,24,768]{2,1,0:T(8,128)S(1)}, f32[2,24,768]{2,1,0:T(8,128)S(1)}, u32[]{:S(2)}, u32[]{:S(2)}) %collective-permute-start.23) | collective-permute-done | bytes 147488 | tf_op jit(solution)/shard_map/ppermute | solution.py:399
  (94 shorter events, 47.9 us)
Async XLA Ops:
  9.5 23.7 %collective-permute-start.4 = (bf16[1,112,768]{2,1,0:T(8,128)(2,1)}, bf16[1,112,768]{2,1,0:T(8,128)(2,1)}, u32[]{:S(2)}, u32[]{:S(2)}) collective-permute-start(bf16[1,112,768]{2,1,0:T(8,128)(2,1)} %get-tuple-element.75), channel_id=1, source_target_pairs={{0,96},{32,0},{64,32},{96,64},{1,97},{33,1},{65,33},{97,65},{2,98}... | collective-permute-start | bytes 516104 | tf_op jit(solution)/shard_map/ppermute | solution.py:309
  10.2 23.9 %collective-permute-start.3 = (bf16[1,112,768]{2,1,0:T(8,128)(2,1)}, bf16[1,112,768]{2,1,0:T(8,128)(2,1)}, u32[]{:S(2)}, u32[]{:S(2)}) collective-permute-start(bf16[1,112,768]{2,1,0:T(8,128)(2,1)} %get-tuple-element.74), channel_id=1, source_target_pairs={{0,64},{32,96},{64,0},{96,32},{1,65},{33,97},{65,1},{97,33},{2,66}... | collective-permute-start | bytes 516104 | tf_op jit(solution)/shard_map/ppermute | solution.py:309
  11.2 23.9 %collective-permute-start.2 = (bf16[1,112,768]{2,1,0:T(8,128)(2,1)}, bf16[1,112,768]{2,1,0:T(8,128)(2,1)}, u32[]{:S(2)}, u32[]{:S(2)}) collective-permute-start(bf16[1,112,768]{2,1,0:T(8,128)(2,1)} %get-tuple-element.73), channel_id=1, source_target_pairs={{0,32},{32,64},{64,96},{96,0},{1,33},{33,65},{65,97},{97,1},{2,34}... | collective-permute-start | bytes 516104 | tf_op jit(solution)/shard_map/ppermute | solution.py:309
  13.3 30.4 %collective-permute-start = (bf16[2,256,1024]{2,1,0:T(8,128)(2,1)S(1)}, bf16[2,256,1024]{2,1,0:T(8,128)(2,1)S(1)}, u32[]{:S(2)}, u32[]{:S(2)}) collective-permute-start(bf16[2,256,1024]{2,1,0:T(8,128)(2,1)S(1)} %adjacency.1.own_ref), channel_id=1, source_target_pairs={{0,32},{32,64},{64,96},{96,0},{1,33},{33,65},{65,97},{97,1},{2,34}... | collective-permute-start | bytes 3145736 | tf_op jit(solution)/shard_map/ppermute | solution.py:296
  14.3 29.5 %collective-permute-start.1 = (bf16[2,256,1024]{2,1,0:T(8,128)(2,1)S(1)}, bf16[2,256,1024]{2,1,0:T(8,128)(2,1)S(1)}, u32[]{:S(2)}, u32[]{:S(2)}) collective-permute-start(bf16[2,256,1024]{2,1,0:T(8,128)(2,1)S(1)} %adjacency.1.own_ref), channel_id=1, source_target_pairs={{0,96},{32,0},{64,32},{96,64},{1,97},{33,1},{65,33},{97,65},{2,98}... | collective-permute-start | bytes 3145736 | tf_op jit(solution)/shard_map/ppermute | solution.py:296
  18.6 53.2 %all-to-all-start = ((bf16[32,192,128]{2,1,0:T(8,128)(2,1)}), bf16[32,192,128]{2,1,0:T(8,128)(2,1)}, u32[]{:S(2)}, u32[]{:S(2)}) async-start(bf16[32,192,128]{2,1,0:T(8,128)(2,1)} %outgoing.1), calls=%async_computation | async-start | bytes 3145728 | tf_op jit(solution)/shard_map/all_to_all | solution.py:304
  37.8 27.2 %collective-permute-start.5 = (bf16[4,96,768]{2,1,0:T(8,128)(2,1)}, bf16[4,96,768]{2,1,0:T(8,128)(2,1)}, u32[]{:S(2)}, u32[]{:S(2)}) collective-permute-start(bf16[4,96,768]{2,1,0:T(8,128)(2,1)} %pad_maximum_fusion.1), channel_id=1, source_target_pairs={{0,16},{16,0},{1,17},{17,1},{2,18},{18,2},{3,19},{19,3},{4,20},{20... | collective-permute-start | bytes 1769480 | tf_op jit(solution)/shard_map/ppermute | solution.py:300
  45.5 19.4 %collective-permute-start.6 = (bf16[1,256,1024]{2,1,0:T(8,128)(2,1)}, bf16[1,256,1024]{2,1,0:T(8,128)(2,1)S(1)}, u32[]{:S(2)}, u32[]{:S(2)}) collective-permute-start(bf16[1,256,1024]{2,1,0:T(8,128)(2,1)} %slice.30), channel_id=1, source_target_pairs={{0,32},{32,64},{64,96},{96,0},{1,33},{33,65},{65,97},{97,1},{2,34}... | collective-permute-start | bytes 1572872 | tf_op jit(solution)/shard_map/ppermute | solution.py:296
  49.1 15.9 %collective-permute-start.7 = (bf16[1,256,1024]{2,1,0:T(8,128)(2,1)}, bf16[1,256,1024]{2,1,0:T(8,128)(2,1)S(1)}, u32[]{:S(2)}, u32[]{:S(2)}) collective-permute-start(bf16[1,256,1024]{2,1,0:T(8,128)(2,1)} %slice.31), channel_id=1, source_target_pairs={{0,96},{32,0},{64,32},{96,64},{1,97},{33,1},{65,33},{97,65},{2,98}... | collective-permute-start | bytes 1572872 | tf_op jit(solution)/shard_map/ppermute | solution.py:296
  81.7 11.7 %all-to-all-start.1 = ((bf16[8,96,256]{2,1,0:T(8,128)(2,1)}), bf16[8,96,256]{2,1,0:T(8,128)(2,1)S(1)}, u32[]{:S(2)}, u32[]{:S(2)}) async-start(bf16[8,96,256]{2,1,0:T(8,128)(2,1)} %bitcast.10), calls=%async_computation.1 | async-start | bytes 786432 | tf_op jit(solution)/shard_map/all_to_all | solution.py:304
  95.1 20.5 %all-to-all-start.2 = ((bf16[8,96,256]{2,1,0:T(8,128)(2,1)}), bf16[8,96,256]{2,1,0:T(8,128)(2,1)S(1)}, u32[]{:S(2)}, u32[]{:S(2)}) async-start(bf16[8,96,256]{2,1,0:T(8,128)(2,1)} %get-tuple-element.51), calls=%async_computation.2 | async-start | bytes 786432 | tf_op jit(solution)/shard_map/all_to_all | solution.py:304
  100.9 10.7 %collective-permute-start.11 = (bf16[4,96,256]{2,1,0:T(8,128)(2,1)}, bf16[4,96,256]{2,1,0:T(8,128)(2,1)S(1)}, u32[]{:S(2)}, u32[]{:S(2)}) collective-permute-start(bf16[4,96,256]{2,1,0:T(8,128)(2,1)} %copy-done.6), channel_id=1, source_target_pairs={{0,16},{16,0},{1,17},{17,1},{2,18},{18,2},{3,19},{19,3},{4,20},{20... | collective-permute-start | bytes 589832 | tf_op jit(solution)/shard_map/ppermute | solution.py:300
  102.0 13.0 %collective-permute-start.12 = (bf16[4,96,256]{2,1,0:T(8,128)(2,1)}, bf16[4,96,256]{2,1,0:T(8,128)(2,1)S(1)}, u32[]{:S(2)}, u32[]{:S(2)}) collective-permute-start(bf16[4,96,256]{2,1,0:T(8,128)(2,1)} %collective-permute-done.9), channel_id=1, source_target_pairs={{0,16},{16,0},{1,17},{17,1},{2,18},{18,2},{3,19},{19,3},{4,20},{20... | collective-permute-start | bytes 589832 | tf_op jit(solution)/shard_map/ppermute | solution.py:300
  122.0 57.4 %all-to-all-start.3 = ((bf16[32,192,128]{2,1,0:T(8,128)(2,1)}), bf16[32,192,128]{2,1,0:T(8,128)(2,1)S(1)}, u32[]{:S(2)}, u32[]{:S(2)}) async-start(bf16[32,192,128]{2,1,0:T(8,128)(2,1)} %backward.1), calls=%async_computation.3 | async-start | bytes 3145728 | tf_op jit(solution)/shard_map/all_to_all | solution.py:304
  129.6 22.0 %collective-permute-start.14 = (bf16[768,256]{1,0:T(8,128)(2,1)S(1)}, bf16[768,256]{1,0:T(8,128)(2,1)S(1)}, u32[]{:S(2)}, u32[]{:S(2)}) collective-permute-start(bf16[768,256]{1,0:T(8,128)(2,1)S(1)} %bitcast.29), channel_id=1, source_target_pairs={{0,16},{16,0},{1,17},{17,1},{2,18},{18,2},{3,19},{19,3},{4,20},{20... | collective-permute-start | bytes 1179656 | tf_op jit(solution)/shard_map/ppermute | solution.py:300
  132.7 18.9 %collective-permute-start.13 = (bf16[768,256]{1,0:T(8,128)(2,1)S(1)}, bf16[768,256]{1,0:T(8,128)(2,1)S(1)}, u32[]{:S(2)}, u32[]{:S(2)}) collective-permute-start(bf16[768,256]{1,0:T(8,128)(2,1)S(1)} %bitcast.30), channel_id=1, source_target_pairs={{0,1},{1,0},{2,3},{3,2},{4,5},{5,4},{6,7},{7,6},{8,9},{9,8},{10,11... | collective-permute-start | bytes 1179656 | tf_op jit(solution)/shard_map/ppermute | solution.py:300
  156.7 15.0 %collective-permute-start.22 = (bf16[48,768]{1,0:T(8,128)(2,1)S(1)}, bf16[48,768]{1,0:T(8,128)(2,1)S(1)}, u32[]{:S(2)}, u32[]{:S(2)}) collective-permute-start(bf16[48,768]{1,0:T(8,128)(2,1)S(1)} %get-tuple-element.66), channel_id=1, source_target_pairs={{0,14},{2,12},{4,10},{6,8},{8,6},{10,4},{12,2},{14,0},{1,15},{3,13... | collective-permute-start | bytes 221192 | tf_op jit(solution)/shard_map/ppermute | solution.py:300
  160.2 19.2 %collective-permute-start.21 = (bf16[48,768]{1,0:T(8,128)(2,1)S(1)}, bf16[48,768]{1,0:T(8,128)(2,1)S(1)}, u32[]{:S(2)}, u32[]{:S(2)}) collective-permute-start(bf16[48,768]{1,0:T(8,128)(2,1)S(1)} %get-tuple-element.65), channel_id=1, source_target_pairs={{0,12},{2,14},{4,8},{6,10},{8,4},{10,6},{12,0},{14,2},{1,13},{3,15... | collective-permute-start | bytes 221192 | tf_op jit(solution)/shard_map/ppermute | solution.py:300
  160.2 27.3 %collective-permute-start.20 = (bf16[48,768]{1,0:T(8,128)(2,1)}, bf16[48,768]{1,0:T(8,128)(2,1)S(1)}, u32[]{:S(2)}, u32[]{:S(2)}) collective-permute-start(bf16[48,768]{1,0:T(8,128)(2,1)} %get-tuple-element.64), channel_id=1, source_target_pairs={{0,10},{2,8},{4,14},{6,12},{8,2},{10,0},{12,6},{14,4},{1,11},{3,9}... | collective-permute-start | bytes 221192 | tf_op jit(solution)/shard_map/ppermute | solution.py:300
  166.5 21.0 %collective-permute-start.19 = (bf16[48,768]{1,0:T(8,128)(2,1)}, bf16[48,768]{1,0:T(8,128)(2,1)S(1)}, u32[]{:S(2)}, u32[]{:S(2)}) collective-permute-start(bf16[48,768]{1,0:T(8,128)(2,1)} %get-tuple-element.63), channel_id=1, source_target_pairs={{0,8},{2,10},{4,12},{6,14},{8,0},{10,2},{12,4},{14,6},{1,9},{3,11}... | collective-permute-start | bytes 221192 | tf_op jit(solution)/shard_map/ppermute | solution.py:300
  167.1 20.4 %collective-permute-start.18 = (bf16[48,768]{1,0:T(8,128)(2,1)S(1)}, bf16[48,768]{1,0:T(8,128)(2,1)S(1)}, u32[]{:S(2)}, u32[]{:S(2)}) collective-permute-start(bf16[48,768]{1,0:T(8,128)(2,1)S(1)} %get-tuple-element.62), channel_id=1, source_target_pairs={{0,6},{2,4},{4,2},{6,0},{8,14},{10,12},{12,10},{14,8},{1,7},{3,5},... | collective-permute-start | bytes 221192 | tf_op jit(solution)/shard_map/ppermute | solution.py:300
  171.7 15.8 %collective-permute-start.17 = (bf16[48,768]{1,0:T(8,128)(2,1)S(1)}, bf16[48,768]{1,0:T(8,128)(2,1)S(1)}, u32[]{:S(2)}, u32[]{:S(2)}) collective-permute-start(bf16[48,768]{1,0:T(8,128)(2,1)S(1)} %get-tuple-element.61), channel_id=1, source_target_pairs={{0,4},{2,6},{4,0},{6,2},{8,12},{10,14},{12,8},{14,10},{1,5},{3,7},... | collective-permute-start | bytes 221192 | tf_op jit(solution)/shard_map/ppermute | solution.py:300
  181.9 21.0 %all-to-all-start.4 = ((f32[8,2,16,192]{3,2,1,0:T(8,128)}), f32[8,2,16,192]{3,2,1,0:T(8,128)S(1)}, u32[]{:S(2)}, u32[]{:S(2)}) async-start(f32[8,2,16,192]{3,2,1,0:T(8,128)} %owned.1), calls=%async_computation.4 | async-start | bytes 524288 | tf_op jit(solution)/shard_map/all_to_all | solution.py:304
  187.6 15.3 %collective-permute-start.23 = (f32[2,24,768]{2,1,0:T(8,128)S(1)}, f32[2,24,768]{2,1,0:T(8,128)S(1)}, u32[]{:S(2)}, u32[]{:S(2)}) collective-permute-start(f32[2,24,768]{2,1,0:T(8,128)S(1)} %bitcast.35), channel_id=1, source_target_pairs={{0,0},{1,4},{2,1},{3,5},{4,2},{5,6},{6,3},{7,7},{8,32},{9,36},{10,... | collective-permute-start | bytes 442376 | tf_op jit(solution)/shard_map/ppermute | solution.py:399
  (18 other events, 186.3 us)

commit v9 on v8

--- a/solution.py
+++ b/solution.py
@@ -263,6 +263,7 @@
         scratch_shapes=[pltpu.VMEM((8, 48, width), F32)],
         compiler_params=params(),
         name="weight_terms",
+        cost_estimate=pl.CostEstimate(flops=24500000000, transcendentals=0, bytes_accessed=0),
     )(place, *operands)
 
 
@@ -375,7 +376,9 @@
     )
     of_core, of_far = swap(for_core, "core"), swap(far_terms, "xh")
     of_far_core = swap(for_far_core, "core")
-    arrived, of_far_core = lax.optimization_barrier((exchange(part.reshape(groups, share, -1), REL), of_far_core))
+    arrived, of_far, of_far_core = lax.optimization_barrier(
+        (exchange(part.reshape(groups, share, -1), REL), of_far, of_far_core)
+    )
     arrived = resident(arrived)
     activated, grad_copies = activation_of(arrived, bias_share, cotangent_share)
     output = activated.T
@@ -389,7 +392,7 @@
     columns = exchange(cut, REL).reshape(2, 4, 2, BLK // groups, 192).sum(axis=0)
     grad_features = columns.transpose(1, 2, 0, 3).reshape(2, BLK // groups, width)
 
-    far_grads = swap(grads, "xh")
+    far_grads, _ = lax.optimization_barrier((swap(grads, "xh"), partial))
     piece, *others = weight_terms_of(
         place, own_terms, of_core, of_far, of_far_core,
         grads, swap(grads, "core"), far_grads, swap(far_grads, "core"),

time: 208 us -> 206 us (level); the launches traced: 204 us -> 205 us
  starting transfers between devices: 79.6 us -> 73.5 us
  local copies, waits for them, and re-layouts: 15.7 us -> 19.2 us
  waiting for transfers between devices: 70.4 us -> 73.1 us
    ppermute x16, waiting for transfers between devices: 54 us -> 59.2 us  [swap(): return lax.ppermute(value, axis, [(i, i ^ flip) for i in range(size)])]
    all_to_all x5, waiting for transfers between devices: 6.66 us -> 2.07 us  [exchange(): return lax.all_to_all(value, axis, 0, 0, tiled=True)]
    ppermute x16, starting transfers between devices: 29.2 us -> 25.6 us  [swap(): return lax.ppermute(value, axis, [(i, i ^ flip) for i in range(size)])]
    unnamed x28 -> x34, local copies, waits for them, and re-layouts: 4.94 us -> 8.39 us
    ppermute x1, waiting for transfers between devices: 9.24 us -> 11.8 us  [per_device(): lax.ppermute(piece.reshape(2, 24, width), ('y', *TGT), to_owner())]
    ppermute x1, starting transfers between devices: 6.04 us -> 3.88 us  [per_device(): lax.ppermute(piece.reshape(2, 24, width), ('y', *TGT), to_owner())]
  transfers between devices with their start and end apart: 29 -> 29, of which waited for: 12 -> 10; matrix products, arithmetic and copies ran while one was open for 8% -> 8% of each run, Pallas kernels for 4% -> 7%
where the time goes in v9:
time: 206 us; the launch traced here: 205 us
  starting transfers between devices  73.5 us (36%)
  waiting for transfers between devices  73.1 us (35%)
  Pallas kernels  29.9 us (15%)
  local copies, waits for them, and re-layouts  19.2 us (9%)
  other arithmetic  7.86 us (4%)
    ppermute x16, waiting for transfers between devices, swap(): return lax.ppermute(value, axis, [(i, i ^ flip) for i in range(size)])  59.2 us
    all_to_all x5, starting transfers between devices, exchange(): return lax.all_to_all(value, axis, 0, 0, tiled=True)  34.7 us
    ppermute x16, starting transfers between devices, swap(): return lax.ppermute(value, axis, [(i, i ^ flip) for i in range(size)])  25.6 us
    ppermute x1, waiting for transfers between devices, per_device(): lax.ppermute(piece.reshape(2, 24, width), ('y', *TGT), to_owner())  11.8 us
    pallas_call x1, Pallas kernels, forward_of(): pl.pallas_call(forward_kernel, in_specs=[smem(), smem()] + [hbm()] * 5 +...  8.49 us
    unnamed x34, local copies, waits for them, and re-layouts  8.39 us
    ppermute x4, starting transfers between devices, step(): return lax.ppermute(value, 'y', [(i, (i + by) % 4) for i in range(4)])  6.5 us
    pallas_call x1, Pallas kernels, backward_of(): pl.pallas_call(backward_kernel, in_specs=[smem(), smem()] + [hbm()] * 5 +...  6.28 us
  transfers between devices with their start and end apart: 29, of which 10 were waited for; matrix products, arithmetic and copies ran while one was open for 8% of the time, Pallas kernels for 7%

profile of v9, /device:TPU:56, one launch (start us, length us, event | category | flops | bytes accessed | tf_op | source)
XLA Modules:
  0.0 204.5 jit_solution(11100813172956050219)
XLA Ops:
  1.5 4.9 %adjacency.1.own_ref = bf16[2,256,1024]{2,1,0:T(8,128)(2,1)S(1)} custom-call(s32[2,2]{1,0:T(2,128)} %count_ref.1, s32[2,256,8,128]{3,2,1,0:T(8,128)} %values_ref.1), custom_call_target="tpu_custom_call" | custom-call | tf_op jit(solution)/shard_map/adjacency/pallas_call | solution.py:61
  9.7 2.6 %collective-permute-start.3 = (bf16[1,112,768]{2,1,0:T(8,128)(2,1)}, bf16[1,112,768]{2,1,0:T(8,128)(2,1)}, u32[]{:S(2)}, u32[]{:S(2)}) collective-permute-start(bf16[1,112,768]{2,1,0:T(8,128)(2,1)} %get-tuple-element.78), channel_id=1, source_target_pairs={{0,64},{32,96},{64,0},{96,32},{1,65},{33,97},{65,1},{97,33},{2,66}... | collective-permute-start | bytes 516104 | tf_op jit(solution)/shard_map/ppermute | solution.py:310
  16.2 2.6 %outgoing.1 = bf16[32,192,128]{2,1,0:T(8,128)(2,1)} custom-call(s32[6]{0:T(128)} %stack.27.place_ref, s32[32,32]{1,0:T(8,128)} %table_ref.3, bf16[256,768]{1,0:T(8,128)(2,1)} %features_ref), custom_call_target="tpu_custom_call" | custom-call | tf_op jit(solution)/shard_map/outgoing/pallas_call | solution.py:85
  18.8 11.4 %all-to-all-start = ((bf16[32,192,128]{2,1,0:T(8,128)(2,1)}), bf16[32,192,128]{2,1,0:T(8,128)(2,1)}, u32[]{:S(2)}, u32[]{:S(2)}) async-start(bf16[32,192,128]{2,1,0:T(8,128)(2,1)} %outgoing.1), calls=%async_computation | async-start | bytes 3145728 | tf_op jit(solution)/shard_map/all_to_all | solution.py:305
  37.9 3.0 %collective-permute-start.5 = (bf16[4,96,768]{2,1,0:T(8,128)(2,1)}, bf16[4,96,768]{2,1,0:T(8,128)(2,1)}, u32[]{:S(2)}, u32[]{:S(2)}) collective-permute-start(bf16[4,96,768]{2,1,0:T(8,128)(2,1)} %pad_maximum_fusion.1), channel_id=1, source_target_pairs={{0,16},{16,0},{1,17},{17,1},{2,18},{18,2},{3,19},{19,3},{4,20},{20... | collective-permute-start | bytes 1769480 | tf_op jit(solution)/shard_map/ppermute | solution.py:301
  49.4 15.7 %collective-permute-done.5 = bf16[4,96,768]{2,1,0:T(8,128)(2,1)} collective-permute-done((bf16[4,96,768]{2,1,0:T(8,128)(2,1)}, bf16[4,96,768]{2,1,0:T(8,128)(2,1)}, u32[]{:S(2)}, u32[]{:S(2)}) %collective-permute-start.5) | collective-permute-done | bytes 589856 | tf_op jit(solution)/shard_map/ppermute | solution.py:301
  67.1 2.8 %collective-permute-done.8.w_theirs_ref = bf16[4,192,768]{2,1,0:T(8,128)(2,1)S(1)} collective-permute-done((bf16[4,192,768]{2,1,0:T(8,128)(2,1)S(1)}, bf16[4,192,768]{2,1,0:T(8,128)(2,1)S(1)}, u32[]{:S(2)}, u32[]{:S(2)}) %collective-permute-start.8) | collective-permute-done | bytes 1179680 | tf_op jit(solution)/shard_map/ppermute | solution.py:301
  72.0 8.5 %forward.1 = (bf16[4,96,256]{2,1,0:T(8,128)(2,1)S(1)}, bf16[4,96,256]{2,1,0:T(8,128)(2,1)S(1)}, bf16[4,96,256]{2,1,0:T(8,128)(2,1)S(1)}, bf16[4,96,256]{2,1,0:T(8,128)(2,1)S(1)}, bf16[768,256]{1,0:T(8,128)(2,1)}) custom-call(s32[6]{0:T(128)} %stack.27.place_ref, s32[128]{0:T(128)} %pad_add_fusion.slot_ref, bf16[2,256,1024]{2,1,0:T(8,128)(2,1)} %copy-done.1, ...), custom_call_target="tpu_custom_call" | custom-call | tf_op jit(solution)/shard_map/forward/pallas_call | solution.py:164
  81.8 5.3 %all-to-all-start.1 = ((bf16[8,96,256]{2,1,0:T(8,128)(2,1)}), bf16[8,96,256]{2,1,0:T(8,128)(2,1)S(1)}, u32[]{:S(2)}, u32[]{:S(2)}) async-start(bf16[8,96,256]{2,1,0:T(8,128)(2,1)} %bitcast.10), calls=%async_computation.1 | async-start | bytes 786432 | tf_op jit(solution)/shard_map/all_to_all | solution.py:305
  88.0 9.3 %collective-permute-done.9.far_ref = bf16[4,96,256]{2,1,0:T(8,128)(2,1)S(1)} collective-permute-done((bf16[4,96,256]{2,1,0:T(8,128)(2,1)}, bf16[4,96,256]{2,1,0:T(8,128)(2,1)S(1)}, u32[]{:S(2)}, u32[]{:S(2)}) %collective-permute-start.9) | collective-permute-done | bytes 196640 | tf_op jit(solution)/shard_map/ppermute | solution.py:301
  99.8 5.1 %all-to-all-start.2 = ((bf16[8,96,256]{2,1,0:T(8,128)(2,1)}), bf16[8,96,256]{2,1,0:T(8,128)(2,1)S(1)}, u32[]{:S(2)}, u32[]{:S(2)}) async-start(bf16[8,96,256]{2,1,0:T(8,128)(2,1)} %get-tuple-element.54), calls=%async_computation.2 | async-start | bytes 786432 | tf_op jit(solution)/shard_map/all_to_all | solution.py:305
  104.9 3.4 %collective-permute-start.12 = (bf16[4,96,256]{2,1,0:T(8,128)(2,1)}, bf16[4,96,256]{2,1,0:T(8,128)(2,1)S(1)}, u32[]{:S(2)}, u32[]{:S(2)}) collective-permute-start(bf16[4,96,256]{2,1,0:T(8,128)(2,1)} %collective-permute-done.10), channel_id=1, source_target_pairs={{0,16},{16,0},{1,17},{17,1},{2,18},{18,2},{3,19},{19,3},{4,20},{20... | collective-permute-start | bytes 589832 | tf_op jit(solution)/shard_map/ppermute | solution.py:301
  109.0 7.2 %collective-permute-done.12.far_core_ref = bf16[4,96,256]{2,1,0:T(8,128)(2,1)S(1)} collective-permute-done((bf16[4,96,256]{2,1,0:T(8,128)(2,1)}, bf16[4,96,256]{2,1,0:T(8,128)(2,1)S(1)}, u32[]{:S(2)}, u32[]{:S(2)}) %collective-permute-start.12) | collective-permute-done | bytes 196640 | tf_op jit(solution)/shard_map/ppermute | solution.py:301
  118.0 6.3 %backward.1 = bf16[32,192,128]{2,1,0:T(8,128)(2,1)} custom-call(s32[6]{0:T(128)} %stack.27.place_ref, s32[128]{0:T(128)} %pad_add_fusion.slot_ref, bf16[2,256,1024]{2,1,0:T(8,128)(2,1)} %copy-done.1, bf16[2,256,1024]{2,1,0:T(8,128)(2,1)} %copy-done.12, bf16[2,256,1024]{2,1,0:T(8,128)(2,1)} %copy-done.11, bf16[1,256,1024]{2,1,0:T(8,128)(2,1)} %copy-done.14, ...), custom_call_target="tpu_custom_call" | custom-call | tf_op jit(solution)/shard_map/backward/pallas_call | solution.py:226
  124.3 7.8 %all-to-all-start.3 = ((bf16[32,192,128]{2,1,0:T(8,128)(2,1)}), bf16[32,192,128]{2,1,0:T(8,128)(2,1)S(1)}, u32[]{:S(2)}, u32[]{:S(2)}) async-start(bf16[32,192,128]{2,1,0:T(8,128)(2,1)} %backward.1), calls=%async_computation.3 | async-start | bytes 3145728 | tf_op jit(solution)/shard_map/all_to_all | solution.py:305
  137.3 3.4 %weight_terms.1 = (f32[48,768]{1,0:T(8,128)S(1)}, bf16[48,768]{1,0:T(8,128)(2,1)S(1)}, bf16[48,768]{1,0:T(8,128)(2,1)S(1)}, bf16[48,768]{1,0:T(8,128)(2,1)}, bf1...) custom-call(s32[6]{0:T(128)} %stack.27.place_ref, ...), custom_call_target="tpu_custom_call" | custom-call | flops 24500000768 | tf_op jit(solution)/shard_map/weight_terms/pallas_call | solution.py:258
  140.9 2.7 %collective-permute-start.17 = (bf16[48,768]{1,0:T(8,128)(2,1)S(1)}, bf16[48,768]{1,0:T(8,128)(2,1)S(1)}, u32[]{:S(2)}, u32[]{:S(2)}) collective-permute-start(bf16[48,768]{1,0:T(8,128)(2,1)S(1)} %get-tuple-element.65), channel_id=1, source_target_pairs={{0,4},{2,6},{4,0},{6,2},{8,12},{10,14},{12,8},{14,10},{1,5},{3,7},... | collective-permute-start | bytes 221192 | tf_op jit(solution)/shard_map/ppermute | solution.py:301
  144.2 4.5 %collective-permute-start.19 = (bf16[48,768]{1,0:T(8,128)(2,1)}, bf16[48,768]{1,0:T(8,128)(2,1)S(1)}, u32[]{:S(2)}, u32[]{:S(2)}) collective-permute-start(bf16[48,768]{1,0:T(8,128)(2,1)} %get-tuple-element.67), channel_id=1, source_target_pairs={{0,8},{2,10},{4,12},{6,14},{8,0},{10,2},{12,4},{14,6},{1,9},{3,11}... | collective-permute-start | bytes 221192 | tf_op jit(solution)/shard_map/ppermute | solution.py:301
  149.8 20.0 %collective-permute-done.16 = bf16[48,768]{1,0:T(8,128)(2,1)S(1)} collective-permute-done((bf16[48,768]{1,0:T(8,128)(2,1)S(1)}, bf16[48,768]{1,0:T(8,128)(2,1)S(1)}, u32[]{:S(2)}, u32[]{:S(2)}) %collective-permute-start.16) | collective-permute-done | bytes 73760 | tf_op jit(solution)/shard_map/ppermute | solution.py:301
  169.8 4.0 %collective-permute-start.21 = (bf16[48,768]{1,0:T(8,128)(2,1)}, bf16[48,768]{1,0:T(8,128)(2,1)S(1)}, u32[]{:S(2)}, u32[]{:S(2)}) collective-permute-start(bf16[48,768]{1,0:T(8,128)(2,1)} %get-tuple-element.69), channel_id=1, source_target_pairs={{0,12},{2,14},{4,8},{6,10},{8,4},{10,6},{12,0},{14,2},{1,13},{3,15... | collective-permute-start | bytes 221192 | tf_op jit(solution)/shard_map/ppermute | solution.py:301
  176.2 3.4 %collective-permute-start.22 = (bf16[48,768]{1,0:T(8,128)(2,1)}, bf16[48,768]{1,0:T(8,128)(2,1)S(1)}, u32[]{:S(2)}, u32[]{:S(2)}) collective-permute-start(bf16[48,768]{1,0:T(8,128)(2,1)} %get-tuple-element.70), channel_id=1, source_target_pairs={{0,14},{2,12},{4,10},{6,8},{8,6},{10,4},{12,2},{14,0},{1,15},{3,13... | collective-permute-start | bytes 221192 | tf_op jit(solution)/shard_map/ppermute | solution.py:301
  182.1 5.1 %all-to-all-start.4 = ((f32[8,2,16,192]{3,2,1,0:T(8,128)}), f32[8,2,16,192]{3,2,1,0:T(8,128)S(1)}, u32[]{:S(2)}, u32[]{:S(2)}) async-start(f32[8,2,16,192]{3,2,1,0:T(8,128)} %owned.1), calls=%async_computation.4 | async-start | bytes 524288 | tf_op jit(solution)/shard_map/all_to_all | solution.py:305
  187.3 3.9 %collective-permute-start.23 = (f32[2,24,768]{2,1,0:T(8,128)S(1)}, f32[2,24,768]{2,1,0:T(8,128)S(1)}, u32[]{:S(2)}, u32[]{:S(2)}) collective-permute-start(f32[2,24,768]{2,1,0:T(8,128)S(1)} %bitcast.35), channel_id=1, source_target_pairs={{0,0},{1,4},{2,1},{3,5},{4,2},{5,6},{6,3},{7,7},{8,32},{9,36},{10,... | collective-permute-start | bytes 442376 | tf_op jit(solution)/shard_map/ppermute | solution.py:402
  191.2 11.8 %collective-permute-done.23 = f32[2,24,768]{2,1,0:T(8,128)S(1)} collective-permute-done((f32[2,24,768]{2,1,0:T(8,128)S(1)}, f32[2,24,768]{2,1,0:T(8,128)S(1)}, u32[]{:S(2)}, u32[]{:S(2)}) %collective-permute-start.23) | collective-permute-done | bytes 147488 | tf_op jit(solution)/shard_map/ppermute | solution.py:402
  (100 shorter events, 48.9 us)
Async XLA Ops:
  9.5 23.9 %collective-permute-start.2 = (bf16[1,112,768]{2,1,0:T(8,128)(2,1)}, bf16[1,112,768]{2,1,0:T(8,128)(2,1)}, u32[]{:S(2)}, u32[]{:S(2)}) collective-permute-start(bf16[1,112,768]{2,1,0:T(8,128)(2,1)} %get-tuple-element.77), channel_id=1, source_target_pairs={{0,32},{32,64},{64,96},{96,0},{1,33},{33,65},{65,97},{97,1},{2,34}... | collective-permute-start | bytes 516104 | tf_op jit(solution)/shard_map/ppermute | solution.py:310
  9.7 24.6 %collective-permute-start.3 = (bf16[1,112,768]{2,1,0:T(8,128)(2,1)}, bf16[1,112,768]{2,1,0:T(8,128)(2,1)}, u32[]{:S(2)}, u32[]{:S(2)}) collective-permute-start(bf16[1,112,768]{2,1,0:T(8,128)(2,1)} %get-tuple-element.78), channel_id=1, source_target_pairs={{0,64},{32,96},{64,0},{96,32},{1,65},{33,97},{65,1},{97,33},{2,66}... | collective-permute-start | bytes 516104 | tf_op jit(solution)/shard_map/ppermute | solution.py:310
  12.3 22.9 %collective-permute-start.4 = (bf16[1,112,768]{2,1,0:T(8,128)(2,1)}, bf16[1,112,768]{2,1,0:T(8,128)(2,1)}, u32[]{:S(2)}, u32[]{:S(2)}) collective-permute-start(bf16[1,112,768]{2,1,0:T(8,128)(2,1)} %get-tuple-element.79), channel_id=1, source_target_pairs={{0,96},{32,0},{64,32},{96,64},{1,97},{33,1},{65,33},{97,65},{2,98}... | collective-permute-start | bytes 516104 | tf_op jit(solution)/shard_map/ppermute | solution.py:310
  12.3 31.3 %collective-permute-start.1 = (bf16[2,256,1024]{2,1,0:T(8,128)(2,1)S(1)}, bf16[2,256,1024]{2,1,0:T(8,128)(2,1)S(1)}, u32[]{:S(2)}, u32[]{:S(2)}) collective-permute-start(bf16[2,256,1024]{2,1,0:T(8,128)(2,1)S(1)} %adjacency.1.own_ref), channel_id=1, source_target_pairs={{0,96},{32,0},{64,32},{96,64},{1,97},{33,1},{65,33},{97,65},{2,98}... | collective-permute-start | bytes 3145736 | tf_op jit(solution)/shard_map/ppermute | solution.py:297
  13.2 30.4 %collective-permute-start = (bf16[2,256,1024]{2,1,0:T(8,128)(2,1)S(1)}, bf16[2,256,1024]{2,1,0:T(8,128)(2,1)S(1)}, u32[]{:S(2)}, u32[]{:S(2)}) collective-permute-start(bf16[2,256,1024]{2,1,0:T(8,128)(2,1)S(1)} %adjacency.1.own_ref), channel_id=1, source_target_pairs={{0,32},{32,64},{64,96},{96,0},{1,33},{33,65},{65,97},{97,1},{2,34}... | collective-permute-start | bytes 3145736 | tf_op jit(solution)/shard_map/ppermute | solution.py:297
  18.8 53.2 %all-to-all-start = ((bf16[32,192,128]{2,1,0:T(8,128)(2,1)}), bf16[32,192,128]{2,1,0:T(8,128)(2,1)}, u32[]{:S(2)}, u32[]{:S(2)}) async-start(bf16[32,192,128]{2,1,0:T(8,128)(2,1)} %outgoing.1), calls=%async_computation | async-start | bytes 3145728 | tf_op jit(solution)/shard_map/all_to_all | solution.py:305
  37.9 27.2 %collective-permute-start.5 = (bf16[4,96,768]{2,1,0:T(8,128)(2,1)}, bf16[4,96,768]{2,1,0:T(8,128)(2,1)}, u32[]{:S(2)}, u32[]{:S(2)}) collective-permute-start(bf16[4,96,768]{2,1,0:T(8,128)(2,1)} %pad_maximum_fusion.1), channel_id=1, source_target_pairs={{0,16},{16,0},{1,17},{17,1},{2,18},{18,2},{3,19},{19,3},{4,20},{20... | collective-permute-start | bytes 1769480 | tf_op jit(solution)/shard_map/ppermute | solution.py:301
  46.2 18.9 %collective-permute-start.7 = (bf16[1,256,1024]{2,1,0:T(8,128)(2,1)}, bf16[1,256,1024]{2,1,0:T(8,128)(2,1)S(1)}, u32[]{:S(2)}, u32[]{:S(2)}) collective-permute-start(bf16[1,256,1024]{2,1,0:T(8,128)(2,1)} %slice.31), channel_id=1, source_target_pairs={{0,96},{32,0},{64,32},{96,64},{1,97},{33,1},{65,33},{97,65},{2,98}... | collective-permute-start | bytes 1572872 | tf_op jit(solution)/shard_map/ppermute | solution.py:297
  47.2 18.0 %collective-permute-start.6 = (bf16[1,256,1024]{2,1,0:T(8,128)(2,1)}, bf16[1,256,1024]{2,1,0:T(8,128)(2,1)S(1)}, u32[]{:S(2)}, u32[]{:S(2)}) collective-permute-start(bf16[1,256,1024]{2,1,0:T(8,128)(2,1)} %slice.30), channel_id=1, source_target_pairs={{0,32},{32,64},{64,96},{96,0},{1,33},{33,65},{65,97},{97,1},{2,34}... | collective-permute-start | bytes 1572872 | tf_op jit(solution)/shard_map/ppermute | solution.py:297
  81.8 16.2 %all-to-all-start.1 = ((bf16[8,96,256]{2,1,0:T(8,128)(2,1)}), bf16[8,96,256]{2,1,0:T(8,128)(2,1)S(1)}, u32[]{:S(2)}, u32[]{:S(2)}) async-start(bf16[8,96,256]{2,1,0:T(8,128)(2,1)} %bitcast.10), calls=%async_computation.1 | async-start | bytes 786432 | tf_op jit(solution)/shard_map/all_to_all | solution.py:305
  87.2 10.2 %collective-permute-start.9 = (bf16[4,96,256]{2,1,0:T(8,128)(2,1)}, bf16[4,96,256]{2,1,0:T(8,128)(2,1)S(1)}, u32[]{:S(2)}, u32[]{:S(2)}) collective-permute-start(bf16[4,96,256]{2,1,0:T(8,128)(2,1)} %copy-done.10), channel_id=1, source_target_pairs={{0,16},{16,0},{1,17},{17,1},{2,18},{18,2},{3,19},{19,3},{4,20},{20... | collective-permute-start | bytes 589832 | tf_op jit(solution)/shard_map/ppermute | solution.py:301
  99.8 17.1 %all-to-all-start.2 = ((bf16[8,96,256]{2,1,0:T(8,128)(2,1)}), bf16[8,96,256]{2,1,0:T(8,128)(2,1)S(1)}, u32[]{:S(2)}, u32[]{:S(2)}) async-start(bf16[8,96,256]{2,1,0:T(8,128)(2,1)} %get-tuple-element.54), calls=%async_computation.2 | async-start | bytes 786432 | tf_op jit(solution)/shard_map/all_to_all | solution.py:305
  104.9 11.3 %collective-permute-start.12 = (bf16[4,96,256]{2,1,0:T(8,128)(2,1)}, bf16[4,96,256]{2,1,0:T(8,128)(2,1)S(1)}, u32[]{:S(2)}, u32[]{:S(2)}) collective-permute-start(bf16[4,96,256]{2,1,0:T(8,128)(2,1)} %collective-permute-done.10), channel_id=1, source_target_pairs={{0,16},{16,0},{1,17},{17,1},{2,18},{18,2},{3,19},{19,3},{4,20},{20... | collective-permute-start | bytes 589832 | tf_op jit(solution)/shard_map/ppermute | solution.py:301
  116.9 15.5 %collective-permute-start.14 = (bf16[768,256]{1,0:T(8,128)(2,1)S(1)}, bf16[768,256]{1,0:T(8,128)(2,1)S(1)}, u32[]{:S(2)}, u32[]{:S(2)}) collective-permute-start(bf16[768,256]{1,0:T(8,128)(2,1)S(1)} %bitcast.28), channel_id=1, source_target_pairs={{0,16},{16,0},{1,17},{17,1},{2,18},{18,2},{3,19},{19,3},{4,20},{20... | collective-permute-start | bytes 1179656 | tf_op jit(solution)/shard_map/ppermute | solution.py:301
  124.3 55.3 %all-to-all-start.3 = ((bf16[32,192,128]{2,1,0:T(8,128)(2,1)}), bf16[32,192,128]{2,1,0:T(8,128)(2,1)S(1)}, u32[]{:S(2)}, u32[]{:S(2)}) async-start(bf16[32,192,128]{2,1,0:T(8,128)(2,1)} %backward.1), calls=%async_computation.3 | async-start | bytes 3145728 | tf_op jit(solution)/shard_map/all_to_all | solution.py:305
  140.7 29.1 %collective-permute-start.16 = (bf16[48,768]{1,0:T(8,128)(2,1)S(1)}, bf16[48,768]{1,0:T(8,128)(2,1)S(1)}, u32[]{:S(2)}, u32[]{:S(2)}) collective-permute-start(bf16[48,768]{1,0:T(8,128)(2,1)S(1)} %get-tuple-element.64), channel_id=1, source_target_pairs={{0,2},{2,0},{4,6},{6,4},{8,10},{10,8},{12,14},{14,12},{1,3},{3,1},... | collective-permute-start | bytes 221192 | tf_op jit(solution)/shard_map/ppermute | solution.py:301
  140.9 35.2 %collective-permute-start.17 = (bf16[48,768]{1,0:T(8,128)(2,1)S(1)}, bf16[48,768]{1,0:T(8,128)(2,1)S(1)}, u32[]{:S(2)}, u32[]{:S(2)}) collective-permute-start(bf16[48,768]{1,0:T(8,128)(2,1)S(1)} %get-tuple-element.65), channel_id=1, source_target_pairs={{0,4},{2,6},{4,0},{6,2},{8,12},{10,14},{12,8},{14,10},{1,5},{3,7},... | collective-permute-start | bytes 221192 | tf_op jit(solution)/shard_map/ppermute | solution.py:301
  143.6 43.6 %collective-permute-start.18 = (bf16[48,768]{1,0:T(8,128)(2,1)}, bf16[48,768]{1,0:T(8,128)(2,1)S(1)}, u32[]{:S(2)}, u32[]{:S(2)}) collective-permute-start(bf16[48,768]{1,0:T(8,128)(2,1)} %get-tuple-element.66), channel_id=1, source_target_pairs={{0,6},{2,4},{4,2},{6,0},{8,14},{10,12},{12,10},{14,8},{1,7},{3,5},... | collective-permute-start | bytes 221192 | tf_op jit(solution)/shard_map/ppermute | solution.py:301
  144.2 43.0 %collective-permute-start.19 = (bf16[48,768]{1,0:T(8,128)(2,1)}, bf16[48,768]{1,0:T(8,128)(2,1)S(1)}, u32[]{:S(2)}, u32[]{:S(2)}) collective-permute-start(bf16[48,768]{1,0:T(8,128)(2,1)} %get-tuple-element.67), channel_id=1, source_target_pairs={{0,8},{2,10},{4,12},{6,14},{8,0},{10,2},{12,4},{14,6},{1,9},{3,11}... | collective-permute-start | bytes 221192 | tf_op jit(solution)/shard_map/ppermute | solution.py:301
  148.7 38.5 %collective-permute-start.20 = (bf16[48,768]{1,0:T(8,128)(2,1)}, bf16[48,768]{1,0:T(8,128)(2,1)S(1)}, u32[]{:S(2)}, u32[]{:S(2)}) collective-permute-start(bf16[48,768]{1,0:T(8,128)(2,1)} %get-tuple-element.68), channel_id=1, source_target_pairs={{0,10},{2,8},{4,14},{6,12},{8,2},{10,0},{12,6},{14,4},{1,11},{3,9}... | collective-permute-start | bytes 221192 | tf_op jit(solution)/shard_map/ppermute | solution.py:301
  169.8 17.4 %collective-permute-start.21 = (bf16[48,768]{1,0:T(8,128)(2,1)}, bf16[48,768]{1,0:T(8,128)(2,1)S(1)}, u32[]{:S(2)}, u32[]{:S(2)}) collective-permute-start(bf16[48,768]{1,0:T(8,128)(2,1)} %get-tuple-element.69), channel_id=1, source_target_pairs={{0,12},{2,14},{4,8},{6,10},{8,4},{10,6},{12,0},{14,2},{1,13},{3,15... | collective-permute-start | bytes 221192 | tf_op jit(solution)/shard_map/ppermute | solution.py:301
  176.2 11.0 %collective-permute-start.22 = (bf16[48,768]{1,0:T(8,128)(2,1)}, bf16[48,768]{1,0:T(8,128)(2,1)S(1)}, u32[]{:S(2)}, u32[]{:S(2)}) collective-permute-start(bf16[48,768]{1,0:T(8,128)(2,1)} %get-tuple-element.70), channel_id=1, source_target_pairs={{0,14},{2,12},{4,10},{6,8},{8,6},{10,4},{12,2},{14,0},{1,15},{3,13... | collective-permute-start | bytes 221192 | tf_op jit(solution)/shard_map/ppermute | solution.py:301
  182.1 20.9 %all-to-all-start.4 = ((f32[8,2,16,192]{3,2,1,0:T(8,128)}), f32[8,2,16,192]{3,2,1,0:T(8,128)S(1)}, u32[]{:S(2)}, u32[]{:S(2)}) async-start(f32[8,2,16,192]{3,2,1,0:T(8,128)} %owned.1), calls=%async_computation.4 | async-start | bytes 524288 | tf_op jit(solution)/shard_map/all_to_all | solution.py:305
  187.3 15.7 %collective-permute-start.23 = (f32[2,24,768]{2,1,0:T(8,128)S(1)}, f32[2,24,768]{2,1,0:T(8,128)S(1)}, u32[]{:S(2)}, u32[]{:S(2)}) collective-permute-start(f32[2,24,768]{2,1,0:T(8,128)S(1)} %bitcast.35), channel_id=1, source_target_pairs={{0,0},{1,4},{2,1},{3,5},{4,2},{5,6},{6,3},{7,7},{8,32},{9,36},{10,... | collective-permute-start | bytes 442376 | tf_op jit(solution)/shard_map/ppermute | solution.py:402
  (21 other events, 140.8 us)

commit v10 on v8

--- a/solution.py
+++ b/solution.py
@@ -160,7 +160,7 @@
 def forward_of(place, slots, adjacency, fetched, w_mine, w_theirs):
     _, rows, wide = adjacency[0].shape
     width = w_mine.shape[2]
-    half = jax.ShapeDtypeStruct((4, 96, rows), BF16)
+    half = pltpu.MemorySpace.HBM((4, 96, rows), BF16)
     return pl.pallas_call(
         forward_kernel,
         in_specs=[smem(), smem()] + [hbm()] * 5 + [vmem()] * 3,
@@ -263,6 +263,7 @@
         scratch_shapes=[pltpu.VMEM((8, 48, width), F32)],
         compiler_params=params(),
         name="weight_terms",
+        cost_estimate=pl.CostEstimate(flops=24500000000, transcendentals=0, bytes_accessed=0),
     )(place, *operands)
 
 
@@ -380,16 +381,18 @@
     activated, grad_copies = activation_of(arrived, bias_share, cotangent_share)
     output = activated.T
     of_far_core = swap(of_far_core, "xh")
-    grads, of_core, of_far, of_far_core = lax.optimization_barrier(
-        (exchange(grad_copies, REL).reshape(width, -1), of_core, of_far, of_far_core)
-    )
+    grad_copies, of_far = lax.optimization_barrier((grad_copies, of_far))
+    grads, of_core, of_far_core = lax.optimization_barrier(
+        (exchange(grad_copies, REL).reshape(width, -1), of_core, of_far_core)
+    )
+    of_core, of_far, of_far_core = in_hbm(of_core), in_hbm(of_far), in_hbm(of_far_core)
     partial = backward_of(place, slots, adjacency, resident(grads), w_mine, w_theirs, owners)
     returned = resident(exchange(in_hbm(partial), TGT))
     cut = owned_of(place, source_blocks, returned, groups)
     columns = exchange(cut, REL).reshape(2, 4, 2, BLK // groups, 192).sum(axis=0)
     grad_features = columns.transpose(1, 2, 0, 3).reshape(2, BLK // groups, width)
 
-    far_grads = swap(grads, "xh")
+    far_grads, _ = lax.optimization_barrier((swap(grads, "xh"), partial))
     piece, *others = weight_terms_of(
         place, own_terms, of_core, of_far, of_far_core,
         grads, swap(grads, "core"), far_grads, swap(far_grads, "core"),

time: 208 us -> 202 us (0.971)
  starting transfers between devices: 79.6 us -> 73.7 us
  waiting for transfers between devices: 70.4 us -> 73.7 us
    ppermute x16, starting transfers between devices: 29.2 us -> 25.7 us  [swap(): return lax.ppermute(value, axis, [(i, i ^ flip) for i in range(size)])]
    ppermute x1, waiting for transfers between devices: 9.24 us -> 11.8 us  [per_device(): lax.ppermute(piece.reshape(2, 24, width), ('y', *TGT), to_owner())]
    ppermute x1, starting transfers between devices: 6.04 us -> 3.85 us  [per_device(): lax.ppermute(piece.reshape(2, 24, width), ('y', *TGT), to_owner())]
    unnamed x28 -> x24, local copies, waits for them, and re-layouts: 4.94 us -> 2.94 us
  transfers between devices with their start and end apart: 29 -> 29, of which waited for: 12 -> 12; matrix products, arithmetic and copies ran while one was open for 8% -> 8% of each run, Pallas kernels for 4% -> 9%
where the time goes in v10:
time: 202 us; the launch traced here: 200 us
  starting transfers between devices  73.7 us (36%)
  waiting for transfers between devices  73.7 us (36%)
  Pallas kernels  30.5 us (15%)
  local copies, waits for them, and re-layouts  13.7 us (7%)
  other arithmetic  7.92 us (4%)
    ppermute x16, waiting for transfers between devices, swap(): return lax.ppermute(value, axis, [(i, i ^ flip) for i in range(size)])  54.1 us
    all_to_all x5, starting transfers between devices, exchange(): return lax.all_to_all(value, axis, 0, 0, tiled=True)  34.9 us
    ppermute x16, starting transfers between devices, swap(): return lax.ppermute(value, axis, [(i, i ^ flip) for i in range(size)])  25.7 us
    ppermute x1, waiting for transfers between devices, per_device(): lax.ppermute(piece.reshape(2, 24, width), ('y', *TGT), to_owner())  11.8 us
    pallas_call x1, Pallas kernels, forward_of(): pl.pallas_call(forward_kernel, in_specs=[smem(), smem()] + [hbm()] * 5 +...  8.51 us
    all_to_all x5, waiting for transfers between devices, exchange(): return lax.all_to_all(value, axis, 0, 0, tiled=True)  7.76 us
    ppermute x4, starting transfers between devices, step(): return lax.ppermute(value, 'y', [(i, (i + by) % 4) for i in range(4)])  6.5 us
    pallas_call x1, Pallas kernels, backward_of(): pl.pallas_call(backward_kernel, in_specs=[smem(), smem()] + [hbm()] * 5 +...  6.3 us
  transfers between devices with their start and end apart: 29, of which 12 were waited for; matrix products, arithmetic and copies ran while one was open for 8% of the time, Pallas kernels for 9%

profile of v10, /device:TPU:56, one launch (start us, length us, event | category | flops | bytes accessed | tf_op | source)
XLA Modules:
  0.0 200.5 jit_solution(11147210829737529136)
XLA Ops:
  1.5 4.9 %adjacency.1.own_ref = bf16[2,256,1024]{2,1,0:T(8,128)(2,1)S(1)} custom-call(s32[2,2]{1,0:T(2,128)} %count_ref.1, s32[2,256,8,128]{3,2,1,0:T(8,128)} %values_ref.1), custom_call_target="tpu_custom_call" | custom-call | tf_op jit(solution)/shard_map/adjacency/pallas_call | solution.py:61
  9.7 2.6 %collective-permute-start.3 = (bf16[1,112,768]{2,1,0:T(8,128)(2,1)}, bf16[1,112,768]{2,1,0:T(8,128)(2,1)}, u32[]{:S(2)}, u32[]{:S(2)}) collective-permute-start(bf16[1,112,768]{2,1,0:T(8,128)(2,1)} %get-tuple-element.78), channel_id=1, source_target_pairs={{0,64},{32,96},{64,0},{96,32},{1,65},{33,97},{65,1},{97,33},{2,66}... | collective-permute-start | bytes 516104 | tf_op jit(solution)/shard_map/ppermute | solution.py:310
  16.3 2.6 %outgoing.1 = bf16[32,192,128]{2,1,0:T(8,128)(2,1)} custom-call(s32[6]{0:T(128)} %stack.27.place_ref, s32[32,32]{1,0:T(8,128)} %table_ref.3, bf16[256,768]{1,0:T(8,128)(2,1)} %features_ref), custom_call_target="tpu_custom_call" | custom-call | tf_op jit(solution)/shard_map/outgoing/pallas_call | solution.py:85
  18.9 11.4 %all-to-all-start = ((bf16[32,192,128]{2,1,0:T(8,128)(2,1)}), bf16[32,192,128]{2,1,0:T(8,128)(2,1)}, u32[]{:S(2)}, u32[]{:S(2)}) async-start(bf16[32,192,128]{2,1,0:T(8,128)(2,1)} %outgoing.1), calls=%async_computation | async-start | bytes 3145728 | tf_op jit(solution)/shard_map/all_to_all | solution.py:305
  38.0 3.0 %collective-permute-start.5 = (bf16[4,96,768]{2,1,0:T(8,128)(2,1)}, bf16[4,96,768]{2,1,0:T(8,128)(2,1)}, u32[]{:S(2)}, u32[]{:S(2)}) collective-permute-start(bf16[4,96,768]{2,1,0:T(8,128)(2,1)} %pad_maximum_fusion.1), channel_id=1, source_target_pairs={{0,16},{16,0},{1,17},{17,1},{2,18},{18,2},{3,19},{19,3},{4,20},{20... | collective-permute-start | bytes 1769480 | tf_op jit(solution)/shard_map/ppermute | solution.py:301
  49.5 15.7 %collective-permute-done.5 = bf16[4,96,768]{2,1,0:T(8,128)(2,1)} collective-permute-done((bf16[4,96,768]{2,1,0:T(8,128)(2,1)}, bf16[4,96,768]{2,1,0:T(8,128)(2,1)}, u32[]{:S(2)}, u32[]{:S(2)}) %collective-permute-start.5) | collective-permute-done | bytes 589856 | tf_op jit(solution)/shard_map/ppermute | solution.py:301
  67.1 2.8 %collective-permute-done.8.w_theirs_ref = bf16[4,192,768]{2,1,0:T(8,128)(2,1)S(1)} collective-permute-done((bf16[4,192,768]{2,1,0:T(8,128)(2,1)S(1)}, bf16[4,192,768]{2,1,0:T(8,128)(2,1)S(1)}, u32[]{:S(2)}, u32[]{:S(2)}) %collective-permute-start.8) | collective-permute-done | bytes 1179680 | tf_op jit(solution)/shard_map/ppermute | solution.py:301
  72.0 8.5 %forward.1 = (bf16[4,96,256]{2,1,0:T(8,128)(2,1)}, bf16[4,96,256]{2,1,0:T(8,128)(2,1)}, bf16[4,96,256]{2,1,0:T(8,128)(2,1)}, bf16[4,96,256]{2,1,0:T(8,128)(2,1)}, bf16[768,256]{1,0:T(8,128)(2,1)}) custom-call(s32[6]{0:T(128)} %stack.27.place_ref, s32[128]{0:T(128)} %pad_add_fusion.slot_ref, bf16[2,256,1024]{2,1,0:T(8,128)(2,1)} %copy-done.1, ...), custom_call_target="tpu_custom_call" | custom-call | tf_op jit(solution)/shard_map/forward/pallas_call | solution.py:164
  80.6 5.5 %all-to-all-start.1 = ((bf16[8,96,256]{2,1,0:T(8,128)(2,1)}), bf16[8,96,256]{2,1,0:T(8,128)(2,1)S(1)}, u32[]{:S(2)}, u32[]{:S(2)}) async-start(bf16[8,96,256]{2,1,0:T(8,128)(2,1)} %bitcast.10), calls=%async_computation.1 | async-start | bytes 786432 | tf_op jit(solution)/shard_map/all_to_all | solution.py:305
  87.8 5.7 %all-to-all-done.1.arrived_ref = bf16[8,96,256]{2,1,0:T(8,128)(2,1)S(1)} async-done(((bf16[8,96,256]{2,1,0:T(8,128)(2,1)}), bf16[8,96,256]{2,1,0:T(8,128)(2,1)S(1)}, u32[]{:S(2)}, u32[]{:S(2)}) %all-to-all-start.1) | async-done | bytes 393248 | tf_op jit(solution)/shard_map/all_to_all | solution.py:305
  96.3 5.1 %all-to-all-start.2 = ((bf16[8,96,256]{2,1,0:T(8,128)(2,1)}), bf16[8,96,256]{2,1,0:T(8,128)(2,1)S(1)}, u32[]{:S(2)}, u32[]{:S(2)}) async-start(bf16[8,96,256]{2,1,0:T(8,128)(2,1)} %get-tuple-element.55), calls=%async_computation.2 | async-start | bytes 786432 | tf_op jit(solution)/shard_map/all_to_all | solution.py:305
  101.4 3.4 %collective-permute-start.12 = (bf16[4,96,256]{2,1,0:T(8,128)(2,1)}, bf16[4,96,256]{2,1,0:T(8,128)(2,1)}, u32[]{:S(2)}, u32[]{:S(2)}) collective-permute-start(bf16[4,96,256]{2,1,0:T(8,128)(2,1)} %collective-permute-done.9), channel_id=1, source_target_pairs={{0,16},{16,0},{1,17},{17,1},{2,18},{18,2},{3,19},{19,3},{4,20},{20... | collective-permute-start | bytes 589832 | tf_op jit(solution)/shard_map/ppermute | solution.py:301
  105.5 7.2 %collective-permute-done.12.far_core_ref = bf16[4,96,256]{2,1,0:T(8,128)(2,1)} collective-permute-done((bf16[4,96,256]{2,1,0:T(8,128)(2,1)}, bf16[4,96,256]{2,1,0:T(8,128)(2,1)}, u32[]{:S(2)}, u32[]{:S(2)}) %collective-permute-start.12) | collective-permute-done | bytes 196640 | tf_op jit(solution)/shard_map/ppermute | solution.py:301
  113.9 6.3 %backward.1 = bf16[32,192,128]{2,1,0:T(8,128)(2,1)} custom-call(s32[6]{0:T(128)} %stack.27.place_ref, s32[128]{0:T(128)} %pad_add_fusion.slot_ref, bf16[2,256,1024]{2,1,0:T(8,128)(2,1)} %copy-done.1, bf16[2,256,1024]{2,1,0:T(8,128)(2,1)} %copy-done.4, bf16[2,256,1024]{2,1,0:T(8,128)(2,1)} %copy-done.3, bf16[1,256,1024]{2,1,0:T(8,128)(2,1)} %copy-done.6, ...), custom_call_target="tpu_custom_call" | custom-call | tf_op jit(solution)/shard_map/backward/pallas_call | solution.py:226
  120.2 7.8 %all-to-all-start.3 = ((bf16[32,192,128]{2,1,0:T(8,128)(2,1)}), bf16[32,192,128]{2,1,0:T(8,128)(2,1)S(1)}, u32[]{:S(2)}, u32[]{:S(2)}) async-start(bf16[32,192,128]{2,1,0:T(8,128)(2,1)} %backward.1), calls=%async_computation.3 | async-start | bytes 3145728 | tf_op jit(solution)/shard_map/all_to_all | solution.py:305
  130.4 3.9 %weight_terms.1 = (f32[48,768]{1,0:T(8,128)S(1)}, bf16[48,768]{1,0:T(8,128)(2,1)S(1)}, bf16[48,768]{1,0:T(8,128)(2,1)S(1)}, bf16[48,768]{1,0:T(8,128)(2,1)}, bf1...) custom-call(s32[6]{0:T(128)} %stack.27.place_ref, ...), custom_call_target="tpu_custom_call" | custom-call | flops 24500000768 | tf_op jit(solution)/shard_map/weight_terms/pallas_call | solution.py:258
  134.5 2.7 %collective-permute-start.17 = (bf16[48,768]{1,0:T(8,128)(2,1)S(1)}, bf16[48,768]{1,0:T(8,128)(2,1)S(1)}, u32[]{:S(2)}, u32[]{:S(2)}) collective-permute-start(bf16[48,768]{1,0:T(8,128)(2,1)S(1)} %get-tuple-element.65), channel_id=1, source_target_pairs={{0,4},{2,6},{4,0},{6,2},{8,12},{10,14},{12,8},{14,10},{1,5},{3,7},... | collective-permute-start | bytes 221192 | tf_op jit(solution)/shard_map/ppermute | solution.py:301
  137.8 4.5 %collective-permute-start.19 = (bf16[48,768]{1,0:T(8,128)(2,1)}, bf16[48,768]{1,0:T(8,128)(2,1)S(1)}, u32[]{:S(2)}, u32[]{:S(2)}) collective-permute-start(bf16[48,768]{1,0:T(8,128)(2,1)} %get-tuple-element.67), channel_id=1, source_target_pairs={{0,8},{2,10},{4,12},{6,14},{8,0},{10,2},{12,4},{14,6},{1,9},{3,11}... | collective-permute-start | bytes 221192 | tf_op jit(solution)/shard_map/ppermute | solution.py:301
  143.4 22.3 %collective-permute-done.16 = bf16[48,768]{1,0:T(8,128)(2,1)S(1)} collective-permute-done((bf16[48,768]{1,0:T(8,128)(2,1)S(1)}, bf16[48,768]{1,0:T(8,128)(2,1)S(1)}, u32[]{:S(2)}, u32[]{:S(2)}) %collective-permute-start.16) | collective-permute-done | bytes 73760 | tf_op jit(solution)/shard_map/ppermute | solution.py:301
  165.7 4.0 %collective-permute-start.21 = (bf16[48,768]{1,0:T(8,128)(2,1)}, bf16[48,768]{1,0:T(8,128)(2,1)S(1)}, u32[]{:S(2)}, u32[]{:S(2)}) collective-permute-start(bf16[48,768]{1,0:T(8,128)(2,1)} %get-tuple-element.69), channel_id=1, source_target_pairs={{0,12},{2,14},{4,8},{6,10},{8,4},{10,6},{12,0},{14,2},{1,13},{3,15... | collective-permute-start | bytes 221192 | tf_op jit(solution)/shard_map/ppermute | solution.py:301
  172.1 3.4 %collective-permute-start.22 = (bf16[48,768]{1,0:T(8,128)(2,1)}, bf16[48,768]{1,0:T(8,128)(2,1)S(1)}, u32[]{:S(2)}, u32[]{:S(2)}) collective-permute-start(bf16[48,768]{1,0:T(8,128)(2,1)} %get-tuple-element.70), channel_id=1, source_target_pairs={{0,14},{2,12},{4,10},{6,8},{8,6},{10,4},{12,2},{14,0},{1,15},{3,13... | collective-permute-start | bytes 221192 | tf_op jit(solution)/shard_map/ppermute | solution.py:301
  178.0 5.1 %all-to-all-start.4 = ((f32[8,2,16,192]{3,2,1,0:T(8,128)}), f32[8,2,16,192]{3,2,1,0:T(8,128)S(1)}, u32[]{:S(2)}, u32[]{:S(2)}) async-start(f32[8,2,16,192]{3,2,1,0:T(8,128)} %owned.1), calls=%async_computation.4 | async-start | bytes 524288 | tf_op jit(solution)/shard_map/all_to_all | solution.py:305
  183.2 3.9 %collective-permute-start.23 = (f32[2,24,768]{2,1,0:T(8,128)S(1)}, f32[2,24,768]{2,1,0:T(8,128)S(1)}, u32[]{:S(2)}, u32[]{:S(2)}) collective-permute-start(f32[2,24,768]{2,1,0:T(8,128)S(1)} %bitcast.35), channel_id=1, source_target_pairs={{0,0},{1,4},{2,1},{3,5},{4,2},{5,6},{6,3},{7,7},{8,32},{9,36},{10,... | collective-permute-start | bytes 442376 | tf_op jit(solution)/shard_map/ppermute | solution.py:402
  187.1 11.8 %collective-permute-done.23 = f32[2,24,768]{2,1,0:T(8,128)S(1)} collective-permute-done((f32[2,24,768]{2,1,0:T(8,128)S(1)}, f32[2,24,768]{2,1,0:T(8,128)S(1)}, u32[]{:S(2)}, u32[]{:S(2)}) %collective-permute-start.23) | collective-permute-done | bytes 147488 | tf_op jit(solution)/shard_map/ppermute | solution.py:402
  (90 shorter events, 45.3 us)
Async XLA Ops:
  9.5 23.9 %collective-permute-start.2 = (bf16[1,112,768]{2,1,0:T(8,128)(2,1)}, bf16[1,112,768]{2,1,0:T(8,128)(2,1)}, u32[]{:S(2)}, u32[]{:S(2)}) collective-permute-start(bf16[1,112,768]{2,1,0:T(8,128)(2,1)} %get-tuple-element.77), channel_id=1, source_target_pairs={{0,32},{32,64},{64,96},{96,0},{1,33},{33,65},{65,97},{97,1},{2,34}... | collective-permute-start | bytes 516104 | tf_op jit(solution)/shard_map/ppermute | solution.py:310
  9.7 24.6 %collective-permute-start.3 = (bf16[1,112,768]{2,1,0:T(8,128)(2,1)}, bf16[1,112,768]{2,1,0:T(8,128)(2,1)}, u32[]{:S(2)}, u32[]{:S(2)}) collective-permute-start(bf16[1,112,768]{2,1,0:T(8,128)(2,1)} %get-tuple-element.78), channel_id=1, source_target_pairs={{0,64},{32,96},{64,0},{96,32},{1,65},{33,97},{65,1},{97,33},{2,66}... | collective-permute-start | bytes 516104 | tf_op jit(solution)/shard_map/ppermute | solution.py:310
  12.3 22.9 %collective-permute-start.4 = (bf16[1,112,768]{2,1,0:T(8,128)(2,1)}, bf16[1,112,768]{2,1,0:T(8,128)(2,1)}, u32[]{:S(2)}, u32[]{:S(2)}) collective-permute-start(bf16[1,112,768]{2,1,0:T(8,128)(2,1)} %get-tuple-element.79), channel_id=1, source_target_pairs={{0,96},{32,0},{64,32},{96,64},{1,97},{33,1},{65,33},{97,65},{2,98}... | collective-permute-start | bytes 516104 | tf_op jit(solution)/shard_map/ppermute | solution.py:310
  12.3 31.3 %collective-permute-start.1 = (bf16[2,256,1024]{2,1,0:T(8,128)(2,1)S(1)}, bf16[2,256,1024]{2,1,0:T(8,128)(2,1)S(1)}, u32[]{:S(2)}, u32[]{:S(2)}) collective-permute-start(bf16[2,256,1024]{2,1,0:T(8,128)(2,1)S(1)} %adjacency.1.own_ref), channel_id=1, source_target_pairs={{0,96},{32,0},{64,32},{96,64},{1,97},{33,1},{65,33},{97,65},{2,98}... | collective-permute-start | bytes 3145736 | tf_op jit(solution)/shard_map/ppermute | solution.py:297
  13.2 30.4 %collective-permute-start = (bf16[2,256,1024]{2,1,0:T(8,128)(2,1)S(1)}, bf16[2,256,1024]{2,1,0:T(8,128)(2,1)S(1)}, u32[]{:S(2)}, u32[]{:S(2)}) collective-permute-start(bf16[2,256,1024]{2,1,0:T(8,128)(2,1)S(1)} %adjacency.1.own_ref), channel_id=1, source_target_pairs={{0,32},{32,64},{64,96},{96,0},{1,33},{33,65},{65,97},{97,1},{2,34}... | collective-permute-start | bytes 3145736 | tf_op jit(solution)/shard_map/ppermute | solution.py:297
  18.9 53.2 %all-to-all-start = ((bf16[32,192,128]{2,1,0:T(8,128)(2,1)}), bf16[32,192,128]{2,1,0:T(8,128)(2,1)}, u32[]{:S(2)}, u32[]{:S(2)}) async-start(bf16[32,192,128]{2,1,0:T(8,128)(2,1)} %outgoing.1), calls=%async_computation | async-start | bytes 3145728 | tf_op jit(solution)/shard_map/all_to_all | solution.py:305
  38.0 27.2 %collective-permute-start.5 = (bf16[4,96,768]{2,1,0:T(8,128)(2,1)}, bf16[4,96,768]{2,1,0:T(8,128)(2,1)}, u32[]{:S(2)}, u32[]{:S(2)}) collective-permute-start(bf16[4,96,768]{2,1,0:T(8,128)(2,1)} %pad_maximum_fusion.1), channel_id=1, source_target_pairs={{0,16},{16,0},{1,17},{17,1},{2,18},{18,2},{3,19},{19,3},{4,20},{20... | collective-permute-start | bytes 1769480 | tf_op jit(solution)/shard_map/ppermute | solution.py:301
  46.2 19.0 %collective-permute-start.7 = (bf16[1,256,1024]{2,1,0:T(8,128)(2,1)}, bf16[1,256,1024]{2,1,0:T(8,128)(2,1)S(1)}, u32[]{:S(2)}, u32[]{:S(2)}) collective-permute-start(bf16[1,256,1024]{2,1,0:T(8,128)(2,1)} %slice.31), channel_id=1, source_target_pairs={{0,96},{32,0},{64,32},{96,64},{1,97},{33,1},{65,33},{97,65},{2,98}... | collective-permute-start | bytes 1572872 | tf_op jit(solution)/shard_map/ppermute | solution.py:297
  47.2 18.0 %collective-permute-start.6 = (bf16[1,256,1024]{2,1,0:T(8,128)(2,1)}, bf16[1,256,1024]{2,1,0:T(8,128)(2,1)S(1)}, u32[]{:S(2)}, u32[]{:S(2)}) collective-permute-start(bf16[1,256,1024]{2,1,0:T(8,128)(2,1)} %slice.30), channel_id=1, source_target_pairs={{0,32},{32,64},{64,96},{96,0},{1,33},{33,65},{65,97},{97,1},{2,34}... | collective-permute-start | bytes 1572872 | tf_op jit(solution)/shard_map/ppermute | solution.py:297
  80.6 13.0 %all-to-all-start.1 = ((bf16[8,96,256]{2,1,0:T(8,128)(2,1)}), bf16[8,96,256]{2,1,0:T(8,128)(2,1)S(1)}, u32[]{:S(2)}, u32[]{:S(2)}) async-start(bf16[8,96,256]{2,1,0:T(8,128)(2,1)} %bitcast.10), calls=%async_computation.1 | async-start | bytes 786432 | tf_op jit(solution)/shard_map/all_to_all | solution.py:305
  86.1 10.2 %collective-permute-start.10 = (bf16[4,96,256]{2,1,0:T(8,128)(2,1)}, bf16[4,96,256]{2,1,0:T(8,128)(2,1)S(1)}, u32[]{:S(2)}, u32[]{:S(2)}) collective-permute-start(bf16[4,96,256]{2,1,0:T(8,128)(2,1)} %get-tuple-element.54), channel_id=1, source_target_pairs={{0,16},{16,0},{1,17},{17,1},{2,18},{18,2},{3,19},{19,3},{4,20},{20... | collective-permute-start | bytes 589832 | tf_op jit(solution)/shard_map/ppermute | solution.py:301
  96.3 16.5 %all-to-all-start.2 = ((bf16[8,96,256]{2,1,0:T(8,128)(2,1)}), bf16[8,96,256]{2,1,0:T(8,128)(2,1)S(1)}, u32[]{:S(2)}, u32[]{:S(2)}) async-start(bf16[8,96,256]{2,1,0:T(8,128)(2,1)} %get-tuple-element.55), calls=%async_computation.2 | async-start | bytes 786432 | tf_op jit(solution)/shard_map/all_to_all | solution.py:305
  101.4 11.3 %collective-permute-start.12 = (bf16[4,96,256]{2,1,0:T(8,128)(2,1)}, bf16[4,96,256]{2,1,0:T(8,128)(2,1)}, u32[]{:S(2)}, u32[]{:S(2)}) collective-permute-start(bf16[4,96,256]{2,1,0:T(8,128)(2,1)} %collective-permute-done.9), channel_id=1, source_target_pairs={{0,16},{16,0},{1,17},{17,1},{2,18},{18,2},{3,19},{19,3},{4,20},{20... | collective-permute-start | bytes 589832 | tf_op jit(solution)/shard_map/ppermute | solution.py:301
  112.8 15.5 %collective-permute-start.14 = (bf16[768,256]{1,0:T(8,128)(2,1)S(1)}, bf16[768,256]{1,0:T(8,128)(2,1)S(1)}, u32[]{:S(2)}, u32[]{:S(2)}) collective-permute-start(bf16[768,256]{1,0:T(8,128)(2,1)S(1)} %bitcast.28), channel_id=1, source_target_pairs={{0,16},{16,0},{1,17},{17,1},{2,18},{18,2},{3,19},{19,3},{4,20},{20... | collective-permute-start | bytes 1179656 | tf_op jit(solution)/shard_map/ppermute | solution.py:301
  120.2 55.3 %all-to-all-start.3 = ((bf16[32,192,128]{2,1,0:T(8,128)(2,1)}), bf16[32,192,128]{2,1,0:T(8,128)(2,1)S(1)}, u32[]{:S(2)}, u32[]{:S(2)}) async-start(bf16[32,192,128]{2,1,0:T(8,128)(2,1)} %backward.1), calls=%async_computation.3 | async-start | bytes 3145728 | tf_op jit(solution)/shard_map/all_to_all | solution.py:305
  134.3 31.4 %collective-permute-start.16 = (bf16[48,768]{1,0:T(8,128)(2,1)S(1)}, bf16[48,768]{1,0:T(8,128)(2,1)S(1)}, u32[]{:S(2)}, u32[]{:S(2)}) collective-permute-start(bf16[48,768]{1,0:T(8,128)(2,1)S(1)} %get-tuple-element.64), channel_id=1, source_target_pairs={{0,2},{2,0},{4,6},{6,4},{8,10},{10,8},{12,14},{14,12},{1,3},{3,1},... | collective-permute-start | bytes 221192 | tf_op jit(solution)/shard_map/ppermute | solution.py:301
  134.5 37.5 %collective-permute-start.17 = (bf16[48,768]{1,0:T(8,128)(2,1)S(1)}, bf16[48,768]{1,0:T(8,128)(2,1)S(1)}, u32[]{:S(2)}, u32[]{:S(2)}) collective-permute-start(bf16[48,768]{1,0:T(8,128)(2,1)S(1)} %get-tuple-element.65), channel_id=1, source_target_pairs={{0,4},{2,6},{4,0},{6,2},{8,12},{10,14},{12,8},{14,10},{1,5},{3,7},... | collective-permute-start | bytes 221192 | tf_op jit(solution)/shard_map/ppermute | solution.py:301
  137.2 45.9 %collective-permute-start.18 = (bf16[48,768]{1,0:T(8,128)(2,1)}, bf16[48,768]{1,0:T(8,128)(2,1)S(1)}, u32[]{:S(2)}, u32[]{:S(2)}) collective-permute-start(bf16[48,768]{1,0:T(8,128)(2,1)} %get-tuple-element.66), channel_id=1, source_target_pairs={{0,6},{2,4},{4,2},{6,0},{8,14},{10,12},{12,10},{14,8},{1,7},{3,5},... | collective-permute-start | bytes 221192 | tf_op jit(solution)/shard_map/ppermute | solution.py:301
  137.8 45.3 %collective-permute-start.19 = (bf16[48,768]{1,0:T(8,128)(2,1)}, bf16[48,768]{1,0:T(8,128)(2,1)S(1)}, u32[]{:S(2)}, u32[]{:S(2)}) collective-permute-start(bf16[48,768]{1,0:T(8,128)(2,1)} %get-tuple-element.67), channel_id=1, source_target_pairs={{0,8},{2,10},{4,12},{6,14},{8,0},{10,2},{12,4},{14,6},{1,9},{3,11}... | collective-permute-start | bytes 221192 | tf_op jit(solution)/shard_map/ppermute | solution.py:301
  142.3 40.9 %collective-permute-start.20 = (bf16[48,768]{1,0:T(8,128)(2,1)}, bf16[48,768]{1,0:T(8,128)(2,1)S(1)}, u32[]{:S(2)}, u32[]{:S(2)}) collective-permute-start(bf16[48,768]{1,0:T(8,128)(2,1)} %get-tuple-element.68), channel_id=1, source_target_pairs={{0,10},{2,8},{4,14},{6,12},{8,2},{10,0},{12,6},{14,4},{1,11},{3,9}... | collective-permute-start | bytes 221192 | tf_op jit(solution)/shard_map/ppermute | solution.py:301
  165.7 17.4 %collective-permute-start.21 = (bf16[48,768]{1,0:T(8,128)(2,1)}, bf16[48,768]{1,0:T(8,128)(2,1)S(1)}, u32[]{:S(2)}, u32[]{:S(2)}) collective-permute-start(bf16[48,768]{1,0:T(8,128)(2,1)} %get-tuple-element.69), channel_id=1, source_target_pairs={{0,12},{2,14},{4,8},{6,10},{8,4},{10,6},{12,0},{14,2},{1,13},{3,15... | collective-permute-start | bytes 221192 | tf_op jit(solution)/shard_map/ppermute | solution.py:301
  172.1 11.1 %collective-permute-start.22 = (bf16[48,768]{1,0:T(8,128)(2,1)}, bf16[48,768]{1,0:T(8,128)(2,1)S(1)}, u32[]{:S(2)}, u32[]{:S(2)}) collective-permute-start(bf16[48,768]{1,0:T(8,128)(2,1)} %get-tuple-element.70), channel_id=1, source_target_pairs={{0,14},{2,12},{4,10},{6,8},{8,6},{10,4},{12,2},{14,0},{1,15},{3,13... | collective-permute-start | bytes 221192 | tf_op jit(solution)/shard_map/ppermute | solution.py:301
  178.0 20.9 %all-to-all-start.4 = ((f32[8,2,16,192]{3,2,1,0:T(8,128)}), f32[8,2,16,192]{3,2,1,0:T(8,128)S(1)}, u32[]{:S(2)}, u32[]{:S(2)}) async-start(f32[8,2,16,192]{3,2,1,0:T(8,128)} %owned.1), calls=%async_computation.4 | async-start | bytes 524288 | tf_op jit(solution)/shard_map/all_to_all | solution.py:305
  183.2 15.7 %collective-permute-start.23 = (f32[2,24,768]{2,1,0:T(8,128)S(1)}, f32[2,24,768]{2,1,0:T(8,128)S(1)}, u32[]{:S(2)}, u32[]{:S(2)}) collective-permute-start(f32[2,24,768]{2,1,0:T(8,128)S(1)} %bitcast.35), channel_id=1, source_target_pairs={{0,0},{1,4},{2,1},{3,5},{4,2},{5,6},{6,3},{7,7},{8,32},{9,36},{10,... | collective-permute-start | bytes 442376 | tf_op jit(solution)/shard_map/ppermute | solution.py:402
  (16 other events, 164.6 us)

commit v11 on v10

--- a/solution.py
+++ b/solution.py
@@ -118,6 +118,28 @@
     return pl.BlockSpec(memory_space=pltpu.MemorySpace.HBM)
 
 
+def join_kernel(own_ref, own_slots_ref, came1_ref, came2_ref, came3_ref, part_ref, slots_ref):
+    part_ref[0] = own_ref[0]
+    slots_ref[0:1] = own_slots_ref[0, :, :BLK].astype(F32).astype(jnp.int32)[0:1]
+    for k, ref in enumerate((came1_ref, came2_ref, came3_ref), 1):
+        part_ref[k] = ref[0, :96]
+        slots_ref[k : k + 1] = ref[0, 96:, :BLK].astype(F32).astype(jnp.int32)[0:1]
+
+
+def join(own, own_slots, came):
+    return pl.pallas_call(
+        join_kernel,
+        in_specs=[vmem()] * 5,
+        out_specs=[vmem(), vmem()],
+        out_shape=[
+            jax.ShapeDtypeStruct((4, *own.shape[1:]), BF16),
+            jax.ShapeDtypeStruct((4, BLK), jnp.int32),
+        ],
+        compiler_params=params(),
+        name="join",
+    )(own, own_slots, *came)
+
+
 def forward_kernel(
     place_ref, slot_ref, own_ref, back_ref, fore_ref, far0_ref, far1_ref, fetched_ref, w_mine_ref, w_theirs_ref,
     keep_ref, keep_far_ref, send_ref, send_far_ref, pre_ref, adj_buf, sems, both_ref, acc_ref,
@@ -129,8 +151,8 @@
             load.wait()
         for p in range(2):
             for q in range(2):
-                base = ((k * 2 + p) * 2 + q) * 8
-                wide = jnp.concatenate([fetched_ref[slot_ref[base + s]] for s in range(8)], axis=1)
+                base = (p * 2 + q) * 8
+                wide = jnp.concatenate([fetched_ref[slot_ref[k, base + s]] for s in range(8)], axis=1)
                 part = adj_buf[2 * n + p, q * BLK : (q + 1) * BLK, :]
                 both_ref[p, :, q * BLK : (q + 1) * BLK] = dot(wide, part, 1, 1).astype(BF16)
         j = (y - k) & 3
@@ -213,11 +235,11 @@
             load.wait()
         for p in range(2):
             for q in range(2):
-                base = ((k * 2 + p) * 2 + q) * 8
+                base = (p * 2 + q) * 8
                 part = adj_buf[2 * n + p, q * BLK : (q + 1) * BLK, :]
                 wide = dot(both_ref[p, :, q * BLK : (q + 1) * BLK], part, 1, 0)
                 for s in range(8):
-                    acc_ref[slot_ref[base + s]] += wide[:, s * BLK : (s + 1) * BLK]
+                    acc_ref[slot_ref[k, base + s]] += wide[:, s * BLK : (s + 1) * BLK]
     out_ref[...] = acc_ref[...].astype(BF16)
 
 
@@ -352,17 +374,14 @@
         cut = lax.dynamic_slice(weights, (core, ((y + k) & 3) * 192 + 96 * xh, 0), (1, 96, width))
         pieces.append(jnp.concatenate([cut, own_slots], axis=1) if k else cut)
     came = around(pieces[1:], "y", 4)
-    slots = jnp.concatenate([tile_slot.reshape(-1)] + [c[0, 96, :32].astype(jnp.int32) for c in came])
     share = width // groups
     bias_share = lax.dynamic_slice_in_dim(bias, group * share, share)
     bias_share = jnp.broadcast_to(bias_share[:, None], (share, features.shape[0]))
     cotangent_share = lax.dynamic_slice_in_dim(cotangent, group * share, share, 1).T
-    back, fore, slots, bias_share, cotangent_share = lax.optimization_barrier(
-        (back, fore, slots, bias_share, cotangent_share)
-    )
+    w_part, slots = join(pieces[0], own_slots, came)
+    w_part, bias_share, cotangent_share = lax.optimization_barrier((w_part, bias_share, cotangent_share))
     slots, bias_share, cotangent_share = in_hbm(slots), in_hbm(bias_share), in_hbm(cotangent_share)
     far0, far1 = step(back[:1], 1), step(fore[1:], -1)
-    w_part = jnp.concatenate([pieces[0]] + [c[:, :96] for c in came], axis=0)
     w_other = swap(w_part, "xh")
     w_part, w_other, far0, far1 = lax.optimization_barrier((w_part, w_other, far0, far1))
     w_mine = jnp.concatenate(

time: 202 us -> 201 us (level)
  waiting for transfers between devices: 73.7 us -> 80.4 us
  other arithmetic: 7.92 us -> 1.74 us
  local copies, waits for them, and re-layouts: 13.7 us -> 9.41 us
  starting transfers between devices: 73.7 us -> 76.1 us
    ppermute x3, waiting for transfers between devices: 0.01 us -> 9.33 us  [around(): lax.ppermute(v, axis, [(i, (i + k) % size) for i in range(size)])]
    slice x3 -> x0, local copies, waits for them, and re-layouts: 2.76 us -> none  [per_device(): w_part = jnp.concatenate([pieces[0]] + [c[:, :96] for c in came], axis=0)]
    all_to_all x5, waiting for transfers between devices: 7.76 us -> 5.29 us  [exchange(): return lax.all_to_all(value, axis, 0, 0, tiled=True)]
    concatenate x2 -> x0, other arithmetic: 2.4 us -> none  [the longest x1 1.81 us: per_device(): w_part = jnp.concatenate([pieces[0]] + [c[:, :96] for c in came], axis=0)]
    convert_element_type x3 -> x0, other arithmetic: 2.04 us -> none  [per_device(): c[0, 96, :32].astype(jnp.int32)]
  transfers between devices with their start and end apart: 29 -> 29, of which waited for: 12 -> 11; matrix products, arithmetic and copies ran while one was open for 8% -> 4% of each run, Pallas kernels for 9% -> 9%
where the time goes in v11:
time: 201 us; the launch traced here: 199 us
  waiting for transfers between devices  80.4 us (40%)
  starting transfers between devices  76.1 us (38%)
  Pallas kernels  30.4 us (15%)
  local copies, waits for them, and re-layouts  9.41 us (5%)
    ppermute x16, waiting for transfers between devices, swap(): return lax.ppermute(value, axis, [(i, i ^ flip) for i in range(size)])  53.9 us
    all_to_all x5, starting transfers between devices, exchange(): return lax.all_to_all(value, axis, 0, 0, tiled=True)  36.4 us
    ppermute x16, starting transfers between devices, swap(): return lax.ppermute(value, axis, [(i, i ^ flip) for i in range(size)])  26.1 us
    ppermute x1, waiting for transfers between devices, per_device(): lax.ppermute(piece.reshape(2, 24, width), ('y', *TGT), to_owner())  11.9 us
    ppermute x3, waiting for transfers between devices, around(): lax.ppermute(v, axis, [(i, (i + k) % size) for i in range(size)])  9.33 us
    pallas_call x1, Pallas kernels, forward_of(): pl.pallas_call(forward_kernel, in_specs=[smem(), smem()] + [hbm()] * 5 +...  8.33 us
    ppermute x4, starting transfers between devices, step(): return lax.ppermute(value, 'y', [(i, (i + by) % 4) for i in range(4)])  6.62 us
    pallas_call x1, Pallas kernels, backward_of(): pl.pallas_call(backward_kernel, in_specs=[smem(), smem()] + [hbm()] * 5 +...  6.33 us
  transfers between devices with their start and end apart: 29, of which 11 were waited for; matrix products, arithmetic and copies ran while one was open for 4% of the time, Pallas kernels for 9%

profile of v11, /device:TPU:56, one launch (start us, length us, event | category | flops | bytes accessed | tf_op | source)
XLA Modules:
  0.0 199.1 jit_solution(197247647998855677)
XLA Ops:
  0.6 5.0 %adjacency.1.own_ref = bf16[2,256,1024]{2,1,0:T(8,128)(2,1)S(1)} custom-call(s32[2,2]{1,0:T(2,128)} %count_ref.1, s32[2,256,8,128]{3,2,1,0:T(8,128)} %values_ref.1), custom_call_target="tpu_custom_call" | custom-call | tf_op jit(solution)/shard_map/adjacency/pallas_call | solution.py:61
  12.2 11.4 %all-to-all-start = ((bf16[32,192,128]{2,1,0:T(8,128)(2,1)}), bf16[32,192,128]{2,1,0:T(8,128)(2,1)}, u32[]{:S(2)}, u32[]{:S(2)}) async-start(bf16[32,192,128]{2,1,0:T(8,128)(2,1)} %outgoing.1), calls=%async_computation | async-start | bytes 3145728 | tf_op jit(solution)/shard_map/all_to_all | solution.py:327
  29.9 9.3 %collective-permute-done.2.came3_ref = bf16[1,112,768]{2,1,0:T(8,128)(2,1)S(1)} collective-permute-done((bf16[1,112,768]{2,1,0:T(8,128)(2,1)S(1)}, bf16[1,112,768]{2,1,0:T(8,128)(2,1)S(1)}, u32[]{:S(2)}, u32[]{:S(2)}) %collective-permute-start.2) | collective-permute-done | bytes 172064 | tf_op jit(solution)/shard_map/ppermute | solution.py:332
  40.0 3.0 %collective-permute-start.5 = (bf16[4,96,768]{2,1,0:T(8,128)(2,1)S(1)}, bf16[4,96,768]{2,1,0:T(8,128)(2,1)}, u32[]{:S(2)}, u32[]{:S(2)}) collective-permute-start(bf16[4,96,768]{2,1,0:T(8,128)(2,1)S(1)} %get-tuple-element.44), channel_id=1, source_target_pairs={{0,16},{16,0},{1,17},{17,1},{2,18},{18,2},{3,19},{19,3},{4,20},{20... | collective-permute-start | bytes 1769480 | tf_op jit(solution)/shard_map/ppermute | solution.py:323
  46.0 3.3 %collective-permute-start.6 = (bf16[1,256,1024]{2,1,0:T(8,128)(2,1)S(1)}, bf16[1,256,1024]{2,1,0:T(8,128)(2,1)S(1)}, u32[]{:S(2)}, u32[]{:S(2)}) collective-permute-start(bf16[1,256,1024]{2,1,0:T(8,128)(2,1)S(1)} %slice.8), channel_id=1, source_target_pairs={{0,32},{32,64},{64,96},{96,0},{1,33},{33,65},{65,97},{97,1},{2,34}... | collective-permute-start | bytes 1572872 | tf_op jit(solution)/shard_map/ppermute | solution.py:319
  49.3 14.7 %collective-permute-done.5 = bf16[4,96,768]{2,1,0:T(8,128)(2,1)} collective-permute-done((bf16[4,96,768]{2,1,0:T(8,128)(2,1)S(1)}, bf16[4,96,768]{2,1,0:T(8,128)(2,1)}, u32[]{:S(2)}, u32[]{:S(2)}) %collective-permute-start.5) | collective-permute-done | bytes 589856 | tf_op jit(solution)/shard_map/ppermute | solution.py:323
  65.8 2.8 %collective-permute-done.8.w_theirs_ref = bf16[4,192,768]{2,1,0:T(8,128)(2,1)S(1)} collective-permute-done((bf16[4,192,768]{2,1,0:T(8,128)(2,1)S(1)}, bf16[4,192,768]{2,1,0:T(8,128)(2,1)S(1)}, u32[]{:S(2)}, u32[]{:S(2)}) %collective-permute-start.8) | collective-permute-done | bytes 1179680 | tf_op jit(solution)/shard_map/ppermute | solution.py:323
  68.6 8.3 %forward.1 = (bf16[4,96,256]{2,1,0:T(8,128)(2,1)}, bf16[4,96,256]{2,1,0:T(8,128)(2,1)}, bf16[4,96,256]{2,1,0:T(8,128)(2,1)}, bf16[4,96,256]{2,1,0:T(8,128)(2,1)}, bf16[768,256]{1,0:T(8,128)(2,1)}) custom-call(s32[6]{0:T(128)} %stack.27.place_ref, s32[4,128]{1,0:T(4,128)} %copy-done.2, bf16[2,256,1024]{2,1,0:T(8,128)(2,1)} %copy-done.1, ...), custom_call_target="tpu_custom_call" | custom-call | tf_op jit(solution)/shard_map/forward/pallas_call | solution.py:186
  76.9 5.4 %all-to-all-start.1 = ((bf16[8,96,256]{2,1,0:T(8,128)(2,1)}), bf16[8,96,256]{2,1,0:T(8,128)(2,1)S(1)}, u32[]{:S(2)}, u32[]{:S(2)}) async-start(bf16[8,96,256]{2,1,0:T(8,128)(2,1)} %bitcast.7), calls=%async_computation.1 | async-start | bytes 786432 | tf_op jit(solution)/shard_map/all_to_all | solution.py:327
  84.6 5.3 %all-to-all-done.1.arrived_ref = bf16[8,96,256]{2,1,0:T(8,128)(2,1)S(1)} async-done(((bf16[8,96,256]{2,1,0:T(8,128)(2,1)}), bf16[8,96,256]{2,1,0:T(8,128)(2,1)S(1)}, u32[]{:S(2)}, u32[]{:S(2)}) %all-to-all-start.1) | async-done | bytes 393248 | tf_op jit(solution)/shard_map/all_to_all | solution.py:327
  93.9 5.1 %all-to-all-start.2 = ((bf16[8,96,256]{2,1,0:T(8,128)(2,1)}), bf16[8,96,256]{2,1,0:T(8,128)(2,1)S(1)}, u32[]{:S(2)}, u32[]{:S(2)}) async-start(bf16[8,96,256]{2,1,0:T(8,128)(2,1)} %get-tuple-element.55), calls=%async_computation.2 | async-start | bytes 786432 | tf_op jit(solution)/shard_map/all_to_all | solution.py:327
  99.0 2.6 %collective-permute-start.12 = (bf16[4,96,256]{2,1,0:T(8,128)(2,1)}, bf16[4,96,256]{2,1,0:T(8,128)(2,1)}, u32[]{:S(2)}, u32[]{:S(2)}) collective-permute-start(bf16[4,96,256]{2,1,0:T(8,128)(2,1)} %collective-permute-done.9), channel_id=1, source_target_pairs={{0,16},{16,0},{1,17},{17,1},{2,18},{18,2},{3,19},{19,3},{4,20},{20... | collective-permute-start | bytes 589832 | tf_op jit(solution)/shard_map/ppermute | solution.py:323
  102.3 7.6 %collective-permute-done.12.far_core_ref = bf16[4,96,256]{2,1,0:T(8,128)(2,1)} collective-permute-done((bf16[4,96,256]{2,1,0:T(8,128)(2,1)}, bf16[4,96,256]{2,1,0:T(8,128)(2,1)}, u32[]{:S(2)}, u32[]{:S(2)}) %collective-permute-start.12) | collective-permute-done | bytes 196640 | tf_op jit(solution)/shard_map/ppermute | solution.py:323
  110.9 6.3 %backward.1 = bf16[32,192,128]{2,1,0:T(8,128)(2,1)} custom-call(s32[6]{0:T(128)} %stack.27.place_ref, s32[4,128]{1,0:T(4,128)} %copy-done.2, bf16[2,256,1024]{2,1,0:T(8,128)(2,1)} %copy-done.1, bf16[2,256,1024]{2,1,0:T(8,128)(2,1)} %collective-permute-done.3.back_ref, bf16[2,256,1024]{2,1,0:T(8,128)(2,1)} %collective-permute-done.4.fore_ref, ...), custom_call_target="tpu_custom_call" | custom-call | tf_op jit(solution)/shard_map/backward/pallas_call | solution.py:248
  117.2 9.3 %all-to-all-start.3 = ((bf16[32,192,128]{2,1,0:T(8,128)(2,1)}), bf16[32,192,128]{2,1,0:T(8,128)(2,1)S(1)}, u32[]{:S(2)}, u32[]{:S(2)}) async-start(bf16[32,192,128]{2,1,0:T(8,128)(2,1)} %backward.1), calls=%async_computation.3 | async-start | bytes 3145728 | tf_op jit(solution)/shard_map/all_to_all | solution.py:327
  128.9 3.9 %weight_terms.1 = (f32[48,768]{1,0:T(8,128)S(1)}, bf16[48,768]{1,0:T(8,128)(2,1)S(1)}, bf16[48,768]{1,0:T(8,128)(2,1)S(1)}, bf16[48,768]{1,0:T(8,128)(2,1)}, bf1...) custom-call(s32[6]{0:T(128)} %stack.27.place_ref, ...), custom_call_target="tpu_custom_call" | custom-call | flops 24500000768 | tf_op jit(solution)/shard_map/weight_terms/pallas_call | solution.py:280
  133.0 2.7 %collective-permute-start.17 = (bf16[48,768]{1,0:T(8,128)(2,1)S(1)}, bf16[48,768]{1,0:T(8,128)(2,1)S(1)}, u32[]{:S(2)}, u32[]{:S(2)}) collective-permute-start(bf16[48,768]{1,0:T(8,128)(2,1)S(1)} %get-tuple-element.65), channel_id=1, source_target_pairs={{0,4},{2,6},{4,0},{6,2},{8,12},{10,14},{12,8},{14,10},{1,5},{3,7},... | collective-permute-start | bytes 221192 | tf_op jit(solution)/shard_map/ppermute | solution.py:323
  136.3 4.5 %collective-permute-start.19 = (bf16[48,768]{1,0:T(8,128)(2,1)}, bf16[48,768]{1,0:T(8,128)(2,1)S(1)}, u32[]{:S(2)}, u32[]{:S(2)}) collective-permute-start(bf16[48,768]{1,0:T(8,128)(2,1)} %get-tuple-element.67), channel_id=1, source_target_pairs={{0,8},{2,10},{4,12},{6,14},{8,0},{10,2},{12,4},{14,6},{1,9},{3,11}... | collective-permute-start | bytes 221192 | tf_op jit(solution)/shard_map/ppermute | solution.py:323
  141.9 22.3 %collective-permute-done.16 = bf16[48,768]{1,0:T(8,128)(2,1)S(1)} collective-permute-done((bf16[48,768]{1,0:T(8,128)(2,1)S(1)}, bf16[48,768]{1,0:T(8,128)(2,1)S(1)}, u32[]{:S(2)}, u32[]{:S(2)}) %collective-permute-start.16) | collective-permute-done | bytes 73760 | tf_op jit(solution)/shard_map/ppermute | solution.py:323
  164.2 4.0 %collective-permute-start.21 = (bf16[48,768]{1,0:T(8,128)(2,1)}, bf16[48,768]{1,0:T(8,128)(2,1)S(1)}, u32[]{:S(2)}, u32[]{:S(2)}) collective-permute-start(bf16[48,768]{1,0:T(8,128)(2,1)} %get-tuple-element.69), channel_id=1, source_target_pairs={{0,12},{2,14},{4,8},{6,10},{8,4},{10,6},{12,0},{14,2},{1,13},{3,15... | collective-permute-start | bytes 221192 | tf_op jit(solution)/shard_map/ppermute | solution.py:323
  170.6 3.4 %collective-permute-start.22 = (bf16[48,768]{1,0:T(8,128)(2,1)}, bf16[48,768]{1,0:T(8,128)(2,1)S(1)}, u32[]{:S(2)}, u32[]{:S(2)}) collective-permute-start(bf16[48,768]{1,0:T(8,128)(2,1)} %get-tuple-element.70), channel_id=1, source_target_pairs={{0,14},{2,12},{4,10},{6,8},{8,6},{10,4},{12,2},{14,0},{1,15},{3,13... | collective-permute-start | bytes 221192 | tf_op jit(solution)/shard_map/ppermute | solution.py:323
  176.5 5.2 %all-to-all-start.4 = ((f32[8,2,16,192]{3,2,1,0:T(8,128)}), f32[8,2,16,192]{3,2,1,0:T(8,128)S(1)}, u32[]{:S(2)}, u32[]{:S(2)}) async-start(f32[8,2,16,192]{3,2,1,0:T(8,128)} %owned.1), calls=%async_computation.4 | async-start | bytes 524288 | tf_op jit(solution)/shard_map/all_to_all | solution.py:327
  181.8 3.7 %collective-permute-start.23 = (f32[2,24,768]{2,1,0:T(8,128)S(1)}, f32[2,24,768]{2,1,0:T(8,128)S(1)}, u32[]{:S(2)}, u32[]{:S(2)}) collective-permute-start(f32[2,24,768]{2,1,0:T(8,128)S(1)} %bitcast.20), channel_id=1, source_target_pairs={{0,0},{1,4},{2,1},{3,5},{4,2},{5,6},{6,3},{7,7},{8,32},{9,36},{10,... | collective-permute-start | bytes 442376 | tf_op jit(solution)/shard_map/ppermute | solution.py:421
  185.6 11.9 %collective-permute-done.23 = f32[2,24,768]{2,1,0:T(8,128)S(1)} collective-permute-done((f32[2,24,768]{2,1,0:T(8,128)S(1)}, f32[2,24,768]{2,1,0:T(8,128)S(1)}, u32[]{:S(2)}, u32[]{:S(2)}) %collective-permute-start.23) | collective-permute-done | bytes 147488 | tf_op jit(solution)/shard_map/ppermute | solution.py:421
  (81 shorter events, 36.9 us)
Async XLA Ops:
  5.7 37.4 %collective-permute-start.4 = (bf16[2,256,1024]{2,1,0:T(8,128)(2,1)S(1)}, bf16[2,256,1024]{2,1,0:T(8,128)(2,1)}, u32[]{:S(2)}, u32[]{:S(2)}) collective-permute-start(bf16[2,256,1024]{2,1,0:T(8,128)(2,1)S(1)} %adjacency.1.own_ref), channel_id=1, source_target_pairs={{0,96},{32,0},{64,32},{96,64},{1,97},{33,1},{65,33},{97,65},{2,98}... | collective-permute-start | bytes 3145736 | tf_op jit(solution)/shard_map/ppermute | solution.py:319
  6.5 38.4 %collective-permute-start.3 = (bf16[2,256,1024]{2,1,0:T(8,128)(2,1)S(1)}, bf16[2,256,1024]{2,1,0:T(8,128)(2,1)}, u32[]{:S(2)}, u32[]{:S(2)}) collective-permute-start(bf16[2,256,1024]{2,1,0:T(8,128)(2,1)S(1)} %adjacency.1.own_ref), channel_id=1, source_target_pairs={{0,32},{32,64},{64,96},{96,0},{1,33},{33,65},{65,97},{97,1},{2,34}... | collective-permute-start | bytes 3145736 | tf_op jit(solution)/shard_map/ppermute | solution.py:319
  12.2 56.4 %all-to-all-start = ((bf16[32,192,128]{2,1,0:T(8,128)(2,1)}), bf16[32,192,128]{2,1,0:T(8,128)(2,1)}, u32[]{:S(2)}, u32[]{:S(2)}) async-start(bf16[32,192,128]{2,1,0:T(8,128)(2,1)} %outgoing.1), calls=%async_computation | async-start | bytes 3145728 | tf_op jit(solution)/shard_map/all_to_all | solution.py:327
  25.0 14.2 %collective-permute-start.2 = (bf16[1,112,768]{2,1,0:T(8,128)(2,1)S(1)}, bf16[1,112,768]{2,1,0:T(8,128)(2,1)S(1)}, u32[]{:S(2)}, u32[]{:S(2)}) collective-permute-start(bf16[1,112,768]{2,1,0:T(8,128)(2,1)S(1)} %get-tuple-element.77), channel_id=1, source_target_pairs={{0,96},{32,0},{64,32},{96,64},{1,97},{33,1},{65,33},{97,65},{2,98}... | collective-permute-start | bytes 516104 | tf_op jit(solution)/shard_map/ppermute | solution.py:332
  25.1 14.1 %collective-permute-start.1 = (bf16[1,112,768]{2,1,0:T(8,128)(2,1)S(1)}, bf16[1,112,768]{2,1,0:T(8,128)(2,1)S(1)}, u32[]{:S(2)}, u32[]{:S(2)}) collective-permute-start(bf16[1,112,768]{2,1,0:T(8,128)(2,1)S(1)} %get-tuple-element.78), channel_id=1, source_target_pairs={{0,64},{32,96},{64,0},{96,32},{1,65},{33,97},{65,1},{97,33},{2,66}... | collective-permute-start | bytes 516104 | tf_op jit(solution)/shard_map/ppermute | solution.py:332
  26.5 12.7 %collective-permute-start = (bf16[1,112,768]{2,1,0:T(8,128)(2,1)S(1)}, bf16[1,112,768]{2,1,0:T(8,128)(2,1)S(1)}, u32[]{:S(2)}, u32[]{:S(2)}) collective-permute-start(bf16[1,112,768]{2,1,0:T(8,128)(2,1)S(1)} %get-tuple-element.79), channel_id=1, source_target_pairs={{0,32},{32,64},{64,96},{96,0},{1,33},{33,65},{65,97},{97,1},{2,34}... | collective-permute-start | bytes 516104 | tf_op jit(solution)/shard_map/ppermute | solution.py:332
  40.0 24.0 %collective-permute-start.5 = (bf16[4,96,768]{2,1,0:T(8,128)(2,1)S(1)}, bf16[4,96,768]{2,1,0:T(8,128)(2,1)}, u32[]{:S(2)}, u32[]{:S(2)}) collective-permute-start(bf16[4,96,768]{2,1,0:T(8,128)(2,1)S(1)} %get-tuple-element.44), channel_id=1, source_target_pairs={{0,16},{16,0},{1,17},{17,1},{2,18},{18,2},{3,19},{19,3},{4,20},{20... | collective-permute-start | bytes 1769480 | tf_op jit(solution)/shard_map/ppermute | solution.py:323
  44.9 19.1 %collective-permute-start.7 = (bf16[1,256,1024]{2,1,0:T(8,128)(2,1)}, bf16[1,256,1024]{2,1,0:T(8,128)(2,1)S(1)}, u32[]{:S(2)}, u32[]{:S(2)}) collective-permute-start(bf16[1,256,1024]{2,1,0:T(8,128)(2,1)} %slice.9), channel_id=1, source_target_pairs={{0,96},{32,0},{64,32},{96,64},{1,97},{33,1},{65,33},{97,65},{2,98}... | collective-permute-start | bytes 1572872 | tf_op jit(solution)/shard_map/ppermute | solution.py:319
  46.0 18.0 %collective-permute-start.6 = (bf16[1,256,1024]{2,1,0:T(8,128)(2,1)S(1)}, bf16[1,256,1024]{2,1,0:T(8,128)(2,1)S(1)}, u32[]{:S(2)}, u32[]{:S(2)}) collective-permute-start(bf16[1,256,1024]{2,1,0:T(8,128)(2,1)S(1)} %slice.8), channel_id=1, source_target_pairs={{0,32},{32,64},{64,96},{96,0},{1,33},{33,65},{65,97},{97,1},{2,34}... | collective-permute-start | bytes 1572872 | tf_op jit(solution)/shard_map/ppermute | solution.py:319
  76.9 12.9 %all-to-all-start.1 = ((bf16[8,96,256]{2,1,0:T(8,128)(2,1)}), bf16[8,96,256]{2,1,0:T(8,128)(2,1)S(1)}, u32[]{:S(2)}, u32[]{:S(2)}) async-start(bf16[8,96,256]{2,1,0:T(8,128)(2,1)} %bitcast.7), calls=%async_computation.1 | async-start | bytes 786432 | tf_op jit(solution)/shard_map/all_to_all | solution.py:327
  82.4 11.5 %collective-permute-start.10 = (bf16[4,96,256]{2,1,0:T(8,128)(2,1)}, bf16[4,96,256]{2,1,0:T(8,128)(2,1)S(1)}, u32[]{:S(2)}, u32[]{:S(2)}) collective-permute-start(bf16[4,96,256]{2,1,0:T(8,128)(2,1)} %get-tuple-element.54), channel_id=1, source_target_pairs={{0,16},{16,0},{1,17},{17,1},{2,18},{18,2},{3,19},{19,3},{4,20},{20... | collective-permute-start | bytes 589832 | tf_op jit(solution)/shard_map/ppermute | solution.py:323
  93.9 16.0 %all-to-all-start.2 = ((bf16[8,96,256]{2,1,0:T(8,128)(2,1)}), bf16[8,96,256]{2,1,0:T(8,128)(2,1)S(1)}, u32[]{:S(2)}, u32[]{:S(2)}) async-start(bf16[8,96,256]{2,1,0:T(8,128)(2,1)} %get-tuple-element.55), calls=%async_computation.2 | async-start | bytes 786432 | tf_op jit(solution)/shard_map/all_to_all | solution.py:327
  99.0 10.9 %collective-permute-start.12 = (bf16[4,96,256]{2,1,0:T(8,128)(2,1)}, bf16[4,96,256]{2,1,0:T(8,128)(2,1)}, u32[]{:S(2)}, u32[]{:S(2)}) collective-permute-start(bf16[4,96,256]{2,1,0:T(8,128)(2,1)} %collective-permute-done.9), channel_id=1, source_target_pairs={{0,16},{16,0},{1,17},{17,1},{2,18},{18,2},{3,19},{19,3},{4,20},{20... | collective-permute-start | bytes 589832 | tf_op jit(solution)/shard_map/ppermute | solution.py:323
  109.9 16.9 %collective-permute-start.14 = (bf16[768,256]{1,0:T(8,128)(2,1)S(1)}, bf16[768,256]{1,0:T(8,128)(2,1)S(1)}, u32[]{:S(2)}, u32[]{:S(2)}) collective-permute-start(bf16[768,256]{1,0:T(8,128)(2,1)S(1)} %bitcast.13), channel_id=1, source_target_pairs={{0,16},{16,0},{1,17},{17,1},{2,18},{18,2},{3,19},{19,3},{4,20},{20... | collective-permute-start | bytes 1179656 | tf_op jit(solution)/shard_map/ppermute | solution.py:323
  117.2 56.8 %all-to-all-start.3 = ((bf16[32,192,128]{2,1,0:T(8,128)(2,1)}), bf16[32,192,128]{2,1,0:T(8,128)(2,1)S(1)}, u32[]{:S(2)}, u32[]{:S(2)}) async-start(bf16[32,192,128]{2,1,0:T(8,128)(2,1)} %backward.1), calls=%async_computation.3 | async-start | bytes 3145728 | tf_op jit(solution)/shard_map/all_to_all | solution.py:327
  132.8 31.4 %collective-permute-start.16 = (bf16[48,768]{1,0:T(8,128)(2,1)S(1)}, bf16[48,768]{1,0:T(8,128)(2,1)S(1)}, u32[]{:S(2)}, u32[]{:S(2)}) collective-permute-start(bf16[48,768]{1,0:T(8,128)(2,1)S(1)} %get-tuple-element.64), channel_id=1, source_target_pairs={{0,2},{2,0},{4,6},{6,4},{8,10},{10,8},{12,14},{14,12},{1,3},{3,1},... | collective-permute-start | bytes 221192 | tf_op jit(solution)/shard_map/ppermute | solution.py:323
  133.0 37.6 %collective-permute-start.17 = (bf16[48,768]{1,0:T(8,128)(2,1)S(1)}, bf16[48,768]{1,0:T(8,128)(2,1)S(1)}, u32[]{:S(2)}, u32[]{:S(2)}) collective-permute-start(bf16[48,768]{1,0:T(8,128)(2,1)S(1)} %get-tuple-element.65), channel_id=1, source_target_pairs={{0,4},{2,6},{4,0},{6,2},{8,12},{10,14},{12,8},{14,10},{1,5},{3,7},... | collective-permute-start | bytes 221192 | tf_op jit(solution)/shard_map/ppermute | solution.py:323
  135.7 46.0 %collective-permute-start.18 = (bf16[48,768]{1,0:T(8,128)(2,1)}, bf16[48,768]{1,0:T(8,128)(2,1)S(1)}, u32[]{:S(2)}, u32[]{:S(2)}) collective-permute-start(bf16[48,768]{1,0:T(8,128)(2,1)} %get-tuple-element.66), channel_id=1, source_target_pairs={{0,6},{2,4},{4,2},{6,0},{8,14},{10,12},{12,10},{14,8},{1,7},{3,5},... | collective-permute-start | bytes 221192 | tf_op jit(solution)/shard_map/ppermute | solution.py:323
  136.3 45.5 %collective-permute-start.19 = (bf16[48,768]{1,0:T(8,128)(2,1)}, bf16[48,768]{1,0:T(8,128)(2,1)S(1)}, u32[]{:S(2)}, u32[]{:S(2)}) collective-permute-start(bf16[48,768]{1,0:T(8,128)(2,1)} %get-tuple-element.67), channel_id=1, source_target_pairs={{0,8},{2,10},{4,12},{6,14},{8,0},{10,2},{12,4},{14,6},{1,9},{3,11}... | collective-permute-start | bytes 221192 | tf_op jit(solution)/shard_map/ppermute | solution.py:323
  140.8 41.0 %collective-permute-start.20 = (bf16[48,768]{1,0:T(8,128)(2,1)}, bf16[48,768]{1,0:T(8,128)(2,1)S(1)}, u32[]{:S(2)}, u32[]{:S(2)}) collective-permute-start(bf16[48,768]{1,0:T(8,128)(2,1)} %get-tuple-element.68), channel_id=1, source_target_pairs={{0,10},{2,8},{4,14},{6,12},{8,2},{10,0},{12,6},{14,4},{1,11},{3,9}... | collective-permute-start | bytes 221192 | tf_op jit(solution)/shard_map/ppermute | solution.py:323
  164.2 17.5 %collective-permute-start.21 = (bf16[48,768]{1,0:T(8,128)(2,1)}, bf16[48,768]{1,0:T(8,128)(2,1)S(1)}, u32[]{:S(2)}, u32[]{:S(2)}) collective-permute-start(bf16[48,768]{1,0:T(8,128)(2,1)} %get-tuple-element.69), channel_id=1, source_target_pairs={{0,12},{2,14},{4,8},{6,10},{8,4},{10,6},{12,0},{14,2},{1,13},{3,15... | collective-permute-start | bytes 221192 | tf_op jit(solution)/shard_map/ppermute | solution.py:323
  170.6 11.2 %collective-permute-start.22 = (bf16[48,768]{1,0:T(8,128)(2,1)}, bf16[48,768]{1,0:T(8,128)(2,1)S(1)}, u32[]{:S(2)}, u32[]{:S(2)}) collective-permute-start(bf16[48,768]{1,0:T(8,128)(2,1)} %get-tuple-element.70), channel_id=1, source_target_pairs={{0,14},{2,12},{4,10},{6,8},{8,6},{10,4},{12,2},{14,0},{1,15},{3,13... | collective-permute-start | bytes 221192 | tf_op jit(solution)/shard_map/ppermute | solution.py:323
  176.5 21.1 %all-to-all-start.4 = ((f32[8,2,16,192]{3,2,1,0:T(8,128)}), f32[8,2,16,192]{3,2,1,0:T(8,128)S(1)}, u32[]{:S(2)}, u32[]{:S(2)}) async-start(f32[8,2,16,192]{3,2,1,0:T(8,128)} %owned.1), calls=%async_computation.4 | async-start | bytes 524288 | tf_op jit(solution)/shard_map/all_to_all | solution.py:327
  181.8 15.7 %collective-permute-start.23 = (f32[2,24,768]{2,1,0:T(8,128)S(1)}, f32[2,24,768]{2,1,0:T(8,128)S(1)}, u32[]{:S(2)}, u32[]{:S(2)}) collective-permute-start(f32[2,24,768]{2,1,0:T(8,128)S(1)} %bitcast.20), channel_id=1, source_target_pairs={{0,0},{1,4},{2,1},{3,5},{4,2},{5,6},{6,3},{7,7},{8,32},{9,36},{10,... | collective-permute-start | bytes 442376 | tf_op jit(solution)/shard_map/ppermute | solution.py:421
  (15 other events, 117.4 us)

commit v12 on v11

--- a/solution.py
+++ b/solution.py
@@ -118,26 +118,25 @@
     return pl.BlockSpec(memory_space=pltpu.MemorySpace.HBM)
 
 
-def join_kernel(own_ref, own_slots_ref, came1_ref, came2_ref, came3_ref, part_ref, slots_ref):
-    part_ref[0] = own_ref[0]
+def join_kernel(own_slots_ref, came1_ref, came2_ref, came3_ref, part_ref, slots_ref):
     slots_ref[0:1] = own_slots_ref[0, :, :BLK].astype(F32).astype(jnp.int32)[0:1]
     for k, ref in enumerate((came1_ref, came2_ref, came3_ref), 1):
-        part_ref[k] = ref[0, :96]
+        part_ref[k - 1] = ref[0, :96]
         slots_ref[k : k + 1] = ref[0, 96:, :BLK].astype(F32).astype(jnp.int32)[0:1]
 
 
-def join(own, own_slots, came):
+def join(own_slots, came):
     return pl.pallas_call(
         join_kernel,
-        in_specs=[vmem()] * 5,
+        in_specs=[vmem()] * 4,
         out_specs=[vmem(), vmem()],
         out_shape=[
-            jax.ShapeDtypeStruct((4, *own.shape[1:]), BF16),
+            jax.ShapeDtypeStruct((3, 96, came[0].shape[2]), BF16),
             jax.ShapeDtypeStruct((4, BLK), jnp.int32),
         ],
         compiler_params=params(),
         name="join",
-    )(own, own_slots, *came)
+    )(own_slots, *came)
 
 
 def forward_kernel(
@@ -378,11 +377,14 @@
     bias_share = lax.dynamic_slice_in_dim(bias, group * share, share)
     bias_share = jnp.broadcast_to(bias_share[:, None], (share, features.shape[0]))
     cotangent_share = lax.dynamic_slice_in_dim(cotangent, group * share, share, 1).T
-    w_part, slots = join(pieces[0], own_slots, came)
-    w_part, bias_share, cotangent_share = lax.optimization_barrier((w_part, bias_share, cotangent_share))
+    own_other = swap(pieces[0], "xh")
+    w_rest, slots = join(own_slots, came)
+    w_rest, own_other = lax.optimization_barrier((w_rest, own_other))
+    w_rest, bias_share, cotangent_share = lax.optimization_barrier((w_rest, bias_share, cotangent_share))
     slots, bias_share, cotangent_share = in_hbm(slots), in_hbm(bias_share), in_hbm(cotangent_share)
     far0, far1 = step(back[:1], 1), step(fore[1:], -1)
-    w_other = swap(w_part, "xh")
+    w_part = jnp.concatenate([pieces[0], w_rest])
+    w_other = jnp.concatenate([own_other, swap(w_rest, "xh")])
     w_part, w_other, far0, far1 = lax.optimization_barrier((w_part, w_other, far0, far1))
     w_mine = jnp.concatenate(
         [jnp.where(xh == 0, w_part, w_other), jnp.where(xh == 0, w_other, w_part)], axis=1

time: 201 us -> 207 us (1.030)
  starting transfers between devices: 76.1 us -> 80.1 us
    ppermute x16 -> x17, starting transfers between devices: 26.1 us -> 28 us  [swap(): return lax.ppermute(value, axis, [(i, i ^ flip) for i in range(size)])]
    ppermute x16 -> x17, waiting for transfers between devices: 53.9 us -> 54.5 us  [swap(): return lax.ppermute(value, axis, [(i, i ^ flip) for i in range(size)])]
  transfers between devices with their start and end apart: 29 -> 30, of which waited for: 11 -> 12; matrix products, arithmetic and copies ran while one was open for 4% -> 5% of each run, Pallas kernels for 9% -> 8%
where the time goes in v12:
time: 207 us; the launch traced here: 206 us
  waiting for transfers between devices  81.1 us (39%)
  starting transfers between devices  80.1 us (39%)
  Pallas kernels  30.5 us (15%)
  local copies, waits for them, and re-layouts  9.9 us (5%)
  other arithmetic  3.09 us (1%)
    ppermute x17, waiting for transfers between devices, swap(): return lax.ppermute(value, axis, [(i, i ^ flip) for i in range(size)])  54.5 us
    all_to_all x5, starting transfers between devices, exchange(): return lax.all_to_all(value, axis, 0, 0, tiled=True)  38.3 us
    ppermute x17, starting transfers between devices, swap(): return lax.ppermute(value, axis, [(i, i ^ flip) for i in range(size)])  28 us
    ppermute x1, waiting for transfers between devices, per_device(): lax.ppermute(piece.reshape(2, 24, width), ('y', *TGT), to_owner())  11.7 us
    ppermute x3, waiting for transfers between devices, around(): lax.ppermute(v, axis, [(i, (i + k) % size) for i in range(size)])  9.67 us
    pallas_call x1, Pallas kernels, forward_of(): pl.pallas_call(forward_kernel, in_specs=[smem(), smem()] + [hbm()] * 5 +...  8.49 us
    ppermute x4, starting transfers between devices, step(): return lax.ppermute(value, 'y', [(i, (i + by) % 4) for i in range(4)])  6.62 us
    pallas_call x1, Pallas kernels, backward_of(): pl.pallas_call(backward_kernel, in_specs=[smem(), smem()] + [hbm()] * 5 +...  6.33 us
  transfers between devices with their start and end apart: 30, of which 12 were waited for; matrix products, arithmetic and copies ran while one was open for 5% of the time, Pallas kernels for 8%

profile of v12, /device:TPU:56, one launch (start us, length us, event | category | flops | bytes accessed | tf_op | source)
XLA Modules:
  0.0 205.6 jit_solution(5981376696559455410)
XLA Ops:
  0.6 5.0 %adjacency.1.own_ref = bf16[2,256,1024]{2,1,0:T(8,128)(2,1)S(1)} custom-call(s32[2,2]{1,0:T(2,128)} %count_ref.1, s32[2,256,8,128]{3,2,1,0:T(8,128)} %values_ref.1), custom_call_target="tpu_custom_call" | custom-call | tf_op jit(solution)/shard_map/adjacency/pallas_call | solution.py:61
  12.2 11.4 %all-to-all-start = ((bf16[32,192,128]{2,1,0:T(8,128)(2,1)}), bf16[32,192,128]{2,1,0:T(8,128)(2,1)}, u32[]{:S(2)}, u32[]{:S(2)}) async-start(bf16[32,192,128]{2,1,0:T(8,128)(2,1)} %outgoing.1), calls=%async_computation | async-start | bytes 3145728 | tf_op jit(solution)/shard_map/all_to_all | solution.py:326
  29.5 9.7 %collective-permute-done.2.came3_ref = bf16[1,112,768]{2,1,0:T(8,128)(2,1)S(1)} collective-permute-done((bf16[1,112,768]{2,1,0:T(8,128)(2,1)S(1)}, bf16[1,112,768]{2,1,0:T(8,128)(2,1)S(1)}, u32[]{:S(2)}, u32[]{:S(2)}) %collective-permute-start.2) | collective-permute-done | bytes 172064 | tf_op jit(solution)/shard_map/ppermute | solution.py:331
  39.2 3.0 %collective-permute-start.5 = (bf16[1,96,768]{2,1,0:T(8,128)(2,1)}, bf16[1,96,768]{2,1,0:T(8,128)(2,1)}, u32[]{:S(2)}, u32[]{:S(2)}) collective-permute-start(bf16[1,96,768]{2,1,0:T(8,128)(2,1)} %get-tuple-element.75), channel_id=1, source_target_pairs={{0,16},{16,0},{1,17},{17,1},{2,18},{18,2},{3,19},{19,3},{4,20},{20... | collective-permute-start | bytes 442376 | tf_op jit(solution)/shard_map/ppermute | solution.py:322
  43.9 4.8 %collective-permute-done.5 = bf16[1,96,768]{2,1,0:T(8,128)(2,1)} collective-permute-done((bf16[1,96,768]{2,1,0:T(8,128)(2,1)}, bf16[1,96,768]{2,1,0:T(8,128)(2,1)}, u32[]{:S(2)}, u32[]{:S(2)}) %collective-permute-start.5) | collective-permute-done | bytes 147488 | tf_op jit(solution)/shard_map/ppermute | solution.py:322
  53.1 3.3 %collective-permute-start.7 = (bf16[1,256,1024]{2,1,0:T(8,128)(2,1)S(1)}, bf16[1,256,1024]{2,1,0:T(8,128)(2,1)S(1)}, u32[]{:S(2)}, u32[]{:S(2)}) collective-permute-start(bf16[1,256,1024]{2,1,0:T(8,128)(2,1)S(1)} %slice.8), channel_id=1, source_target_pairs={{0,32},{32,64},{64,96},{96,0},{1,33},{33,65},{65,97},{97,1},{2,34}... | collective-permute-start | bytes 1572872 | tf_op jit(solution)/shard_map/ppermute | solution.py:318
  57.4 10.6 %collective-permute-done.6 = bf16[3,96,768]{2,1,0:T(8,128)(2,1)} collective-permute-done((bf16[3,96,768]{2,1,0:T(8,128)(2,1)S(1)}, bf16[3,96,768]{2,1,0:T(8,128)(2,1)}, u32[]{:S(2)}, u32[]{:S(2)}) %collective-permute-start.6) | collective-permute-done | bytes 442400 | tf_op jit(solution)/shard_map/ppermute | solution.py:322
  70.3 2.8 %collective-permute-done.9.w_theirs_ref = bf16[4,192,768]{2,1,0:T(8,128)(2,1)S(1)} collective-permute-done((bf16[4,192,768]{2,1,0:T(8,128)(2,1)S(1)}, bf16[4,192,768]{2,1,0:T(8,128)(2,1)S(1)}, u32[]{:S(2)}, u32[]{:S(2)}) %collective-permute-start.9) | collective-permute-done | bytes 1179680 | tf_op jit(solution)/shard_map/ppermute | solution.py:322
  73.1 8.5 %forward.1 = (bf16[4,96,256]{2,1,0:T(8,128)(2,1)}, bf16[4,96,256]{2,1,0:T(8,128)(2,1)}, bf16[4,96,256]{2,1,0:T(8,128)(2,1)}, bf16[4,96,256]{2,1,0:T(8,128)(2,1)}, bf16[768,256]{1,0:T(8,128)(2,1)}) custom-call(s32[6]{0:T(128)} %stack.27.place_ref, s32[4,128]{1,0:T(4,128)} %copy-done.2, bf16[2,256,1024]{2,1,0:T(8,128)(2,1)} %copy-done.1, ...), custom_call_target="tpu_custom_call" | custom-call | tf_op jit(solution)/shard_map/forward/pallas_call | solution.py:185
  81.6 4.7 %all-to-all-start.1 = ((bf16[8,96,256]{2,1,0:T(8,128)(2,1)}), bf16[8,96,256]{2,1,0:T(8,128)(2,1)S(1)}, u32[]{:S(2)}, u32[]{:S(2)}) async-start(bf16[8,96,256]{2,1,0:T(8,128)(2,1)} %bitcast.7), calls=%async_computation.1 | async-start | bytes 786432 | tf_op jit(solution)/shard_map/all_to_all | solution.py:326
  88.5 5.2 %all-to-all-done.1.arrived_ref = bf16[8,96,256]{2,1,0:T(8,128)(2,1)S(1)} async-done(((bf16[8,96,256]{2,1,0:T(8,128)(2,1)}), bf16[8,96,256]{2,1,0:T(8,128)(2,1)S(1)}, u32[]{:S(2)}, u32[]{:S(2)}) %all-to-all-start.1) | async-done | bytes 393248 | tf_op jit(solution)/shard_map/all_to_all | solution.py:326
  97.9 5.1 %all-to-all-start.2 = ((bf16[8,96,256]{2,1,0:T(8,128)(2,1)}), bf16[8,96,256]{2,1,0:T(8,128)(2,1)S(1)}, u32[]{:S(2)}, u32[]{:S(2)}) async-start(bf16[8,96,256]{2,1,0:T(8,128)(2,1)} %get-tuple-element.59), calls=%async_computation.2 | async-start | bytes 786432 | tf_op jit(solution)/shard_map/all_to_all | solution.py:326
  105.9 7.4 %collective-permute-done.13.far_core_ref = bf16[4,96,256]{2,1,0:T(8,128)(2,1)} collective-permute-done((bf16[4,96,256]{2,1,0:T(8,128)(2,1)}, bf16[4,96,256]{2,1,0:T(8,128)(2,1)}, u32[]{:S(2)}, u32[]{:S(2)}) %collective-permute-start.13) | collective-permute-done | bytes 196640 | tf_op jit(solution)/shard_map/ppermute | solution.py:322
  114.9 6.3 %backward.1 = bf16[32,192,128]{2,1,0:T(8,128)(2,1)} custom-call(s32[6]{0:T(128)} %stack.27.place_ref, s32[4,128]{1,0:T(4,128)} %copy-done.2, bf16[2,256,1024]{2,1,0:T(8,128)(2,1)} %copy-done.1, bf16[2,256,1024]{2,1,0:T(8,128)(2,1)} %collective-permute-done.3.back_ref, bf16[2,256,1024]{2,1,0:T(8,128)(2,1)} %copy-done.4, bf16[1,256,1024]{2,1,0:T(8,128)(2,1)} %copy-done.6, ...), custom_call_target="tpu_custom_call" | custom-call | tf_op jit(solution)/shard_map/backward/pallas_call | solution.py:247
  121.2 12.0 %all-to-all-start.3 = ((bf16[32,192,128]{2,1,0:T(8,128)(2,1)}), bf16[32,192,128]{2,1,0:T(8,128)(2,1)S(1)}, u32[]{:S(2)}, u32[]{:S(2)}) async-start(bf16[32,192,128]{2,1,0:T(8,128)(2,1)} %backward.1), calls=%async_computation.3 | async-start | bytes 3145728 | tf_op jit(solution)/shard_map/all_to_all | solution.py:326
  135.6 3.9 %weight_terms.1 = (f32[48,768]{1,0:T(8,128)S(1)}, bf16[48,768]{1,0:T(8,128)(2,1)S(1)}, bf16[48,768]{1,0:T(8,128)(2,1)S(1)}, bf16[48,768]{1,0:T(8,128)(2,1)}, bf1...) custom-call(s32[6]{0:T(128)} %stack.27.place_ref, ...), custom_call_target="tpu_custom_call" | custom-call | flops 24500000768 | tf_op jit(solution)/shard_map/weight_terms/pallas_call | solution.py:279
  139.8 2.7 %collective-permute-start.18 = (bf16[48,768]{1,0:T(8,128)(2,1)S(1)}, bf16[48,768]{1,0:T(8,128)(2,1)S(1)}, u32[]{:S(2)}, u32[]{:S(2)}) collective-permute-start(bf16[48,768]{1,0:T(8,128)(2,1)S(1)} %get-tuple-element.69), channel_id=1, source_target_pairs={{0,4},{2,6},{4,0},{6,2},{8,12},{10,14},{12,8},{14,10},{1,5},{3,7},... | collective-permute-start | bytes 221192 | tf_op jit(solution)/shard_map/ppermute | solution.py:322
  143.0 4.5 %collective-permute-start.20 = (bf16[48,768]{1,0:T(8,128)(2,1)}, bf16[48,768]{1,0:T(8,128)(2,1)S(1)}, u32[]{:S(2)}, u32[]{:S(2)}) collective-permute-start(bf16[48,768]{1,0:T(8,128)(2,1)} %get-tuple-element.71), channel_id=1, source_target_pairs={{0,8},{2,10},{4,12},{6,14},{8,0},{10,2},{12,4},{14,6},{1,9},{3,11}... | collective-permute-start | bytes 221192 | tf_op jit(solution)/shard_map/ppermute | solution.py:322
  148.6 22.3 %collective-permute-done.17 = bf16[48,768]{1,0:T(8,128)(2,1)S(1)} collective-permute-done((bf16[48,768]{1,0:T(8,128)(2,1)S(1)}, bf16[48,768]{1,0:T(8,128)(2,1)S(1)}, u32[]{:S(2)}, u32[]{:S(2)}) %collective-permute-start.17) | collective-permute-done | bytes 73760 | tf_op jit(solution)/shard_map/ppermute | solution.py:322
  170.9 4.0 %collective-permute-start.22 = (bf16[48,768]{1,0:T(8,128)(2,1)}, bf16[48,768]{1,0:T(8,128)(2,1)S(1)}, u32[]{:S(2)}, u32[]{:S(2)}) collective-permute-start(bf16[48,768]{1,0:T(8,128)(2,1)} %get-tuple-element.73), channel_id=1, source_target_pairs={{0,12},{2,14},{4,8},{6,10},{8,4},{10,6},{12,0},{14,2},{1,13},{3,15... | collective-permute-start | bytes 221192 | tf_op jit(solution)/shard_map/ppermute | solution.py:322
  177.3 3.4 %collective-permute-start.23 = (bf16[48,768]{1,0:T(8,128)(2,1)}, bf16[48,768]{1,0:T(8,128)(2,1)S(1)}, u32[]{:S(2)}, u32[]{:S(2)}) collective-permute-start(bf16[48,768]{1,0:T(8,128)(2,1)} %get-tuple-element.74), channel_id=1, source_target_pairs={{0,14},{2,12},{4,10},{6,8},{8,6},{10,4},{12,2},{14,0},{1,15},{3,13... | collective-permute-start | bytes 221192 | tf_op jit(solution)/shard_map/ppermute | solution.py:322
  183.2 5.1 %all-to-all-start.4 = ((f32[8,2,16,192]{3,2,1,0:T(8,128)}), f32[8,2,16,192]{3,2,1,0:T(8,128)S(1)}, u32[]{:S(2)}, u32[]{:S(2)}) async-start(f32[8,2,16,192]{3,2,1,0:T(8,128)} %owned.1), calls=%async_computation.4 | async-start | bytes 524288 | tf_op jit(solution)/shard_map/all_to_all | solution.py:326
  188.4 3.9 %collective-permute-start.24 = (f32[2,24,768]{2,1,0:T(8,128)S(1)}, f32[2,24,768]{2,1,0:T(8,128)S(1)}, u32[]{:S(2)}, u32[]{:S(2)}) collective-permute-start(f32[2,24,768]{2,1,0:T(8,128)S(1)} %bitcast.20), channel_id=1, source_target_pairs={{0,0},{1,4},{2,1},{3,5},{4,2},{5,6},{6,3},{7,7},{8,32},{9,36},{10,... | collective-permute-start | bytes 442376 | tf_op jit(solution)/shard_map/ppermute | solution.py:423
  192.3 11.7 %collective-permute-done.24 = f32[2,24,768]{2,1,0:T(8,128)S(1)} collective-permute-done((f32[2,24,768]{2,1,0:T(8,128)S(1)}, f32[2,24,768]{2,1,0:T(8,128)S(1)}, u32[]{:S(2)}, u32[]{:S(2)}) %collective-permute-start.24) | collective-permute-done | bytes 147488 | tf_op jit(solution)/shard_map/ppermute | solution.py:423
  (87 shorter events, 43.4 us)
Async XLA Ops:
  5.7 45.4 %collective-permute-start.4 = (bf16[2,256,1024]{2,1,0:T(8,128)(2,1)S(1)}, bf16[2,256,1024]{2,1,0:T(8,128)(2,1)S(1)}, u32[]{:S(2)}, u32[]{:S(2)}) collective-permute-start(bf16[2,256,1024]{2,1,0:T(8,128)(2,1)S(1)} %adjacency.1.own_ref), channel_id=1, source_target_pairs={{0,96},{32,0},{64,32},{96,64},{1,97},{33,1},{65,33},{97,65},{2,98}... | collective-permute-start | bytes 3145736 | tf_op jit(solution)/shard_map/ppermute | solution.py:318
  6.5 45.5 %collective-permute-start.3 = (bf16[2,256,1024]{2,1,0:T(8,128)(2,1)S(1)}, bf16[2,256,1024]{2,1,0:T(8,128)(2,1)}, u32[]{:S(2)}, u32[]{:S(2)}) collective-permute-start(bf16[2,256,1024]{2,1,0:T(8,128)(2,1)S(1)} %adjacency.1.own_ref), channel_id=1, source_target_pairs={{0,32},{32,64},{64,96},{96,0},{1,33},{33,65},{65,97},{97,1},{2,34}... | collective-permute-start | bytes 3145736 | tf_op jit(solution)/shard_map/ppermute | solution.py:318
  12.2 60.9 %all-to-all-start = ((bf16[32,192,128]{2,1,0:T(8,128)(2,1)}), bf16[32,192,128]{2,1,0:T(8,128)(2,1)}, u32[]{:S(2)}, u32[]{:S(2)}) async-start(bf16[32,192,128]{2,1,0:T(8,128)(2,1)} %outgoing.1), calls=%async_computation | async-start | bytes 3145728 | tf_op jit(solution)/shard_map/all_to_all | solution.py:326
  26.3 12.9 %collective-permute-start.2 = (bf16[1,112,768]{2,1,0:T(8,128)(2,1)S(1)}, bf16[1,112,768]{2,1,0:T(8,128)(2,1)S(1)}, u32[]{:S(2)}, u32[]{:S(2)}) collective-permute-start(bf16[1,112,768]{2,1,0:T(8,128)(2,1)S(1)} %get-tuple-element.81), channel_id=1, source_target_pairs={{0,96},{32,0},{64,32},{96,64},{1,97},{33,1},{65,33},{97,65},{2,98}... | collective-permute-start | bytes 516104 | tf_op jit(solution)/shard_map/ppermute | solution.py:331
  26.3 17.5 %collective-permute-start.1 = (bf16[1,112,768]{2,1,0:T(8,128)(2,1)}, bf16[1,112,768]{2,1,0:T(8,128)(2,1)S(1)}, u32[]{:S(2)}, u32[]{:S(2)}) collective-permute-start(bf16[1,112,768]{2,1,0:T(8,128)(2,1)} %get-tuple-element.82), channel_id=1, source_target_pairs={{0,64},{32,96},{64,0},{96,32},{1,65},{33,97},{65,1},{97,33},{2,66}... | collective-permute-start | bytes 516104 | tf_op jit(solution)/shard_map/ppermute | solution.py:331
  27.8 16.1 %collective-permute-start = (bf16[1,112,768]{2,1,0:T(8,128)(2,1)}, bf16[1,112,768]{2,1,0:T(8,128)(2,1)S(1)}, u32[]{:S(2)}, u32[]{:S(2)}) collective-permute-start(bf16[1,112,768]{2,1,0:T(8,128)(2,1)} %get-tuple-element.83), channel_id=1, source_target_pairs={{0,32},{32,64},{64,96},{96,0},{1,33},{33,65},{65,97},{97,1},{2,34}... | collective-permute-start | bytes 516104 | tf_op jit(solution)/shard_map/ppermute | solution.py:331
  49.4 18.6 %collective-permute-start.6 = (bf16[3,96,768]{2,1,0:T(8,128)(2,1)S(1)}, bf16[3,96,768]{2,1,0:T(8,128)(2,1)}, u32[]{:S(2)}, u32[]{:S(2)}) collective-permute-start(bf16[3,96,768]{2,1,0:T(8,128)(2,1)S(1)} %get-tuple-element.43), channel_id=1, source_target_pairs={{0,16},{16,0},{1,17},{17,1},{2,18},{18,2},{3,19},{19,3},{4,20},{20... | collective-permute-start | bytes 1327112 | tf_op jit(solution)/shard_map/ppermute | solution.py:322
  52.0 17.1 %collective-permute-start.8 = (bf16[1,256,1024]{2,1,0:T(8,128)(2,1)}, bf16[1,256,1024]{2,1,0:T(8,128)(2,1)S(1)}, u32[]{:S(2)}, u32[]{:S(2)}) collective-permute-start(bf16[1,256,1024]{2,1,0:T(8,128)(2,1)} %slice.9), channel_id=1, source_target_pairs={{0,96},{32,0},{64,32},{96,64},{1,97},{33,1},{65,33},{97,65},{2,98}... | collective-permute-start | bytes 1572872 | tf_op jit(solution)/shard_map/ppermute | solution.py:318
  53.1 16.0 %collective-permute-start.7 = (bf16[1,256,1024]{2,1,0:T(8,128)(2,1)S(1)}, bf16[1,256,1024]{2,1,0:T(8,128)(2,1)S(1)}, u32[]{:S(2)}, u32[]{:S(2)}) collective-permute-start(bf16[1,256,1024]{2,1,0:T(8,128)(2,1)S(1)} %slice.8), channel_id=1, source_target_pairs={{0,32},{32,64},{64,96},{96,0},{1,33},{33,65},{65,97},{97,1},{2,34}... | collective-permute-start | bytes 1572872 | tf_op jit(solution)/shard_map/ppermute | solution.py:318
  81.6 12.1 %all-to-all-start.1 = ((bf16[8,96,256]{2,1,0:T(8,128)(2,1)}), bf16[8,96,256]{2,1,0:T(8,128)(2,1)S(1)}, u32[]{:S(2)}, u32[]{:S(2)}) async-start(bf16[8,96,256]{2,1,0:T(8,128)(2,1)} %bitcast.7), calls=%async_computation.1 | async-start | bytes 786432 | tf_op jit(solution)/shard_map/all_to_all | solution.py:326
  86.2 11.6 %collective-permute-start.11 = (bf16[4,96,256]{2,1,0:T(8,128)(2,1)}, bf16[4,96,256]{2,1,0:T(8,128)(2,1)S(1)}, u32[]{:S(2)}, u32[]{:S(2)}) collective-permute-start(bf16[4,96,256]{2,1,0:T(8,128)(2,1)} %get-tuple-element.58), channel_id=1, source_target_pairs={{0,16},{16,0},{1,17},{17,1},{2,18},{18,2},{3,19},{19,3},{4,20},{20... | collective-permute-start | bytes 589832 | tf_op jit(solution)/shard_map/ppermute | solution.py:322
  97.9 15.5 %all-to-all-start.2 = ((bf16[8,96,256]{2,1,0:T(8,128)(2,1)}), bf16[8,96,256]{2,1,0:T(8,128)(2,1)S(1)}, u32[]{:S(2)}, u32[]{:S(2)}) async-start(bf16[8,96,256]{2,1,0:T(8,128)(2,1)} %get-tuple-element.59), calls=%async_computation.2 | async-start | bytes 786432 | tf_op jit(solution)/shard_map/all_to_all | solution.py:326
  103.0 10.3 %collective-permute-start.13 = (bf16[4,96,256]{2,1,0:T(8,128)(2,1)}, bf16[4,96,256]{2,1,0:T(8,128)(2,1)}, u32[]{:S(2)}, u32[]{:S(2)}) collective-permute-start(bf16[4,96,256]{2,1,0:T(8,128)(2,1)} %collective-permute-done.10), channel_id=1, source_target_pairs={{0,16},{16,0},{1,17},{17,1},{2,18},{18,2},{3,19},{19,3},{4,20},{20... | collective-permute-start | bytes 589832 | tf_op jit(solution)/shard_map/ppermute | solution.py:322
  113.3 20.2 %collective-permute-start.15 = (bf16[768,256]{1,0:T(8,128)(2,1)S(1)}, bf16[768,256]{1,0:T(8,128)(2,1)S(1)}, u32[]{:S(2)}, u32[]{:S(2)}) collective-permute-start(bf16[768,256]{1,0:T(8,128)(2,1)S(1)} %bitcast.13), channel_id=1, source_target_pairs={{0,16},{16,0},{1,17},{17,1},{2,18},{18,2},{3,19},{19,3},{4,20},{20... | collective-permute-start | bytes 1179656 | tf_op jit(solution)/shard_map/ppermute | solution.py:322
  121.2 59.5 %all-to-all-start.3 = ((bf16[32,192,128]{2,1,0:T(8,128)(2,1)}), bf16[32,192,128]{2,1,0:T(8,128)(2,1)S(1)}, u32[]{:S(2)}, u32[]{:S(2)}) async-start(bf16[32,192,128]{2,1,0:T(8,128)(2,1)} %backward.1), calls=%async_computation.3 | async-start | bytes 3145728 | tf_op jit(solution)/shard_map/all_to_all | solution.py:326
  139.5 31.4 %collective-permute-start.17 = (bf16[48,768]{1,0:T(8,128)(2,1)S(1)}, bf16[48,768]{1,0:T(8,128)(2,1)S(1)}, u32[]{:S(2)}, u32[]{:S(2)}) collective-permute-start(bf16[48,768]{1,0:T(8,128)(2,1)S(1)} %get-tuple-element.68), channel_id=1, source_target_pairs={{0,2},{2,0},{4,6},{6,4},{8,10},{10,8},{12,14},{14,12},{1,3},{3,1},... | collective-permute-start | bytes 221192 | tf_op jit(solution)/shard_map/ppermute | solution.py:322
  139.8 37.6 %collective-permute-start.18 = (bf16[48,768]{1,0:T(8,128)(2,1)S(1)}, bf16[48,768]{1,0:T(8,128)(2,1)S(1)}, u32[]{:S(2)}, u32[]{:S(2)}) collective-permute-start(bf16[48,768]{1,0:T(8,128)(2,1)S(1)} %get-tuple-element.69), channel_id=1, source_target_pairs={{0,4},{2,6},{4,0},{6,2},{8,12},{10,14},{12,8},{14,10},{1,5},{3,7},... | collective-permute-start | bytes 221192 | tf_op jit(solution)/shard_map/ppermute | solution.py:322
  142.5 45.9 %collective-permute-start.19 = (bf16[48,768]{1,0:T(8,128)(2,1)}, bf16[48,768]{1,0:T(8,128)(2,1)S(1)}, u32[]{:S(2)}, u32[]{:S(2)}) collective-permute-start(bf16[48,768]{1,0:T(8,128)(2,1)} %get-tuple-element.70), channel_id=1, source_target_pairs={{0,6},{2,4},{4,2},{6,0},{8,14},{10,12},{12,10},{14,8},{1,7},{3,5},... | collective-permute-start | bytes 221192 | tf_op jit(solution)/shard_map/ppermute | solution.py:322
  143.0 45.3 %collective-permute-start.20 = (bf16[48,768]{1,0:T(8,128)(2,1)}, bf16[48,768]{1,0:T(8,128)(2,1)S(1)}, u32[]{:S(2)}, u32[]{:S(2)}) collective-permute-start(bf16[48,768]{1,0:T(8,128)(2,1)} %get-tuple-element.71), channel_id=1, source_target_pairs={{0,8},{2,10},{4,12},{6,14},{8,0},{10,2},{12,4},{14,6},{1,9},{3,11}... | collective-permute-start | bytes 221192 | tf_op jit(solution)/shard_map/ppermute | solution.py:322
  147.5 40.8 %collective-permute-start.21 = (bf16[48,768]{1,0:T(8,128)(2,1)}, bf16[48,768]{1,0:T(8,128)(2,1)S(1)}, u32[]{:S(2)}, u32[]{:S(2)}) collective-permute-start(bf16[48,768]{1,0:T(8,128)(2,1)} %get-tuple-element.72), channel_id=1, source_target_pairs={{0,10},{2,8},{4,14},{6,12},{8,2},{10,0},{12,6},{14,4},{1,11},{3,9}... | collective-permute-start | bytes 221192 | tf_op jit(solution)/shard_map/ppermute | solution.py:322
  170.9 17.4 %collective-permute-start.22 = (bf16[48,768]{1,0:T(8,128)(2,1)}, bf16[48,768]{1,0:T(8,128)(2,1)S(1)}, u32[]{:S(2)}, u32[]{:S(2)}) collective-permute-start(bf16[48,768]{1,0:T(8,128)(2,1)} %get-tuple-element.73), channel_id=1, source_target_pairs={{0,12},{2,14},{4,8},{6,10},{8,4},{10,6},{12,0},{14,2},{1,13},{3,15... | collective-permute-start | bytes 221192 | tf_op jit(solution)/shard_map/ppermute | solution.py:322
  177.3 11.0 %collective-permute-start.23 = (bf16[48,768]{1,0:T(8,128)(2,1)}, bf16[48,768]{1,0:T(8,128)(2,1)S(1)}, u32[]{:S(2)}, u32[]{:S(2)}) collective-permute-start(bf16[48,768]{1,0:T(8,128)(2,1)} %get-tuple-element.74), channel_id=1, source_target_pairs={{0,14},{2,12},{4,10},{6,8},{8,6},{10,4},{12,2},{14,0},{1,15},{3,13... | collective-permute-start | bytes 221192 | tf_op jit(solution)/shard_map/ppermute | solution.py:322
  183.2 20.8 %all-to-all-start.4 = ((f32[8,2,16,192]{3,2,1,0:T(8,128)}), f32[8,2,16,192]{3,2,1,0:T(8,128)S(1)}, u32[]{:S(2)}, u32[]{:S(2)}) async-start(f32[8,2,16,192]{3,2,1,0:T(8,128)} %owned.1), calls=%async_computation.4 | async-start | bytes 524288 | tf_op jit(solution)/shard_map/all_to_all | solution.py:326
  188.4 15.6 %collective-permute-start.24 = (f32[2,24,768]{2,1,0:T(8,128)S(1)}, f32[2,24,768]{2,1,0:T(8,128)S(1)}, u32[]{:S(2)}, u32[]{:S(2)}) collective-permute-start(f32[2,24,768]{2,1,0:T(8,128)S(1)} %bitcast.20), channel_id=1, source_target_pairs={{0,0},{1,4},{2,1},{3,5},{4,2},{5,6},{6,3},{7,7},{8,32},{9,36},{10,... | collective-permute-start | bytes 442376 | tf_op jit(solution)/shard_map/ppermute | solution.py:423
  (17 other events, 149.4 us)

commit v13 on v11

--- a/solution.py
+++ b/solution.py
@@ -401,9 +401,7 @@
     output = activated.T
     of_far_core = swap(of_far_core, "xh")
     grad_copies, of_far = lax.optimization_barrier((grad_copies, of_far))
-    grads, of_core, of_far_core = lax.optimization_barrier(
-        (exchange(grad_copies, REL).reshape(width, -1), of_core, of_far_core)
-    )
+    grads, of_core = lax.optimization_barrier((exchange(grad_copies, REL).reshape(width, -1), of_core))
     of_core, of_far, of_far_core = in_hbm(of_core), in_hbm(of_far), in_hbm(of_far_core)
     partial = backward_of(place, slots, adjacency, resident(grads), w_mine, w_theirs, owners)
     returned = resident(exchange(in_hbm(partial), TGT))

time: 201 us -> 196 us (0.975)
  waiting for transfers between devices: 80.4 us -> 71.6 us
  starting transfers between devices: 76.1 us -> 79.7 us
    ppermute x16, waiting for transfers between devices: 53.9 us -> 42.9 us  [swap(): return lax.ppermute(value, axis, [(i, i ^ flip) for i in range(size)])]
    all_to_all x5, waiting for transfers between devices: 5.29 us -> 9.23 us  [exchange(): return lax.all_to_all(value, axis, 0, 0, tiled=True)]
    ppermute x16, starting transfers between devices: 26.1 us -> 29.3 us  [swap(): return lax.ppermute(value, axis, [(i, i ^ flip) for i in range(size)])]
  transfers between devices with their start and end apart: 29 -> 29, of which waited for: 11 -> 11; matrix products, arithmetic and copies ran while one was open for 4% -> 5% of each run, Pallas kernels for 9% -> 9%
where the time goes in v13:
time: 196 us; the launch traced here: 194 us
  starting transfers between devices  79.7 us (41%)
  waiting for transfers between devices  71.6 us (37%)
  Pallas kernels  30.4 us (16%)
  local copies, waits for them, and re-layouts  9.4 us (5%)
    ppermute x16, waiting for transfers between devices, swap(): return lax.ppermute(value, axis, [(i, i ^ flip) for i in range(size)])  42.9 us
    all_to_all x5, starting transfers between devices, exchange(): return lax.all_to_all(value, axis, 0, 0, tiled=True)  35.2 us
    ppermute x16, starting transfers between devices, swap(): return lax.ppermute(value, axis, [(i, i ^ flip) for i in range(size)])  29.3 us
    ppermute x1, waiting for transfers between devices, per_device(): lax.ppermute(piece.reshape(2, 24, width), ('y', *TGT), to_owner())  10.1 us
    ppermute x3, waiting for transfers between devices, around(): lax.ppermute(v, axis, [(i, (i + k) % size) for i in range(size)])  9.33 us
    all_to_all x5, waiting for transfers between devices, exchange(): return lax.all_to_all(value, axis, 0, 0, tiled=True)  9.23 us
    pallas_call x1, Pallas kernels, forward_of(): pl.pallas_call(forward_kernel, in_specs=[smem(), smem()] + [hbm()] * 5 +...  8.33 us
    ppermute x4, starting transfers between devices, step(): return lax.ppermute(value, 'y', [(i, (i + by) % 4) for i in range(4)])  6.62 us
  transfers between devices with their start and end apart: 29, of which 11 were waited for; matrix products, arithmetic and copies ran while one was open for 5% of the time, Pallas kernels for 9%

profile of v13, /device:TPU:56, one launch (start us, length us, event | category | flops | bytes accessed | tf_op | source)
XLA Modules:
  0.0 193.8 jit_solution(15231699138995909894)
XLA Ops:
  0.6 5.0 %adjacency.1.own_ref = bf16[2,256,1024]{2,1,0:T(8,128)(2,1)S(1)} custom-call(s32[2,2]{1,0:T(2,128)} %count_ref.1, s32[2,256,8,128]{3,2,1,0:T(8,128)} %values_ref.1), custom_call_target="tpu_custom_call" | custom-call | tf_op jit(solution)/shard_map/adjacency/pallas_call | solution.py:61
  12.2 11.4 %all-to-all-start = ((bf16[32,192,128]{2,1,0:T(8,128)(2,1)}), bf16[32,192,128]{2,1,0:T(8,128)(2,1)}, u32[]{:S(2)}, u32[]{:S(2)}) async-start(bf16[32,192,128]{2,1,0:T(8,128)(2,1)} %outgoing.1), calls=%async_computation | async-start | bytes 3145728 | tf_op jit(solution)/shard_map/all_to_all | solution.py:327
  29.9 9.3 %collective-permute-done.2.came3_ref = bf16[1,112,768]{2,1,0:T(8,128)(2,1)S(1)} collective-permute-done((bf16[1,112,768]{2,1,0:T(8,128)(2,1)S(1)}, bf16[1,112,768]{2,1,0:T(8,128)(2,1)S(1)}, u32[]{:S(2)}, u32[]{:S(2)}) %collective-permute-start.2) | collective-permute-done | bytes 172064 | tf_op jit(solution)/shard_map/ppermute | solution.py:332
  40.0 3.0 %collective-permute-start.5 = (bf16[4,96,768]{2,1,0:T(8,128)(2,1)S(1)}, bf16[4,96,768]{2,1,0:T(8,128)(2,1)}, u32[]{:S(2)}, u32[]{:S(2)}) collective-permute-start(bf16[4,96,768]{2,1,0:T(8,128)(2,1)S(1)} %get-tuple-element.43), channel_id=1, source_target_pairs={{0,16},{16,0},{1,17},{17,1},{2,18},{18,2},{3,19},{19,3},{4,20},{20... | collective-permute-start | bytes 1769480 | tf_op jit(solution)/shard_map/ppermute | solution.py:323
  46.0 3.3 %collective-permute-start.6 = (bf16[1,256,1024]{2,1,0:T(8,128)(2,1)S(1)}, bf16[1,256,1024]{2,1,0:T(8,128)(2,1)S(1)}, u32[]{:S(2)}, u32[]{:S(2)}) collective-permute-start(bf16[1,256,1024]{2,1,0:T(8,128)(2,1)S(1)} %slice.8), channel_id=1, source_target_pairs={{0,32},{32,64},{64,96},{96,0},{1,33},{33,65},{65,97},{97,1},{2,34}... | collective-permute-start | bytes 1572872 | tf_op jit(solution)/shard_map/ppermute | solution.py:319
  49.3 14.7 %collective-permute-done.5 = bf16[4,96,768]{2,1,0:T(8,128)(2,1)} collective-permute-done((bf16[4,96,768]{2,1,0:T(8,128)(2,1)S(1)}, bf16[4,96,768]{2,1,0:T(8,128)(2,1)}, u32[]{:S(2)}, u32[]{:S(2)}) %collective-permute-start.5) | collective-permute-done | bytes 589856 | tf_op jit(solution)/shard_map/ppermute | solution.py:323
  68.6 8.3 %forward.1 = (bf16[4,96,256]{2,1,0:T(8,128)(2,1)}, bf16[4,96,256]{2,1,0:T(8,128)(2,1)}, bf16[4,96,256]{2,1,0:T(8,128)(2,1)}, bf16[4,96,256]{2,1,0:T(8,128)(2,1)}, bf16[768,256]{1,0:T(8,128)(2,1)}) custom-call(s32[6]{0:T(128)} %stack.27.place_ref, s32[4,128]{1,0:T(4,128)} %copy-done.2, bf16[2,256,1024]{2,1,0:T(8,128)(2,1)} %copy-done.1, ...), custom_call_target="tpu_custom_call" | custom-call | tf_op jit(solution)/shard_map/forward/pallas_call | solution.py:186
  76.9 5.4 %all-to-all-start.1 = ((bf16[8,96,256]{2,1,0:T(8,128)(2,1)}), bf16[8,96,256]{2,1,0:T(8,128)(2,1)S(1)}, u32[]{:S(2)}, u32[]{:S(2)}) async-start(bf16[8,96,256]{2,1,0:T(8,128)(2,1)} %bitcast.7), calls=%async_computation.1 | async-start | bytes 786432 | tf_op jit(solution)/shard_map/all_to_all | solution.py:327
  84.6 5.3 %all-to-all-done.1.arrived_ref = bf16[8,96,256]{2,1,0:T(8,128)(2,1)S(1)} async-done(((bf16[8,96,256]{2,1,0:T(8,128)(2,1)}), bf16[8,96,256]{2,1,0:T(8,128)(2,1)S(1)}, u32[]{:S(2)}, u32[]{:S(2)}) %all-to-all-start.1) | async-done | bytes 393248 | tf_op jit(solution)/shard_map/all_to_all | solution.py:327
  93.9 5.1 %all-to-all-start.2 = ((bf16[8,96,256]{2,1,0:T(8,128)(2,1)}), bf16[8,96,256]{2,1,0:T(8,128)(2,1)S(1)}, u32[]{:S(2)}, u32[]{:S(2)}) async-start(bf16[8,96,256]{2,1,0:T(8,128)(2,1)} %get-tuple-element.54), calls=%async_computation.2 | async-start | bytes 786432 | tf_op jit(solution)/shard_map/all_to_all | solution.py:327
  100.6 4.0 %all-to-all-done.2 = bf16[8,96,256]{2,1,0:T(8,128)(2,1)S(1)} async-done(((bf16[8,96,256]{2,1,0:T(8,128)(2,1)}), bf16[8,96,256]{2,1,0:T(8,128)(2,1)S(1)}, u32[]{:S(2)}, u32[]{:S(2)}) %all-to-all-start.2) | async-done | bytes 393248 | tf_op jit(solution)/shard_map/all_to_all | solution.py:327
  107.1 6.3 %backward.1 = bf16[32,192,128]{2,1,0:T(8,128)(2,1)} custom-call(s32[6]{0:T(128)} %stack.27.place_ref, s32[4,128]{1,0:T(4,128)} %copy-done.2, bf16[2,256,1024]{2,1,0:T(8,128)(2,1)} %copy-done.1, bf16[2,256,1024]{2,1,0:T(8,128)(2,1)} %collective-permute-done.3.back_ref, bf16[2,256,1024]{2,1,0:T(8,128)(2,1)} %collective-permute-done.4.fore_ref, ...), custom_call_target="tpu_custom_call" | custom-call | tf_op jit(solution)/shard_map/backward/pallas_call | solution.py:248
  113.4 7.6 %all-to-all-start.3 = ((bf16[32,192,128]{2,1,0:T(8,128)(2,1)}), bf16[32,192,128]{2,1,0:T(8,128)(2,1)S(1)}, u32[]{:S(2)}, u32[]{:S(2)}) async-start(bf16[32,192,128]{2,1,0:T(8,128)(2,1)} %backward.1), calls=%async_computation.3 | async-start | bytes 3145728 | tf_op jit(solution)/shard_map/all_to_all | solution.py:327
  121.6 3.0 %collective-permute-start.12 = (bf16[4,96,256]{2,1,0:T(8,128)(2,1)}, bf16[4,96,256]{2,1,0:T(8,128)(2,1)S(1)}, u32[]{:S(2)}, u32[]{:S(2)}) collective-permute-start(bf16[4,96,256]{2,1,0:T(8,128)(2,1)} %collective-permute-done.9), channel_id=1, source_target_pairs={{0,16},{16,0},{1,17},{17,1},{2,18},{18,2},{3,19},{19,3},{4,20},{20... | collective-permute-start | bytes 589832 | tf_op jit(solution)/shard_map/ppermute | solution.py:323
  124.6 10.4 %collective-permute-done.12.far_core_ref = bf16[4,96,256]{2,1,0:T(8,128)(2,1)S(1)} collective-permute-done((bf16[4,96,256]{2,1,0:T(8,128)(2,1)}, bf16[4,96,256]{2,1,0:T(8,128)(2,1)S(1)}, u32[]{:S(2)}, u32[]{:S(2)}) %collective-permute-start.12) | collective-permute-done | bytes 196640 | tf_op jit(solution)/shard_map/ppermute | solution.py:323
  135.7 3.9 %weight_terms.1 = (f32[48,768]{1,0:T(8,128)S(1)}, bf16[48,768]{1,0:T(8,128)(2,1)S(1)}, bf16[48,768]{1,0:T(8,128)(2,1)S(1)}, bf16[48,768]{1,0:T(8,128)(2,1)}, bf1...) custom-call(s32[6]{0:T(128)} %stack.27.place_ref, ...), custom_call_target="tpu_custom_call" | custom-call | flops 24500000768 | tf_op jit(solution)/shard_map/weight_terms/pallas_call | solution.py:280
  140.2 3.0 %collective-permute-start.17 = (bf16[48,768]{1,0:T(8,128)(2,1)S(1)}, bf16[48,768]{1,0:T(8,128)(2,1)S(1)}, u32[]{:S(2)}, u32[]{:S(2)}) collective-permute-start(bf16[48,768]{1,0:T(8,128)(2,1)S(1)} %get-tuple-element.63), channel_id=1, source_target_pairs={{0,4},{2,6},{4,0},{6,2},{8,12},{10,14},{12,8},{14,10},{1,5},{3,7},... | collective-permute-start | bytes 221192 | tf_op jit(solution)/shard_map/ppermute | solution.py:323
  143.2 5.4 %collective-permute-start.19 = (bf16[48,768]{1,0:T(8,128)(2,1)}, bf16[48,768]{1,0:T(8,128)(2,1)S(1)}, u32[]{:S(2)}, u32[]{:S(2)}) collective-permute-start(bf16[48,768]{1,0:T(8,128)(2,1)} %get-tuple-element.65), channel_id=1, source_target_pairs={{0,8},{2,10},{4,12},{6,14},{8,0},{10,2},{12,4},{14,6},{1,9},{3,11}... | collective-permute-start | bytes 221192 | tf_op jit(solution)/shard_map/ppermute | solution.py:323
  150.0 8.7 %collective-permute-done.16 = bf16[48,768]{1,0:T(8,128)(2,1)S(1)} collective-permute-done((bf16[48,768]{1,0:T(8,128)(2,1)S(1)}, bf16[48,768]{1,0:T(8,128)(2,1)S(1)}, u32[]{:S(2)}, u32[]{:S(2)}) %collective-permute-start.16) | collective-permute-done | bytes 73760 | tf_op jit(solution)/shard_map/ppermute | solution.py:323
  158.7 4.0 %collective-permute-start.21 = (bf16[48,768]{1,0:T(8,128)(2,1)}, bf16[48,768]{1,0:T(8,128)(2,1)S(1)}, u32[]{:S(2)}, u32[]{:S(2)}) collective-permute-start(bf16[48,768]{1,0:T(8,128)(2,1)} %get-tuple-element.67), channel_id=1, source_target_pairs={{0,12},{2,14},{4,8},{6,10},{8,4},{10,6},{12,0},{14,2},{1,13},{3,15... | collective-permute-start | bytes 221192 | tf_op jit(solution)/shard_map/ppermute | solution.py:323
  165.1 3.4 %collective-permute-start.22 = (bf16[48,768]{1,0:T(8,128)(2,1)}, bf16[48,768]{1,0:T(8,128)(2,1)S(1)}, u32[]{:S(2)}, u32[]{:S(2)}) collective-permute-start(bf16[48,768]{1,0:T(8,128)(2,1)} %get-tuple-element.68), channel_id=1, source_target_pairs={{0,14},{2,12},{4,10},{6,8},{8,6},{10,4},{12,2},{14,0},{1,15},{3,13... | collective-permute-start | bytes 221192 | tf_op jit(solution)/shard_map/ppermute | solution.py:323
  171.0 5.7 %all-to-all-start.4 = ((f32[8,2,16,192]{3,2,1,0:T(8,128)}), f32[8,2,16,192]{3,2,1,0:T(8,128)S(1)}, u32[]{:S(2)}, u32[]{:S(2)}) async-start(f32[8,2,16,192]{3,2,1,0:T(8,128)} %owned.1), calls=%async_computation.4 | async-start | bytes 524288 | tf_op jit(solution)/shard_map/all_to_all | solution.py:327
  176.8 5.3 %collective-permute-start.23 = (f32[2,24,768]{2,1,0:T(8,128)S(1)}, f32[2,24,768]{2,1,0:T(8,128)S(1)}, u32[]{:S(2)}, u32[]{:S(2)}) collective-permute-start(f32[2,24,768]{2,1,0:T(8,128)S(1)} %bitcast.20), channel_id=1, source_target_pairs={{0,0},{1,4},{2,1},{3,5},{4,2},{5,6},{6,3},{7,7},{8,32},{9,36},{10,... | collective-permute-start | bytes 442376 | tf_op jit(solution)/shard_map/ppermute | solution.py:419
  182.2 10.1 %collective-permute-done.23 = f32[2,24,768]{2,1,0:T(8,128)S(1)} collective-permute-done((f32[2,24,768]{2,1,0:T(8,128)S(1)}, f32[2,24,768]{2,1,0:T(8,128)S(1)}, u32[]{:S(2)}, u32[]{:S(2)}) %collective-permute-start.23) | collective-permute-done | bytes 147488 | tf_op jit(solution)/shard_map/ppermute | solution.py:419
  (81 shorter events, 41.2 us)
Async XLA Ops:
  5.7 37.4 %collective-permute-start.4 = (bf16[2,256,1024]{2,1,0:T(8,128)(2,1)S(1)}, bf16[2,256,1024]{2,1,0:T(8,128)(2,1)}, u32[]{:S(2)}, u32[]{:S(2)}) collective-permute-start(bf16[2,256,1024]{2,1,0:T(8,128)(2,1)S(1)} %adjacency.1.own_ref), channel_id=1, source_target_pairs={{0,96},{32,0},{64,32},{96,64},{1,97},{33,1},{65,33},{97,65},{2,98}... | collective-permute-start | bytes 3145736 | tf_op jit(solution)/shard_map/ppermute | solution.py:319
  6.5 38.4 %collective-permute-start.3 = (bf16[2,256,1024]{2,1,0:T(8,128)(2,1)S(1)}, bf16[2,256,1024]{2,1,0:T(8,128)(2,1)}, u32[]{:S(2)}, u32[]{:S(2)}) collective-permute-start(bf16[2,256,1024]{2,1,0:T(8,128)(2,1)S(1)} %adjacency.1.own_ref), channel_id=1, source_target_pairs={{0,32},{32,64},{64,96},{96,0},{1,33},{33,65},{65,97},{97,1},{2,34}... | collective-permute-start | bytes 3145736 | tf_op jit(solution)/shard_map/ppermute | solution.py:319
  12.2 56.4 %all-to-all-start = ((bf16[32,192,128]{2,1,0:T(8,128)(2,1)}), bf16[32,192,128]{2,1,0:T(8,128)(2,1)}, u32[]{:S(2)}, u32[]{:S(2)}) async-start(bf16[32,192,128]{2,1,0:T(8,128)(2,1)} %outgoing.1), calls=%async_computation | async-start | bytes 3145728 | tf_op jit(solution)/shard_map/all_to_all | solution.py:327
  25.0 14.2 %collective-permute-start.2 = (bf16[1,112,768]{2,1,0:T(8,128)(2,1)S(1)}, bf16[1,112,768]{2,1,0:T(8,128)(2,1)S(1)}, u32[]{:S(2)}, u32[]{:S(2)}) collective-permute-start(bf16[1,112,768]{2,1,0:T(8,128)(2,1)S(1)} %get-tuple-element.75), channel_id=1, source_target_pairs={{0,96},{32,0},{64,32},{96,64},{1,97},{33,1},{65,33},{97,65},{2,98}... | collective-permute-start | bytes 516104 | tf_op jit(solution)/shard_map/ppermute | solution.py:332
  25.1 14.1 %collective-permute-start.1 = (bf16[1,112,768]{2,1,0:T(8,128)(2,1)S(1)}, bf16[1,112,768]{2,1,0:T(8,128)(2,1)S(1)}, u32[]{:S(2)}, u32[]{:S(2)}) collective-permute-start(bf16[1,112,768]{2,1,0:T(8,128)(2,1)S(1)} %get-tuple-element.76), channel_id=1, source_target_pairs={{0,64},{32,96},{64,0},{96,32},{1,65},{33,97},{65,1},{97,33},{2,66}... | collective-permute-start | bytes 516104 | tf_op jit(solution)/shard_map/ppermute | solution.py:332
  26.5 12.7 %collective-permute-start = (bf16[1,112,768]{2,1,0:T(8,128)(2,1)S(1)}, bf16[1,112,768]{2,1,0:T(8,128)(2,1)S(1)}, u32[]{:S(2)}, u32[]{:S(2)}) collective-permute-start(bf16[1,112,768]{2,1,0:T(8,128)(2,1)S(1)} %get-tuple-element.77), channel_id=1, source_target_pairs={{0,32},{32,64},{64,96},{96,0},{1,33},{33,65},{65,97},{97,1},{2,34}... | collective-permute-start | bytes 516104 | tf_op jit(solution)/shard_map/ppermute | solution.py:332
  40.0 24.0 %collective-permute-start.5 = (bf16[4,96,768]{2,1,0:T(8,128)(2,1)S(1)}, bf16[4,96,768]{2,1,0:T(8,128)(2,1)}, u32[]{:S(2)}, u32[]{:S(2)}) collective-permute-start(bf16[4,96,768]{2,1,0:T(8,128)(2,1)S(1)} %get-tuple-element.43), channel_id=1, source_target_pairs={{0,16},{16,0},{1,17},{17,1},{2,18},{18,2},{3,19},{19,3},{4,20},{20... | collective-permute-start | bytes 1769480 | tf_op jit(solution)/shard_map/ppermute | solution.py:323
  44.9 19.1 %collective-permute-start.7 = (bf16[1,256,1024]{2,1,0:T(8,128)(2,1)}, bf16[1,256,1024]{2,1,0:T(8,128)(2,1)S(1)}, u32[]{:S(2)}, u32[]{:S(2)}) collective-permute-start(bf16[1,256,1024]{2,1,0:T(8,128)(2,1)} %slice.9), channel_id=1, source_target_pairs={{0,96},{32,0},{64,32},{96,64},{1,97},{33,1},{65,33},{97,65},{2,98}... | collective-permute-start | bytes 1572872 | tf_op jit(solution)/shard_map/ppermute | solution.py:319
  46.0 18.0 %collective-permute-start.6 = (bf16[1,256,1024]{2,1,0:T(8,128)(2,1)S(1)}, bf16[1,256,1024]{2,1,0:T(8,128)(2,1)S(1)}, u32[]{:S(2)}, u32[]{:S(2)}) collective-permute-start(bf16[1,256,1024]{2,1,0:T(8,128)(2,1)S(1)} %slice.8), channel_id=1, source_target_pairs={{0,32},{32,64},{64,96},{96,0},{1,33},{33,65},{65,97},{97,1},{2,34}... | collective-permute-start | bytes 1572872 | tf_op jit(solution)/shard_map/ppermute | solution.py:319
  76.9 12.9 %all-to-all-start.1 = ((bf16[8,96,256]{2,1,0:T(8,128)(2,1)}), bf16[8,96,256]{2,1,0:T(8,128)(2,1)S(1)}, u32[]{:S(2)}, u32[]{:S(2)}) async-start(bf16[8,96,256]{2,1,0:T(8,128)(2,1)} %bitcast.7), calls=%async_computation.1 | async-start | bytes 786432 | tf_op jit(solution)/shard_map/all_to_all | solution.py:327
  104.5 16.7 %collective-permute-start.14 = (bf16[768,256]{1,0:T(8,128)(2,1)S(1)}, bf16[768,256]{1,0:T(8,128)(2,1)S(1)}, u32[]{:S(2)}, u32[]{:S(2)}) collective-permute-start(bf16[768,256]{1,0:T(8,128)(2,1)S(1)} %bitcast.13), channel_id=1, source_target_pairs={{0,16},{16,0},{1,17},{17,1},{2,18},{18,2},{3,19},{19,3},{4,20},{20... | collective-permute-start | bytes 1179656 | tf_op jit(solution)/shard_map/ppermute | solution.py:323
  113.4 55.1 %all-to-all-start.3 = ((bf16[32,192,128]{2,1,0:T(8,128)(2,1)}), bf16[32,192,128]{2,1,0:T(8,128)(2,1)S(1)}, u32[]{:S(2)}, u32[]{:S(2)}) async-start(bf16[32,192,128]{2,1,0:T(8,128)(2,1)} %backward.1), calls=%async_computation.3 | async-start | bytes 3145728 | tf_op jit(solution)/shard_map/all_to_all | solution.py:327
  121.0 14.0 %collective-permute-start.13 = (bf16[768,256]{1,0:T(8,128)(2,1)S(1)}, bf16[768,256]{1,0:T(8,128)(2,1)S(1)}, u32[]{:S(2)}, u32[]{:S(2)}) collective-permute-start(bf16[768,256]{1,0:T(8,128)(2,1)S(1)} %bitcast.15), channel_id=1, source_target_pairs={{0,1},{1,0},{2,3},{3,2},{4,5},{5,4},{6,7},{7,6},{8,9},{9,8},{10,11... | collective-permute-start | bytes 1179656 | tf_op jit(solution)/shard_map/ppermute | solution.py:323
  121.3 13.8 %collective-permute-start.15 = (bf16[768,256]{1,0:T(8,128)(2,1)S(1)}, bf16[768,256]{1,0:T(8,128)(2,1)S(1)}, u32[]{:S(2)}, u32[]{:S(2)}) collective-permute-start(bf16[768,256]{1,0:T(8,128)(2,1)S(1)} %collective-permute-done.14.far_grad_ref), channel_id=1, source_target_pairs={{0,1},{1,0},{2,3},{3,2},{4,5},{5,4},{6,7},{7,6},{8,9},{9,8},{10,11... | collective-permute-start | bytes 1179656 | tf_op jit(solution)/shard_map/ppermute | solution.py:323
  121.6 13.4 %collective-permute-start.12 = (bf16[4,96,256]{2,1,0:T(8,128)(2,1)}, bf16[4,96,256]{2,1,0:T(8,128)(2,1)S(1)}, u32[]{:S(2)}, u32[]{:S(2)}) collective-permute-start(bf16[4,96,256]{2,1,0:T(8,128)(2,1)} %collective-permute-done.9), channel_id=1, source_target_pairs={{0,16},{16,0},{1,17},{17,1},{2,18},{18,2},{3,19},{19,3},{4,20},{20... | collective-permute-start | bytes 589832 | tf_op jit(solution)/shard_map/ppermute | solution.py:323
  139.6 19.1 %collective-permute-start.16 = (bf16[48,768]{1,0:T(8,128)(2,1)S(1)}, bf16[48,768]{1,0:T(8,128)(2,1)S(1)}, u32[]{:S(2)}, u32[]{:S(2)}) collective-permute-start(bf16[48,768]{1,0:T(8,128)(2,1)S(1)} %get-tuple-element.62), channel_id=1, source_target_pairs={{0,2},{2,0},{4,6},{6,4},{8,10},{10,8},{12,14},{14,12},{1,3},{3,1},... | collective-permute-start | bytes 221192 | tf_op jit(solution)/shard_map/ppermute | solution.py:323
  140.2 24.8 %collective-permute-start.17 = (bf16[48,768]{1,0:T(8,128)(2,1)S(1)}, bf16[48,768]{1,0:T(8,128)(2,1)S(1)}, u32[]{:S(2)}, u32[]{:S(2)}) collective-permute-start(bf16[48,768]{1,0:T(8,128)(2,1)S(1)} %get-tuple-element.63), channel_id=1, source_target_pairs={{0,4},{2,6},{4,0},{6,2},{8,12},{10,14},{12,8},{14,10},{1,5},{3,7},... | collective-permute-start | bytes 221192 | tf_op jit(solution)/shard_map/ppermute | solution.py:323
  143.2 33.5 %collective-permute-start.18 = (bf16[48,768]{1,0:T(8,128)(2,1)}, bf16[48,768]{1,0:T(8,128)(2,1)S(1)}, u32[]{:S(2)}, u32[]{:S(2)}) collective-permute-start(bf16[48,768]{1,0:T(8,128)(2,1)} %get-tuple-element.64), channel_id=1, source_target_pairs={{0,6},{2,4},{4,2},{6,0},{8,14},{10,12},{12,10},{14,8},{1,7},{3,5},... | collective-permute-start | bytes 221192 | tf_op jit(solution)/shard_map/ppermute | solution.py:323
  143.2 33.5 %collective-permute-start.19 = (bf16[48,768]{1,0:T(8,128)(2,1)}, bf16[48,768]{1,0:T(8,128)(2,1)S(1)}, u32[]{:S(2)}, u32[]{:S(2)}) collective-permute-start(bf16[48,768]{1,0:T(8,128)(2,1)} %get-tuple-element.65), channel_id=1, source_target_pairs={{0,8},{2,10},{4,12},{6,14},{8,0},{10,2},{12,4},{14,6},{1,9},{3,11}... | collective-permute-start | bytes 221192 | tf_op jit(solution)/shard_map/ppermute | solution.py:323
  148.6 28.1 %collective-permute-start.20 = (bf16[48,768]{1,0:T(8,128)(2,1)}, bf16[48,768]{1,0:T(8,128)(2,1)S(1)}, u32[]{:S(2)}, u32[]{:S(2)}) collective-permute-start(bf16[48,768]{1,0:T(8,128)(2,1)} %get-tuple-element.66), channel_id=1, source_target_pairs={{0,10},{2,8},{4,14},{6,12},{8,2},{10,0},{12,6},{14,4},{1,11},{3,9}... | collective-permute-start | bytes 221192 | tf_op jit(solution)/shard_map/ppermute | solution.py:323
  158.7 18.0 %collective-permute-start.21 = (bf16[48,768]{1,0:T(8,128)(2,1)}, bf16[48,768]{1,0:T(8,128)(2,1)S(1)}, u32[]{:S(2)}, u32[]{:S(2)}) collective-permute-start(bf16[48,768]{1,0:T(8,128)(2,1)} %get-tuple-element.67), channel_id=1, source_target_pairs={{0,12},{2,14},{4,8},{6,10},{8,4},{10,6},{12,0},{14,2},{1,13},{3,15... | collective-permute-start | bytes 221192 | tf_op jit(solution)/shard_map/ppermute | solution.py:323
  165.1 11.7 %collective-permute-start.22 = (bf16[48,768]{1,0:T(8,128)(2,1)}, bf16[48,768]{1,0:T(8,128)(2,1)S(1)}, u32[]{:S(2)}, u32[]{:S(2)}) collective-permute-start(bf16[48,768]{1,0:T(8,128)(2,1)} %get-tuple-element.68), channel_id=1, source_target_pairs={{0,14},{2,12},{4,10},{6,8},{8,6},{10,4},{12,2},{14,0},{1,15},{3,13... | collective-permute-start | bytes 221192 | tf_op jit(solution)/shard_map/ppermute | solution.py:323
  171.0 21.3 %all-to-all-start.4 = ((f32[8,2,16,192]{3,2,1,0:T(8,128)}), f32[8,2,16,192]{3,2,1,0:T(8,128)S(1)}, u32[]{:S(2)}, u32[]{:S(2)}) async-start(f32[8,2,16,192]{3,2,1,0:T(8,128)} %owned.1), calls=%async_computation.4 | async-start | bytes 524288 | tf_op jit(solution)/shard_map/all_to_all | solution.py:327
  176.8 15.4 %collective-permute-start.23 = (f32[2,24,768]{2,1,0:T(8,128)S(1)}, f32[2,24,768]{2,1,0:T(8,128)S(1)}, u32[]{:S(2)}, u32[]{:S(2)}) collective-permute-start(f32[2,24,768]{2,1,0:T(8,128)S(1)} %bitcast.20), channel_id=1, source_target_pairs={{0,0},{1,4},{2,1},{3,5},{4,2},{5,6},{6,3},{7,7},{8,32},{9,36},{10,... | collective-permute-start | bytes 442376 | tf_op jit(solution)/shard_map/ppermute | solution.py:419
  (15 other events, 139.8 us)
